TPU v7x, 32 devices: a whole 2x2x4 slice. The times are simulated.
32 devices in a mesh: groups: 2 (over x), region: 8 (over z, y), head: 2 (over core).
Axes of the slice: x: 2, y: 2, z: 4, core: 2. Of those that a mesh axis runs over, the one named last changes fastest.
Arguments:
- features: bfloat16 [16384, 256], P(('groups', 'region'), 'head'), parts along dimension 0, may hold values from -6 to 6
- element_kinds: int32 [16384], P(('groups', 'region')), parts along dimension 0, may hold values from 0 to 11
- bin_cells: int32 [16384], P(('groups', 'region')), parts along dimension 0, may hold values from 0 to 16383, as said below
- kind_embed: bfloat16 [12, 256], P(None, 'head'), may hold values from -3 to 3
- norm_gain: float32 [256], replicated, may hold values from 0.5 to 1.5
- w_query: bfloat16 [256, 256], P(None, 'head'), may hold values from -10 to 10
- w_key: bfloat16 [256, 256], P(None, 'head'), may hold values from -1 to 1
- w_value: bfloat16 [256, 256], P(None, 'head'), may hold values from -0.375 to 0.375
- w_out: bfloat16 [256, 256], P('head'), may hold values from -0.375 to 0.375
- cotangent: bfloat16 [16384, 256], P(('groups', 'region'), 'head'), parts along dimension 0, may hold values from -6 to 6
Outputs:
- attended: bfloat16 [16384, 256], P(('groups', 'region'), 'head'), parts along dimension 0
- grad_feats: bfloat16 [16384, 256], P(('groups', 'region'), 'head'), parts along dimension 0
- grad_w_query: float32 [512, 256], P('groups', 'head'), parts along dimension 0
- grad_w_key: float32 [512, 256], P('groups', 'head'), parts along dimension 0
- grad_w_value: float32 [512, 256], P('groups', 'head'), parts along dimension 0
- grad_w_out: float32 [512, 256], P(('groups', 'head')), parts along dimension 0
- grad_gain: float32 [512], P('groups'), parts along dimension 0
- grad_embed: float32 [24, 256], P('groups', 'head'), parts along dimension 0
There are 2 independent parts, one for each index of `groups`. A program takes and returns all parts, laid end to end along the dimension named above; an argument that names none is the same for every part. Nothing has to cross between parts.
Inputs may be any that keep to these rules, and one draw needn't show every extreme that they name: No two elements share a cell. The bin block of a cell, bin_cells[e] // 2048, is the index of region that owns that bin. The elements of one index of region put at most 256 cells into one bin block, and in every draw some bin block receives exactly 256 from every index of region.
All inputs are finite; a program needn't handle non-finite values.
Results may differ from a plain program's by a relative error of at most 0.018.
The roundings to bfloat16 on the way count: a program that leaves them out, or rounds other values in their place, can miss the bound.
Values may be sent and summed in bfloat16 or wider, within the bound.
No kernel may reach another device: no remote copies, remote signals or barrier semaphores. Data moves between devices by JAX's collectives and lax.ppermute only.
A program may use at most 128 MiB of HBM per device.

v0:
```python
import jax
import jax.numpy as jnp
from jax import lax
from jax.sharding import PartitionSpec as P

HEAD_DIM = 32
KINDS = 12
SLOTS = 1024
BINS_DEV = 2


MASKED = -1000000000.0
EPSILON = 1e-06


def tile_pass(queries, key_rows, values, keep_mask, d_context):
    factor = queries.shape[1] ** (-0.5)
    scores = jnp.dot(queries, key_rows.T, preferred_element_type=jnp.float32) * factor
    scores = jnp.where(keep_mask[None, :] > 0, scores, MASKED)
    shifted = jnp.exp(scores - jnp.max(scores, axis=1, keepdims=True))
    probs_full = shifted / jnp.sum(shifted, axis=1, keepdims=True)
    probs_low = probs_full.astype(jnp.bfloat16)
    context = jnp.dot(probs_low, values, preferred_element_type=jnp.float32).astype(jnp.bfloat16)
    d_probs = jnp.dot(d_context, values.T, preferred_element_type=jnp.float32)
    inner = jnp.sum(probs_full * d_probs, axis=1, keepdims=True)
    d_scores = (probs_full * (d_probs - inner) * factor).astype(jnp.bfloat16)
    d_query = jnp.dot(d_scores, key_rows, preferred_element_type=jnp.float32).astype(jnp.bfloat16)
    d_key = jnp.dot(d_scores.T, queries, preferred_element_type=jnp.float32).astype(jnp.bfloat16)
    d_value = jnp.dot(probs_low.T, d_context, preferred_element_type=jnp.float32).astype(
        jnp.bfloat16
    )
    return (context, d_query, d_key, d_value)


def on_device(
    features,
    element_kinds,
    bin_cells,
    kind_embed,
    norm_gain,
    w_query,
    w_key,
    w_value,
    w_out,
    cotangent,
):
    regions = lax.axis_size("region")
    local_rows = BINS_DEV * SLOTS
    capacity = local_rows // regions
    element_count = features.shape[0]
    full_width = w_query.shape[0]
    half_width = w_query.shape[1]
    kinds_hot = (element_kinds[:, None] == jnp.arange(KINDS, dtype=jnp.int32)[None, :]).astype(
        jnp.bfloat16
    )
    base_rows = (
        features.astype(jnp.float32)
        + jnp.dot(kinds_hot, kind_embed, preferred_element_type=jnp.float32)
    ).astype(jnp.bfloat16)
    owners = bin_cells // local_rows
    owner_hot = (owners[:, None] == jnp.arange(regions, dtype=jnp.int32)[None, :]).astype(jnp.int32)
    ranked = jnp.sum(jnp.cumsum(owner_hot, axis=0) * owner_hot, axis=1) - 1
    target = owners * capacity + ranked
    tagged = (
        jnp.zeros((regions * capacity,), jnp.int32)
        .at[target]
        .set(bin_cells % local_rows + 1)
        .reshape(regions, capacity)
    )

    def packed(row_block):
        filled = (
            jnp.zeros((regions * capacity, row_block.shape[1]), row_block.dtype)
            .at[target]
            .set(row_block)
        )
        return filled.reshape(regions, capacity, row_block.shape[1])

    got_base, got_grad, got_tags = (
        lax.all_to_all(packed(base_rows), "region", split_axis=0, concat_axis=0, tiled=True),
        lax.all_to_all(packed(cotangent), "region", split_axis=0, concat_axis=0, tiled=True),
        lax.all_to_all(tagged, "region", split_axis=0, concat_axis=0, tiled=True),
    )
    got_base, got_grad = (
        lax.all_gather(got_base, "head", axis=2, tiled=True),
        lax.all_gather(got_grad, "head", axis=2, tiled=True),
    )
    tags_flat = got_tags.reshape(-1)
    landing = jnp.where(tags_flat > 0, tags_flat - 1, local_rows)
    slab = (
        jnp.zeros((local_rows, full_width), jnp.bfloat16)
        .at[landing]
        .set(got_base.reshape(-1, full_width), mode="drop")
    )
    grad_slab = (
        jnp.zeros((local_rows, full_width), jnp.bfloat16)
        .at[landing]
        .set(got_grad.reshape(-1, full_width), mode="drop")
    )
    keep_mask = jnp.zeros((local_rows,), jnp.int32).at[landing].set(1, mode="drop")
    widened = slab.astype(jnp.float32)
    inverse = lax.rsqrt(jnp.mean(widened * widened, axis=1, keepdims=True) + EPSILON)
    normed = (widened * inverse * norm_gain).astype(jnp.bfloat16)
    queries = jnp.dot(normed, w_query, preferred_element_type=jnp.float32).astype(jnp.bfloat16)
    key_rows = jnp.dot(normed, w_key, preferred_element_type=jnp.float32).astype(jnp.bfloat16)
    values = jnp.dot(normed, w_value, preferred_element_type=jnp.float32).astype(jnp.bfloat16)
    d_context = jnp.dot(grad_slab, w_out.T, preferred_element_type=jnp.float32).astype(jnp.bfloat16)
    heads_here = half_width // HEAD_DIM
    tile_count = BINS_DEV * heads_here

    def to_tiles(row_block):
        return (
            row_block.reshape(BINS_DEV, SLOTS, heads_here, HEAD_DIM)
            .transpose(0, 2, 1, 3)
            .reshape(tile_count, SLOTS, HEAD_DIM)
        )

    def from_tiles(blocks):
        return (
            blocks.reshape(BINS_DEV, heads_here, SLOTS, HEAD_DIM)
            .transpose(0, 2, 1, 3)
            .reshape(local_rows, half_width)
        )

    keep_tiles = jnp.broadcast_to(
        keep_mask.reshape(BINS_DEV, 1, SLOTS), (BINS_DEV, heads_here, SLOTS)
    ).reshape(tile_count, SLOTS)

    def run_tile(packed_tile):
        return tile_pass(*packed_tile)

    results = lax.map(
        run_tile,
        (to_tiles(queries), to_tiles(key_rows), to_tiles(values), keep_tiles, to_tiles(d_context)),
    )
    context, d_query, d_key, d_value = tuple((from_tiles(block_set) for block_set in results))
    normed_part = (
        jnp.dot(d_query, w_query.T, preferred_element_type=jnp.float32)
        + jnp.dot(d_key, w_key.T, preferred_element_type=jnp.float32)
        + jnp.dot(d_value, w_value.T, preferred_element_type=jnp.float32)
    )
    column_start = lax.axis_index("head") * half_width
    factor = float(element_count * regions) ** (-0.5)
    attn_part = jnp.dot(context, w_out, preferred_element_type=jnp.float32)
    attn_half = lax.psum_scatter(attn_part, "head", scatter_dimension=1, tiled=True)
    d_normed = lax.psum(normed_part, "head")
    scaled = norm_gain * d_normed
    d_slab = (
        inverse * scaled
        - widened * inverse**3 * jnp.sum(scaled * widened, axis=1, keepdims=True) / full_width
    )
    d_half = lax.dynamic_slice_in_dim(d_slab, column_start, half_width, 1).astype(jnp.bfloat16)
    grad_gain_part = jnp.sum(d_normed * widened * inverse, axis=0) * factor
    picked = jnp.clip(landing, 0, local_rows - 1)
    back_attn = jnp.take(attn_half.astype(jnp.bfloat16), picked, axis=0).reshape(
        regions, capacity, half_width
    )
    back_grad = jnp.take(d_half, picked, axis=0).reshape(regions, capacity, half_width)
    home_attn, home_grad = (
        lax.all_to_all(back_attn, "region", split_axis=0, concat_axis=0, tiled=True),
        lax.all_to_all(back_grad, "region", split_axis=0, concat_axis=0, tiled=True),
    )
    attended = jnp.take(home_attn.reshape(-1, half_width), target, axis=0)
    grad_feats = jnp.take(home_grad.reshape(-1, half_width), target, axis=0)
    grad_query_part = jnp.dot(normed.T, d_query, preferred_element_type=jnp.float32) * factor
    grad_key_part = jnp.dot(normed.T, d_key, preferred_element_type=jnp.float32) * factor
    grad_value_part = jnp.dot(normed.T, d_value, preferred_element_type=jnp.float32) * factor
    grad_out_part = jnp.dot(context.T, grad_slab, preferred_element_type=jnp.float32) * factor
    grad_embed_part = jnp.dot(kinds_hot.T, grad_feats, preferred_element_type=jnp.float32) * factor
    summed = lax.psum(
        (
            grad_query_part,
            grad_key_part,
            grad_value_part,
            grad_out_part,
            grad_gain_part,
            grad_embed_part,
        ),
        "region",
    )
    return (attended, grad_feats, summed[0], summed[1], summed[2], summed[3], summed[4], summed[5])


def solution(mesh):
    placed = (
        P(("groups", "region"), "head"),
        P(("groups", "region")),
        P(("groups", "region")),
        P(None, "head"),
        P(),
        P(None, "head"),
        P(None, "head"),
        P(None, "head"),
        P("head", None),
        P(("groups", "region"), "head"),
    )
    return jax.shard_map(
        on_device,
        mesh=mesh,
        in_specs=placed,
        out_specs=(
            P(("groups", "region"), "head"),
            P(("groups", "region"), "head"),
            P("groups", "head"),
            P("groups", "head"),
            P("groups", "head"),
            P(("groups", "head"), None),
            P("groups"),
            P("groups", "head"),
        ),
        check_vma=False,
    )
```

profile of v0, /device:TPU:0, one launch (start us, length us, event | category | flops | bytes accessed | tf_op | source)
XLA Modules:
  0.0 429.1 jit_solution(17076719411651091404)
XLA Ops:
  15.4 21.7 %all_to_all.29 = bf16[8,256,128]{2,1,0:T(8,128)(2,1)} all-to-all(bf16[8,256,128]{2,1,0:T(8,128)(2,1)S(1)} %bitcast.188), channel_id=1, replica_groups=mesh['groups'=2,'region'=8,'head'=2] {'region'}, dimensions={0} | all-to-all | bytes 1048576 | tf_op jit(solution)/shard_map/all_to_all | solution.py:80
  37.2 4.9 %scatter_custom_fusion = s32[2048]{0:T(1024)} fusion(s32[1024]{0:T(1024)S(1)} %get-tuple-element.109, s32[1024]{0:T(1024)S(1)} %get-tuple-element.118, s32[]{:T(128)} %constant.70.clone.1), kind=kCustom, calls=%fused_computation.121 | custom fusion | bytes 8196 | tf_op jit(solution)/shard_map/scatter | solution.py:67
  42.1 3.6 all-to-all-start
  45.7 4.4 %scatter_custom_fusion.4 = bf16[2048,128]{1,0:T(8,128)(2,1)} fusion(s32[1024]{0:T(1024)S(1)} %get-tuple-element.109, bf16[1024,128]{1,0:T(8,128)(2,1)} %param.25, bf16[]{:T(256)} %constant.71.clone.1), kind=kCustom, calls=%fused_computation.89 | custom fusion | bytes 524800 | tf_op jit(solution)/shard_map/scatter | solution.py:75
  52.2 3.8 all-to-all-start.2
  56.2 8.0 %scatter_custom_fusion.1 = s32[2048]{0:T(1024)S(1)} fusion(s32[2048]{0:T(1024)S(1)} %bitcast.203, s32[2048]{0:T(1024)S(1)} %broadcast.158, s32[]{:T(128)} %constant.70.clone.1), kind=kCustom, calls=%fused_computation.119 | custom fusion | bytes 8196 | tf_op jit(solution)/shard_map/scatter | solution.py:100
  64.3 5.3 %all-to-all-done.2 = bf16[8,256,128]{2,1,0:T(8,128)(2,1)S(1)} async-done(((bf16[8,256,128]{2,1,0:T(8,128)(2,1)}), bf16[8,256,128]{2,1,0:T(8,128)(2,1)S(1)}, u32[]{:S(2)}, u32[]{:S(2)}) %all-to-all-start.2) | async-done | bytes 524320 | tf_op jit(solution)/shard_map/all_to_all | solution.py:81
  70.5 10.1 %scatter_custom_fusion.3 = bf16[2048,256]{1,0:T(8,128)(2,1)S(1)} fusion(s32[2048]{0:T(1024)S(1)} %bitcast.204, bf16[2048,256]{1,0:T(8,128)(2,1)} %bitcast.206, bf16[]{:T(256)} %constant.71.clone.1), kind=kCustom, calls=%fused_computation.83 | custom fusion | bytes 1049088 | tf_op jit(solution)/shard_map/scatter | solution.py:93
  103.7 10.8 %scatter_custom_fusion.5 = bf16[2048,256]{1,0:T(8,128)(2,1)} fusion(s32[2048]{0:T(1024)S(1)} %bitcast.205, bf16[2048,256]{1,0:T(8,128)(2,1)} %bitcast.207, bf16[]{:T(256)} %constant.71.clone.1), kind=kCustom, calls=%fused_computation.81 | custom fusion | bytes 1049088 | tf_op jit(solution)/shard_map/scatter | solution.py:98
  124.5 137.4 %while.16 = (s32[]{:T(128)}, bf16[8,1024,32]{1,2,0:T(8,128)(2,1)}, bf16[8,1024,32]{1,2,0:T(8,128)(2,1)}, bf16[8,1024,32]{1,2,0:T(8,128)(2,1)}, bf16[8,1024,32]{1...) while((s32[]{:T(128)}, bf16[8,1024,32]{1,2,0:T(8,128)(2,1)}, ...), condition=%wide.region_14.15_spmd, body=%wide.region_10.14_spmd.sunk | while | flops 435288064 | bytes 42275952 | solution.py:132
  127.2 3.5 fusion.116
  178.7 3.5 fusion.116
  195.9 3.5 fusion.116
  230.3 3.5 fusion.116
  247.5 3.5 fusion.116
  274.7 14.4 %all-reduce.5.cloned.1.call-done = f32[2048,256]{1,0:T(8,128)} async-done(((f32[2048,256]{1,0:T(8,128)}), f32[2048,256]{1,0:T(8,128)}) %all-reduce.5.cloned.1.call-update) | async-done | bytes 2097168 | tf_op jit(solution)/shard_map/psum | solution.py:146
  292.8 6.2 %gather_fusion.2 = bf16[2048,128]{1,0:T(8,128)(2,1)S(1)} fusion(bf16[2048,128]{1,0:T(8,128)(2,1)S(1)} %fusion.41, s32[2048]{0:T(1024)S(1)} %fusion.57), kind=kCustom, calls=%fused_computation.2.clone | custom fusion | bytes 1056768 | tf_op jit(solution)/shard_map/jit(_take)/gather | solution.py:158
  303.3 6.2 %gather_fusion = bf16[2048,128]{1,0:T(8,128)(2,1)S(1)} fusion(bf16[2048,128]{1,0:T(8,128)(2,1)S(1)} %convert_element_type.63, s32[2048]{0:T(1024)S(1)} %fusion.57), kind=kCustom, calls=%fused_computation.clone | custom fusion | bytes 1056768 | tf_op jit(solution)/shard_map/jit(_take)/gather | solution.py:155
  310.8 6.0 %all-to-all-start.3 = ((bf16[8,256,128]{2,1,0:T(8,128)(2,1)}), bf16[8,256,128]{2,1,0:T(8,128)(2,1)S(1)}, u32[]{:S(2)}, u32[]{:S(2)}) async-start(bf16[8,256,128]{2,1,0:T(8,128)(2,1)} %bitcast.183), calls=%async_computation.4 | async-start | bytes 1048576 | tf_op jit(solution)/shard_map/all_to_all | solution.py:160
  319.4 12.2 %all-to-all-done.3 = bf16[8,256,128]{2,1,0:T(8,128)(2,1)S(1)} async-done(((bf16[8,256,128]{2,1,0:T(8,128)(2,1)}), bf16[8,256,128]{2,1,0:T(8,128)(2,1)S(1)}, u32[]{:S(2)}, u32[]{:S(2)}) %all-to-all-start.3) | async-done | bytes 524320 | tf_op jit(solution)/shard_map/all_to_all | solution.py:160
  331.6 3.6 all-to-all-start.4
  344.7 5.2 %all-to-all-done.4 = bf16[8,256,128]{2,1,0:T(8,128)(2,1)S(1)} async-done(((bf16[8,256,128]{2,1,0:T(8,128)(2,1)}), bf16[8,256,128]{2,1,0:T(8,128)(2,1)S(1)}, u32[]{:S(2)}, u32[]{:S(2)}) %all-to-all-start.4) | async-done | bytes 524320 | tf_op jit(solution)/shard_map/all_to_all | solution.py:161
  354.5 20.7 %all-reduce = (f32[256]{0:T(256)}, f32[12,128]{1,0:T(8,128)}) all-reduce(f32[256]{0:T(256)S(1)} %broadcast_multiply_fusion.1, f32[12,128]{1,0:T(8,128)S(1)} %convolution_multiply_fusion.4), channel_id=1, replica_groups=mesh['groups'=2,'region'=8,'head'=2] {'region'}, use_global_device_ids=true, to_apply=%region_23.26 | all-reduce | flops 1792 | bytes 14336 | tf_op jit(solution)/shard_map/psum | solution.py:170
  375.1 41.1 %all-reduce.7.cloned.1.call-done = (f32[256,128]{1,0:T(8,128)}, f32[256,128]{1,0:T(8,128)}, f32[256,128]{1,0:T(8,128)}, f32[128,256]{1,0:T(8,128)}) async-done(((f32[256,128]{1,0:T(8,128)}, f32[256,128]{1,0:T(8,128)}, f32[256,128]{1,0:T(8,128)}, f32[128,256]{1,0:T(8,128)}), (f32[256,128]{1,0:T(8,128)}, f32[256,128]{1,0:T(8,128)}, f32[256,128]{1,0:T(8,128)}, ...) | async-done | bytes 524304 | tf_op jit(solution)/shard_map/psum | solution.py:170
  (186 shorter events, 208.7 us)
Async XLA Ops:
  7.2 87.5 %copy-start = (bf16[256,128]{1,0:T(8,128)(2,1)S(1)}, bf16[256,128]{1,0:T(8,128)(2,1)}, u32[]{:S(2)}) copy-start(bf16[256,128]{1,0:T(8,128)(2,1)} %param.21) | copy-start | bytes 196612
  7.2 63.3 %all-gather.3.cloned.1.call-start = ((), (), s32[]{:S(2)}) async-start(), calls=%async_computation.6 | async-start | bytes 1572864 | tf_op jit(solution)/shard_map/all_gather | solution.py:85
  42.1 10.1 %all-to-all-start = ((s32[8,1,256]{2,1,0:T(1,128)}), s32[8,1,256]{2,1,0:T(1,128)S(1)}, u32[]{:S(2)}, u32[]{:S(2)}) async-start(s32[8,1,256]{2,1,0:T(1,128)} %bitcast.10), calls=%async_computation | async-start | bytes 16384 | tf_op jit(solution)/shard_map/all_to_all | solution.py:82
  45.7 35.3 %copy-start.13 = (bf16[256,128]{1,0:T(8,128)(2,1)S(1)}, bf16[256,128]{1,0:T(8,128)(2,1)}, u32[]{:S(2)}) copy-start(bf16[256,128]{1,0:T(8,128)(2,1)} %param.22) | copy-start | bytes 196612
  45.7 35.3 %copy-start.16 = (f32[256]{0:T(256)S(1)}, f32[256]{0:T(256)}, u32[]{:S(2)}) copy-start(f32[256]{0:T(256)} %param.20) | copy-start | bytes 3076
  52.2 17.4 %all-to-all-start.2 = ((bf16[8,256,128]{2,1,0:T(8,128)(2,1)}), bf16[8,256,128]{2,1,0:T(8,128)(2,1)S(1)}, u32[]{:S(2)}, u32[]{:S(2)}) async-start(bf16[8,256,128]{2,1,0:T(8,128)(2,1)} %bitcast.25), calls=%async_computation.2 | async-start | bytes 1048576 | tf_op jit(solution)/shard_map/all_to_all | solution.py:81
  56.0 47.6 %all-gather.5.cloned.1.call-start = ((), (), s32[]{:S(2)}) async-start(), calls=%async_computation.7 | async-start | bytes 1572864 | tf_op jit(solution)/shard_map/all_gather | solution.py:86
  70.4 218.7 %all-reduce.5.cloned.1.call-start = ((), (), s32[]{:S(2)}) async-start(), calls=%async_computation.9 | async-start | bytes 4194304 | tf_op jit(solution)/shard_map/psum | solution.py:146
  81.7 3.9 copy-start.14
  100.2 14.2 %copy-start.12 = (bf16[128,256]{1,0:T(8,128)(2,1)S(1)}, bf16[128,256]{1,0:T(8,128)(2,1)}, u32[]{:S(2)}) copy-start(bf16[128,256]{1,0:T(8,128)(2,1)} %param.24) | copy-start | bytes 196612
  263.6 1.1 copy-start.9
  263.7 0.8 copy-start.7
  263.7 1.6 copy-start.10
  265.3 1.2 copy-start.4
  268.6 33.5 %reduce-scatter.2.cloned.1.call-start = ((), (), s32[]{:S(2)}) async-start(), calls=%async_computation.8 | async-start | bytes 3145728 | tf_op jit(solution)/shard_map/reduce_scatter | solution.py:145
  270.6 0.8 copy-start.3
  289.1 2.6 copy-start.2
  310.8 24.5 %copy-start.1 = (bf16[2048,256]{1,0:T(8,128)(2,1)S(1)}, bf16[2048,256]{1,0:T(8,128)(2,1)}, u32[]{:S(2)}) copy-start(bf16[2048,256]{1,0:T(8,128)(2,1)} %scatter_custom_fusion.5) | copy-start | bytes 3145732
  310.8 20.8 %all-to-all-start.3 = ((bf16[8,256,128]{2,1,0:T(8,128)(2,1)}), bf16[8,256,128]{2,1,0:T(8,128)(2,1)S(1)}, u32[]{:S(2)}, u32[]{:S(2)}) async-start(bf16[8,256,128]{2,1,0:T(8,128)(2,1)} %bitcast.183), calls=%async_computation.4 | async-start | bytes 1048576 | tf_op jit(solution)/shard_map/all_to_all | solution.py:160
  331.6 18.3 %all-to-all-start.4 = ((bf16[8,256,128]{2,1,0:T(8,128)(2,1)}), bf16[8,256,128]{2,1,0:T(8,128)(2,1)S(1)}, u32[]{:S(2)}, u32[]{:S(2)}) async-start(bf16[8,256,128]{2,1,0:T(8,128)(2,1)} %bitcast.182), calls=%async_computation.5 | async-start | bytes 1048576 | tf_op jit(solution)/shard_map/all_to_all | solution.py:161
  335.3 81.0 %all-reduce.7.cloned.1.call-start = ((), (), s32[]{:S(2)}) async-start(), calls=%async_computation.10 | async-start | bytes 1048576 | tf_op jit(solution)/shard_map/psum | solution.py:170
  335.3 4.6 %copy-start.8 = (bf16[16,8,2,1024]{3,1,2,0:T(8,128)(2,1)S(1)}, bf16[16,8,2,1024]{3,1,2,0:T(8,128)(2,1)}, u32[]{:S(2)}) copy-start(bf16[16,8,2,1024]{3,1,2,0:T(8,128)(2,1)} %copy-done.7) | copy-start | bytes 1572868
  344.7 9.3 %copy-start.15 = (s32[1024]{0:T(1024)S(1)}, s32[1024]{0:T(1024)}, u32[]{:S(2)}) copy-start(s32[1024]{0:T(1024)} %param.17) | copy-start | bytes 12292
  354.0 68.5 %copy-start.11 = (bf16[1024,128]{1,0:T(8,128)(2,1)}, bf16[1024,128]{1,0:T(8,128)(2,1)S(1)}, u32[]{:S(2)}) copy-start(bf16[1024,128]{1,0:T(8,128)(2,1)S(1)} %get-tuple-element.227) | copy-start | bytes 786436
  (2 other events, 1.6 us)
Sparse Core Ops, SparseCore 0:
  37.3 7.7 all-gather.2
  70.6 7.8 all-gather.4
  268.7 20.3 all-reduce.4
  291.2 10.7 reduce-scatter.1
  341.6 74.6 all-reduce.6
where the time goes:
time: 432 us; the launch traced here: 429 us
  matrix products  135 us (31%)
  local copies, waits for them, and re-layouts  101 us (23%)
  waiting for transfers between devices  83.6 us (19%)
  blocking collectives  42.4 us (10%)
  other arithmetic  34.6 us (8%)
  starting transfers between devices  17.5 us (4%)
  between operations  14.2 us (3%)
    psum x1, waiting for transfers between devices, on_device(): lax.psum((grad_query_part, grad_key_part, grad_value_part, grad_out_part,...  41.1 us
    dot_general x8, matrix products, tile_pass(): jnp.dot(probs_low.T, d_context, preferred_element_type=jnp.float32)  28.2 us
    dot_general x8, matrix products, tile_pass(): jnp.dot(probs_low, values, preferred_element_type=jnp.float32)  23 us
    dot_general x8, matrix products, tile_pass(): d_probs = jnp.dot(d_context, values.T, preferred_element_type=jnp.float32)  22.5 us
    all_to_all x1, blocking collectives, on_device(): lax.all_to_all(packed(base_rows), 'region', split_axis=0, concat_axis=0,...  21.7 us
    psum x1, blocking collectives, on_device(): lax.psum((grad_query_part, grad_key_part, grad_value_part, grad_out_part,...  20.7 us
    dot_general x8, matrix products, tile_pass(): jnp.dot(d_scores.T, queries, preferred_element_type=jnp.float32)  18.4 us
    convert_element_type x8, other arithmetic, tile_pass(): d_scores = (probs_full * (d_probs - inner) * factor).astype(jnp.bfloat16)  14.7 us
  transfers between devices with their start and end apart: 9, of which 7 were waited for; matrix products, arithmetic and copies ran while one was open for 19% of the time, Pallas kernels for 0%

commit v1 on v0

v1 whole, which is shorter than its diff:
```python
import functools

import jax
import jax.numpy as jnp
from jax import lax
from jax.experimental import pallas as pl
from jax.experimental.pallas import tpu as pltpu
from jax.sharding import PartitionSpec as P

HEAD_DIM = 32
KINDS = 12
SLOTS = 1024
BINS_DEV = 2
MASKED = -1000000000.0
EPSILON = 1e-06
LOG2E = 1.4426950408889634

F32 = jnp.float32
BF16 = jnp.bfloat16
I32 = jnp.int32
LANES = 128
TAG_ROWS = 16
KIND_ROWS = 16
FAR = 1 << 20
NT = (((1,), (1,)), ((), ()))
TN = (((0,), (0,)), ((), ()))


def iota(shape, axis):
    return lax.broadcasted_iota(I32, shape, axis)


def mm(a, b):
    return jnp.dot(a, b, preferred_element_type=F32)


def mm_nt(a, b):
    return lax.dot_general(a, b, NT, preferred_element_type=F32)


def mm_tn(a, b):
    return lax.dot_general(a, b, TN, preferred_element_type=F32)


def hot(condition):
    return jnp.where(condition, 1.0, 0.0).astype(BF16)


def log2_of(n):
    return n.bit_length() - 1


def pack_kernel(regions, capacity, cells, kinds, feats, embed, cot, w_q, w_k, w_v, w_o, out_base, out_cot, out_target, out_w):
    local_rows = BINS_DEV * SLOTS
    count = feats.shape[0]
    half = feats.shape[1]
    cell = cells[...]
    kind = kinds[...]
    owner = lax.shift_right_logical(cell, log2_of(local_rows))
    local = jnp.bitwise_and(cell, local_rows - 1)
    region_rows = max(regions, 16)
    owner_hot = jnp.where(iota((region_rows, count), 0) == owner, 1.0, 0.0)
    before = hot(iota((count, count), 0) < iota((count, count), 1))
    rank = jnp.sum(mm(owner_hot.astype(BF16), before) * owner_hot, axis=0, keepdims=True)
    target = owner * capacity + rank.astype(I32)
    out_target[...] = target
    kinds_hot = hot(iota((KIND_ROWS, count), 0) == kind)
    base = (feats[...].astype(F32) + mm_tn(kinds_hot, embed[...])).astype(BF16)
    rows = jnp.concatenate([base, cot[...]], axis=1)
    place = iota((TAG_ROWS, count), 0)
    high = lax.shift_right_logical(local, 7) + 1
    low = jnp.bitwise_and(local, 127)
    tags = jnp.where(place == 0, high, jnp.where(place == 1, low, jnp.where(place == 2, kind, 0)))
    tags = tags.astype(F32).astype(BF16)
    for r in range(regions):
        chosen = hot(iota((capacity, count), 0) + r * capacity == target)
        moved = mm(chosen, rows).astype(BF16)
        out_base[r, 0:capacity, :] = moved[:, :half]
        out_cot[r, :, :] = moved[:, half:]
        tag = mm_nt(tags, chosen)
        if capacity >= LANES:
            tag = jnp.concatenate([tag[0:8, 0:LANES], tag[0:8, LANES : 2 * LANES]], axis=0)
        else:
            tag = jnp.concatenate([tag, jnp.zeros((TAG_ROWS, LANES - capacity), F32)], axis=1)
        out_base[r, capacity : capacity + TAG_ROWS, :] = tag.astype(BF16)
    out_w[0] = w_q[...]
    out_w[1] = w_k[...]
    out_w[2] = w_v[...]
    out_w[3, 0:half, :] = w_o[:, 0:half]
    out_w[3, half:, :] = w_o[:, half:]


def group_kernel(regions, capacity, core, got, mine, theirs, out_landing, out_info, flat):
    total = regions * capacity
    tag_rows = jnp.zeros((8, total), F32) if capacity < LANES else None
    pieces = []
    for r in range(regions):
        flat[r * capacity : (r + 1) * capacity, :] = got[r, 0:capacity, :]
        block = got[r, capacity : capacity + TAG_ROWS, :]
        if capacity >= LANES:
            block = block.astype(F32)
            pieces += [block[0:8], block[8:16]]
        else:
            shift = hot(iota((LANES, total), 1) == iota((LANES, total), 0) + r * capacity)
            lanes = jnp.where(iota(block.shape, 1) < capacity, block.astype(F32), 0.0).astype(BF16)
            tag_rows = tag_rows + mm(lanes, shift)[0:8]
    if capacity >= LANES:
        tag_rows = jnp.concatenate(pieces, axis=1)
    tag_rows = tag_rows[0:8]
    high = tag_rows[0:1]
    low = tag_rows[1:2]
    kind = tag_rows[2:3]
    filled = high > 0.5
    local = ((high - 1.0) * 128.0 + low).astype(I32)
    swapped = jnp.bitwise_xor(local, core[0] * SLOTS)
    landing = jnp.where(filled, swapped, FAR)
    out_landing[...] = landing
    place = iota((16, total), 0)
    facts = jnp.where(place == 0, jnp.where(filled, 1.0, 0.0), jnp.where(place == 1, kind, 0.0)).astype(BF16)
    step = 256
    for s in range(0, 2 * SLOTS, step):
        chosen = hot(iota((step, total), 0) + s == landing)
        rows = mm(chosen, flat[...]).astype(BF16)
        if s < SLOTS:
            mine[s : s + step, :] = rows
            out_info[:, s : s + step] = mm_nt(facts, chosen)
        else:
            theirs[s - SLOTS : s - SLOTS + step, :] = rows


def regroup_kernel(regions, capacity, landing_ref, got, mine, theirs):
    total = regions * capacity
    landing = landing_ref[...]
    flat = got[...].reshape(total, got.shape[2])
    step = 256
    for s in range(0, 2 * SLOTS, step):
        chosen = hot(iota((step, total), 0) + s == landing)
        rows = mm(chosen, flat).astype(BF16)
        if s < SLOTS:
            mine[s : s + step, :] = rows
        else:
            theirs[s - SLOTS : s - SLOTS + step, :] = rows


def ungroup_kernel(regions, capacity, landing_ref, mine, other, out):
    total = regions * capacity
    column = jnp.transpose(jnp.broadcast_to(landing_ref[...].astype(F32), (8, total)))[:, 0:1]
    column = column.astype(I32)
    both = jnp.concatenate([mine[...], other[...]], axis=0)
    step = 256
    for s in range(0, total, step):
        chosen = hot(iota((step, 2 * SLOTS), 1) == column[s : s + step])
        rows = mm(chosen, both).astype(BF16)
        if capacity >= step:
            out[s // capacity, s % capacity : s % capacity + step, :] = rows
        else:
            for k in range(step // capacity):
                out[s // capacity + k] = rows[k * capacity : (k + 1) * capacity]


def pick_kernel(target_ref, got, out):
    total = got.shape[0] * got.shape[1]
    count = out.shape[0]
    column = jnp.transpose(jnp.broadcast_to(target_ref[...].astype(F32), (8, count)))[:, 0:1].astype(I32)
    flat = got[...].reshape(total, got.shape[2])
    step = 256
    for s in range(0, count, step):
        chosen = hot(iota((step, total), 1) == column[s : s + step])
        out[s : s + step, :] = mm(chosen, flat).astype(BF16)


def ordered(flag, own, other):
    first = jnp.where(flag, other, own)
    second = jnp.where(flag, own, other)
    return first, second


def full_weights(core, own, other):
    flag = core[0] > 0
    half = own.shape[2]
    columns = []
    for k in range(3):
        columns.append(jnp.concatenate(ordered(flag, own[k], other[k]), axis=1))
    top, bottom = ordered(flag, own[3], other[3])
    rows = [jnp.concatenate([part[0:half], part[half:]], axis=1) for part in (top, bottom)]
    return columns + [jnp.concatenate(rows, axis=0)]


def norm_rows(slab, gain, width):
    wide = slab.astype(F32)
    inverse = lax.rsqrt(jnp.sum(wide * wide, axis=1, keepdims=True) / width + EPSILON)
    return wide, inverse, (wide * inverse * gain).astype(BF16)


def spare_lanes(h, heads):
    last = heads * HEAD_DIM - 1
    is_last = h == heads - 1
    return jnp.where(is_last, 0, last), jnp.where(is_last, 1, last - 1)


def forward_kernel(
    heads, core, mine, other, w_own, w_other, gain, info, queries_out, keys_out, values_out, exps_out, context_out, inv_out,
    keep_out, send_out, queries, keys_t, values, w_out, context
):
    h = pl.program_id(0)
    width = heads * HEAD_DIM
    half = width // 2
    flag = core[0] > 0
    lane = iota((1, width), 1)
    scale = HEAD_DIM**-0.5

    @pl.when(h == 0)
    def _():
        w_q, w_k, w_v, w_o = full_weights(core, w_own, w_other)
        w_out[...] = w_o
        slab = jnp.concatenate(ordered(flag, mine[...], other[...]), axis=1)
        _, _, normed = norm_rows(slab, gain[...], width)
        q = mm(normed, w_q).astype(BF16)
        queries[...] = q
        queries_out[...] = q
        k = mm(normed, w_k)
        k_low = k.astype(BF16)
        keys_out[...] = k_low
        k_t = jnp.transpose(k_low.astype(F32))
        bias = jnp.where(info[0:1, :] > 0.5, 0.0, MASKED / scale)
        row = iota(k_t.shape, 0)
        keys_t[0] = jnp.where(row == width - 1, bias, k_t).astype(BF16)
        keys_t[1] = jnp.where(row == 0, bias, k_t).astype(BF16)
        v = mm(normed, w_v).astype(BF16)
        values_out[...] = v
        v_wide = v.astype(F32)
        values[0] = jnp.where(lane == width - 1, 1.0, v_wide).astype(BF16)
        values[1] = jnp.where(lane == 0, 1.0, v_wide).astype(BF16)
        inv_out[...] = jnp.zeros_like(inv_out)

    spare, _ = spare_lanes(h, heads)
    side = jnp.where(h == heads - 1, 1, 0)
    own_lane = lax.shift_right_logical(lane, log2_of(HEAD_DIM)) == h
    step = 256
    for s in range(0, SLOTS, step):
        rows = slice(s, s + step)
        q = jnp.where(own_lane, queries[rows, :].astype(F32), jnp.where(lane == spare, 1.0, 0.0)).astype(BF16)
        scores = mm(q, keys_t[side])
        top = jnp.max(scores, axis=1, keepdims=True)
        exps = jnp.exp2((scores - top) * (scale * LOG2E)).astype(BF16)
        exps_out[0, rows, :] = exps
        summed = mm(exps, values[side])
        inv = 1.0 / jnp.sum(jnp.where(lane == spare, summed, 0.0), axis=1, keepdims=True)
        context[rows, :] = jnp.where(own_lane, summed * inv, context[rows, :])
        lane_small = iota((1, LANES), 1)
        inv_out[rows, :] = jnp.where(lane_small == h, inv, inv_out[rows, :])

    @pl.when(h == heads - 1)
    def _():
        context_out[...] = context[...]
        rows_out = mm(context[...].astype(BF16), w_out[...]).astype(BF16)
        keep_out[...] = jnp.where(flag, rows_out[:, half:], rows_out[:, :half])
        send_out[...] = jnp.where(flag, rows_out[:, :half], rows_out[:, half:])


def backward_kernel(
    heads, core, mine, other, g_mine, g_other, w_own, w_other, gain, info, queries_in, keys_in, values_in, exps_in, context_in,
    inv_in, keep_out, send_out, grad_keep, grad_send, values_t, queries_t, d_context, d_context_t, inv_t, d_query, d_key_t, d_value_t
):
    h = pl.program_id(0)
    width = heads * HEAD_DIM
    half = width // 2
    flag = core[0] > 0
    lane = iota((1, width), 1)
    lane_small = iota((1, LANES), 1)
    scale = HEAD_DIM**-0.5

    def grad_rows():
        return jnp.concatenate(ordered(flag, g_mine[...], g_other[...]), axis=1)

    @pl.when(h == 0)
    def _():
        w_o = full_weights(core, w_own, w_other)[3]
        dc = mm_nt(grad_rows(), w_o).astype(BF16)
        d_context[...] = dc
        d_context_t[...] = jnp.transpose(dc.astype(F32)).astype(BF16)
        inv_t[...] = jnp.transpose(inv_in[...])
        v_t = jnp.transpose(values_in[...].astype(F32))
        row = iota(v_t.shape, 0)
        values_t[0] = jnp.where(row >= width - 2, 1.0, v_t).astype(BF16)
        values_t[1] = jnp.where(row <= 1, 1.0, v_t).astype(BF16)
        queries_t[...] = jnp.transpose(queries_in[...].astype(F32)).astype(BF16)

    spare, spare_low = spare_lanes(h, heads)
    side = jnp.where(h == heads - 1, 1, 0)
    own_lane = lax.shift_right_logical(lane, log2_of(HEAD_DIM)) == h
    base = pl.multiple_of(h * HEAD_DIM, HEAD_DIM)
    head_rows = pl.ds(base, HEAD_DIM)
    inv_row = inv_t[pl.ds(h, 1), :]
    step = 256
    dk = jnp.zeros((HEAD_DIM, SLOTS), F32)
    dv = jnp.zeros((HEAD_DIM, SLOTS), F32)
    for s in range(0, SLOTS, step):
        rows = slice(s, s + step)
        inv = jnp.sum(jnp.where(lane_small == h, inv_in[rows, :], 0.0), axis=1, keepdims=True)
        scaled = jnp.where(own_lane, d_context[rows, :].astype(F32) * inv, 0.0).astype(BF16)
        wide = scaled.astype(F32)
        dot = -jnp.sum(wide * context_in[rows, :], axis=1, keepdims=True)
        dot_high = dot.astype(BF16).astype(F32)
        dot_low = dot - dot_high
        left = jnp.where(lane == spare, dot_high, jnp.where(lane == spare_low, dot_low, wide)).astype(BF16)
        centred = mm(left, values_t[side])
        exps = exps_in[0, rows, :]
        d_scores = (exps.astype(F32) * centred).astype(BF16)
        dq = mm(d_scores, keys_in[...])
        d_query[rows, :] = jnp.where(own_lane, dq * scale, d_query[rows, :])
        dk = dk + mm(queries_t[head_rows, rows], d_scores)
        scaled_t = (d_context_t[head_rows, rows].astype(F32) * inv_row[:, rows]).astype(BF16)
        dv = dv + mm(scaled_t, exps)
    d_key_t[head_rows, :] = dk * scale
    d_value_t[head_rows, :] = dv

    @pl.when(h == heads - 1)
    def _():
        w_q, w_k, w_v, _ = full_weights(core, w_own, w_other)
        slab = jnp.concatenate(ordered(flag, mine[...], other[...]), axis=1)
        wide, inverse, normed = norm_rows(slab, gain[...], width)
        dq = d_query[...].astype(BF16)
        dk = jnp.transpose(d_key_t[...]).astype(BF16)
        dv = jnp.transpose(d_value_t[...]).astype(BF16)
        d_normed = mm_nt(dq, w_q) + mm_nt(dk, w_k) + mm_nt(dv, w_v)
        scaled = gain[...] * d_normed
        along = jnp.sum(scaled * wide, axis=1, keepdims=True)
        d_slab = (inverse * scaled - wide * (inverse * inverse * inverse) * along / width).astype(BF16)
        keep_out[...] = jnp.where(flag, d_slab[:, half:], d_slab[:, :half])
        send_out[...] = jnp.where(flag, d_slab[:, :half], d_slab[:, half:])
        normed_t = jnp.transpose(normed.astype(F32)).astype(BF16)
        context_t = jnp.transpose(context_in[...]).astype(BF16)
        place = 0
        for d_rows in (dq, dk, dv):
            grad = mm(normed_t, d_rows)
            grad_keep[place : place + width, :] = jnp.where(flag, grad[:, half:], grad[:, :half])
            grad_send[place : place + width, :] = jnp.where(flag, grad[:, :half], grad[:, half:]).astype(BF16)
            place += width
        grad = mm(context_t, grad_rows())
        for part in range(2):
            block = grad[:, part * half : (part + 1) * half]
            grad_keep[place : place + half, :] = jnp.where(flag, block[half:], block[:half])
            grad_send[place : place + half, :] = jnp.where(flag, block[:half], block[half:]).astype(BF16)
            place += half
        kinds_hot = hot(jnp.logical_and(iota((KIND_ROWS, SLOTS), 0) == info[1:2, :].astype(I32), info[0:1, :] > 0.5))
        grad = mm(kinds_hot, d_slab)
        grad_keep[place : place + KIND_ROWS, :] = jnp.where(flag, grad[:, half:], grad[:, :half])
        grad_send[place : place + KIND_ROWS, :] = jnp.where(flag, grad[:, :half], grad[:, half:]).astype(BF16)
        place += KIND_ROWS
        gain_grad = jnp.sum(d_normed * wide * inverse, axis=0, keepdims=True)
        pick = iota((16, half), 0)
        block = jnp.where(pick == 0, gain_grad[:, :half], jnp.where(pick == 1, gain_grad[:, half:], 0.0))
        grad_keep[place : place + 16, :] = block
        grad_send[place : place + 16, :] = block.astype(BF16)
        place += 16
        rest = grad_keep.shape[0] - place
        if rest:
            grad_keep[place:, :] = jnp.zeros((rest, half), F32)
            grad_send[place:, :] = jnp.zeros((rest, half), BF16)


def shape(dims, dtype):
    return jax.ShapeDtypeStruct(tuple(dims), dtype)


SMEM_SPEC = pl.BlockSpec(memory_space=pltpu.SMEM)


def whole(array):
    zeros = (0,) * len(array.shape)
    return pl.BlockSpec(tuple(array.shape), lambda *_: zeros)


def simple_call(kernel, outs, name, inputs, scratch=(), scalars=0):
    specs = [SMEM_SPEC] * scalars + [whole(x) for x in inputs[scalars:]]
    return pl.pallas_call(
        kernel,
        out_shape=outs,
        in_specs=specs,
        out_specs=tuple(whole(x) for x in outs),
        scratch_shapes=scratch,
        name=name,
    )(*inputs)


def on_device(
    features,
    element_kinds,
    bin_cells,
    kind_embed,
    norm_gain,
    w_query,
    w_key,
    w_value,
    w_out,
    cotangent,
):
    regions = lax.axis_size("region")
    cores = lax.axis_size("head")
    local_rows = BINS_DEV * SLOTS
    capacity = local_rows // regions
    count, half = features.shape
    width = w_query.shape[0]
    heads = width // HEAD_DIM
    assert cores == BINS_DEV and half * cores == width and half == LANES
    core = lax.axis_index("head").astype(I32).reshape(1)
    swap = [(i, (i + 1) % cores) for i in range(cores)]

    def other_core(x):
        return lax.ppermute(x, "head", swap)

    def exchange(x):
        return lax.all_to_all(x, "region", split_axis=0, concat_axis=0, tiled=True)

    embed = jnp.concatenate([kind_embed, jnp.zeros((KIND_ROWS - KINDS, half), BF16)], axis=0)
    gain = norm_gain.reshape(1, width)
    packed_base, packed_cot, target, w_own = simple_call(
        functools.partial(pack_kernel, regions, capacity),
        (
            shape((regions, capacity + TAG_ROWS, half), BF16),
            shape((regions, capacity, half), BF16),
            shape((1, count), I32),
            shape((4, width, half), BF16),
        ),
        "pack",
        (bin_cells.reshape(1, count), element_kinds.reshape(1, count), features, embed, cotangent, w_query, w_key, w_value, w_out),
    )
    w_other = other_core(w_own)
    got_base = exchange(packed_base)
    got_cot = exchange(packed_cot)
    rows_shape = shape((SLOTS, half), BF16)
    mine, theirs, landing, info = simple_call(
        functools.partial(group_kernel, regions, capacity),
        (rows_shape, rows_shape, shape((1, local_rows), I32), shape((16, SLOTS), F32)),
        "group",
        (core, got_base),
        scratch=(pltpu.VMEM((local_rows, half), BF16),),
        scalars=1,
    )
    other = other_core(theirs)

    full_shape = shape((SLOTS, width), BF16)
    exps_shape = shape((heads, SLOTS, SLOTS), BF16)
    exps_spec = pl.BlockSpec((1, SLOTS, SLOTS), lambda h: (h, 0, 0))
    inputs = (core, mine, other, w_own, w_other, gain, info)
    outs = (
        full_shape,
        full_shape,
        full_shape,
        exps_shape,
        shape((SLOTS, width), F32),
        shape((SLOTS, LANES), F32),
        rows_shape,
        rows_shape,
    )
    work = heads * SLOTS * SLOTS
    queries, keys, values, exps, context, inv, attn_keep, attn_send = pl.pallas_call(
        functools.partial(forward_kernel, heads),
        grid=(heads,),
        out_shape=outs,
        in_specs=[SMEM_SPEC] + [whole(x) for x in inputs[1:]],
        out_specs=tuple(exps_spec if x is exps_shape else whole(x) for x in outs),
        scratch_shapes=(
            pltpu.VMEM((SLOTS, width), BF16),
            pltpu.VMEM((2, width, SLOTS), BF16),
            pltpu.VMEM((2, SLOTS, width), BF16),
            pltpu.VMEM((width, width), BF16),
            pltpu.VMEM((SLOTS, width), F32),
        ),
        cost_estimate=pl.CostEstimate(flops=4 * work * width, transcendentals=work, bytes_accessed=2 * work),
        name="forward",
    )(*inputs)
    attn_other = other_core(attn_send)

    g_mine, g_theirs = simple_call(
        functools.partial(regroup_kernel, regions, capacity), (rows_shape, rows_shape), "regroup", (landing, got_cot)
    )
    g_other = other_core(g_theirs)

    unit = 16 * regions
    grad_rows = -(-(4 * width + KIND_ROWS + 16) // unit) * unit
    inputs = (core, mine, other, g_mine, g_other, w_own, w_other, gain, info, queries, keys, values, exps, context, inv)
    outs = (rows_shape, rows_shape, shape((grad_rows, half), F32), shape((grad_rows, half), BF16))
    d_keep, d_send, grad_keep, grad_send = pl.pallas_call(
        functools.partial(backward_kernel, heads),
        grid=(heads,),
        out_shape=outs,
        in_specs=[SMEM_SPEC] + [exps_spec if x is exps else whole(x) for x in inputs[1:]],
        out_specs=tuple(whole(x) for x in outs),
        scratch_shapes=(
            pltpu.VMEM((2, width, SLOTS), BF16),
            pltpu.VMEM((width, SLOTS), BF16),
            pltpu.VMEM((SLOTS, width), BF16),
            pltpu.VMEM((width, SLOTS), BF16),
            pltpu.VMEM((LANES, SLOTS), F32),
            pltpu.VMEM((SLOTS, width), F32),
            pltpu.VMEM((width, SLOTS), F32),
            pltpu.VMEM((width, SLOTS), F32),
        ),
        cost_estimate=pl.CostEstimate(flops=8 * work * width, transcendentals=0, bytes_accessed=2 * work),
        name="backward",
    )(*inputs)

    packed_shape = shape((regions, capacity, half), BF16)

    def back(keep, received):
        (packed,) = simple_call(
            functools.partial(ungroup_kernel, regions, capacity), (packed_shape,), "ungroup", (landing, keep, received)
        )
        home = exchange(packed)
        (rows,) = simple_call(pick_kernel, (shape((count, half), BF16),), "pick", (target, home))
        return rows

    attended = back(attn_keep, attn_other)
    grad_feats = back(d_keep, other_core(d_send))

    part = (grad_keep + other_core(grad_send).astype(F32)).astype(BF16)
    shares = exchange(part.reshape(regions, grad_rows // regions, half))
    share = jnp.sum(shares.astype(F32), axis=0).astype(BF16)
    summed = exchange(jnp.broadcast_to(share[None], (regions,) + share.shape)).reshape(grad_rows, half)
    total = summed.astype(F32) * float(count * regions) ** (-0.5)
    place = 3 * width
    grad_out = jnp.concatenate([total[place : place + half], total[place + half : place + width]], axis=1)
    place += width
    grad_embed = total[place : place + KINDS]
    place += KIND_ROWS
    grad_gain = total[place : place + 2].reshape(width)
    return (
        attended,
        grad_feats,
        total[0:width],
        total[width : 2 * width],
        total[2 * width : 3 * width],
        grad_out,
        grad_gain,
        grad_embed,
    )


def solution(mesh):
    placed = (
        P(("groups", "region"), "head"),
        P(("groups", "region")),
        P(("groups", "region")),
        P(None, "head"),
        P(),
        P(None, "head"),
        P(None, "head"),
        P(None, "head"),
        P("head", None),
        P(("groups", "region"), "head"),
    )
    return jax.shard_map(
        on_device,
        mesh=mesh,
        in_specs=placed,
        out_specs=(
            P(("groups", "region"), "head"),
            P(("groups", "region"), "head"),
            P("groups", "head"),
            P("groups", "head"),
            P("groups", "head"),
            P(("groups", "head"), None),
            P("groups"),
            P("groups", "head"),
        ),
        check_vma=False,
    )
```

time: 432 us -> 170 us (0.39)
  matrix products: 135 us -> 0 us
  local copies, waits for them, and re-layouts: 101 us -> 7.7 us
  Pallas kernels: 0 us -> 76.5 us
  waiting for transfers between devices: 83.6 us -> 38.8 us
  other arithmetic: 34.6 us -> 2.62 us
  blocking collectives: 42.4 us -> 23.4 us
  between operations: 14.2 us -> 0.74 us
    dot_general x62 -> x0, matrix products: 135 us -> none  [the longest x8 28.2 us: tile_pass(): jnp.dot(probs_low.T, d_context, preferred_element_type=jnp.float32)]
    pallas_call x0 -> x9, Pallas kernels: none -> 76.5 us  [the longest x7 32.3 us: simple_call(): pl.pallas_call(kernel, out_shape=outs, in_specs=specs, out_specs=tuple((w...]
    psum x2 -> x0, waiting for transfers between devices: 55.5 us -> none  [the longest x1 41.1 us: on_device(): lax.psum((grad_query_part, grad_key_part, grad_value_part, grad_out_part,...]
    scatter x6 -> x0, local copies, waits for them, and re-layouts: 41.5 us -> none  [the longest x1 10.8 us: on_device(): grad_slab = jnp.zeros((local_rows, full_width), jnp.bfloat16).at[landing]...]
    reshape x13 -> x1, local copies, waits for them, and re-layouts: 25.1 us -> 0.56 us  [on_device(): grad_gain = total[place:place + 2].reshape(width)]
    psum x1 -> x0, blocking collectives: 20.7 us -> none  [on_device(): lax.psum((grad_query_part, grad_key_part, grad_value_part, grad_out_part,...]
    gather x4 -> x0, local copies, waits for them, and re-layouts: 18.8 us -> none  [the longest x1 6.19 us: on_device(): jnp.take(d_half, picked, axis=0).reshape(regions, capacity, half_width)]
    convert_element_type x12 -> x1, other arithmetic: 18.5 us -> 1.87 us  [on_device(): part = (grad_keep + other_core(grad_send).astype(F32)).astype(BF16)]
  transfers between devices with their start and end apart: 9 -> 11, of which waited for: 7 -> 8; matrix products, arithmetic and copies ran while one was open for 19% -> 0% of each run, Pallas kernels for 0% -> 28%
where the time goes in v1:
time: 170 us; the launch traced here: 169 us
  Pallas kernels  76.5 us (45%)
  waiting for transfers between devices  38.8 us (23%)
  blocking collectives  23.4 us (14%)
  starting transfers between devices  19.4 us (11%)
  local copies, waits for them, and re-layouts  7.7 us (5%)
  other arithmetic  2.62 us (2%)
    all_to_all x5, waiting for transfers between devices, exchange(): return lax.all_to_all(x, 'region', split_axis=0, concat_axis=0, tiled=True)  34.3 us
    pallas_call x7, Pallas kernels, simple_call(): pl.pallas_call(kernel, out_shape=outs, in_specs=specs, out_specs=tuple((w...  32.3 us
    pallas_call x1, Pallas kernels, on_device(): pl.pallas_call(functools.partial(backward_kernel, heads), grid=(heads,),...  23.8 us
    all_to_all x1, blocking collectives, exchange(): return lax.all_to_all(x, 'region', split_axis=0, concat_axis=0, tiled=True)  23.4 us
    pallas_call x1, Pallas kernels, on_device(): pl.pallas_call(functools.partial(forward_kernel, heads), grid=(heads,), o...  20.4 us
    all_to_all x5, starting transfers between devices, exchange(): return lax.all_to_all(x, 'region', split_axis=0, concat_axis=0, tiled=True)  18.1 us
    ppermute x6, waiting for transfers between devices, other_core(): return lax.ppermute(x, 'head', swap)  4.54 us
    unnamed x18, local copies, waits for them, and re-layouts  3.68 us
  transfers between devices with their start and end apart: 11, of which 8 were waited for; matrix products, arithmetic and copies ran while one was open for 0% of the time, Pallas kernels for 28%

profile of v1, /device:TPU:0, one launch (start us, length us, event | category | flops | bytes accessed | tf_op | source)
XLA Modules:
  0.0 169.1 jit_solution(15086176221943362013)
XLA Ops:
  1.9 4.8 %pack.1 = (bf16[8,272,128]{2,1,0:T(8,128)(2,1)}, bf16[8,256,128]{2,1,0:T(8,128)(2,1)}, s32[1,1024]{1,0:T(1,128)}, bf16[4,256,128]{2,1,0:T(8,128)(2,1)}) custom-call(s32[1,1024]{1,0:T(1,128)} %bitcast.12, s32[1,1024]{1,0:T(1,128)} %bitcast.13, bf16[1024,128]{1,0:T(8,128)(2,1)} %feats.1, bf16[16,128]{1,0:T(8,128)(2,1)} %concatenate.6.embed, ...), custom_call_target="tpu_custom_call" | custom-call | tf_op jit(solution)/shard_map/pack/pallas_call | solution.py:377
  6.8 23.4 %all_to_all.30.got = bf16[8,272,128]{2,1,0:T(8,128)(2,1)} all-to-all(bf16[8,272,128]{2,1,0:T(8,128)(2,1)} %get-tuple-element.31), channel_id=1, replica_groups=mesh['groups'=2,'region'=8,'head'=2] {'region'}, dimensions={0} | all-to-all | bytes 1114112 | tf_op jit(solution)/shard_map/all_to_all | solution.py:414
  30.1 3.5 %all-to-all-start.2 = ((bf16[8,256,128]{2,1,0:T(8,128)(2,1)}), bf16[8,256,128]{2,1,0:T(8,128)(2,1)S(1)}, u32[]{:S(2)}, u32[]{:S(2)}) async-start(bf16[8,256,128]{2,1,0:T(8,128)(2,1)} %get-tuple-element.39), calls=%async_computation.2 | async-start | bytes 1048576 | tf_op jit(solution)/shard_map/all_to_all | solution.py:414
  33.7 5.2 %group.1 = (bf16[1024,128]{1,0:T(8,128)(2,1)}, bf16[1024,128]{1,0:T(8,128)(2,1)}, s32[1,2048]{1,0:T(1,128)}, f32[16,1024]{1,0:T(8,128)}) custom-call(s32[1]{0:T(128)} %bitcast.2.core, bf16[8,272,128]{2,1,0:T(8,128)(2,1)} %all_to_all.30.got), custom_call_target="tpu_custom_call" | custom-call | tf_op jit(solution)/shard_map/group/pallas_call | solution.py:377
  39.4 8.0 %all-to-all-done.2.got = bf16[8,256,128]{2,1,0:T(8,128)(2,1)S(1)} async-done(((bf16[8,256,128]{2,1,0:T(8,128)(2,1)}), bf16[8,256,128]{2,1,0:T(8,128)(2,1)S(1)}, u32[]{:S(2)}, u32[]{:S(2)}) %all-to-all-start.2) | async-done | bytes 524320 | tf_op jit(solution)/shard_map/all_to_all | solution.py:414
  48.2 4.1 %regroup.1 = (bf16[1024,128]{1,0:T(8,128)(2,1)}, bf16[1024,128]{1,0:T(8,128)(2,1)}) custom-call(s32[1,2048]{1,0:T(1,128)} %get-tuple-element.32.landing_ref, bf16[8,256,128]{2,1,0:T(8,128)(2,1)} %copy-done.1), custom_call_target="tpu_custom_call" | custom-call | tf_op jit(solution)/shard_map/regroup/pallas_call | solution.py:377
  53.1 20.4 %forward.1 = (bf16[1024,256]{1,0:T(8,128)(2,1)}, bf16[1024,256]{1,0:T(8,128)(2,1)}, bf16[1024,256]{1,0:T(8,128)(2,1)}, bf16[8,1024,1024]{2,1,0:T(8,128)(2,1)}, f...) custom-call(s32[1]{0:T(128)} %bitcast.2.core, ...), custom_call_target="tpu_custom_call" | custom-call | flops 8589934592 | bytes 16777216 | tf_op jit(solution)/shard_map/forward/pallas_call | solution.py:458
  74.2 23.8 %backward.1 = (bf16[1024,128]{1,0:T(8,128)(2,1)}, bf16[1024,128]{1,0:T(8,128)(2,1)}, f32[1152,128]{1,0:T(8,128)}, bf16[1152,128]{1,0:T(8,128)(2,1)}) custom-call(s32[1]{0:T(128)} %bitcast.2.core, bf16[1024,128]{1,0:T(8,128)(2,1)} %get-tuple-element.33.mine, bf16[1024,128]{1,0:T(8,128)(2,1)} %copy-done.7, bf16[1024,128]{1,0:T(8,128)(2,1)} %get-tuple-element.40.g_mine, ...), custom_call_target="tpu_custom_call" | custom-call | flops 17179869184 | bytes 16777216 | tf_op jit(solution)/shard_map/backward/pallas_call | solution.py:485
  98.5 1.4 collective-permute-done.5
  99.9 1.9 %add_convert_fusion = bf16[1152,128]{1,0:T(8,128)(2,1)} fusion(f32[1152,128]{1,0:T(8,128)} %get-tuple-element.50, bf16[1152,128]{1,0:T(8,128)(2,1)S(1)} %collective-permute-done.5), kind=kLoop, calls=%fused_computation.1 | loop fusion | flops 442368 | bytes 1179648 | tf_op jit(solution)/shard_map/convert_element_type | solution.py:518
  101.8 3.6 %all-to-all-start.4 = ((bf16[8,144,128]{2,1,0:T(8,128)(2,1)}), bf16[8,144,128]{2,1,0:T(8,128)(2,1)S(1)}, u32[]{:S(2)}, u32[]{:S(2)}) async-start(bf16[8,144,128]{2,1,0:T(8,128)(2,1)} %bitcast.4), calls=%async_computation.4 | async-start | bytes 589824 | tf_op jit(solution)/shard_map/all_to_all | solution.py:414
  105.7 1.4 collective-permute-done.2.other
  107.8 5.4 %ungroup.2 = bf16[8,256,128]{2,1,0:T(8,128)(2,1)} custom-call(s32[1,2048]{1,0:T(1,128)} %get-tuple-element.32.landing_ref, bf16[1024,128]{1,0:T(8,128)(2,1)} %get-tuple-element.37.mine, bf16[1024,128]{1,0:T(8,128)(2,1)} %copy-done.4), custom_call_target="tpu_custom_call" | custom-call | tf_op jit(solution)/shard_map/ungroup/pallas_call | solution.py:377
  113.2 2.4 %all-to-all-done.4 = bf16[8,144,128]{2,1,0:T(8,128)(2,1)S(1)} async-done(((bf16[8,144,128]{2,1,0:T(8,128)(2,1)}), bf16[8,144,128]{2,1,0:T(8,128)(2,1)S(1)}, u32[]{:S(2)}, u32[]{:S(2)}) %all-to-all-start.4) | async-done | bytes 294944 | tf_op jit(solution)/shard_map/all_to_all | solution.py:414
  115.6 3.6 %all-to-all-start.1 = ((bf16[8,256,128]{2,1,0:T(8,128)(2,1)}), bf16[8,256,128]{2,1,0:T(8,128)(2,1)S(1)}, u32[]{:S(2)}, u32[]{:S(2)}) async-start(bf16[8,256,128]{2,1,0:T(8,128)(2,1)} %ungroup.2), calls=%async_computation.1 | async-start | bytes 1048576 | tf_op jit(solution)/shard_map/all_to_all | solution.py:414
  119.2 1.7 %collective-permute-done.4.other = bf16[1024,128]{1,0:T(8,128)(2,1)S(1)} collective-permute-done((bf16[1024,128]{1,0:T(8,128)(2,1)}, bf16[1024,128]{1,0:T(8,128)(2,1)S(1)}, u32[]{:S(2)}, u32[]{:S(2)}) %collective-permute-start.4) | collective-permute-done | bytes 262176 | tf_op jit(solution)/shard_map/ppermute | solution.py:411
  121.6 5.4 %ungroup.3 = bf16[8,256,128]{2,1,0:T(8,128)(2,1)} custom-call(s32[1,2048]{1,0:T(1,128)} %get-tuple-element.32.landing_ref, bf16[1024,128]{1,0:T(8,128)(2,1)} %get-tuple-element.48.mine, bf16[1024,128]{1,0:T(8,128)(2,1)} %copy-done.3), custom_call_target="tpu_custom_call" | custom-call | tf_op jit(solution)/shard_map/ungroup/pallas_call | solution.py:377
  127.1 6.8 %all-to-all-done.1.got = bf16[8,256,128]{2,1,0:T(8,128)(2,1)S(1)} async-done(((bf16[8,256,128]{2,1,0:T(8,128)(2,1)}), bf16[8,256,128]{2,1,0:T(8,128)(2,1)S(1)}, u32[]{:S(2)}, u32[]{:S(2)}) %all-to-all-start.1) | async-done | bytes 524320 | tf_op jit(solution)/shard_map/all_to_all | solution.py:414
  133.9 3.6 %all-to-all-start.3 = ((bf16[8,256,128]{2,1,0:T(8,128)(2,1)}), bf16[8,256,128]{2,1,0:T(8,128)(2,1)S(1)}, u32[]{:S(2)}, u32[]{:S(2)}) async-start(bf16[8,256,128]{2,1,0:T(8,128)(2,1)} %ungroup.3), calls=%async_computation.3 | async-start | bytes 1048576 | tf_op jit(solution)/shard_map/all_to_all | solution.py:414
  137.6 14.6 %all-to-all-done.3.got = bf16[8,256,128]{2,1,0:T(8,128)(2,1)S(1)} async-done(((bf16[8,256,128]{2,1,0:T(8,128)(2,1)}), bf16[8,256,128]{2,1,0:T(8,128)(2,1)S(1)}, u32[]{:S(2)}, u32[]{:S(2)}) %all-to-all-start.3) | async-done | bytes 524320 | tf_op jit(solution)/shard_map/all_to_all | solution.py:414
  153.0 3.6 %all-to-all-start.5 = ((bf16[8,144,128]{2,1,0:T(8,128)(2,1)}), bf16[8,144,128]{2,1,0:T(8,128)(2,1)S(1)}, u32[]{:S(2)}, u32[]{:S(2)}) async-start(bf16[8,144,128]{2,1,0:T(8,128)(2,1)} %broadcast_in_dim.2), calls=%async_computation.5 | async-start | bytes 589824 | tf_op jit(solution)/shard_map/all_to_all | solution.py:414
  156.7 3.6 %pick.2 = bf16[1024,128]{1,0:T(8,128)(2,1)} custom-call(s32[1,1024]{1,0:T(1,128)} %get-tuple-element.30.target_ref, bf16[8,256,128]{2,1,0:T(8,128)(2,1)} %copy-done), custom_call_target="tpu_custom_call" | custom-call | tf_op jit(solution)/shard_map/pick/pallas_call | solution.py:377
  160.3 3.6 %pick.3 = bf16[1024,128]{1,0:T(8,128)(2,1)} custom-call(s32[1,1024]{1,0:T(1,128)} %get-tuple-element.30.target_ref, bf16[8,256,128]{2,1,0:T(8,128)(2,1)} %copy-done.2), custom_call_target="tpu_custom_call" | custom-call | tf_op jit(solution)/shard_map/pick/pallas_call | solution.py:377
  164.0 2.4 %all-to-all-done.5 = bf16[8,144,128]{2,1,0:T(8,128)(2,1)S(1)} async-done(((bf16[8,144,128]{2,1,0:T(8,128)(2,1)}), bf16[8,144,128]{2,1,0:T(8,128)(2,1)S(1)}, u32[]{:S(2)}, u32[]{:S(2)}) %all-to-all-start.5) | async-done | bytes 294944 | tf_op jit(solution)/shard_map/all_to_all | solution.py:414
  (36 shorter events, 9.8 us)
Async XLA Ops:
  30.1 17.3 %all-to-all-start.2 = ((bf16[8,256,128]{2,1,0:T(8,128)(2,1)}), bf16[8,256,128]{2,1,0:T(8,128)(2,1)S(1)}, u32[]{:S(2)}, u32[]{:S(2)}) async-start(bf16[8,256,128]{2,1,0:T(8,128)(2,1)} %get-tuple-element.39), calls=%async_computation.2 | async-start | bytes 1048576 | tf_op jit(solution)/shard_map/all_to_all | solution.py:414
  33.6 18.7 %collective-permute-start.1 = (bf16[4,256,128]{2,1,0:T(8,128)(2,1)}, bf16[4,256,128]{2,1,0:T(8,128)(2,1)S(1)}, u32[]{:S(2)}, u32[]{:S(2)}) collective-permute-start(bf16[4,256,128]{2,1,0:T(8,128)(2,1)} %get-tuple-element.35.w_own), channel_id=1, source_target_pairs={{0,1},{1,0},{2,3},{3,2},{4,5},{5,4},{6,7},{7,6},{8,9},{9,8},{10,11... | collective-permute-start | bytes 786440 | tf_op jit(solution)/shard_map/ppermute | solution.py:411
  38.9 13.4 %collective-permute-start = (bf16[1024,128]{1,0:T(8,128)(2,1)}, bf16[1024,128]{1,0:T(8,128)(2,1)S(1)}, u32[]{:S(2)}, u32[]{:S(2)}) collective-permute-start(bf16[1024,128]{1,0:T(8,128)(2,1)} %get-tuple-element.34), channel_id=1, source_target_pairs={{0,1},{1,0},{2,3},{3,2},{4,5},{5,4},{6,7},{7,6},{8,9},{9,8},{10,11... | collective-permute-start | bytes 786440 | tf_op jit(solution)/shard_map/ppermute | solution.py:411
  47.4 0.8 copy-start.1
  52.3 21.2 %collective-permute-start.3 = (bf16[1024,128]{1,0:T(8,128)(2,1)}, bf16[1024,128]{1,0:T(8,128)(2,1)S(1)}, u32[]{:S(2)}, u32[]{:S(2)}) collective-permute-start(bf16[1024,128]{1,0:T(8,128)(2,1)} %get-tuple-element.41), channel_id=1, source_target_pairs={{0,1},{1,0},{2,3},{3,2},{4,5},{5,4},{6,7},{7,6},{8,9},{9,8},{10,11... | collective-permute-start | bytes 786440 | tf_op jit(solution)/shard_map/ppermute | solution.py:411
  52.3 0.7 copy-start.5
  52.3 0.8 copy-start.7
  73.5 0.7 copy-start.8
  74.2 31.3 %copy-start.6 = (bf16[1024,128]{1,0:T(8,128)(2,1)S(1)}, bf16[1024,128]{1,0:T(8,128)(2,1)}, u32[]{:S(2)}) copy-start(bf16[1024,128]{1,0:T(8,128)(2,1)} %get-tuple-element.38) | copy-start | bytes 786436
  98.0 1.9 %collective-permute-start.5 = (bf16[1152,128]{1,0:T(8,128)(2,1)}, bf16[1152,128]{1,0:T(8,128)(2,1)S(1)}, u32[]{:S(2)}, u32[]{:S(2)}) collective-permute-start(bf16[1152,128]{1,0:T(8,128)(2,1)} %get-tuple-element.51), channel_id=1, source_target_pairs={{0,1},{1,0},{2,3},{3,2},{4,5},{5,4},{6,7},{7,6},{8,9},{9,8},{10,11... | collective-permute-start | bytes 884744 | tf_op jit(solution)/shard_map/ppermute | solution.py:411
  101.8 13.8 %all-to-all-start.4 = ((bf16[8,144,128]{2,1,0:T(8,128)(2,1)}), bf16[8,144,128]{2,1,0:T(8,128)(2,1)S(1)}, u32[]{:S(2)}, u32[]{:S(2)}) async-start(bf16[8,144,128]{2,1,0:T(8,128)(2,1)} %bitcast.4), calls=%async_computation.4 | async-start | bytes 589824 | tf_op jit(solution)/shard_map/all_to_all | solution.py:414
  105.5 1.6 collective-permute-start.2
  107.1 0.7 copy-start.4
  115.6 18.3 %all-to-all-start.1 = ((bf16[8,256,128]{2,1,0:T(8,128)(2,1)}), bf16[8,256,128]{2,1,0:T(8,128)(2,1)S(1)}, u32[]{:S(2)}, u32[]{:S(2)}) async-start(bf16[8,256,128]{2,1,0:T(8,128)(2,1)} %ungroup.2), calls=%async_computation.1 | async-start | bytes 1048576 | tf_op jit(solution)/shard_map/all_to_all | solution.py:414
  119.2 1.7 %collective-permute-start.4 = (bf16[1024,128]{1,0:T(8,128)(2,1)}, bf16[1024,128]{1,0:T(8,128)(2,1)S(1)}, u32[]{:S(2)}, u32[]{:S(2)}) collective-permute-start(bf16[1024,128]{1,0:T(8,128)(2,1)} %get-tuple-element.49), channel_id=1, source_target_pairs={{0,1},{1,0},{2,3},{3,2},{4,5},{5,4},{6,7},{7,6},{8,9},{9,8},{10,11... | collective-permute-start | bytes 786440 | tf_op jit(solution)/shard_map/ppermute | solution.py:411
  120.9 0.7 copy-start.3
  133.9 22.8 %copy-start = (bf16[8,256,128]{2,1,0:T(8,128)(2,1)}, bf16[8,256,128]{2,1,0:T(8,128)(2,1)S(1)}, u32[]{:S(2)}) copy-start(bf16[8,256,128]{2,1,0:T(8,128)(2,1)S(1)} %all-to-all-done.1.got) | copy-start | bytes 1572868
  133.9 18.3 %all-to-all-start.3 = ((bf16[8,256,128]{2,1,0:T(8,128)(2,1)}), bf16[8,256,128]{2,1,0:T(8,128)(2,1)S(1)}, u32[]{:S(2)}, u32[]{:S(2)}) async-start(bf16[8,256,128]{2,1,0:T(8,128)(2,1)} %ungroup.3), calls=%async_computation.3 | async-start | bytes 1048576 | tf_op jit(solution)/shard_map/all_to_all | solution.py:414
  152.2 8.1 %copy-start.2 = (bf16[8,256,128]{2,1,0:T(8,128)(2,1)}, bf16[8,256,128]{2,1,0:T(8,128)(2,1)S(1)}, u32[]{:S(2)}) copy-start(bf16[8,256,128]{2,1,0:T(8,128)(2,1)S(1)} %all-to-all-done.3.got) | copy-start | bytes 1572868
  153.0 13.4 %all-to-all-start.5 = ((bf16[8,144,128]{2,1,0:T(8,128)(2,1)}), bf16[8,144,128]{2,1,0:T(8,128)(2,1)S(1)}, u32[]{:S(2)}, u32[]{:S(2)}) async-start(bf16[8,144,128]{2,1,0:T(8,128)(2,1)} %broadcast_in_dim.2), calls=%async_computation.5 | async-start | bytes 589824 | tf_op jit(solution)/shard_map/all_to_all | solution.py:414

commit v2 on v1

--- a/solution.py
+++ b/solution.py
@@ -6,6 +6,7 @@
 from jax.experimental import pallas as pl
 from jax.experimental.pallas import tpu as pltpu
 from jax.sharding import PartitionSpec as P
+
 
 HEAD_DIM = 32
 KINDS = 12
@@ -64,7 +65,7 @@
     rank = jnp.sum(mm(owner_hot.astype(BF16), before) * owner_hot, axis=0, keepdims=True)
     target = owner * capacity + rank.astype(I32)
     out_target[...] = target
-    kinds_hot = hot(iota((KIND_ROWS, count), 0) == kind)
+    kinds_hot = hot(iota((KINDS, count), 0) == kind)
     base = (feats[...].astype(F32) + mm_tn(kinds_hot, embed[...])).astype(BF16)
     rows = jnp.concatenate([base, cot[...]], axis=1)
     place = iota((TAG_ROWS, count), 0)
@@ -142,7 +143,8 @@
             theirs[s - SLOTS : s - SLOTS + step, :] = rows
 
 
-def ungroup_kernel(regions, capacity, landing_ref, mine, other, out):
+def ungroup_kernel(regions, capacity, landing_ref, mine, other, *rest):
+    out = rest[-1]
     total = regions * capacity
     column = jnp.transpose(jnp.broadcast_to(landing_ref[...].astype(F32), (8, total)))[:, 0:1]
     column = column.astype(I32)
@@ -155,14 +157,46 @@
             out[s // capacity, s % capacity : s % capacity + step, :] = rows
         else:
             for k in range(step // capacity):
-                out[s // capacity + k] = rows[k * capacity : (k + 1) * capacity]
+                out[s // capacity + k, 0:capacity, :] = rows[k * capacity : (k + 1) * capacity]
+    if len(rest) > 1:
+        own, received, _ = rest
+        share = own.shape[0] // regions
+        for r in range(regions):
+            rows = slice(r * share, (r + 1) * share)
+            out[r, capacity : capacity + share, :] = (own[rows, :] + received[rows, :].astype(F32)).astype(BF16)
+
+
+def share_kernel(regions, capacity, got, out):
+    total = got[0, capacity:, :].astype(F32)
+    for r in range(1, regions):
+        total = total + got[r, capacity:, :].astype(F32)
+    total = total.astype(BF16)
+    for r in range(regions):
+        out[r] = total
+
+
+def spread_kernel(factor, got, out_q, out_k, out_v, out_o, out_gain, out_embed):
+    total = got[...].reshape(got.shape[0] * got.shape[1], got.shape[2]).astype(F32) * factor
+    width, half = out_q.shape
+    out_q[...] = total[0:width]
+    out_k[...] = total[width : 2 * width]
+    out_v[...] = total[2 * width : 3 * width]
+    place = 3 * width
+    out_o[:, 0:half] = total[place : place + half]
+    out_o[:, half:] = total[place + half : place + width]
+    place += width
+    out_embed[...] = total[place : place + KINDS]
+    place += KIND_ROWS
+    out_gain[:, 0:half] = total[place : place + 1]
+    out_gain[:, half:] = total[place + 1 : place + 2]
 
 
 def pick_kernel(target_ref, got, out):
-    total = got.shape[0] * got.shape[1]
+    capacity = BINS_DEV * SLOTS // got.shape[0]
+    total = got.shape[0] * capacity
     count = out.shape[0]
     column = jnp.transpose(jnp.broadcast_to(target_ref[...].astype(F32), (8, count)))[:, 0:1].astype(I32)
-    flat = got[...].reshape(total, got.shape[2])
+    flat = got[:, 0:capacity, :].reshape(total, got.shape[2])
     step = 256
     for s in range(0, count, step):
         chosen = hot(iota((step, total), 1) == column[s : s + step])
@@ -372,15 +406,10 @@
     return pl.BlockSpec(tuple(array.shape), lambda *_: zeros)
 
 
-def simple_call(kernel, outs, name, inputs, scratch=(), scalars=0):
+def simple_call(kernel, outs, inputs, scratch=(), scalars=0):
     specs = [SMEM_SPEC] * scalars + [whole(x) for x in inputs[scalars:]]
     return pl.pallas_call(
-        kernel,
-        out_shape=outs,
-        in_specs=specs,
-        out_specs=tuple(whole(x) for x in outs),
-        scratch_shapes=scratch,
-        name=name,
+        kernel, out_shape=outs, in_specs=specs, out_specs=tuple(whole(x) for x in outs), scratch_shapes=scratch
     )(*inputs)
 
 
@@ -413,7 +442,6 @@
     def exchange(x):
         return lax.all_to_all(x, "region", split_axis=0, concat_axis=0, tiled=True)
 
-    embed = jnp.concatenate([kind_embed, jnp.zeros((KIND_ROWS - KINDS, half), BF16)], axis=0)
     gain = norm_gain.reshape(1, width)
     packed_base, packed_cot, target, w_own = simple_call(
         functools.partial(pack_kernel, regions, capacity),
@@ -423,17 +451,16 @@
             shape((1, count), I32),
             shape((4, width, half), BF16),
         ),
-        "pack",
-        (bin_cells.reshape(1, count), element_kinds.reshape(1, count), features, embed, cotangent, w_query, w_key, w_value, w_out),
+        (bin_cells.reshape(1, count), element_kinds.reshape(1, count), features, kind_embed, cotangent, w_query, w_key, w_value, w_out),
     )
     w_other = other_core(w_own)
     got_base = exchange(packed_base)
+    got_base, packed_cot = lax.optimization_barrier((got_base, packed_cot))
     got_cot = exchange(packed_cot)
     rows_shape = shape((SLOTS, half), BF16)
     mine, theirs, landing, info = simple_call(
         functools.partial(group_kernel, regions, capacity),
         (rows_shape, rows_shape, shape((1, local_rows), I32), shape((16, SLOTS), F32)),
-        "group",
         (core, got_base),
         scratch=(pltpu.VMEM((local_rows, half), BF16),),
         scalars=1,
@@ -472,9 +499,14 @@
         name="forward",
     )(*inputs)
     attn_other = other_core(attn_send)
+    (packed_attn,) = simple_call(
+        functools.partial(ungroup_kernel, regions, capacity),
+        (shape((regions, capacity, half), BF16),),
+        (landing, attn_keep, attn_other),
+    )
 
     g_mine, g_theirs = simple_call(
-        functools.partial(regroup_kernel, regions, capacity), (rows_shape, rows_shape), "regroup", (landing, got_cot)
+        functools.partial(regroup_kernel, regions, capacity), (rows_shape, rows_shape), (landing, got_cot)
     )
     g_other = other_core(g_theirs)
 
@@ -502,40 +534,33 @@
         name="backward",
     )(*inputs)
 
-    packed_shape = shape((regions, capacity, half), BF16)
-
-    def back(keep, received):
-        (packed,) = simple_call(
-            functools.partial(ungroup_kernel, regions, capacity), (packed_shape,), "ungroup", (landing, keep, received)
-        )
-        home = exchange(packed)
-        (rows,) = simple_call(pick_kernel, (shape((count, half), BF16),), "pick", (target, home))
+    def pick(home):
+        (rows,) = simple_call(pick_kernel, (shape((count, half), BF16),), (target, home))
         return rows
 
-    attended = back(attn_keep, attn_other)
-    grad_feats = back(d_keep, other_core(d_send))
-
-    part = (grad_keep + other_core(grad_send).astype(F32)).astype(BF16)
-    shares = exchange(part.reshape(regions, grad_rows // regions, half))
-    share = jnp.sum(shares.astype(F32), axis=0).astype(BF16)
-    summed = exchange(jnp.broadcast_to(share[None], (regions,) + share.shape)).reshape(grad_rows, half)
-    total = summed.astype(F32) * float(count * regions) ** (-0.5)
-    place = 3 * width
-    grad_out = jnp.concatenate([total[place : place + half], total[place + half : place + width]], axis=1)
-    place += width
-    grad_embed = total[place : place + KINDS]
-    place += KIND_ROWS
-    grad_gain = total[place : place + 2].reshape(width)
-    return (
-        attended,
-        grad_feats,
-        total[0:width],
-        total[width : 2 * width],
-        total[2 * width : 3 * width],
-        grad_out,
-        grad_gain,
-        grad_embed,
-    )
+    share = grad_rows // regions
+    (packed_grad,) = simple_call(
+        functools.partial(ungroup_kernel, regions, capacity),
+        (shape((regions, capacity + share, half), BF16),),
+        (landing, d_keep, other_core(d_send), grad_keep, other_core(grad_send)),
+    )
+    got_cot, packed_attn = lax.optimization_barrier((got_cot, packed_attn))
+    home_attn = exchange(packed_attn)
+    home_attn, packed_grad = lax.optimization_barrier((home_attn, packed_grad))
+    home_grad = exchange(packed_grad)
+    (shares,) = simple_call(
+        functools.partial(share_kernel, regions, capacity), (shape((regions, share, half), BF16),), (home_grad,)
+    )
+    summed = exchange(shares)
+    attended = pick(home_attn)
+    grad_feats = pick(home_grad)
+    column_shape = shape((width, half), F32)
+    grad_q, grad_k, grad_v, grad_o, grad_gain, grad_embed = simple_call(
+        functools.partial(spread_kernel, float(count * regions) ** (-0.5)),
+        (column_shape, column_shape, column_shape, shape((half, width), F32), shape((1, width), F32), shape((KINDS, half), F32)),
+        (summed,),
+    )
+    return (attended, grad_feats, grad_q, grad_k, grad_v, grad_o, grad_gain.reshape(width), grad_embed)
 
 
 def solution(mesh):
@@ -551,6 +576,7 @@
         P("head", None),
         P(("groups", "region"), "head"),
     )
+
     return jax.shard_map(
         on_device,
         mesh=mesh,

time: 170 us -> 155 us (0.912)
  waiting for transfers between devices: 38.8 us -> 18.4 us
  blocking collectives: 23.4 us -> 28 us
  Pallas kernels: 76.5 us -> 80.4 us
  other arithmetic: 2.62 us -> 0 us
  local copies, waits for them, and re-layouts: 7.7 us -> 5.35 us
  starting transfers between devices: 19.4 us -> 21.4 us
    all_to_all x5 -> x4, waiting for transfers between devices: 34.3 us -> 16.7 us  [exchange(): return lax.all_to_all(x, 'region', split_axis=0, concat_axis=0, tiled=True)]
    all_to_all x1, blocking collectives: 23.4 us -> 28 us  [exchange(): return lax.all_to_all(x, 'region', split_axis=0, concat_axis=0, tiled=True)]
    pallas_call x7 -> x9, Pallas kernels: 32.3 us -> 36.4 us  [simple_call(): pl.pallas_call(kernel, out_shape=outs, in_specs=specs, out_specs=tuple((w...]
    ppermute x6, waiting for transfers between devices: 4.54 us -> 1.67 us  [other_core(): return lax.ppermute(x, 'head', swap)]
    all_to_all x5 -> x4, starting transfers between devices: 18.1 us -> 20.3 us  [exchange(): return lax.all_to_all(x, 'region', split_axis=0, concat_axis=0, tiled=True)]
    convert_element_type x1 -> x0, other arithmetic: 1.87 us -> none  [on_device(): part = (grad_keep + other_core(grad_send).astype(F32)).astype(BF16)]
    unnamed x18 -> x20, local copies, waits for them, and re-layouts: 3.68 us -> 5.35 us
  transfers between devices with their start and end apart: 11 -> 10, of which waited for: 8 -> 3; matrix products, arithmetic and copies ran while one was open for 0% -> 0% of each run, Pallas kernels for 28% -> 47%
where the time goes in v2:
time: 155 us; the launch traced here: 154 us
  Pallas kernels  80.4 us (52%)
  blocking collectives  28 us (18%)
  starting transfers between devices  21.4 us (14%)
  waiting for transfers between devices  18.4 us (12%)
  local copies, waits for them, and re-layouts  5.35 us (3%)
    pallas_call x9, Pallas kernels, simple_call(): pl.pallas_call(kernel, out_shape=outs, in_specs=specs, out_specs=tuple((w...  36.4 us
    all_to_all x1, blocking collectives, exchange(): return lax.all_to_all(x, 'region', split_axis=0, concat_axis=0, tiled=True)  28 us
    pallas_call x1, Pallas kernels, on_device(): pl.pallas_call(functools.partial(backward_kernel, heads), grid=(heads,),...  23.6 us
    pallas_call x1, Pallas kernels, on_device(): pl.pallas_call(functools.partial(forward_kernel, heads), grid=(heads,), o...  20.4 us
    all_to_all x4, starting transfers between devices, exchange(): return lax.all_to_all(x, 'region', split_axis=0, concat_axis=0, tiled=True)  20.3 us
    all_to_all x4, waiting for transfers between devices, exchange(): return lax.all_to_all(x, 'region', split_axis=0, concat_axis=0, tiled=True)  16.7 us
    unnamed x20, local copies, waits for them, and re-layouts  5.35 us
  transfers between devices with their start and end apart: 10, of which 3 were waited for; matrix products, arithmetic and copies ran while one was open for 0% of the time, Pallas kernels for 47%

profile of v2, /device:TPU:0, one launch (start us, length us, event | category | flops | bytes accessed | tf_op | source)
XLA Modules:
  0.0 154.2 jit_solution(16315955521314462293)
XLA Ops:
  0.6 4.8 %shard_map.161 = (bf16[8,272,128]{2,1,0:T(8,128)(2,1)}, bf16[8,256,128]{2,1,0:T(8,128)(2,1)}, s32[1,1024]{1,0:T(1,128)}, bf16[4,256,128]{2,1,0:T(8,128)(2,1)}) custom-call(s32[1,1024]{1,0:T(1,128)} %bitcast.5, s32[1,1024]{1,0:T(1,128)} %bitcast.6, bf16[1024,128]{1,0:T(8,128)(2,1)} %feats.1, bf16[12,128]{1,0:T(8,128)(2,1)} %embed.1, bf16[1024,128]{1,0:T(8,128)(2,1)} %cot.1, ...), custom_call_target="tpu_custom_call" | custom-call | tf_op jit(solution)/shard_map/pallas_call | solution.py:411
  5.5 7.3 %all-to-all-start = ((bf16[8,272,128]{2,1,0:T(8,128)(2,1)}), bf16[8,272,128]{2,1,0:T(8,128)(2,1)S(1)}, u32[]{:S(2)}, u32[]{:S(2)}) async-start(bf16[8,272,128]{2,1,0:T(8,128)(2,1)} %get-tuple-element.42), calls=%async_computation | async-start | bytes 1114112 | tf_op jit(solution)/shard_map/all_to_all | solution.py:443
  12.8 15.2 %all-to-all-done.got = bf16[8,272,128]{2,1,0:T(8,128)(2,1)S(1)} async-done(((bf16[8,272,128]{2,1,0:T(8,128)(2,1)}), bf16[8,272,128]{2,1,0:T(8,128)(2,1)S(1)}, u32[]{:S(2)}, u32[]{:S(2)}) %all-to-all-start) | async-done | bytes 557088 | tf_op jit(solution)/shard_map/all_to_all | solution.py:443
  28.0 0.8 copy-done
  28.8 5.2 %shard_map.162 = (bf16[1024,128]{1,0:T(8,128)(2,1)}, bf16[1024,128]{1,0:T(8,128)(2,1)}, s32[1,2048]{1,0:T(1,128)}, f32[16,1024]{1,0:T(8,128)}) custom-call(s32[1]{0:T(128)} %bitcast.2.core, bf16[8,272,128]{2,1,0:T(8,128)(2,1)} %copy-done), custom_call_target="tpu_custom_call" | custom-call | tf_op jit(solution)/shard_map/pallas_call | solution.py:411
  34.0 3.7 %all-to-all-start.1 = ((bf16[8,256,128]{2,1,0:T(8,128)(2,1)}), bf16[8,256,128]{2,1,0:T(8,128)(2,1)S(1)}, u32[]{:S(2)}, u32[]{:S(2)}) async-start(bf16[8,256,128]{2,1,0:T(8,128)(2,1)} %get-tuple-element.44), calls=%async_computation.1 | async-start | bytes 1048576 | tf_op jit(solution)/shard_map/all_to_all | solution.py:443
  38.5 20.4 %forward.1 = (bf16[1024,256]{1,0:T(8,128)(2,1)}, bf16[1024,256]{1,0:T(8,128)(2,1)}, bf16[1024,256]{1,0:T(8,128)(2,1)}, bf16[8,1024,1024]{2,1,0:T(8,128)(2,1)}, f...) custom-call(s32[1]{0:T(128)} %bitcast.2.core, ...), custom_call_target="tpu_custom_call" | custom-call | flops 8589934592 | bytes 16777216 | tf_op jit(solution)/shard_map/forward/pallas_call | solution.py:485
  59.4 0.8 copy-done.2
  60.2 4.1 %shard_map.164 = (bf16[1024,128]{1,0:T(8,128)(2,1)}, bf16[1024,128]{1,0:T(8,128)(2,1)}) custom-call(s32[1,2048]{1,0:T(1,128)} %get-tuple-element.46.landing_ref, bf16[8,256,128]{2,1,0:T(8,128)(2,1)} %copy-done.2), custom_call_target="tpu_custom_call" | custom-call | tf_op jit(solution)/shard_map/pallas_call | solution.py:411
  64.4 0.7 copy-done.6
  65.1 5.4 %shard_map.163 = bf16[8,256,128]{2,1,0:T(8,128)(2,1)} custom-call(s32[1,2048]{1,0:T(1,128)} %get-tuple-element.46.landing_ref, bf16[1024,128]{1,0:T(8,128)(2,1)} %get-tuple-element.51.mine, bf16[1024,128]{1,0:T(8,128)(2,1)} %copy-done.6), custom_call_target="tpu_custom_call" | custom-call | tf_op jit(solution)/shard_map/pallas_call | solution.py:411
  70.5 5.9 %all-to-all-start.2 = ((bf16[8,256,128]{2,1,0:T(8,128)(2,1)}), bf16[8,256,128]{2,1,0:T(8,128)(2,1)S(1)}, u32[]{:S(2)}, u32[]{:S(2)}) async-start(bf16[8,256,128]{2,1,0:T(8,128)(2,1)} %shard_map.163), calls=%async_computation.2 | async-start | bytes 1048576 | tf_op jit(solution)/shard_map/all_to_all | solution.py:443
  77.1 23.6 %backward.1 = (bf16[1024,128]{1,0:T(8,128)(2,1)}, bf16[1024,128]{1,0:T(8,128)(2,1)}, f32[1152,128]{1,0:T(8,128)}, bf16[1152,128]{1,0:T(8,128)(2,1)}) custom-call(s32[1]{0:T(128)} %bitcast.2.core, bf16[1024,128]{1,0:T(8,128)(2,1)} %get-tuple-element.47.mine, bf16[1024,128]{1,0:T(8,128)(2,1)} %copy-done.8, bf16[1024,128]{1,0:T(8,128)(2,1)} %get-tuple-element.54.g_mine, ...), custom_call_target="tpu_custom_call" | custom-call | flops 17179869184 | bytes 16777216 | tf_op jit(solution)/shard_map/backward/pallas_call | solution.py:517
  101.2 1.7 %collective-permute-done.4.other = bf16[1024,128]{1,0:T(8,128)(2,1)S(1)} collective-permute-done((bf16[1024,128]{1,0:T(8,128)(2,1)}, bf16[1024,128]{1,0:T(8,128)(2,1)S(1)}, u32[]{:S(2)}, u32[]{:S(2)}) %collective-permute-start.4) | collective-permute-done | bytes 262176 | tf_op jit(solution)/shard_map/ppermute | solution.py:440
  102.9 0.7 copy-done.5
  103.7 5.8 %shard_map.165 = bf16[8,400,128]{2,1,0:T(8,128)(2,1)} custom-call(s32[1,2048]{1,0:T(1,128)} %get-tuple-element.46.landing_ref, bf16[1024,128]{1,0:T(8,128)(2,1)} %get-tuple-element.62.mine, bf16[1024,128]{1,0:T(8,128)(2,1)} %copy-done.5, f32[1152,128]{1,0:T(8,128)} %get-tuple-element.64.rest_0_, bf16[1152,128]{1,0:T(8,128)(2,1)} %copy-done.4), custom_call_target="tpu_custom_call" | custom-call | tf_op jit(solution)/shard_map/pallas_call | solution.py:411
  109.5 28.0 %all_to_all.25.got = bf16[8,400,128]{2,1,0:T(8,128)(2,1)} all-to-all(bf16[8,400,128]{2,1,0:T(8,128)(2,1)} %shard_map.165), channel_id=1, replica_groups=mesh['groups'=2,'region'=8,'head'=2] {'region'}, dimensions={0} | all-to-all | bytes 1638400 | tf_op jit(solution)/shard_map/all_to_all | solution.py:443
  137.5 1.9 %shard_map.168 = bf16[8,144,128]{2,1,0:T(8,128)(2,1)} custom-call(bf16[8,400,128]{2,1,0:T(8,128)(2,1)} %all_to_all.25.got), custom_call_target="tpu_custom_call" | custom-call | tf_op jit(solution)/shard_map/pallas_call | solution.py:411
  139.4 3.4 %all-to-all-start.4 = ((bf16[8,144,128]{2,1,0:T(8,128)(2,1)}), bf16[8,144,128]{2,1,0:T(8,128)(2,1)S(1)}, u32[]{:S(2)}, u32[]{:S(2)}) async-start(bf16[8,144,128]{2,1,0:T(8,128)(2,1)} %shard_map.168), calls=%async_computation.4 | async-start | bytes 589824 | tf_op jit(solution)/shard_map/all_to_all | solution.py:443
  142.8 3.6 %shard_map.166 = bf16[1024,128]{1,0:T(8,128)(2,1)} custom-call(s32[1,1024]{1,0:T(1,128)} %get-tuple-element.41.target_ref, bf16[8,256,128]{2,1,0:T(8,128)(2,1)} %copy-done.1), custom_call_target="tpu_custom_call" | custom-call | tf_op jit(solution)/shard_map/pallas_call | solution.py:411
  146.5 3.7 %shard_map.167 = bf16[1024,128]{1,0:T(8,128)(2,1)} custom-call(s32[1,1024]{1,0:T(1,128)} %get-tuple-element.41.target_ref, bf16[8,400,128]{2,1,0:T(8,128)(2,1)} %all_to_all.25.got), custom_call_target="tpu_custom_call" | custom-call | tf_op jit(solution)/shard_map/pallas_call | solution.py:411
  150.2 1.5 all-to-all-done.4.got
  151.7 0.7 copy-done.3
  152.5 1.8 %shard_map.169 = (f32[256,128]{1,0:T(8,128)}, f32[256,128]{1,0:T(8,128)}, f32[256,128]{1,0:T(8,128)}, f32[128,256]{1,0:T(8,128)}, f32[1,256]{1,0:T(1,128)}, /*index=5*/f32[12,128]{1,0:T(8,128)}) custom-call(bf16[8,144,128]{2,1,0:T(8,128)(2,1)} %copy-done.3), custom_call_target="tpu_custom_call" | custom-call | tf_op jit(solution)/shard_map/pallas_call | solution.py:411
  (28 shorter events, 2.7 us)
Async XLA Ops:
  5.5 22.5 %all-to-all-start = ((bf16[8,272,128]{2,1,0:T(8,128)(2,1)}), bf16[8,272,128]{2,1,0:T(8,128)(2,1)S(1)}, u32[]{:S(2)}, u32[]{:S(2)}) async-start(bf16[8,272,128]{2,1,0:T(8,128)(2,1)} %get-tuple-element.42), calls=%async_computation | async-start | bytes 1114112 | tf_op jit(solution)/shard_map/all_to_all | solution.py:443
  12.8 24.9 %collective-permute-start.1 = (bf16[4,256,128]{2,1,0:T(8,128)(2,1)}, bf16[4,256,128]{2,1,0:T(8,128)(2,1)S(1)}, u32[]{:S(2)}, u32[]{:S(2)}) collective-permute-start(bf16[4,256,128]{2,1,0:T(8,128)(2,1)} %get-tuple-element.49.w_own), channel_id=1, source_target_pairs={{0,1},{1,0},{2,3},{3,2},{4,5},{5,4},{6,7},{7,6},{8,9},{9,8},{10,11... | collective-permute-start | bytes 786440 | tf_op jit(solution)/shard_map/ppermute | solution.py:440
  28.0 0.8 copy-start
  34.0 3.7 %collective-permute-start = (bf16[1024,128]{1,0:T(8,128)(2,1)}, bf16[1024,128]{1,0:T(8,128)(2,1)S(1)}, u32[]{:S(2)}, u32[]{:S(2)}) collective-permute-start(bf16[1024,128]{1,0:T(8,128)(2,1)} %get-tuple-element.48), channel_id=1, source_target_pairs={{0,1},{1,0},{2,3},{3,2},{4,5},{5,4},{6,7},{7,6},{8,9},{9,8},{10,11... | collective-permute-start | bytes 786440 | tf_op jit(solution)/shard_map/ppermute | solution.py:440
  34.0 25.4 %all-to-all-start.1 = ((bf16[8,256,128]{2,1,0:T(8,128)(2,1)}), bf16[8,256,128]{2,1,0:T(8,128)(2,1)S(1)}, u32[]{:S(2)}, u32[]{:S(2)}) async-start(bf16[8,256,128]{2,1,0:T(8,128)(2,1)} %get-tuple-element.44), calls=%async_computation.1 | async-start | bytes 1048576 | tf_op jit(solution)/shard_map/all_to_all | solution.py:443
  37.7 0.7 copy-start.7
  37.7 0.8 copy-start.8
  58.9 5.5 %collective-permute-start.2 = (bf16[1024,128]{1,0:T(8,128)(2,1)}, bf16[1024,128]{1,0:T(8,128)(2,1)S(1)}, u32[]{:S(2)}, u32[]{:S(2)}) collective-permute-start(bf16[1024,128]{1,0:T(8,128)(2,1)} %get-tuple-element.52), channel_id=1, source_target_pairs={{0,1},{1,0},{2,3},{3,2},{4,5},{5,4},{6,7},{7,6},{8,9},{9,8},{10,11... | collective-permute-start | bytes 786440 | tf_op jit(solution)/shard_map/ppermute | solution.py:440
  59.4 0.8 copy-start.2
  64.3 12.1 %collective-permute-start.3 = (bf16[1024,128]{1,0:T(8,128)(2,1)}, bf16[1024,128]{1,0:T(8,128)(2,1)S(1)}, u32[]{:S(2)}, u32[]{:S(2)}) collective-permute-start(bf16[1024,128]{1,0:T(8,128)(2,1)} %get-tuple-element.55), channel_id=1, source_target_pairs={{0,1},{1,0},{2,3},{3,2},{4,5},{5,4},{6,7},{7,6},{8,9},{9,8},{10,11... | collective-permute-start | bytes 786440 | tf_op jit(solution)/shard_map/ppermute | solution.py:440
  64.4 0.7 copy-start.6
  70.5 39.0 %all-to-all-start.2 = ((bf16[8,256,128]{2,1,0:T(8,128)(2,1)}), bf16[8,256,128]{2,1,0:T(8,128)(2,1)S(1)}, u32[]{:S(2)}, u32[]{:S(2)}) async-start(bf16[8,256,128]{2,1,0:T(8,128)(2,1)} %shard_map.163), calls=%async_computation.2 | async-start | bytes 1048576 | tf_op jit(solution)/shard_map/all_to_all | solution.py:443
  76.4 0.7 copy-start.9
  100.7 2.2 %collective-permute-start.5 = (bf16[1152,128]{1,0:T(8,128)(2,1)}, bf16[1152,128]{1,0:T(8,128)(2,1)S(1)}, u32[]{:S(2)}, u32[]{:S(2)}) collective-permute-start(bf16[1152,128]{1,0:T(8,128)(2,1)} %get-tuple-element.65), channel_id=1, source_target_pairs={{0,1},{1,0},{2,3},{3,2},{4,5},{5,4},{6,7},{7,6},{8,9},{9,8},{10,11... | collective-permute-start | bytes 884744 | tf_op jit(solution)/shard_map/ppermute | solution.py:440
  100.7 2.2 %collective-permute-start.4 = (bf16[1024,128]{1,0:T(8,128)(2,1)}, bf16[1024,128]{1,0:T(8,128)(2,1)S(1)}, u32[]{:S(2)}, u32[]{:S(2)}) collective-permute-start(bf16[1024,128]{1,0:T(8,128)(2,1)} %get-tuple-element.63), channel_id=1, source_target_pairs={{0,1},{1,0},{2,3},{3,2},{4,5},{5,4},{6,7},{7,6},{8,9},{9,8},{10,11... | collective-permute-start | bytes 786440 | tf_op jit(solution)/shard_map/ppermute | solution.py:440
  102.9 0.7 copy-start.5
  102.9 0.8 copy-start.4
  109.5 33.3 %copy-start.1 = (bf16[8,256,128]{2,1,0:T(8,128)(2,1)}, bf16[8,256,128]{2,1,0:T(8,128)(2,1)S(1)}, u32[]{:S(2)}) copy-start(bf16[8,256,128]{2,1,0:T(8,128)(2,1)S(1)} %all-to-all-done.2.got) | copy-start | bytes 1572868
  139.4 12.4 %all-to-all-start.4 = ((bf16[8,144,128]{2,1,0:T(8,128)(2,1)}), bf16[8,144,128]{2,1,0:T(8,128)(2,1)S(1)}, u32[]{:S(2)}, u32[]{:S(2)}) async-start(bf16[8,144,128]{2,1,0:T(8,128)(2,1)} %shard_map.168), calls=%async_computation.4 | async-start | bytes 589824 | tf_op jit(solution)/shard_map/all_to_all | solution.py:443
  151.7 0.7 copy-start.3

commit v3 on v2

--- a/solution.py
+++ b/solution.py
@@ -22,7 +22,6 @@
 LANES = 128
 TAG_ROWS = 16
 KIND_ROWS = 16
-FAR = 1 << 20
 NT = (((1,), (1,)), ((), ()))
 TN = (((0,), (0,)), ((), ()))
 
@@ -51,144 +50,153 @@
     return n.bit_length() - 1
 
 
-def pack_kernel(regions, capacity, cells, kinds, feats, embed, cot, w_q, w_k, w_v, w_o, out_base, out_cot, out_target, out_w):
+def positions(regions, capacity, cell):
+    count = cell.shape[1]
     local_rows = BINS_DEV * SLOTS
-    count = feats.shape[0]
-    half = feats.shape[1]
-    cell = cells[...]
-    kind = kinds[...]
     owner = lax.shift_right_logical(cell, log2_of(local_rows))
-    local = jnp.bitwise_and(cell, local_rows - 1)
-    region_rows = max(regions, 16)
-    owner_hot = jnp.where(iota((region_rows, count), 0) == owner, 1.0, 0.0)
+    group = lax.shift_right_logical(cell, log2_of(SLOTS))
+    classes = max(BINS_DEV * regions, 16)
+    group_hot = jnp.where(iota((classes, count), 0) == group, 1.0, 0.0)
     before = hot(iota((count, count), 0) < iota((count, count), 1))
-    rank = jnp.sum(mm(owner_hot.astype(BF16), before) * owner_hot, axis=0, keepdims=True)
-    target = owner * capacity + rank.astype(I32)
+    rank = jnp.sum(mm(group_hot.astype(BF16), before) * group_hot, axis=0, keepdims=True).astype(I32)
+    second = jnp.bitwise_and(group, 1) > 0
+    target = owner * capacity + jnp.where(second, capacity - 1 - rank, rank)
+    return target, jnp.sum(group_hot, axis=1, keepdims=True)
+
+
+def pack_kernel(regions, capacity, cells, kinds, feats, embed, w_q, w_k, w_v, w_o, out_base, out_target, out_w):
+    count, half = feats.shape
+    target, counts = positions(regions, capacity, cells[...])
     out_target[...] = target
-    kinds_hot = hot(iota((KINDS, count), 0) == kind)
+    kinds_hot = hot(iota((KINDS, count), 0) == kinds[...])
     base = (feats[...].astype(F32) + mm_tn(kinds_hot, embed[...])).astype(BF16)
-    rows = jnp.concatenate([base, cot[...]], axis=1)
-    place = iota((TAG_ROWS, count), 0)
-    high = lax.shift_right_logical(local, 7) + 1
-    low = jnp.bitwise_and(local, 127)
-    tags = jnp.where(place == 0, high, jnp.where(place == 1, low, jnp.where(place == 2, kind, 0)))
-    tags = tags.astype(F32).astype(BF16)
+    place = iota((TAG_ROWS, half), 0)
     for r in range(regions):
         chosen = hot(iota((capacity, count), 0) + r * capacity == target)
-        moved = mm(chosen, rows).astype(BF16)
-        out_base[r, 0:capacity, :] = moved[:, :half]
-        out_cot[r, :, :] = moved[:, half:]
+        out_base[r, 0:capacity, :] = mm(chosen, base).astype(BF16)
+        first = counts[2 * r : 2 * r + 1]
+        second = counts[2 * r + 1 : 2 * r + 2]
+        tags = jnp.where(place == 0, first, jnp.where(place == 1, second, 0.0))
+        out_base[r, capacity : capacity + TAG_ROWS, :] = tags.astype(BF16)
+    out_w[0] = w_q[...]
+    out_w[1] = w_k[...]
+    out_w[2] = w_v[...]
+    out_w[3, 0:half, :] = w_o[:, 0:half]
+    out_w[3, half:, :] = w_o[:, half:]
+
+
+def pack_cot_kernel(regions, capacity, target_ref, kinds, cot, out_cot):
+    count = cot.shape[0]
+    target = target_ref[...]
+    rows = cot[...]
+    tags = jnp.where(iota((TAG_ROWS, count), 0) == 0, kinds[...] + 1, 0).astype(F32).astype(BF16)
+    for r in range(regions):
+        chosen = hot(iota((capacity, count), 0) + r * capacity == target)
+        out_cot[r, 0:capacity, :] = mm(chosen, rows).astype(BF16)
         tag = mm_nt(tags, chosen)
         if capacity >= LANES:
             tag = jnp.concatenate([tag[0:8, 0:LANES], tag[0:8, LANES : 2 * LANES]], axis=0)
         else:
             tag = jnp.concatenate([tag, jnp.zeros((TAG_ROWS, LANES - capacity), F32)], axis=1)
-        out_base[r, capacity : capacity + TAG_ROWS, :] = tag.astype(BF16)
-    out_w[0] = w_q[...]
-    out_w[1] = w_k[...]
-    out_w[2] = w_v[...]
-    out_w[3, 0:half, :] = w_o[:, 0:half]
-    out_w[3, half:, :] = w_o[:, half:]
-
-
-def group_kernel(regions, capacity, core, got, mine, theirs, out_landing, out_info, flat):
-    total = regions * capacity
-    tag_rows = jnp.zeros((8, total), F32) if capacity < LANES else None
-    pieces = []
+        out_cot[r, capacity : capacity + TAG_ROWS, :] = tag.astype(BF16)
+
+
+def place_rows(regions, capacity, got, marks, front, back):
     for r in range(regions):
-        flat[r * capacity : (r + 1) * capacity, :] = got[r, 0:capacity, :]
-        block = got[r, capacity : capacity + TAG_ROWS, :]
+        rows = got[r, 0:capacity, :].astype(F32)
+        front[pl.ds(marks[0, r], capacity), :] = rows
+        back[pl.ds(marks[1, r], capacity), :] = rows
+
+
+def bins_of(regions, capacity, core, marks, front, back):
+    row = iota((SLOTS, 1), 0)
+    first = jnp.where(row < marks[0, regions], front[0:SLOTS, :], 0.0)
+    second = jnp.where(row >= marks[1, regions], back[capacity : capacity + SLOTS, :], 0.0)
+    flag = core[0] > 0
+    return jnp.where(flag, second, first).astype(BF16), jnp.where(flag, first, second).astype(BF16)
+
+
+def group_kernel(regions, capacity, core, got, mine, theirs, keep, marks, front, back):
+    start = jnp.int32(0)
+    end = jnp.int32(SLOTS)
+    for r in range(regions):
+        block = got[r, capacity : capacity + TAG_ROWS, :].astype(F32)
+        marks[0, r] = start
+        marks[1, r] = end
+        start = start + jnp.max(block[0:1, :]).astype(I32)
+        end = end - jnp.max(block[1:2, :]).astype(I32)
+    marks[0, regions] = start
+    marks[1, regions] = end
+    place_rows(regions, capacity, got, marks, front, back)
+    mine[...], theirs[...] = bins_of(regions, capacity, core, marks, front, back)
+    lane = iota((8, SLOTS), 1)
+    filled = jnp.where(core[0] > 0, jnp.where(lane >= end, 1.0, 0.0), jnp.where(lane < start, 1.0, 0.0))
+    keep[...] = filled
+
+
+def regroup_kernel(regions, capacity, core, marks, got, mine, theirs, front, back):
+    place_rows(regions, capacity, got, marks, front, back)
+    mine[...], theirs[...] = bins_of(regions, capacity, core, marks, front, back)
+
+
+def arrival_rows(regions, capacity, core, marks, own, other, out, front, back):
+    flag = core[0] > 0
+    x = own[...].astype(F32)
+    y = other[...].astype(F32)
+    front[0:SLOTS, :] = jnp.where(flag, y, x)
+    front[SLOTS:, :] = jnp.zeros((capacity, x.shape[1]), F32)
+    back[0:capacity, :] = jnp.zeros((capacity, x.shape[1]), F32)
+    back[capacity:, :] = jnp.where(flag, x, y)
+    row = iota((capacity, 1), 0)
+    for r in range(regions):
+        held = marks[0, r + 1] - marks[0, r]
+        rows = jnp.where(row < held, front[pl.ds(marks[0, r], capacity), :], back[pl.ds(marks[1, r], capacity), :])
+        out[r, 0:capacity, :] = rows.astype(BF16)
+
+
+def ungroup_kernel(regions, capacity, core, marks, own, other, out, front, back):
+    arrival_rows(regions, capacity, core, marks, own, other, out, front, back)
+
+
+def ungroup_grad_kernel(regions, capacity, core, marks, own, other, tagged, out, embed, front, back):
+    arrival_rows(regions, capacity, core, marks, own, other, out, front, back)
+    total = jnp.zeros((KIND_ROWS, own.shape[1]), F32)
+    for r in range(regions):
+        block = tagged[r, capacity : capacity + TAG_ROWS, :].astype(F32)
         if capacity >= LANES:
-            block = block.astype(F32)
-            pieces += [block[0:8], block[8:16]]
+            kind = jnp.concatenate([block[0:1], block[8:9]], axis=1)
         else:
-            shift = hot(iota((LANES, total), 1) == iota((LANES, total), 0) + r * capacity)
-            lanes = jnp.where(iota(block.shape, 1) < capacity, block.astype(F32), 0.0).astype(BF16)
-            tag_rows = tag_rows + mm(lanes, shift)[0:8]
-    if capacity >= LANES:
-        tag_rows = jnp.concatenate(pieces, axis=1)
-    tag_rows = tag_rows[0:8]
-    high = tag_rows[0:1]
-    low = tag_rows[1:2]
-    kind = tag_rows[2:3]
-    filled = high > 0.5
-    local = ((high - 1.0) * 128.0 + low).astype(I32)
-    swapped = jnp.bitwise_xor(local, core[0] * SLOTS)
-    landing = jnp.where(filled, swapped, FAR)
-    out_landing[...] = landing
-    place = iota((16, total), 0)
-    facts = jnp.where(place == 0, jnp.where(filled, 1.0, 0.0), jnp.where(place == 1, kind, 0.0)).astype(BF16)
-    step = 256
-    for s in range(0, 2 * SLOTS, step):
-        chosen = hot(iota((step, total), 0) + s == landing)
-        rows = mm(chosen, flat[...]).astype(BF16)
-        if s < SLOTS:
-            mine[s : s + step, :] = rows
-            out_info[:, s : s + step] = mm_nt(facts, chosen)
-        else:
-            theirs[s - SLOTS : s - SLOTS + step, :] = rows
-
-
-def regroup_kernel(regions, capacity, landing_ref, got, mine, theirs):
-    total = regions * capacity
-    landing = landing_ref[...]
-    flat = got[...].reshape(total, got.shape[2])
-    step = 256
-    for s in range(0, 2 * SLOTS, step):
-        chosen = hot(iota((step, total), 0) + s == landing)
-        rows = mm(chosen, flat).astype(BF16)
-        if s < SLOTS:
-            mine[s : s + step, :] = rows
-        else:
-            theirs[s - SLOTS : s - SLOTS + step, :] = rows
-
-
-def ungroup_kernel(regions, capacity, landing_ref, mine, other, *rest):
-    out = rest[-1]
-    total = regions * capacity
-    column = jnp.transpose(jnp.broadcast_to(landing_ref[...].astype(F32), (8, total)))[:, 0:1]
-    column = column.astype(I32)
-    both = jnp.concatenate([mine[...], other[...]], axis=0)
-    step = 256
-    for s in range(0, total, step):
-        chosen = hot(iota((step, 2 * SLOTS), 1) == column[s : s + step])
-        rows = mm(chosen, both).astype(BF16)
-        if capacity >= step:
-            out[s // capacity, s % capacity : s % capacity + step, :] = rows
-        else:
-            for k in range(step // capacity):
-                out[s // capacity + k, 0:capacity, :] = rows[k * capacity : (k + 1) * capacity]
-    if len(rest) > 1:
-        own, received, _ = rest
-        share = own.shape[0] // regions
-        for r in range(regions):
-            rows = slice(r * share, (r + 1) * share)
-            out[r, capacity : capacity + share, :] = (own[rows, :] + received[rows, :].astype(F32)).astype(BF16)
-
-
-def share_kernel(regions, capacity, got, out):
-    total = got[0, capacity:, :].astype(F32)
-    for r in range(1, regions):
-        total = total + got[r, capacity:, :].astype(F32)
-    total = total.astype(BF16)
+            kind = block[0:1, 0:capacity]
+        kinds_hot = hot(iota((KIND_ROWS, capacity), 0) == kind.astype(I32) - 1)
+        total = total + mm(kinds_hot, out[r, 0:capacity, :])
+    embed[...] = total
+
+
+def pair_kernel(regions, region, own, received, out_wide, out_low):
+    share = out_wide.shape[1]
+    for j in range(regions):
+        first = pl.multiple_of(jnp.bitwise_xor(region[0], j) * share, share)
+        total = own[pl.ds(first, share), :] + received[pl.ds(first, share), :].astype(F32)
+        out_wide[j] = total
+        out_low[j] = total.astype(BF16)
+
+
+def spread_kernel(regions, factor, region, got, out_q, out_k, out_v, out_o, out_gain, out_embed, flat):
+    width, half = out_q.shape
+    share = 4 * width // regions
+    extra = jnp.zeros((KIND_ROWS + 16, half), F32)
     for r in range(regions):
-        out[r] = total
-
-
-def spread_kernel(factor, got, out_q, out_k, out_v, out_o, out_gain, out_embed):
-    total = got[...].reshape(got.shape[0] * got.shape[1], got.shape[2]).astype(F32) * factor
-    width, half = out_q.shape
-    out_q[...] = total[0:width]
-    out_k[...] = total[width : 2 * width]
-    out_v[...] = total[2 * width : 3 * width]
-    place = 3 * width
-    out_o[:, 0:half] = total[place : place + half]
-    out_o[:, half:] = total[place + half : place + width]
-    place += width
-    out_embed[...] = total[place : place + KINDS]
-    place += KIND_ROWS
-    out_gain[:, 0:half] = total[place : place + 1]
-    out_gain[:, half:] = total[place + 1 : place + 2]
+        chunk = got[jnp.bitwise_xor(region[0], r)].astype(F32) * factor
+        flat[r * share : (r + 1) * share, :] = chunk[0:share]
+        extra = extra + chunk[share : share + KIND_ROWS + 16]
+    out_q[...] = flat[0:width]
+    out_k[...] = flat[width : 2 * width]
+    out_v[...] = flat[2 * width : 3 * width]
+    out_o[:, 0:half] = flat[3 * width : 3 * width + half]
+    out_o[:, half:] = flat[3 * width + half : 4 * width]
+    out_embed[...] = extra[0:KINDS]
+    out_gain[:, 0:half] = extra[KIND_ROWS : KIND_ROWS + 1]
+    out_gain[:, half:] = extra[KIND_ROWS + 1 : KIND_ROWS + 2]
 
 
 def pick_kernel(target_ref, got, out):
@@ -377,21 +385,11 @@
             grad_keep[place : place + half, :] = jnp.where(flag, block[half:], block[:half])
             grad_send[place : place + half, :] = jnp.where(flag, block[:half], block[half:]).astype(BF16)
             place += half
-        kinds_hot = hot(jnp.logical_and(iota((KIND_ROWS, SLOTS), 0) == info[1:2, :].astype(I32), info[0:1, :] > 0.5))
-        grad = mm(kinds_hot, d_slab)
-        grad_keep[place : place + KIND_ROWS, :] = jnp.where(flag, grad[:, half:], grad[:, :half])
-        grad_send[place : place + KIND_ROWS, :] = jnp.where(flag, grad[:, :half], grad[:, half:]).astype(BF16)
-        place += KIND_ROWS
         gain_grad = jnp.sum(d_normed * wide * inverse, axis=0, keepdims=True)
         pick = iota((16, half), 0)
         block = jnp.where(pick == 0, gain_grad[:, :half], jnp.where(pick == 1, gain_grad[:, half:], 0.0))
         grad_keep[place : place + 16, :] = block
         grad_send[place : place + 16, :] = block.astype(BF16)
-        place += 16
-        rest = grad_keep.shape[0] - place
-        if rest:
-            grad_keep[place:, :] = jnp.zeros((rest, half), F32)
-            grad_send[place:, :] = jnp.zeros((rest, half), BF16)
 
 
 def shape(dims, dtype):
@@ -406,10 +404,14 @@
     return pl.BlockSpec(tuple(array.shape), lambda *_: zeros)
 
 
-def simple_call(kernel, outs, inputs, scratch=(), scalars=0):
+def simple_call(kernel, outs, inputs, scratch=(), scalars=0, scalar_outs=0):
     specs = [SMEM_SPEC] * scalars + [whole(x) for x in inputs[scalars:]]
     return pl.pallas_call(
-        kernel, out_shape=outs, in_specs=specs, out_specs=tuple(whole(x) for x in outs), scratch_shapes=scratch
+        kernel,
+        out_shape=outs,
+        in_specs=specs,
+        out_specs=tuple(whole(x) for x in outs[: len(outs) - scalar_outs]) + (SMEM_SPEC,) * scalar_outs,
+        scratch_shapes=scratch,
     )(*inputs)
 
 
@@ -443,27 +445,30 @@
         return lax.all_to_all(x, "region", split_axis=0, concat_axis=0, tiled=True)
 
     gain = norm_gain.reshape(1, width)
-    packed_base, packed_cot, target, w_own = simple_call(
+    kinds_row = element_kinds.reshape(1, count)
+    packed_shape = shape((regions, capacity, half), BF16)
+    tagged_shape = shape((regions, capacity + TAG_ROWS, half), BF16)
+    packed_base, target, w_own = simple_call(
         functools.partial(pack_kernel, regions, capacity),
-        (
-            shape((regions, capacity + TAG_ROWS, half), BF16),
-            shape((regions, capacity, half), BF16),
-            shape((1, count), I32),
-            shape((4, width, half), BF16),
-        ),
-        (bin_cells.reshape(1, count), element_kinds.reshape(1, count), features, kind_embed, cotangent, w_query, w_key, w_value, w_out),
+        (tagged_shape, shape((1, count), I32), shape((4, width, half), BF16)),
+        (bin_cells.reshape(1, count), kinds_row, features, kind_embed, w_query, w_key, w_value, w_out),
     )
     w_other = other_core(w_own)
     got_base = exchange(packed_base)
+    (packed_cot,) = simple_call(
+        functools.partial(pack_cot_kernel, regions, capacity), (tagged_shape,), (target, kinds_row, cotangent)
+    )
     got_base, packed_cot = lax.optimization_barrier((got_base, packed_cot))
     got_cot = exchange(packed_cot)
     rows_shape = shape((SLOTS, half), BF16)
-    mine, theirs, landing, info = simple_call(
+    lift = pltpu.VMEM((SLOTS + capacity, half), F32)
+    mine, theirs, info, marks = simple_call(
         functools.partial(group_kernel, regions, capacity),
-        (rows_shape, rows_shape, shape((1, local_rows), I32), shape((16, SLOTS), F32)),
+        (rows_shape, rows_shape, shape((8, SLOTS), F32), shape((2, regions + 1), I32)),
         (core, got_base),
-        scratch=(pltpu.VMEM((local_rows, half), BF16),),
+        scratch=(lift, lift),
         scalars=1,
+        scalar_outs=1,
     )
     other = other_core(theirs)
 
@@ -501,17 +506,22 @@
     attn_other = other_core(attn_send)
     (packed_attn,) = simple_call(
         functools.partial(ungroup_kernel, regions, capacity),
-        (shape((regions, capacity, half), BF16),),
-        (landing, attn_keep, attn_other),
+        (packed_shape,),
+        (core, marks, attn_keep, attn_other),
+        scratch=(lift, lift),
+        scalars=2,
     )
 
     g_mine, g_theirs = simple_call(
-        functools.partial(regroup_kernel, regions, capacity), (rows_shape, rows_shape), (landing, got_cot)
+        functools.partial(regroup_kernel, regions, capacity),
+        (rows_shape, rows_shape),
+        (core, marks, got_cot),
+        scratch=(lift, lift),
+        scalars=2,
     )
     g_other = other_core(g_theirs)
 
-    unit = 16 * regions
-    grad_rows = -(-(4 * width + KIND_ROWS + 16) // unit) * unit
+    grad_rows = 4 * width + 16
     inputs = (core, mine, other, g_mine, g_other, w_own, w_other, gain, info, queries, keys, values, exps, context, inv)
     outs = (rows_shape, rows_shape, shape((grad_rows, half), F32), shape((grad_rows, half), BF16))
     d_keep, d_send, grad_keep, grad_send = pl.pallas_call(
@@ -538,28 +548,53 @@
         (rows,) = simple_call(pick_kernel, (shape((count, half), BF16),), (target, home))
         return rows
 
-    share = grad_rows // regions
-    (packed_grad,) = simple_call(
-        functools.partial(ungroup_kernel, regions, capacity),
-        (shape((regions, capacity + share, half), BF16),),
-        (landing, d_keep, other_core(d_send), grad_keep, other_core(grad_send)),
+    packed_grad, embed_part = simple_call(
+        functools.partial(ungroup_grad_kernel, regions, capacity),
+        (packed_shape, shape((KIND_ROWS, half), F32)),
+        (core, marks, d_keep, other_core(d_send), got_cot),
+        scratch=(lift, lift),
+        scalars=2,
     )
     got_cot, packed_attn = lax.optimization_barrier((got_cot, packed_attn))
     home_attn = exchange(packed_attn)
     home_attn, packed_grad = lax.optimization_barrier((home_attn, packed_grad))
     home_grad = exchange(packed_grad)
-    (shares,) = simple_call(
-        functools.partial(share_kernel, regions, capacity), (shape((regions, share, half), BF16),), (home_grad,)
-    )
-    summed = exchange(shares)
+
+    region = lax.axis_index("region").astype(I32).reshape(1)
+    share = 4 * width // regions
+    grad_other = other_core(grad_send)
+    wide, low = simple_call(
+        functools.partial(pair_kernel, regions),
+        (shape((regions, share, half), F32), shape((regions, share, half), BF16)),
+        (region, grad_keep, grad_other),
+        scalars=1,
+    )
+    gain_part = grad_keep[4 * width :] + grad_other[4 * width :].astype(F32)
+
+    def partner(x, bit):
+        return lax.ppermute(x, "region", [(i, i ^ bit) for i in range(regions)])
+
+    bit = regions // 2
+    while bit:
+        got = partner(low[bit : 2 * bit], bit)
+        wide = wide[:bit] + got.astype(F32)
+        low = wide.astype(BF16)
+        bit //= 2
+    gathered = jnp.concatenate([low[0], embed_part.astype(BF16), gain_part.astype(BF16)], axis=0)[None]
+    bit = 1
+    while bit < regions:
+        gathered = jnp.concatenate([gathered, partner(gathered, bit)], axis=0)
+        bit *= 2
+    column_shape = shape((width, half), F32)
+    grad_q, grad_k, grad_v, grad_o, grad_gain, grad_embed = simple_call(
+        functools.partial(spread_kernel, regions, float(count * regions) ** (-0.5)),
+        (column_shape, column_shape, column_shape, shape((half, width), F32), shape((1, width), F32), shape((KINDS, half), F32)),
+        (region, gathered),
+        scratch=(pltpu.VMEM((4 * width, half), F32),),
+        scalars=1,
+    )
     attended = pick(home_attn)
     grad_feats = pick(home_grad)
-    column_shape = shape((width, half), F32)
-    grad_q, grad_k, grad_v, grad_o, grad_gain, grad_embed = simple_call(
-        functools.partial(spread_kernel, float(count * regions) ** (-0.5)),
-        (column_shape, column_shape, column_shape, shape((half, width), F32), shape((1, width), F32), shape((KINDS, half), F32)),
-        (summed,),
-    )
     return (attended, grad_feats, grad_q, grad_k, grad_v, grad_o, grad_gain.reshape(width), grad_embed)
 
 

time: 155 us -> 160 us (1.032)
  blocking collectives: 28 us -> 0 us
  waiting for transfers between devices: 18.4 us -> 45.2 us
  starting transfers between devices: 21.4 us -> 32.1 us
  Pallas kernels: 80.4 us -> 71.7 us
  other arithmetic: 0 us -> 3.19 us
    all_to_all x1 -> x0, blocking collectives: 28 us -> none  [exchange(): return lax.all_to_all(x, 'region', split_axis=0, concat_axis=0, tiled=True)]
    ppermute x0 -> x6, waiting for transfers between devices: none -> 21.7 us  [partner(): return lax.ppermute(x, 'region', [(i, i ^ bit) for i in range(regions)])]
    ppermute x0 -> x6, starting transfers between devices: none -> 12.6 us  [partner(): return lax.ppermute(x, 'region', [(i, i ^ bit) for i in range(regions)])]
    pallas_call x9 -> x10, Pallas kernels: 36.4 us -> 27.9 us  [simple_call(): pl.pallas_call(kernel, out_shape=outs, in_specs=specs, out_specs=tuple((w...]
    all_to_all x4, waiting for transfers between devices: 16.7 us -> 23.4 us  [exchange(): return lax.all_to_all(x, 'region', split_axis=0, concat_axis=0, tiled=True)]
    all_to_all x4, starting transfers between devices: 20.3 us -> 18.4 us  [exchange(): return lax.all_to_all(x, 'region', split_axis=0, concat_axis=0, tiled=True)]
    ppermute x6, waiting for transfers between devices: 1.67 us -> 0.02 us  [other_core(): return lax.ppermute(x, 'head', swap)]
  transfers between devices with their start and end apart: 10 -> 16, of which waited for: 3 -> 6; matrix products, arithmetic and copies ran while one was open for 0% -> 3% of each run, Pallas kernels for 47% -> 41%
where the time goes in v3:
time: 160 us; the launch traced here: 159 us
  Pallas kernels  71.7 us (45%)
  waiting for transfers between devices  45.2 us (28%)
  starting transfers between devices  32.1 us (20%)
  local copies, waits for them, and re-layouts  6.1 us (4%)
  other arithmetic  3.19 us (2%)
    pallas_call x10, Pallas kernels, simple_call(): pl.pallas_call(kernel, out_shape=outs, in_specs=specs, out_specs=tuple((w...  27.9 us
    pallas_call x1, Pallas kernels, on_device(): pl.pallas_call(functools.partial(backward_kernel, heads), grid=(heads,),...  23.5 us
    all_to_all x4, waiting for transfers between devices, exchange(): return lax.all_to_all(x, 'region', split_axis=0, concat_axis=0, tiled=True)  23.4 us
    ppermute x6, waiting for transfers between devices, partner(): return lax.ppermute(x, 'region', [(i, i ^ bit) for i in range(regions)])  21.7 us
    pallas_call x1, Pallas kernels, on_device(): pl.pallas_call(functools.partial(forward_kernel, heads), grid=(heads,), o...  20.3 us
    all_to_all x4, starting transfers between devices, exchange(): return lax.all_to_all(x, 'region', split_axis=0, concat_axis=0, tiled=True)  18.4 us
    ppermute x6, starting transfers between devices, partner(): return lax.ppermute(x, 'region', [(i, i ^ bit) for i in range(regions)])  12.6 us
    unnamed x20, local copies, waits for them, and re-layouts  5.17 us
  transfers between devices with their start and end apart: 16, of which 6 were waited for; matrix products, arithmetic and copies ran while one was open for 3% of the time, Pallas kernels for 41%

profile of v3, /device:TPU:0, one launch (start us, length us, event | category | flops | bytes accessed | tf_op | source)
XLA Modules:
  0.0 159.1 jit_solution(15419104429332792754)
XLA Ops:
  0.6 3.6 %shard_map.161 = (bf16[8,272,128]{2,1,0:T(8,128)(2,1)}, s32[1,1024]{1,0:T(1,128)}, bf16[4,256,128]{2,1,0:T(8,128)(2,1)}) custom-call(s32[1,1024]{1,0:T(1,128)} %bitcast.12, s32[1,1024]{1,0:T(1,128)} %bitcast.10, bf16[1024,128]{1,0:T(8,128)(2,1)} %feats.1, bf16[12,128]{1,0:T(8,128)(2,1)} %embed.1, bf16[256,128]{1,0:T(8,128)(2,1)} %w_q.1, ...), custom_call_target="tpu_custom_call" | custom-call | tf_op jit(solution)/shard_map/pallas_call | solution.py:409
  4.2 7.3 %all-to-all-start = ((bf16[8,272,128]{2,1,0:T(8,128)(2,1)}), bf16[8,272,128]{2,1,0:T(8,128)(2,1)S(1)}, u32[]{:S(2)}, u32[]{:S(2)}) async-start(bf16[8,272,128]{2,1,0:T(8,128)(2,1)} %get-tuple-element.45), calls=%async_computation | async-start | bytes 1114112 | tf_op jit(solution)/shard_map/all_to_all | solution.py:445
  11.6 4.0 %shard_map.162 = bf16[8,272,128]{2,1,0:T(8,128)(2,1)} custom-call(s32[1,1024]{1,0:T(1,128)} %get-tuple-element.44.target_ref, s32[1,1024]{1,0:T(1,128)} %bitcast.11, bf16[1024,128]{1,0:T(8,128)(2,1)} %cot.1), custom_call_target="tpu_custom_call" | custom-call | tf_op jit(solution)/shard_map/pallas_call | solution.py:409
  15.6 11.1 %all-to-all-done.got = bf16[8,272,128]{2,1,0:T(8,128)(2,1)S(1)} async-done(((bf16[8,272,128]{2,1,0:T(8,128)(2,1)}), bf16[8,272,128]{2,1,0:T(8,128)(2,1)S(1)}, u32[]{:S(2)}, u32[]{:S(2)}) %all-to-all-start) | async-done | bytes 557088 | tf_op jit(solution)/shard_map/all_to_all | solution.py:445
  26.8 3.7 %all-to-all-start.1 = ((bf16[8,272,128]{2,1,0:T(8,128)(2,1)}), bf16[8,272,128]{2,1,0:T(8,128)(2,1)S(1)}, u32[]{:S(2)}, u32[]{:S(2)}) async-start(bf16[8,272,128]{2,1,0:T(8,128)(2,1)} %shard_map.162), calls=%async_computation.1 | async-start | bytes 1114112 | tf_op jit(solution)/shard_map/all_to_all | solution.py:445
  30.6 2.3 %shard_map.163 = (bf16[1024,128]{1,0:T(8,128)(2,1)}, bf16[1024,128]{1,0:T(8,128)(2,1)}, f32[8,1024]{1,0:T(8,128)}, s32[2,9]{1,0:T(2,128)}) custom-call(s32[1]{0:T(128)} %bitcast.2.core, bf16[8,272,128]{2,1,0:T(8,128)(2,1)} %copy-done.1), custom_call_target="tpu_custom_call" | custom-call | tf_op jit(solution)/shard_map/pallas_call | solution.py:409
  33.5 12.3 %all-to-all-done.1.got.tagged = bf16[8,272,128]{2,1,0:T(8,128)(2,1)S(1)} async-done(((bf16[8,272,128]{2,1,0:T(8,128)(2,1)}), bf16[8,272,128]{2,1,0:T(8,128)(2,1)S(1)}, u32[]{:S(2)}, u32[]{:S(2)}) %all-to-all-start.1) | async-done | bytes 557088 | tf_op jit(solution)/shard_map/all_to_all | solution.py:445
  46.6 2.2 %shard_map.165 = (bf16[1024,128]{1,0:T(8,128)(2,1)}, bf16[1024,128]{1,0:T(8,128)(2,1)}) custom-call(s32[1]{0:T(128)} %bitcast.2.core, s32[2,9]{1,0:T(2,128)} %get-tuple-element.48.marks, bf16[8,272,128]{2,1,0:T(8,128)(2,1)} %copy-done), custom_call_target="tpu_custom_call" | custom-call | tf_op jit(solution)/shard_map/pallas_call | solution.py:409
  49.6 20.3 %forward.1 = (bf16[1024,256]{1,0:T(8,128)(2,1)}, bf16[1024,256]{1,0:T(8,128)(2,1)}, bf16[1024,256]{1,0:T(8,128)(2,1)}, bf16[8,1024,1024]{2,1,0:T(8,128)(2,1)}, f...) custom-call(s32[1]{0:T(128)} %bitcast.2.core, ...), custom_call_target="tpu_custom_call" | custom-call | flops 8589934592 | bytes 16777216 | tf_op jit(solution)/shard_map/forward/pallas_call | solution.py:490
  71.1 23.5 %backward.1 = (bf16[1024,128]{1,0:T(8,128)(2,1)}, bf16[1024,128]{1,0:T(8,128)(2,1)}, f32[1040,128]{1,0:T(8,128)}, bf16[1040,128]{1,0:T(8,128)(2,1)}) custom-call(s32[1]{0:T(128)} %bitcast.2.core, bf16[1024,128]{1,0:T(8,128)(2,1)} %get-tuple-element.49.mine, bf16[1024,128]{1,0:T(8,128)(2,1)} %copy-done.8, bf16[1024,128]{1,0:T(8,128)(2,1)} %get-tuple-element.56.g_mine, ...), custom_call_target="tpu_custom_call" | custom-call | flops 17179869184 | bytes 16777216 | tf_op jit(solution)/shard_map/backward/pallas_call | solution.py:527
  95.3 2.2 %shard_map.164 = bf16[8,256,128]{2,1,0:T(8,128)(2,1)} custom-call(s32[1]{0:T(128)} %bitcast.2.core, s32[2,9]{1,0:T(2,128)} %get-tuple-element.48.marks, bf16[1024,128]{1,0:T(8,128)(2,1)} %get-tuple-element.53.own, bf16[1024,128]{1,0:T(8,128)(2,1)} %copy-done.5), custom_call_target="tpu_custom_call" | custom-call | tf_op jit(solution)/shard_map/pallas_call | solution.py:409
  97.5 3.6 %all-to-all-start.2 = ((bf16[8,256,128]{2,1,0:T(8,128)(2,1)}), bf16[8,256,128]{2,1,0:T(8,128)(2,1)S(1)}, u32[]{:S(2)}, u32[]{:S(2)}) async-start(bf16[8,256,128]{2,1,0:T(8,128)(2,1)} %shard_map.164), calls=%async_computation.2 | async-start | bytes 1048576 | tf_op jit(solution)/shard_map/all_to_all | solution.py:445
  101.9 2.1 %shard_map.169 = (f32[8,128,128]{2,1,0:T(8,128)}, bf16[8,128,128]{2,1,0:T(8,128)(2,1)}) custom-call(s32[1]{0:T(128)} %bitcast.4.region, f32[1040,128]{1,0:T(8,128)} %get-tuple-element.69.own, bf16[1040,128]{1,0:T(8,128)(2,1)} %copy-done.4), custom_call_target="tpu_custom_call" | custom-call | tf_op jit(solution)/shard_map/pallas_call | solution.py:409
  104.9 3.0 %collective-permute-start.6 = (bf16[4,128,128]{2,1,0:T(8,128)(2,1)S(1)}, bf16[4,128,128]{2,1,0:T(8,128)(2,1)S(1)}, u32[]{:S(2)}, u32[]{:S(2)}) collective-permute-start(bf16[4,128,128]{2,1,0:T(8,128)(2,1)S(1)} %slice.25), channel_id=1, source_target_pairs={{0,8},{2,10},{4,12},{6,14},{8,0},{10,2},{12,4},{14,6},{1,9},{3,11}... | collective-permute-start | bytes 393224 | tf_op jit(solution)/shard_map/ppermute | solution.py:575
  107.8 14.2 %collective-permute-done.6 = bf16[4,128,128]{2,1,0:T(8,128)(2,1)S(1)} collective-permute-done((bf16[4,128,128]{2,1,0:T(8,128)(2,1)S(1)}, bf16[4,128,128]{2,1,0:T(8,128)(2,1)S(1)}, u32[]{:S(2)}, u32[]{:S(2)}) %collective-permute-start.6) | collective-permute-done | bytes 131104 | tf_op jit(solution)/shard_map/ppermute | solution.py:575
  123.8 2.4 %shard_map.166 = (bf16[8,256,128]{2,1,0:T(8,128)(2,1)}, f32[16,128]{1,0:T(8,128)}) custom-call(s32[1]{0:T(128)} %bitcast.2.core, s32[2,9]{1,0:T(2,128)} %get-tuple-element.48.marks, bf16[1024,128]{1,0:T(8,128)(2,1)} %get-tuple-element.64.own, bf16[1024,128]{1,0:T(8,128)(2,1)} %copy-done.6, bf16[8,272,128]{2,1,0:T(8,128)(2,1)} %copy-done), custom_call_target="tpu_custom_call" | custom-call | tf_op jit(solution)/shard_map/pallas_call | solution.py:409
  129.6 3.7 %all-to-all-start.3 = ((bf16[8,256,128]{2,1,0:T(8,128)(2,1)}), bf16[8,256,128]{2,1,0:T(8,128)(2,1)S(1)}, u32[]{:S(2)}, u32[]{:S(2)}) async-start(bf16[8,256,128]{2,1,0:T(8,128)(2,1)} %get-tuple-element.68), calls=%async_computation.3 | async-start | bytes 1048576 | tf_op jit(solution)/shard_map/all_to_all | solution.py:445
  135.1 3.9 %collective-permute-done.9 = bf16[1,160,128]{2,1,0:T(8,128)(2,1)S(1)} collective-permute-done((bf16[1,160,128]{2,1,0:T(8,128)(2,1)S(1)}, bf16[1,160,128]{2,1,0:T(8,128)(2,1)S(1)}, u32[]{:S(2)}, u32[]{:S(2)}) %collective-permute-start.9) | collective-permute-done | bytes 40992 | tf_op jit(solution)/shard_map/ppermute | solution.py:575
  139.1 2.8 %collective-permute-start.10 = (bf16[2,160,128]{2,1,0:T(8,128)(2,1)S(1)}, bf16[2,160,128]{2,1,0:T(8,128)(2,1)S(1)}, u32[]{:S(2)}, u32[]{:S(2)}) collective-permute-start(bf16[2,160,128]{2,1,0:T(8,128)(2,1)S(1)} %pad_maximum_fusion.2), channel_id=1, source_target_pairs={{0,4},{2,6},{4,0},{6,2},{8,12},{10,14},{12,8},{14,10},{1,5},{3,7},... | collective-permute-start | bytes 245768 | tf_op jit(solution)/shard_map/ppermute | solution.py:575
  141.9 3.2 %collective-permute-done.10 = bf16[2,160,128]{2,1,0:T(8,128)(2,1)S(1)} collective-permute-done((bf16[2,160,128]{2,1,0:T(8,128)(2,1)S(1)}, bf16[2,160,128]{2,1,0:T(8,128)(2,1)S(1)}, u32[]{:S(2)}, u32[]{:S(2)}) %collective-permute-start.10) | collective-permute-done | bytes 81952 | tf_op jit(solution)/shard_map/ppermute | solution.py:575
  145.1 3.4 %collective-permute-start.11 = (bf16[4,160,128]{2,1,0:T(8,128)(2,1)S(1)}, bf16[4,160,128]{2,1,0:T(8,128)(2,1)S(1)}, u32[]{:S(2)}, u32[]{:S(2)}) collective-permute-start(bf16[4,160,128]{2,1,0:T(8,128)(2,1)S(1)} %pad_maximum_fusion.1), channel_id=1, source_target_pairs={{0,8},{2,10},{4,12},{6,14},{8,0},{10,2},{12,4},{14,6},{1,9},{3,11}... | collective-permute-start | bytes 491528 | tf_op jit(solution)/shard_map/ppermute | solution.py:575
  148.5 3.6 %shard_map.167 = bf16[1024,128]{1,0:T(8,128)(2,1)} custom-call(s32[1,1024]{1,0:T(1,128)} %get-tuple-element.44.target_ref, bf16[8,256,128]{2,1,0:T(8,128)(2,1)} %copy-done.2), custom_call_target="tpu_custom_call" | custom-call | tf_op jit(solution)/shard_map/pallas_call | solution.py:409
  152.9 1.8 %shard_map.170 = (f32[256,128]{1,0:T(8,128)}, f32[256,128]{1,0:T(8,128)}, f32[256,128]{1,0:T(8,128)}, f32[128,256]{1,0:T(8,128)}, f32[1,256]{1,0:T(1,128)}, /*index=5*/f32[12,128]{1,0:T(8,128)}) custom-call(s32[1]{0:T(128)} %bitcast.4.region, bf16[8,160,128]{2,1,0:T(8,128)(2,1)} %pad_maximum_fusion.got), custom_call_target="tpu_custom_call" | custom-call | tf_op jit(solution)/shard_map/pallas_call | solution.py:409
  155.5 3.6 %shard_map.168 = bf16[1024,128]{1,0:T(8,128)(2,1)} custom-call(s32[1,1024]{1,0:T(1,128)} %get-tuple-element.44.target_ref, bf16[8,256,128]{2,1,0:T(8,128)(2,1)} %copy-done.3), custom_call_target="tpu_custom_call" | custom-call | tf_op jit(solution)/shard_map/pallas_call | solution.py:409
  (52 shorter events, 14.3 us)
Async XLA Ops:
  4.2 22.5 %all-to-all-start = ((bf16[8,272,128]{2,1,0:T(8,128)(2,1)}), bf16[8,272,128]{2,1,0:T(8,128)(2,1)S(1)}, u32[]{:S(2)}, u32[]{:S(2)}) async-start(bf16[8,272,128]{2,1,0:T(8,128)(2,1)} %get-tuple-element.45), calls=%async_computation | async-start | bytes 1114112 | tf_op jit(solution)/shard_map/all_to_all | solution.py:445
  26.8 3.8 %copy-start.1 = (bf16[8,272,128]{2,1,0:T(8,128)(2,1)}, bf16[8,272,128]{2,1,0:T(8,128)(2,1)S(1)}, u32[]{:S(2)}) copy-start(bf16[8,272,128]{2,1,0:T(8,128)(2,1)S(1)} %all-to-all-done.got) | copy-start | bytes 1671172
  26.8 19.0 %all-to-all-start.1 = ((bf16[8,272,128]{2,1,0:T(8,128)(2,1)}), bf16[8,272,128]{2,1,0:T(8,128)(2,1)S(1)}, u32[]{:S(2)}, u32[]{:S(2)}) async-start(bf16[8,272,128]{2,1,0:T(8,128)(2,1)} %shard_map.162), calls=%async_computation.1 | async-start | bytes 1114112 | tf_op jit(solution)/shard_map/all_to_all | solution.py:445
  30.5 18.3 %collective-permute-start.1 = (bf16[4,256,128]{2,1,0:T(8,128)(2,1)}, bf16[4,256,128]{2,1,0:T(8,128)(2,1)S(1)}, u32[]{:S(2)}, u32[]{:S(2)}) collective-permute-start(bf16[4,256,128]{2,1,0:T(8,128)(2,1)} %get-tuple-element.51.w_own), channel_id=1, source_target_pairs={{0,1},{1,0},{2,3},{3,2},{4,5},{5,4},{6,7},{7,6},{8,9},{9,8},{10,11... | collective-permute-start | bytes 786440 | tf_op jit(solution)/shard_map/ppermute | solution.py:442
  32.9 15.8 %collective-permute-start = (bf16[1024,128]{1,0:T(8,128)(2,1)}, bf16[1024,128]{1,0:T(8,128)(2,1)S(1)}, u32[]{:S(2)}, u32[]{:S(2)}) collective-permute-start(bf16[1024,128]{1,0:T(8,128)(2,1)} %get-tuple-element.50), channel_id=1, source_target_pairs={{0,1},{1,0},{2,3},{3,2},{4,5},{5,4},{6,7},{7,6},{8,9},{9,8},{10,11... | collective-permute-start | bytes 786440 | tf_op jit(solution)/shard_map/ppermute | solution.py:442
  45.8 0.8 copy-start
  48.8 21.6 %collective-permute-start.3 = (bf16[1024,128]{1,0:T(8,128)(2,1)}, bf16[1024,128]{1,0:T(8,128)(2,1)S(1)}, u32[]{:S(2)}, u32[]{:S(2)}) collective-permute-start(bf16[1024,128]{1,0:T(8,128)(2,1)} %get-tuple-element.57), channel_id=1, source_target_pairs={{0,1},{1,0},{2,3},{3,2},{4,5},{5,4},{6,7},{7,6},{8,9},{9,8},{10,11... | collective-permute-start | bytes 786440 | tf_op jit(solution)/shard_map/ppermute | solution.py:442
  48.8 0.8 copy-start.8
  69.9 24.8 %collective-permute-start.2 = (bf16[1024,128]{1,0:T(8,128)(2,1)}, bf16[1024,128]{1,0:T(8,128)(2,1)S(1)}, u32[]{:S(2)}, u32[]{:S(2)}) collective-permute-start(bf16[1024,128]{1,0:T(8,128)(2,1)} %get-tuple-element.54), channel_id=1, source_target_pairs={{0,1},{1,0},{2,3},{3,2},{4,5},{5,4},{6,7},{7,6},{8,9},{9,8},{10,11... | collective-permute-start | bytes 786440 | tf_op jit(solution)/shard_map/ppermute | solution.py:442
  70.4 0.7 copy-start.9
  94.6 6.6 %collective-permute-start.5 = (bf16[1040,128]{1,0:T(8,128)(2,1)}, bf16[1040,128]{1,0:T(8,128)(2,1)S(1)}, u32[]{:S(2)}, u32[]{:S(2)}) collective-permute-start(bf16[1040,128]{1,0:T(8,128)(2,1)} %get-tuple-element.70), channel_id=1, source_target_pairs={{0,1},{1,0},{2,3},{3,2},{4,5},{5,4},{6,7},{7,6},{8,9},{9,8},{10,11... | collective-permute-start | bytes 798728 | tf_op jit(solution)/shard_map/ppermute | solution.py:442
  94.6 0.7 copy-start.5
  97.5 32.1 %all-to-all-start.2 = ((bf16[8,256,128]{2,1,0:T(8,128)(2,1)}), bf16[8,256,128]{2,1,0:T(8,128)(2,1)S(1)}, u32[]{:S(2)}, u32[]{:S(2)}) async-start(bf16[8,256,128]{2,1,0:T(8,128)(2,1)} %shard_map.164), calls=%async_computation.2 | async-start | bytes 1048576 | tf_op jit(solution)/shard_map/all_to_all | solution.py:445
  104.9 17.1 %collective-permute-start.6 = (bf16[4,128,128]{2,1,0:T(8,128)(2,1)S(1)}, bf16[4,128,128]{2,1,0:T(8,128)(2,1)S(1)}, u32[]{:S(2)}, u32[]{:S(2)}) collective-permute-start(bf16[4,128,128]{2,1,0:T(8,128)(2,1)S(1)} %slice.25), channel_id=1, source_target_pairs={{0,8},{2,10},{4,12},{6,14},{8,0},{10,2},{12,4},{14,6},{1,9},{3,11}... | collective-permute-start | bytes 393224 | tf_op jit(solution)/shard_map/ppermute | solution.py:575
  107.8 15.2 %collective-permute-start.4 = (bf16[1024,128]{1,0:T(8,128)(2,1)}, bf16[1024,128]{1,0:T(8,128)(2,1)S(1)}, u32[]{:S(2)}, u32[]{:S(2)}) collective-permute-start(bf16[1024,128]{1,0:T(8,128)(2,1)} %get-tuple-element.65), channel_id=1, source_target_pairs={{0,1},{1,0},{2,3},{3,2},{4,5},{5,4},{6,7},{7,6},{8,9},{9,8},{10,11... | collective-permute-start | bytes 786440 | tf_op jit(solution)/shard_map/ppermute | solution.py:442
  123.0 4.3 %collective-permute-start.7 = (bf16[2,128,128]{2,1,0:T(8,128)(2,1)S(1)}, bf16[2,128,128]{2,1,0:T(8,128)(2,1)S(1)}, u32[]{:S(2)}, u32[]{:S(2)}) collective-permute-start(bf16[2,128,128]{2,1,0:T(8,128)(2,1)S(1)} %slice.48), channel_id=1, source_target_pairs={{0,4},{2,6},{4,0},{6,2},{8,12},{10,14},{12,8},{14,10},{1,5},{3,7},... | collective-permute-start | bytes 196616 | tf_op jit(solution)/shard_map/ppermute | solution.py:575
  123.1 0.7 copy-start.6
  127.4 6.0 %collective-permute-start.8 = (bf16[1,128,128]{2,1,0:T(8,128)(2,1)S(1)}, bf16[1,128,128]{2,1,0:T(8,128)(2,1)S(1)}, u32[]{:S(2)}, u32[]{:S(2)}) collective-permute-start(bf16[1,128,128]{2,1,0:T(8,128)(2,1)S(1)} %slice.49), channel_id=1, source_target_pairs={{0,2},{2,0},{4,6},{6,4},{8,10},{10,8},{12,14},{14,12},{1,3},{3,1},... | collective-permute-start | bytes 98312 | tf_op jit(solution)/shard_map/ppermute | solution.py:575
  129.6 18.9 %copy-start.2 = (bf16[8,256,128]{2,1,0:T(8,128)(2,1)}, bf16[8,256,128]{2,1,0:T(8,128)(2,1)S(1)}, u32[]{:S(2)}) copy-start(bf16[8,256,128]{2,1,0:T(8,128)(2,1)S(1)} %all-to-all-done.2.got) | copy-start | bytes 1572868
  129.6 25.1 %all-to-all-start.3 = ((bf16[8,256,128]{2,1,0:T(8,128)(2,1)}), bf16[8,256,128]{2,1,0:T(8,128)(2,1)S(1)}, u32[]{:S(2)}, u32[]{:S(2)}) async-start(bf16[8,256,128]{2,1,0:T(8,128)(2,1)} %get-tuple-element.68), calls=%async_computation.3 | async-start | bytes 1048576 | tf_op jit(solution)/shard_map/all_to_all | solution.py:445
  133.4 5.7 %collective-permute-start.9 = (bf16[1,160,128]{2,1,0:T(8,128)(2,1)S(1)}, bf16[1,160,128]{2,1,0:T(8,128)(2,1)S(1)}, u32[]{:S(2)}, u32[]{:S(2)}) collective-permute-start(bf16[1,160,128]{2,1,0:T(8,128)(2,1)S(1)} %maximum_bitcast_fusion), channel_id=1, source_target_pairs={{0,2},{2,0},{4,6},{6,4},{8,10},{10,8},{12,14},{14,12},{1,3},{3,1},... | collective-permute-start | bytes 122888 | tf_op jit(solution)/shard_map/ppermute | solution.py:575
  139.1 5.9 %collective-permute-start.10 = (bf16[2,160,128]{2,1,0:T(8,128)(2,1)S(1)}, bf16[2,160,128]{2,1,0:T(8,128)(2,1)S(1)}, u32[]{:S(2)}, u32[]{:S(2)}) collective-permute-start(bf16[2,160,128]{2,1,0:T(8,128)(2,1)S(1)} %pad_maximum_fusion.2), channel_id=1, source_target_pairs={{0,4},{2,6},{4,0},{6,2},{8,12},{10,14},{12,8},{14,10},{1,5},{3,7},... | collective-permute-start | bytes 245768 | tf_op jit(solution)/shard_map/ppermute | solution.py:575
  145.1 7.1 %collective-permute-start.11 = (bf16[4,160,128]{2,1,0:T(8,128)(2,1)S(1)}, bf16[4,160,128]{2,1,0:T(8,128)(2,1)S(1)}, u32[]{:S(2)}, u32[]{:S(2)}) collective-permute-start(bf16[4,160,128]{2,1,0:T(8,128)(2,1)S(1)} %pad_maximum_fusion.1), channel_id=1, source_target_pairs={{0,8},{2,10},{4,12},{6,14},{8,0},{10,2},{12,4},{14,6},{1,9},{3,11}... | collective-permute-start | bytes 491528 | tf_op jit(solution)/shard_map/ppermute | solution.py:575
  154.7 0.8 copy-start.3
  (2 other events, 1.4 us)

commit v4 on v3

--- a/solution.py
+++ b/solution.py
@@ -158,9 +158,10 @@
     arrival_rows(regions, capacity, core, marks, own, other, out, front, back)
 
 
-def ungroup_grad_kernel(regions, capacity, core, marks, own, other, tagged, out, embed, front, back):
+def ungroup_grad_kernel(regions, capacity, core, marks, own, other, tagged, grad_own, grad_other, out, extra, front, back):
     arrival_rows(regions, capacity, core, marks, own, other, out, front, back)
     total = jnp.zeros((KIND_ROWS, own.shape[1]), F32)
+    share = out.shape[1] - capacity
     for r in range(regions):
         block = tagged[r, capacity : capacity + TAG_ROWS, :].astype(F32)
         if capacity >= LANES:
@@ -169,24 +170,30 @@
             kind = block[0:1, 0:capacity]
         kinds_hot = hot(iota((KIND_ROWS, capacity), 0) == kind.astype(I32) - 1)
         total = total + mm(kinds_hot, out[r, 0:capacity, :])
-    embed[...] = total
-
-
-def pair_kernel(regions, region, own, received, out_wide, out_low):
-    share = out_wide.shape[1]
-    for j in range(regions):
-        first = pl.multiple_of(jnp.bitwise_xor(region[0], j) * share, share)
-        total = own[pl.ds(first, share), :] + received[pl.ds(first, share), :].astype(F32)
-        out_wide[j] = total
-        out_low[j] = total.astype(BF16)
-
-
-def spread_kernel(regions, factor, region, got, out_q, out_k, out_v, out_o, out_gain, out_embed, flat):
+        rows = slice(r * share, (r + 1) * share)
+        out[r, capacity:, :] = (grad_own[rows, :] + grad_other[rows, :].astype(F32)).astype(BF16)
+    extra[0:KIND_ROWS, :] = total.astype(BF16)
+    rows = slice(regions * share, regions * share + 16)
+    extra[KIND_ROWS:, :] = (grad_own[rows, :] + grad_other[rows, :].astype(F32)).astype(BF16)
+
+
+def share_kernel(regions, capacity, got, extra, out):
+    total = got[0, capacity:, :].astype(F32)
+    for r in range(1, regions):
+        total = total + got[r, capacity:, :].astype(F32)
+    share = total.shape[0]
+    total = total.astype(BF16)
+    for r in range(regions):
+        out[r, 0:share, :] = total
+        out[r, share:, :] = extra[...]
+
+
+def spread_kernel(regions, factor, got, out_q, out_k, out_v, out_o, out_gain, out_embed, flat):
     width, half = out_q.shape
     share = 4 * width // regions
     extra = jnp.zeros((KIND_ROWS + 16, half), F32)
     for r in range(regions):
-        chunk = got[jnp.bitwise_xor(region[0], r)].astype(F32) * factor
+        chunk = got[r].astype(F32) * factor
         flat[r * share : (r + 1) * share, :] = chunk[0:share]
         extra = extra + chunk[share : share + KIND_ROWS + 16]
     out_q[...] = flat[0:width]
@@ -548,10 +555,11 @@
         (rows,) = simple_call(pick_kernel, (shape((count, half), BF16),), (target, home))
         return rows
 
-    packed_grad, embed_part = simple_call(
+    share = 4 * width // regions
+    packed_grad, extra = simple_call(
         functools.partial(ungroup_grad_kernel, regions, capacity),
-        (packed_shape, shape((KIND_ROWS, half), F32)),
-        (core, marks, d_keep, other_core(d_send), got_cot),
+        (shape((regions, capacity + share, half), BF16), shape((KIND_ROWS + 16, half), BF16)),
+        (core, marks, d_keep, other_core(d_send), got_cot, grad_keep, other_core(grad_send)),
         scratch=(lift, lift),
         scalars=2,
     )
@@ -559,39 +567,18 @@
     home_attn = exchange(packed_attn)
     home_attn, packed_grad = lax.optimization_barrier((home_attn, packed_grad))
     home_grad = exchange(packed_grad)
-
-    region = lax.axis_index("region").astype(I32).reshape(1)
-    share = 4 * width // regions
-    grad_other = other_core(grad_send)
-    wide, low = simple_call(
-        functools.partial(pair_kernel, regions),
-        (shape((regions, share, half), F32), shape((regions, share, half), BF16)),
-        (region, grad_keep, grad_other),
-        scalars=1,
-    )
-    gain_part = grad_keep[4 * width :] + grad_other[4 * width :].astype(F32)
-
-    def partner(x, bit):
-        return lax.ppermute(x, "region", [(i, i ^ bit) for i in range(regions)])
-
-    bit = regions // 2
-    while bit:
-        got = partner(low[bit : 2 * bit], bit)
-        wide = wide[:bit] + got.astype(F32)
-        low = wide.astype(BF16)
-        bit //= 2
-    gathered = jnp.concatenate([low[0], embed_part.astype(BF16), gain_part.astype(BF16)], axis=0)[None]
-    bit = 1
-    while bit < regions:
-        gathered = jnp.concatenate([gathered, partner(gathered, bit)], axis=0)
-        bit *= 2
+    (shares,) = simple_call(
+        functools.partial(share_kernel, regions, capacity),
+        (shape((regions, share + KIND_ROWS + 16, half), BF16),),
+        (home_grad, extra),
+    )
+    summed = exchange(shares)
     column_shape = shape((width, half), F32)
     grad_q, grad_k, grad_v, grad_o, grad_gain, grad_embed = simple_call(
         functools.partial(spread_kernel, regions, float(count * regions) ** (-0.5)),
         (column_shape, column_shape, column_shape, shape((half, width), F32), shape((1, width), F32), shape((KINDS, half), F32)),
-        (region, gathered),
+        (summed,),
         scratch=(pltpu.VMEM((4 * width, half), F32),),
-        scalars=1,
     )
     attended = pick(home_attn)
     grad_feats = pick(home_grad)

time: 160 us -> 143 us (0.89)
  waiting for transfers between devices: 45.2 us -> 15.3 us
  blocking collectives: 0 us -> 26.5 us
  starting transfers between devices: 32.1 us -> 21.7 us
  other arithmetic: 3.19 us -> 0 us
    all_to_all x0 -> x1, blocking collectives: none -> 26.5 us  [exchange(): return lax.all_to_all(x, 'region', split_axis=0, concat_axis=0, tiled=True)]
    ppermute x6 -> x0, waiting for transfers between devices: 21.7 us -> none  [partner(): return lax.ppermute(x, 'region', [(i, i ^ bit) for i in range(regions)])]
    ppermute x6 -> x0, starting transfers between devices: 12.6 us -> none  [partner(): return lax.ppermute(x, 'region', [(i, i ^ bit) for i in range(regions)])]
    all_to_all x4, waiting for transfers between devices: 23.4 us -> 13.7 us  [exchange(): return lax.all_to_all(x, 'region', split_axis=0, concat_axis=0, tiled=True)]
    all_to_all x4, starting transfers between devices: 18.4 us -> 20.6 us  [exchange(): return lax.all_to_all(x, 'region', split_axis=0, concat_axis=0, tiled=True)]
    ppermute x6, waiting for transfers between devices: 0.02 us -> 1.63 us  [other_core(): return lax.ppermute(x, 'head', swap)]
  transfers between devices with their start and end apart: 16 -> 10, of which waited for: 6 -> 3; matrix products, arithmetic and copies ran while one was open for 3% -> 0% of each run, Pallas kernels for 41% -> 46%
where the time goes in v4:
time: 143 us; the launch traced here: 142 us
  Pallas kernels  72.2 us (50%)
  blocking collectives  26.5 us (19%)
  starting transfers between devices  21.7 us (15%)
  waiting for transfers between devices  15.3 us (11%)
  local copies, waits for them, and re-layouts  5.43 us (4%)
    pallas_call x10, Pallas kernels, simple_call(): pl.pallas_call(kernel, out_shape=outs, in_specs=specs, out_specs=tuple((w...  28.3 us
    all_to_all x1, blocking collectives, exchange(): return lax.all_to_all(x, 'region', split_axis=0, concat_axis=0, tiled=True)  26.5 us
    pallas_call x1, Pallas kernels, on_device(): pl.pallas_call(functools.partial(backward_kernel, heads), grid=(heads,),...  23.5 us
    all_to_all x4, starting transfers between devices, exchange(): return lax.all_to_all(x, 'region', split_axis=0, concat_axis=0, tiled=True)  20.6 us
    pallas_call x1, Pallas kernels, on_device(): pl.pallas_call(functools.partial(forward_kernel, heads), grid=(heads,), o...  20.4 us
    all_to_all x4, waiting for transfers between devices, exchange(): return lax.all_to_all(x, 'region', split_axis=0, concat_axis=0, tiled=True)  13.7 us
    unnamed x20, local copies, waits for them, and re-layouts  5.43 us
  transfers between devices with their start and end apart: 10, of which 3 were waited for; matrix products, arithmetic and copies ran while one was open for 0% of the time, Pallas kernels for 46%

profile of v4, /device:TPU:0, one launch (start us, length us, event | category | flops | bytes accessed | tf_op | source)
XLA Modules:
  0.0 141.9 jit_solution(6792051914169898917)
XLA Ops:
  0.6 3.6 %shard_map.161 = (bf16[8,272,128]{2,1,0:T(8,128)(2,1)}, s32[1,1024]{1,0:T(1,128)}, bf16[4,256,128]{2,1,0:T(8,128)(2,1)}) custom-call(s32[1,1024]{1,0:T(1,128)} %bitcast.7, s32[1,1024]{1,0:T(1,128)} %bitcast.5, bf16[1024,128]{1,0:T(8,128)(2,1)} %feats.1, bf16[12,128]{1,0:T(8,128)(2,1)} %embed.1, bf16[256,128]{1,0:T(8,128)(2,1)} %w_q.1, bf16[256,128]{1,0:T(8,128)(2,1)} %w_k.1, ...), custom_call_target="tpu_custom_call" | custom-call | tf_op jit(solution)/shard_map/pallas_call | solution.py:416
  4.2 7.3 %all-to-all-start = ((bf16[8,272,128]{2,1,0:T(8,128)(2,1)}), bf16[8,272,128]{2,1,0:T(8,128)(2,1)S(1)}, u32[]{:S(2)}, u32[]{:S(2)}) async-start(bf16[8,272,128]{2,1,0:T(8,128)(2,1)} %get-tuple-element.43), calls=%async_computation | async-start | bytes 1114112 | tf_op jit(solution)/shard_map/all_to_all | solution.py:452
  11.6 4.1 %shard_map.162 = bf16[8,272,128]{2,1,0:T(8,128)(2,1)} custom-call(s32[1,1024]{1,0:T(1,128)} %get-tuple-element.42.target_ref, s32[1,1024]{1,0:T(1,128)} %bitcast.6, bf16[1024,128]{1,0:T(8,128)(2,1)} %cot.1), custom_call_target="tpu_custom_call" | custom-call | tf_op jit(solution)/shard_map/pallas_call | solution.py:416
  15.7 11.1 %all-to-all-done.got = bf16[8,272,128]{2,1,0:T(8,128)(2,1)S(1)} async-done(((bf16[8,272,128]{2,1,0:T(8,128)(2,1)}), bf16[8,272,128]{2,1,0:T(8,128)(2,1)S(1)}, u32[]{:S(2)}, u32[]{:S(2)}) %all-to-all-start) | async-done | bytes 557088 | tf_op jit(solution)/shard_map/all_to_all | solution.py:452
  26.7 0.8 copy-done.1
  27.6 2.3 %shard_map.163 = (bf16[1024,128]{1,0:T(8,128)(2,1)}, bf16[1024,128]{1,0:T(8,128)(2,1)}, f32[8,1024]{1,0:T(8,128)}, s32[2,9]{1,0:T(2,128)}) custom-call(s32[1]{0:T(128)} %bitcast.2.core, bf16[8,272,128]{2,1,0:T(8,128)(2,1)} %copy-done.1), custom_call_target="tpu_custom_call" | custom-call | tf_op jit(solution)/shard_map/pallas_call | solution.py:416
  30.0 3.6 %all-to-all-start.1 = ((bf16[8,272,128]{2,1,0:T(8,128)(2,1)}), bf16[8,272,128]{2,1,0:T(8,128)(2,1)S(1)}, u32[]{:S(2)}, u32[]{:S(2)}) async-start(bf16[8,272,128]{2,1,0:T(8,128)(2,1)} %shard_map.162), calls=%async_computation.1 | async-start | bytes 1114112 | tf_op jit(solution)/shard_map/all_to_all | solution.py:452
  34.5 20.4 %forward.1 = (bf16[1024,256]{1,0:T(8,128)(2,1)}, bf16[1024,256]{1,0:T(8,128)(2,1)}, bf16[1024,256]{1,0:T(8,128)(2,1)}, bf16[8,1024,1024]{2,1,0:T(8,128)(2,1)}, f...) custom-call(s32[1]{0:T(128)} %bitcast.2.core, ...), custom_call_target="tpu_custom_call" | custom-call | flops 8589934592 | bytes 16777216 | tf_op jit(solution)/shard_map/forward/pallas_call | solution.py:497
  55.3 0.8 copy-done
  56.1 2.2 %shard_map.165 = (bf16[1024,128]{1,0:T(8,128)(2,1)}, bf16[1024,128]{1,0:T(8,128)(2,1)}) custom-call(s32[1]{0:T(128)} %bitcast.2.core, s32[2,9]{1,0:T(2,128)} %get-tuple-element.46.marks, bf16[8,272,128]{2,1,0:T(8,128)(2,1)} %copy-done), custom_call_target="tpu_custom_call" | custom-call | tf_op jit(solution)/shard_map/pallas_call | solution.py:416
  58.5 0.7 copy-done.5
  59.2 2.2 %shard_map.164 = bf16[8,256,128]{2,1,0:T(8,128)(2,1)} custom-call(s32[1]{0:T(128)} %bitcast.2.core, s32[2,9]{1,0:T(2,128)} %get-tuple-element.46.marks, bf16[1024,128]{1,0:T(8,128)(2,1)} %get-tuple-element.51.own, bf16[1024,128]{1,0:T(8,128)(2,1)} %copy-done.5), custom_call_target="tpu_custom_call" | custom-call | tf_op jit(solution)/shard_map/pallas_call | solution.py:416
  61.4 6.0 %all-to-all-start.2 = ((bf16[8,256,128]{2,1,0:T(8,128)(2,1)}), bf16[8,256,128]{2,1,0:T(8,128)(2,1)S(1)}, u32[]{:S(2)}, u32[]{:S(2)}) async-start(bf16[8,256,128]{2,1,0:T(8,128)(2,1)} %shard_map.164), calls=%async_computation.2 | async-start | bytes 1048576 | tf_op jit(solution)/shard_map/all_to_all | solution.py:452
  68.1 23.5 %backward.1 = (bf16[1024,128]{1,0:T(8,128)(2,1)}, bf16[1024,128]{1,0:T(8,128)(2,1)}, f32[1040,128]{1,0:T(8,128)}, bf16[1040,128]{1,0:T(8,128)(2,1)}) custom-call(s32[1]{0:T(128)} %bitcast.2.core, bf16[1024,128]{1,0:T(8,128)(2,1)} %get-tuple-element.47.mine, bf16[1024,128]{1,0:T(8,128)(2,1)} %copy-done.8, bf16[1024,128]{1,0:T(8,128)(2,1)} %get-tuple-element.54.g_mine, ...), custom_call_target="tpu_custom_call" | custom-call | flops 17179869184 | bytes 16777216 | tf_op jit(solution)/shard_map/backward/pallas_call | solution.py:534
  92.1 1.6 %collective-permute-done.4.other = bf16[1024,128]{1,0:T(8,128)(2,1)S(1)} collective-permute-done((bf16[1024,128]{1,0:T(8,128)(2,1)}, bf16[1024,128]{1,0:T(8,128)(2,1)S(1)}, u32[]{:S(2)}, u32[]{:S(2)}) %collective-permute-start.4) | collective-permute-done | bytes 262176 | tf_op jit(solution)/shard_map/ppermute | solution.py:449
  94.6 2.8 %shard_map.166 = (bf16[8,384,128]{2,1,0:T(8,128)(2,1)}, bf16[32,128]{1,0:T(8,128)(2,1)}) custom-call(s32[1]{0:T(128)} %bitcast.2.core, s32[2,9]{1,0:T(2,128)} %get-tuple-element.46.marks, bf16[1024,128]{1,0:T(8,128)(2,1)} %get-tuple-element.62.own, bf16[1024,128]{1,0:T(8,128)(2,1)} %copy-done.6, bf16[8,272,128]{2,1,0:T(8,128)(2,1)} %copy-done, ...), custom_call_target="tpu_custom_call" | custom-call | tf_op jit(solution)/shard_map/pallas_call | solution.py:416
  97.4 26.5 %all_to_all.25.got = bf16[8,384,128]{2,1,0:T(8,128)(2,1)} all-to-all(bf16[8,384,128]{2,1,0:T(8,128)(2,1)} %get-tuple-element.68), channel_id=1, replica_groups=mesh['groups'=2,'region'=8,'head'=2] {'region'}, dimensions={0} | all-to-all | bytes 1572864 | tf_op jit(solution)/shard_map/all_to_all | solution.py:452
  123.9 1.9 %shard_map.169 = bf16[8,160,128]{2,1,0:T(8,128)(2,1)} custom-call(bf16[8,384,128]{2,1,0:T(8,128)(2,1)} %all_to_all.25.got, bf16[32,128]{1,0:T(8,128)(2,1)} %get-tuple-element.69.extra), custom_call_target="tpu_custom_call" | custom-call | tf_op jit(solution)/shard_map/pallas_call | solution.py:416
  125.8 3.6 %all-to-all-start.4 = ((bf16[8,160,128]{2,1,0:T(8,128)(2,1)}), bf16[8,160,128]{2,1,0:T(8,128)(2,1)S(1)}, u32[]{:S(2)}, u32[]{:S(2)}) async-start(bf16[8,160,128]{2,1,0:T(8,128)(2,1)} %shard_map.169), calls=%async_computation.4 | async-start | bytes 655360 | tf_op jit(solution)/shard_map/all_to_all | solution.py:452
  129.4 3.6 %shard_map.167 = bf16[1024,128]{1,0:T(8,128)(2,1)} custom-call(s32[1,1024]{1,0:T(1,128)} %get-tuple-element.42.target_ref, bf16[8,256,128]{2,1,0:T(8,128)(2,1)} %copy-done.2), custom_call_target="tpu_custom_call" | custom-call | tf_op jit(solution)/shard_map/pallas_call | solution.py:416
  133.1 3.7 %shard_map.168 = bf16[1024,128]{1,0:T(8,128)(2,1)} custom-call(s32[1,1024]{1,0:T(1,128)} %get-tuple-element.42.target_ref, bf16[8,384,128]{2,1,0:T(8,128)(2,1)} %all_to_all.25.got), custom_call_target="tpu_custom_call" | custom-call | tf_op jit(solution)/shard_map/pallas_call | solution.py:416
  136.8 2.6 %all-to-all-done.4.got = bf16[8,160,128]{2,1,0:T(8,128)(2,1)S(1)} async-done(((bf16[8,160,128]{2,1,0:T(8,128)(2,1)}), bf16[8,160,128]{2,1,0:T(8,128)(2,1)S(1)}, u32[]{:S(2)}, u32[]{:S(2)}) %all-to-all-start.4) | async-done | bytes 327712 | tf_op jit(solution)/shard_map/all_to_all | solution.py:452
  139.4 0.7 copy-done.3
  140.1 1.8 %shard_map.170 = (f32[256,128]{1,0:T(8,128)}, f32[256,128]{1,0:T(8,128)}, f32[256,128]{1,0:T(8,128)}, f32[128,256]{1,0:T(8,128)}, f32[1,256]{1,0:T(1,128)}, /*index=5*/f32[12,128]{1,0:T(8,128)}) custom-call(bf16[8,160,128]{2,1,0:T(8,128)(2,1)} %copy-done.3), custom_call_target="tpu_custom_call" | custom-call | tf_op jit(solution)/shard_map/pallas_call | solution.py:416
  (29 shorter events, 3.5 us)
Async XLA Ops:
  4.2 22.5 %all-to-all-start = ((bf16[8,272,128]{2,1,0:T(8,128)(2,1)}), bf16[8,272,128]{2,1,0:T(8,128)(2,1)S(1)}, u32[]{:S(2)}, u32[]{:S(2)}) async-start(bf16[8,272,128]{2,1,0:T(8,128)(2,1)} %get-tuple-element.43), calls=%async_computation | async-start | bytes 1114112 | tf_op jit(solution)/shard_map/all_to_all | solution.py:452
  11.6 22.1 %collective-permute-start.1 = (bf16[4,256,128]{2,1,0:T(8,128)(2,1)}, bf16[4,256,128]{2,1,0:T(8,128)(2,1)S(1)}, u32[]{:S(2)}, u32[]{:S(2)}) collective-permute-start(bf16[4,256,128]{2,1,0:T(8,128)(2,1)} %get-tuple-element.49.w_own), channel_id=1, source_target_pairs={{0,1},{1,0},{2,3},{3,2},{4,5},{5,4},{6,7},{7,6},{8,9},{9,8},{10,11... | collective-permute-start | bytes 786440 | tf_op jit(solution)/shard_map/ppermute | solution.py:449
  26.7 0.8 copy-start.1
  29.9 3.7 %collective-permute-start = (bf16[1024,128]{1,0:T(8,128)(2,1)}, bf16[1024,128]{1,0:T(8,128)(2,1)S(1)}, u32[]{:S(2)}, u32[]{:S(2)}) collective-permute-start(bf16[1024,128]{1,0:T(8,128)(2,1)} %get-tuple-element.48), channel_id=1, source_target_pairs={{0,1},{1,0},{2,3},{3,2},{4,5},{5,4},{6,7},{7,6},{8,9},{9,8},{10,11... | collective-permute-start | bytes 786440 | tf_op jit(solution)/shard_map/ppermute | solution.py:449
  30.0 25.3 %all-to-all-start.1 = ((bf16[8,272,128]{2,1,0:T(8,128)(2,1)}), bf16[8,272,128]{2,1,0:T(8,128)(2,1)S(1)}, u32[]{:S(2)}, u32[]{:S(2)}) async-start(bf16[8,272,128]{2,1,0:T(8,128)(2,1)} %shard_map.162), calls=%async_computation.1 | async-start | bytes 1114112 | tf_op jit(solution)/shard_map/all_to_all | solution.py:452
  33.6 0.7 copy-start.7
  33.7 0.8 copy-start.8
  54.9 3.6 %collective-permute-start.2 = (bf16[1024,128]{1,0:T(8,128)(2,1)}, bf16[1024,128]{1,0:T(8,128)(2,1)S(1)}, u32[]{:S(2)}, u32[]{:S(2)}) collective-permute-start(bf16[1024,128]{1,0:T(8,128)(2,1)} %get-tuple-element.52), channel_id=1, source_target_pairs={{0,1},{1,0},{2,3},{3,2},{4,5},{5,4},{6,7},{7,6},{8,9},{9,8},{10,11... | collective-permute-start | bytes 786440 | tf_op jit(solution)/shard_map/ppermute | solution.py:449
  55.3 0.8 copy-start
  58.3 9.1 %collective-permute-start.3 = (bf16[1024,128]{1,0:T(8,128)(2,1)}, bf16[1024,128]{1,0:T(8,128)(2,1)S(1)}, u32[]{:S(2)}, u32[]{:S(2)}) collective-permute-start(bf16[1024,128]{1,0:T(8,128)(2,1)} %get-tuple-element.55), channel_id=1, source_target_pairs={{0,1},{1,0},{2,3},{3,2},{4,5},{5,4},{6,7},{7,6},{8,9},{9,8},{10,11... | collective-permute-start | bytes 786440 | tf_op jit(solution)/shard_map/ppermute | solution.py:449
  58.5 0.7 copy-start.5
  61.4 36.0 %all-to-all-start.2 = ((bf16[8,256,128]{2,1,0:T(8,128)(2,1)}), bf16[8,256,128]{2,1,0:T(8,128)(2,1)S(1)}, u32[]{:S(2)}, u32[]{:S(2)}) async-start(bf16[8,256,128]{2,1,0:T(8,128)(2,1)} %shard_map.164), calls=%async_computation.2 | async-start | bytes 1048576 | tf_op jit(solution)/shard_map/all_to_all | solution.py:452
  67.4 0.7 copy-start.9
  91.6 2.1 %collective-permute-start.5 = (bf16[1040,128]{1,0:T(8,128)(2,1)}, bf16[1040,128]{1,0:T(8,128)(2,1)S(1)}, u32[]{:S(2)}, u32[]{:S(2)}) collective-permute-start(bf16[1040,128]{1,0:T(8,128)(2,1)} %get-tuple-element.65), channel_id=1, source_target_pairs={{0,1},{1,0},{2,3},{3,2},{4,5},{5,4},{6,7},{7,6},{8,9},{9,8},{10,11... | collective-permute-start | bytes 798728 | tf_op jit(solution)/shard_map/ppermute | solution.py:449
  91.6 2.1 %collective-permute-start.4 = (bf16[1024,128]{1,0:T(8,128)(2,1)}, bf16[1024,128]{1,0:T(8,128)(2,1)S(1)}, u32[]{:S(2)}, u32[]{:S(2)}) collective-permute-start(bf16[1024,128]{1,0:T(8,128)(2,1)} %get-tuple-element.63), channel_id=1, source_target_pairs={{0,1},{1,0},{2,3},{3,2},{4,5},{5,4},{6,7},{7,6},{8,9},{9,8},{10,11... | collective-permute-start | bytes 786440 | tf_op jit(solution)/shard_map/ppermute | solution.py:449
  93.8 0.7 copy-start.6
  93.8 0.8 copy-start.4
  97.4 32.1 %copy-start.2 = (bf16[8,256,128]{2,1,0:T(8,128)(2,1)}, bf16[8,256,128]{2,1,0:T(8,128)(2,1)S(1)}, u32[]{:S(2)}) copy-start(bf16[8,256,128]{2,1,0:T(8,128)(2,1)S(1)} %all-to-all-done.2.got) | copy-start | bytes 1572868
  125.8 13.6 %all-to-all-start.4 = ((bf16[8,160,128]{2,1,0:T(8,128)(2,1)}), bf16[8,160,128]{2,1,0:T(8,128)(2,1)S(1)}, u32[]{:S(2)}, u32[]{:S(2)}) async-start(bf16[8,160,128]{2,1,0:T(8,128)(2,1)} %shard_map.169), calls=%async_computation.4 | async-start | bytes 655360 | tf_op jit(solution)/shard_map/all_to_all | solution.py:452
  139.4 0.7 copy-start.3

commit v5 on v4

--- a/solution.py
+++ b/solution.py
@@ -22,6 +22,8 @@
 LANES = 128
 TAG_ROWS = 16
 KIND_ROWS = 16
+HEAD_PAD = 48
+PER_STEP = 2
 NT = (((1,), (1,)), ((), ()))
 TN = (((0,), (0,)), ((), ()))
 
@@ -241,130 +243,93 @@
     return wide, inverse, (wide * inverse * gain).astype(BF16)
 
 
-def spare_lanes(h, heads):
-    last = heads * HEAD_DIM - 1
-    is_last = h == heads - 1
-    return jnp.where(is_last, 0, last), jnp.where(is_last, 1, last - 1)
+def stack_rows(rows, extra):
+    place = iota((HEAD_PAD - HEAD_DIM, rows.shape[1]), 0)
+    tail = jnp.zeros(place.shape, F32)
+    for k, value in enumerate(extra):
+        tail = jnp.where(place == k, value, tail)
+    return jnp.concatenate([rows.astype(F32), tail], axis=0)
 
 
 def forward_kernel(
-    heads, core, mine, other, w_own, w_other, gain, info, queries_out, keys_out, values_out, exps_out, context_out, inv_out,
-    keep_out, send_out, queries, keys_t, values, w_out, context
+    heads, core, mine, other, w_own, w_other, gain, keep, queries_t, keys_out, values_t, exps_out, context_t, inv_t,
+    keep_out, send_out, keys_t, w_out
 ):
-    h = pl.program_id(0)
+    step = pl.program_id(0)
+    width = heads * HEAD_DIM
+    half = width // 2
+    flag = core[0] > 0
+    scale = HEAD_DIM**-0.5
+
+    @pl.when(step == 0)
+    def _():
+        w_q, w_k, w_v, w_o = full_weights(core, w_own, w_other)
+        w_out[...] = w_o
+        slab = jnp.concatenate(ordered(flag, mine[...], other[...]), axis=1)
+        _, _, normed = norm_rows(slab, gain[...], width)
+        queries_t[...] = jnp.transpose(mm(normed, w_q)).astype(BF16)
+        k = mm(normed, w_k)
+        keys_out[...] = k.astype(BF16)
+        keys_t[...] = jnp.transpose(k).astype(BF16)
+        values_t[...] = jnp.transpose(mm(normed, w_v)).astype(BF16)
+
+    bias = jnp.where(keep[0:1, :] > 0.5, 0.0, MASKED / scale)
+    for k in range(PER_STEP):
+        h = step * PER_STEP + k
+        head_rows = pl.ds(pl.multiple_of(h * HEAD_DIM, HEAD_DIM), HEAD_DIM)
+        left = jnp.transpose(stack_rows(queries_t[head_rows, :], (1.0,))).astype(BF16)
+        scores = mm(left, stack_rows(keys_t[head_rows, :], (bias,)).astype(BF16))
+        top = jnp.max(scores, axis=1, keepdims=True)
+        exps = jnp.exp2((scores - top) * (scale * LOG2E)).astype(BF16)
+        exps_out[k] = exps
+        summed = mm_nt(stack_rows(values_t[head_rows, :], (1.0,)).astype(BF16), exps)
+        inv = 1.0 / summed[HEAD_DIM : HEAD_DIM + 1]
+        context_t[head_rows, :] = summed[0:HEAD_DIM] * inv
+        inv_t[pl.ds(h, 1), :] = inv
+
+    @pl.when(step == heads // PER_STEP - 1)
+    def _():
+        rows_out = mm(jnp.transpose(context_t[...]).astype(BF16), w_out[...]).astype(BF16)
+        keep_out[...] = jnp.where(flag, rows_out[:, half:], rows_out[:, :half])
+        send_out[...] = jnp.where(flag, rows_out[:, :half], rows_out[:, half:])
+
+
+def backward_kernel(
+    heads, core, mine, other, g_mine, g_other, w_own, w_other, gain, queries_t, keys_in, values_t, exps_in, context_t,
+    inv_t, keep_out, send_out, grad_keep, grad_send, d_context_t, d_query, d_key_t, d_value_t
+):
+    step = pl.program_id(0)
     width = heads * HEAD_DIM
     half = width // 2
     flag = core[0] > 0
     lane = iota((1, width), 1)
     scale = HEAD_DIM**-0.5
 
-    @pl.when(h == 0)
-    def _():
-        w_q, w_k, w_v, w_o = full_weights(core, w_own, w_other)
-        w_out[...] = w_o
-        slab = jnp.concatenate(ordered(flag, mine[...], other[...]), axis=1)
-        _, _, normed = norm_rows(slab, gain[...], width)
-        q = mm(normed, w_q).astype(BF16)
-        queries[...] = q
-        queries_out[...] = q
-        k = mm(normed, w_k)
-        k_low = k.astype(BF16)
-        keys_out[...] = k_low
-        k_t = jnp.transpose(k_low.astype(F32))
-        bias = jnp.where(info[0:1, :] > 0.5, 0.0, MASKED / scale)
-        row = iota(k_t.shape, 0)
-        keys_t[0] = jnp.where(row == width - 1, bias, k_t).astype(BF16)
-        keys_t[1] = jnp.where(row == 0, bias, k_t).astype(BF16)
-        v = mm(normed, w_v).astype(BF16)
-        values_out[...] = v
-        v_wide = v.astype(F32)
-        values[0] = jnp.where(lane == width - 1, 1.0, v_wide).astype(BF16)
-        values[1] = jnp.where(lane == 0, 1.0, v_wide).astype(BF16)
-        inv_out[...] = jnp.zeros_like(inv_out)
-
-    spare, _ = spare_lanes(h, heads)
-    side = jnp.where(h == heads - 1, 1, 0)
-    own_lane = lax.shift_right_logical(lane, log2_of(HEAD_DIM)) == h
-    step = 256
-    for s in range(0, SLOTS, step):
-        rows = slice(s, s + step)
-        q = jnp.where(own_lane, queries[rows, :].astype(F32), jnp.where(lane == spare, 1.0, 0.0)).astype(BF16)
-        scores = mm(q, keys_t[side])
-        top = jnp.max(scores, axis=1, keepdims=True)
-        exps = jnp.exp2((scores - top) * (scale * LOG2E)).astype(BF16)
-        exps_out[0, rows, :] = exps
-        summed = mm(exps, values[side])
-        inv = 1.0 / jnp.sum(jnp.where(lane == spare, summed, 0.0), axis=1, keepdims=True)
-        context[rows, :] = jnp.where(own_lane, summed * inv, context[rows, :])
-        lane_small = iota((1, LANES), 1)
-        inv_out[rows, :] = jnp.where(lane_small == h, inv, inv_out[rows, :])
-
-    @pl.when(h == heads - 1)
-    def _():
-        context_out[...] = context[...]
-        rows_out = mm(context[...].astype(BF16), w_out[...]).astype(BF16)
-        keep_out[...] = jnp.where(flag, rows_out[:, half:], rows_out[:, :half])
-        send_out[...] = jnp.where(flag, rows_out[:, :half], rows_out[:, half:])
-
-
-def backward_kernel(
-    heads, core, mine, other, g_mine, g_other, w_own, w_other, gain, info, queries_in, keys_in, values_in, exps_in, context_in,
-    inv_in, keep_out, send_out, grad_keep, grad_send, values_t, queries_t, d_context, d_context_t, inv_t, d_query, d_key_t, d_value_t
-):
-    h = pl.program_id(0)
-    width = heads * HEAD_DIM
-    half = width // 2
-    flag = core[0] > 0
-    lane = iota((1, width), 1)
-    lane_small = iota((1, LANES), 1)
-    scale = HEAD_DIM**-0.5
-
     def grad_rows():
         return jnp.concatenate(ordered(flag, g_mine[...], g_other[...]), axis=1)
 
-    @pl.when(h == 0)
+    @pl.when(step == 0)
     def _():
         w_o = full_weights(core, w_own, w_other)[3]
-        dc = mm_nt(grad_rows(), w_o).astype(BF16)
-        d_context[...] = dc
-        d_context_t[...] = jnp.transpose(dc.astype(F32)).astype(BF16)
-        inv_t[...] = jnp.transpose(inv_in[...])
-        v_t = jnp.transpose(values_in[...].astype(F32))
-        row = iota(v_t.shape, 0)
-        values_t[0] = jnp.where(row >= width - 2, 1.0, v_t).astype(BF16)
-        values_t[1] = jnp.where(row <= 1, 1.0, v_t).astype(BF16)
-        queries_t[...] = jnp.transpose(queries_in[...].astype(F32)).astype(BF16)
-
-    spare, spare_low = spare_lanes(h, heads)
-    side = jnp.where(h == heads - 1, 1, 0)
-    own_lane = lax.shift_right_logical(lane, log2_of(HEAD_DIM)) == h
-    base = pl.multiple_of(h * HEAD_DIM, HEAD_DIM)
-    head_rows = pl.ds(base, HEAD_DIM)
-    inv_row = inv_t[pl.ds(h, 1), :]
-    step = 256
-    dk = jnp.zeros((HEAD_DIM, SLOTS), F32)
-    dv = jnp.zeros((HEAD_DIM, SLOTS), F32)
-    for s in range(0, SLOTS, step):
-        rows = slice(s, s + step)
-        inv = jnp.sum(jnp.where(lane_small == h, inv_in[rows, :], 0.0), axis=1, keepdims=True)
-        scaled = jnp.where(own_lane, d_context[rows, :].astype(F32) * inv, 0.0).astype(BF16)
-        wide = scaled.astype(F32)
-        dot = -jnp.sum(wide * context_in[rows, :], axis=1, keepdims=True)
+        d_context_t[...] = mm_nt(w_o, grad_rows()).astype(BF16)
+
+    for k in range(PER_STEP):
+        h = step * PER_STEP + k
+        head_rows = pl.ds(pl.multiple_of(h * HEAD_DIM, HEAD_DIM), HEAD_DIM)
+        own_lane = lax.shift_right_logical(lane, log2_of(HEAD_DIM)) == h
+        scaled = (d_context_t[head_rows, :].astype(F32) * inv_t[pl.ds(h, 1), :]).astype(BF16)
+        dot = -jnp.sum(scaled.astype(F32) * context_t[head_rows, :], axis=0, keepdims=True)
         dot_high = dot.astype(BF16).astype(F32)
-        dot_low = dot - dot_high
-        left = jnp.where(lane == spare, dot_high, jnp.where(lane == spare_low, dot_low, wide)).astype(BF16)
-        centred = mm(left, values_t[side])
-        exps = exps_in[0, rows, :]
+        left = jnp.transpose(stack_rows(scaled, (dot_high, dot - dot_high))).astype(BF16)
+        centred = mm(left, stack_rows(values_t[head_rows, :], (1.0, 1.0)).astype(BF16))
+        exps = exps_in[k]
         d_scores = (exps.astype(F32) * centred).astype(BF16)
         dq = mm(d_scores, keys_in[...])
-        d_query[rows, :] = jnp.where(own_lane, dq * scale, d_query[rows, :])
-        dk = dk + mm(queries_t[head_rows, rows], d_scores)
-        scaled_t = (d_context_t[head_rows, rows].astype(F32) * inv_row[:, rows]).astype(BF16)
-        dv = dv + mm(scaled_t, exps)
-    d_key_t[head_rows, :] = dk * scale
-    d_value_t[head_rows, :] = dv
-
-    @pl.when(h == heads - 1)
+        d_query[...] = jnp.where(own_lane, dq * scale, d_query[...])
+        d_key_t[head_rows, :] = mm(queries_t[head_rows, :], d_scores) * scale
+        d_value_t[head_rows, :] = mm(scaled, exps)
+
+    @pl.when(step == heads // PER_STEP - 1)
     def _():
         w_q, w_k, w_v, _ = full_weights(core, w_own, w_other)
         slab = jnp.concatenate(ordered(flag, mine[...], other[...]), axis=1)
@@ -379,14 +344,13 @@
         keep_out[...] = jnp.where(flag, d_slab[:, half:], d_slab[:, :half])
         send_out[...] = jnp.where(flag, d_slab[:, :half], d_slab[:, half:])
         normed_t = jnp.transpose(normed.astype(F32)).astype(BF16)
-        context_t = jnp.transpose(context_in[...]).astype(BF16)
         place = 0
         for d_rows in (dq, dk, dv):
             grad = mm(normed_t, d_rows)
             grad_keep[place : place + width, :] = jnp.where(flag, grad[:, half:], grad[:, :half])
             grad_send[place : place + width, :] = jnp.where(flag, grad[:, :half], grad[:, half:]).astype(BF16)
             place += width
-        grad = mm(context_t, grad_rows())
+        grad = mm(context_t[...].astype(BF16), grad_rows())
         for part in range(2):
             block = grad[:, part * half : (part + 1) * half]
             grad_keep[place : place + half, :] = jnp.where(flag, block[half:], block[:half])
@@ -479,34 +443,28 @@
     )
     other = other_core(theirs)
 
-    full_shape = shape((SLOTS, width), BF16)
+    turned_shape = shape((width, SLOTS), BF16)
     exps_shape = shape((heads, SLOTS, SLOTS), BF16)
-    exps_spec = pl.BlockSpec((1, SLOTS, SLOTS), lambda h: (h, 0, 0))
+    exps_spec = pl.BlockSpec((PER_STEP, SLOTS, SLOTS), lambda h: (h, 0, 0))
     inputs = (core, mine, other, w_own, w_other, gain, info)
     outs = (
-        full_shape,
-        full_shape,
-        full_shape,
+        turned_shape,
+        shape((SLOTS, width), BF16),
+        turned_shape,
         exps_shape,
-        shape((SLOTS, width), F32),
-        shape((SLOTS, LANES), F32),
+        shape((width, SLOTS), F32),
+        shape((heads, SLOTS), F32),
         rows_shape,
         rows_shape,
     )
     work = heads * SLOTS * SLOTS
-    queries, keys, values, exps, context, inv, attn_keep, attn_send = pl.pallas_call(
+    queries_t, keys, values_t, exps, context_t, inv_t, attn_keep, attn_send = pl.pallas_call(
         functools.partial(forward_kernel, heads),
-        grid=(heads,),
+        grid=(heads // PER_STEP,),
         out_shape=outs,
         in_specs=[SMEM_SPEC] + [whole(x) for x in inputs[1:]],
         out_specs=tuple(exps_spec if x is exps_shape else whole(x) for x in outs),
-        scratch_shapes=(
-            pltpu.VMEM((SLOTS, width), BF16),
-            pltpu.VMEM((2, width, SLOTS), BF16),
-            pltpu.VMEM((2, SLOTS, width), BF16),
-            pltpu.VMEM((width, width), BF16),
-            pltpu.VMEM((SLOTS, width), F32),
-        ),
+        scratch_shapes=(pltpu.VMEM((width, SLOTS), BF16), pltpu.VMEM((width, width), BF16)),
         cost_estimate=pl.CostEstimate(flops=4 * work * width, transcendentals=work, bytes_accessed=2 * work),
         name="forward",
     )(*inputs)
@@ -529,20 +487,16 @@
     g_other = other_core(g_theirs)
 
     grad_rows = 4 * width + 16
-    inputs = (core, mine, other, g_mine, g_other, w_own, w_other, gain, info, queries, keys, values, exps, context, inv)
+    inputs = (core, mine, other, g_mine, g_other, w_own, w_other, gain, queries_t, keys, values_t, exps, context_t, inv_t)
     outs = (rows_shape, rows_shape, shape((grad_rows, half), F32), shape((grad_rows, half), BF16))
     d_keep, d_send, grad_keep, grad_send = pl.pallas_call(
         functools.partial(backward_kernel, heads),
-        grid=(heads,),
+        grid=(heads // PER_STEP,),
         out_shape=outs,
         in_specs=[SMEM_SPEC] + [exps_spec if x is exps else whole(x) for x in inputs[1:]],
         out_specs=tuple(whole(x) for x in outs),
         scratch_shapes=(
-            pltpu.VMEM((2, width, SLOTS), BF16),
             pltpu.VMEM((width, SLOTS), BF16),
-            pltpu.VMEM((SLOTS, width), BF16),
-            pltpu.VMEM((width, SLOTS), BF16),
-            pltpu.VMEM((LANES, SLOTS), F32),
             pltpu.VMEM((SLOTS, width), F32),
             pltpu.VMEM((width, SLOTS), F32),
             pltpu.VMEM((width, SLOTS), F32),

time: 143 us -> 136 us (0.951)
  Pallas kernels: 72.2 us -> 65.6 us
    pallas_call x2, Pallas kernels: 43.9 us -> 37.3 us  [the longest x1 20.5 us: on_device(): pl.pallas_call(functools.partial(backward_kernel, heads), grid=(heads //...]
  transfers between devices with their start and end apart: 10 -> 10, of which waited for: 3 -> 3; matrix products, arithmetic and copies ran while one was open for 0% -> 0% of each run, Pallas kernels for 46% -> 43%
where the time goes in v5:
time: 136 us; the launch traced here: 135 us
  Pallas kernels  65.6 us (48%)
  blocking collectives  26.5 us (19%)
  starting transfers between devices  21.7 us (16%)
  waiting for transfers between devices  15.3 us (11%)
  local copies, waits for them, and re-layouts  5.39 us (4%)
    pallas_call x10, Pallas kernels, simple_call(): pl.pallas_call(kernel, out_shape=outs, in_specs=specs, out_specs=tuple((w...  28.3 us
    all_to_all x1, blocking collectives, exchange(): return lax.all_to_all(x, 'region', split_axis=0, concat_axis=0, tiled=True)  26.5 us
    all_to_all x4, starting transfers between devices, exchange(): return lax.all_to_all(x, 'region', split_axis=0, concat_axis=0, tiled=True)  20.6 us
    pallas_call x1, Pallas kernels, on_device(): pl.pallas_call(functools.partial(backward_kernel, heads), grid=(heads //...  20.5 us
    pallas_call x1, Pallas kernels, on_device(): pl.pallas_call(functools.partial(forward_kernel, heads), grid=(heads // P...  16.8 us
    all_to_all x4, waiting for transfers between devices, exchange(): return lax.all_to_all(x, 'region', split_axis=0, concat_axis=0, tiled=True)  13.7 us
    unnamed x20, local copies, waits for them, and re-layouts  5.39 us
  transfers between devices with their start and end apart: 10, of which 3 were waited for; matrix products, arithmetic and copies ran while one was open for 0% of the time, Pallas kernels for 43%

profile of v5, /device:TPU:0, one launch (start us, length us, event | category | flops | bytes accessed | tf_op | source)
XLA Modules:
  0.0 135.2 jit_solution(10361250056747066858)
XLA Ops:
  0.6 3.6 %shard_map.161 = (bf16[8,272,128]{2,1,0:T(8,128)(2,1)}, s32[1,1024]{1,0:T(1,128)}, bf16[4,256,128]{2,1,0:T(8,128)(2,1)}) custom-call(s32[1,1024]{1,0:T(1,128)} %bitcast.7, s32[1,1024]{1,0:T(1,128)} %bitcast.5, bf16[1024,128]{1,0:T(8,128)(2,1)} %feats.1, bf16[12,128]{1,0:T(8,128)(2,1)} %embed.1, bf16[256,128]{1,0:T(8,128)(2,1)} %w_q.1, bf16[256,128]{1,0:T(8,128)(2,1)} %w_k.1, ...), custom_call_target="tpu_custom_call" | custom-call | tf_op jit(solution)/shard_map/pallas_call | solution.py:380
  4.2 7.3 %all-to-all-start = ((bf16[8,272,128]{2,1,0:T(8,128)(2,1)}), bf16[8,272,128]{2,1,0:T(8,128)(2,1)S(1)}, u32[]{:S(2)}, u32[]{:S(2)}) async-start(bf16[8,272,128]{2,1,0:T(8,128)(2,1)} %get-tuple-element.43), calls=%async_computation | async-start | bytes 1114112 | tf_op jit(solution)/shard_map/all_to_all | solution.py:416
  11.6 4.1 %shard_map.162 = bf16[8,272,128]{2,1,0:T(8,128)(2,1)} custom-call(s32[1,1024]{1,0:T(1,128)} %get-tuple-element.42.target_ref, s32[1,1024]{1,0:T(1,128)} %bitcast.6, bf16[1024,128]{1,0:T(8,128)(2,1)} %cot.1), custom_call_target="tpu_custom_call" | custom-call | tf_op jit(solution)/shard_map/pallas_call | solution.py:380
  15.7 11.1 %all-to-all-done.got = bf16[8,272,128]{2,1,0:T(8,128)(2,1)S(1)} async-done(((bf16[8,272,128]{2,1,0:T(8,128)(2,1)}), bf16[8,272,128]{2,1,0:T(8,128)(2,1)S(1)}, u32[]{:S(2)}, u32[]{:S(2)}) %all-to-all-start) | async-done | bytes 557088 | tf_op jit(solution)/shard_map/all_to_all | solution.py:416
  26.7 0.8 copy-done.1
  27.6 2.3 %shard_map.163 = (bf16[1024,128]{1,0:T(8,128)(2,1)}, bf16[1024,128]{1,0:T(8,128)(2,1)}, f32[8,1024]{1,0:T(8,128)}, s32[2,9]{1,0:T(2,128)}) custom-call(s32[1]{0:T(128)} %bitcast.2.core, bf16[8,272,128]{2,1,0:T(8,128)(2,1)} %copy-done.1), custom_call_target="tpu_custom_call" | custom-call | tf_op jit(solution)/shard_map/pallas_call | solution.py:380
  30.0 3.6 %all-to-all-start.1 = ((bf16[8,272,128]{2,1,0:T(8,128)(2,1)}), bf16[8,272,128]{2,1,0:T(8,128)(2,1)S(1)}, u32[]{:S(2)}, u32[]{:S(2)}) async-start(bf16[8,272,128]{2,1,0:T(8,128)(2,1)} %shard_map.162), calls=%async_computation.1 | async-start | bytes 1114112 | tf_op jit(solution)/shard_map/all_to_all | solution.py:416
  34.5 16.8 %forward.1 = (bf16[256,1024]{1,0:T(8,128)(2,1)}, bf16[1024,256]{1,0:T(8,128)(2,1)}, bf16[256,1024]{1,0:T(8,128)(2,1)}, bf16[8,1024,1024]{2,1,0:T(8,128)(2,1)}, f...) custom-call(s32[1]{0:T(128)} %bitcast.2.core, ...), custom_call_target="tpu_custom_call" | custom-call | flops 8589934592 | bytes 16777216 | tf_op jit(solution)/shard_map/forward/pallas_call | solution.py:461
  51.6 0.8 copy-done
  52.5 2.2 %shard_map.165 = (bf16[1024,128]{1,0:T(8,128)(2,1)}, bf16[1024,128]{1,0:T(8,128)(2,1)}) custom-call(s32[1]{0:T(128)} %bitcast.2.core, s32[2,9]{1,0:T(2,128)} %get-tuple-element.46.marks, bf16[8,272,128]{2,1,0:T(8,128)(2,1)} %copy-done), custom_call_target="tpu_custom_call" | custom-call | tf_op jit(solution)/shard_map/pallas_call | solution.py:380
  54.8 0.7 copy-done.5
  55.5 2.2 %shard_map.164 = bf16[8,256,128]{2,1,0:T(8,128)(2,1)} custom-call(s32[1]{0:T(128)} %bitcast.2.core, s32[2,9]{1,0:T(2,128)} %get-tuple-element.46.marks, bf16[1024,128]{1,0:T(8,128)(2,1)} %get-tuple-element.51.own, bf16[1024,128]{1,0:T(8,128)(2,1)} %copy-done.5), custom_call_target="tpu_custom_call" | custom-call | tf_op jit(solution)/shard_map/pallas_call | solution.py:380
  57.7 6.0 %all-to-all-start.2 = ((bf16[8,256,128]{2,1,0:T(8,128)(2,1)}), bf16[8,256,128]{2,1,0:T(8,128)(2,1)S(1)}, u32[]{:S(2)}, u32[]{:S(2)}) async-start(bf16[8,256,128]{2,1,0:T(8,128)(2,1)} %shard_map.164), calls=%async_computation.2 | async-start | bytes 1048576 | tf_op jit(solution)/shard_map/all_to_all | solution.py:416
  64.5 20.5 %backward.1 = (bf16[1024,128]{1,0:T(8,128)(2,1)}, bf16[1024,128]{1,0:T(8,128)(2,1)}, f32[1040,128]{1,0:T(8,128)}, bf16[1040,128]{1,0:T(8,128)(2,1)}) custom-call(s32[1]{0:T(128)} %bitcast.2.core, bf16[1024,128]{1,0:T(8,128)(2,1)} %get-tuple-element.47.mine, bf16[1024,128]{1,0:T(8,128)(2,1)} %copy-done.8, bf16[1024,128]{1,0:T(8,128)(2,1)} %get-tuple-element.54.g_mine, ...), custom_call_target="tpu_custom_call" | custom-call | flops 17179869184 | bytes 16777216 | tf_op jit(solution)/shard_map/backward/pallas_call | solution.py:492
  85.5 1.6 %collective-permute-done.4.other = bf16[1024,128]{1,0:T(8,128)(2,1)S(1)} collective-permute-done((bf16[1024,128]{1,0:T(8,128)(2,1)}, bf16[1024,128]{1,0:T(8,128)(2,1)S(1)}, u32[]{:S(2)}, u32[]{:S(2)}) %collective-permute-start.4) | collective-permute-done | bytes 262176 | tf_op jit(solution)/shard_map/ppermute | solution.py:413
  87.9 2.8 %shard_map.166 = (bf16[8,384,128]{2,1,0:T(8,128)(2,1)}, bf16[32,128]{1,0:T(8,128)(2,1)}) custom-call(s32[1]{0:T(128)} %bitcast.2.core, s32[2,9]{1,0:T(2,128)} %get-tuple-element.46.marks, bf16[1024,128]{1,0:T(8,128)(2,1)} %get-tuple-element.62.own, bf16[1024,128]{1,0:T(8,128)(2,1)} %copy-done.6, bf16[8,272,128]{2,1,0:T(8,128)(2,1)} %copy-done, ...), custom_call_target="tpu_custom_call" | custom-call | tf_op jit(solution)/shard_map/pallas_call | solution.py:380
  90.7 26.5 %all_to_all.25.got = bf16[8,384,128]{2,1,0:T(8,128)(2,1)} all-to-all(bf16[8,384,128]{2,1,0:T(8,128)(2,1)} %get-tuple-element.68), channel_id=1, replica_groups=mesh['groups'=2,'region'=8,'head'=2] {'region'}, dimensions={0} | all-to-all | bytes 1572864 | tf_op jit(solution)/shard_map/all_to_all | solution.py:416
  117.2 1.9 %shard_map.169 = bf16[8,160,128]{2,1,0:T(8,128)(2,1)} custom-call(bf16[8,384,128]{2,1,0:T(8,128)(2,1)} %all_to_all.25.got, bf16[32,128]{1,0:T(8,128)(2,1)} %get-tuple-element.69.extra), custom_call_target="tpu_custom_call" | custom-call | tf_op jit(solution)/shard_map/pallas_call | solution.py:380
  119.1 3.6 %all-to-all-start.4 = ((bf16[8,160,128]{2,1,0:T(8,128)(2,1)}), bf16[8,160,128]{2,1,0:T(8,128)(2,1)S(1)}, u32[]{:S(2)}, u32[]{:S(2)}) async-start(bf16[8,160,128]{2,1,0:T(8,128)(2,1)} %shard_map.169), calls=%async_computation.4 | async-start | bytes 655360 | tf_op jit(solution)/shard_map/all_to_all | solution.py:416
  122.8 3.6 %shard_map.167 = bf16[1024,128]{1,0:T(8,128)(2,1)} custom-call(s32[1,1024]{1,0:T(1,128)} %get-tuple-element.42.target_ref, bf16[8,256,128]{2,1,0:T(8,128)(2,1)} %copy-done.2), custom_call_target="tpu_custom_call" | custom-call | tf_op jit(solution)/shard_map/pallas_call | solution.py:380
  126.4 3.7 %shard_map.168 = bf16[1024,128]{1,0:T(8,128)(2,1)} custom-call(s32[1,1024]{1,0:T(1,128)} %get-tuple-element.42.target_ref, bf16[8,384,128]{2,1,0:T(8,128)(2,1)} %all_to_all.25.got), custom_call_target="tpu_custom_call" | custom-call | tf_op jit(solution)/shard_map/pallas_call | solution.py:380
  130.1 2.6 %all-to-all-done.4.got = bf16[8,160,128]{2,1,0:T(8,128)(2,1)S(1)} async-done(((bf16[8,160,128]{2,1,0:T(8,128)(2,1)}), bf16[8,160,128]{2,1,0:T(8,128)(2,1)S(1)}, u32[]{:S(2)}, u32[]{:S(2)}) %all-to-all-start.4) | async-done | bytes 327712 | tf_op jit(solution)/shard_map/all_to_all | solution.py:416
  132.7 0.7 copy-done.3
  133.4 1.8 %shard_map.170 = (f32[256,128]{1,0:T(8,128)}, f32[256,128]{1,0:T(8,128)}, f32[256,128]{1,0:T(8,128)}, f32[128,256]{1,0:T(8,128)}, f32[1,256]{1,0:T(1,128)}, /*index=5*/f32[12,128]{1,0:T(8,128)}) custom-call(bf16[8,160,128]{2,1,0:T(8,128)(2,1)} %copy-done.3), custom_call_target="tpu_custom_call" | custom-call | tf_op jit(solution)/shard_map/pallas_call | solution.py:380
  (29 shorter events, 3.4 us)
Async XLA Ops:
  4.2 22.5 %all-to-all-start = ((bf16[8,272,128]{2,1,0:T(8,128)(2,1)}), bf16[8,272,128]{2,1,0:T(8,128)(2,1)S(1)}, u32[]{:S(2)}, u32[]{:S(2)}) async-start(bf16[8,272,128]{2,1,0:T(8,128)(2,1)} %get-tuple-element.43), calls=%async_computation | async-start | bytes 1114112 | tf_op jit(solution)/shard_map/all_to_all | solution.py:416
  11.6 22.1 %collective-permute-start.1 = (bf16[4,256,128]{2,1,0:T(8,128)(2,1)}, bf16[4,256,128]{2,1,0:T(8,128)(2,1)S(1)}, u32[]{:S(2)}, u32[]{:S(2)}) collective-permute-start(bf16[4,256,128]{2,1,0:T(8,128)(2,1)} %get-tuple-element.49.w_own), channel_id=1, source_target_pairs={{0,1},{1,0},{2,3},{3,2},{4,5},{5,4},{6,7},{7,6},{8,9},{9,8},{10,11... | collective-permute-start | bytes 786440 | tf_op jit(solution)/shard_map/ppermute | solution.py:413
  26.7 0.8 copy-start.1
  29.9 3.7 %collective-permute-start = (bf16[1024,128]{1,0:T(8,128)(2,1)}, bf16[1024,128]{1,0:T(8,128)(2,1)S(1)}, u32[]{:S(2)}, u32[]{:S(2)}) collective-permute-start(bf16[1024,128]{1,0:T(8,128)(2,1)} %get-tuple-element.48), channel_id=1, source_target_pairs={{0,1},{1,0},{2,3},{3,2},{4,5},{5,4},{6,7},{7,6},{8,9},{9,8},{10,11... | collective-permute-start | bytes 786440 | tf_op jit(solution)/shard_map/ppermute | solution.py:413
  30.0 21.7 %all-to-all-start.1 = ((bf16[8,272,128]{2,1,0:T(8,128)(2,1)}), bf16[8,272,128]{2,1,0:T(8,128)(2,1)S(1)}, u32[]{:S(2)}, u32[]{:S(2)}) async-start(bf16[8,272,128]{2,1,0:T(8,128)(2,1)} %shard_map.162), calls=%async_computation.1 | async-start | bytes 1114112 | tf_op jit(solution)/shard_map/all_to_all | solution.py:416
  33.6 0.7 copy-start.7
  33.7 0.8 copy-start.8
  51.2 3.6 %collective-permute-start.2 = (bf16[1024,128]{1,0:T(8,128)(2,1)}, bf16[1024,128]{1,0:T(8,128)(2,1)S(1)}, u32[]{:S(2)}, u32[]{:S(2)}) collective-permute-start(bf16[1024,128]{1,0:T(8,128)(2,1)} %get-tuple-element.52), channel_id=1, source_target_pairs={{0,1},{1,0},{2,3},{3,2},{4,5},{5,4},{6,7},{7,6},{8,9},{9,8},{10,11... | collective-permute-start | bytes 786440 | tf_op jit(solution)/shard_map/ppermute | solution.py:413
  51.6 0.8 copy-start
  54.7 9.1 %collective-permute-start.3 = (bf16[1024,128]{1,0:T(8,128)(2,1)}, bf16[1024,128]{1,0:T(8,128)(2,1)S(1)}, u32[]{:S(2)}, u32[]{:S(2)}) collective-permute-start(bf16[1024,128]{1,0:T(8,128)(2,1)} %get-tuple-element.55), channel_id=1, source_target_pairs={{0,1},{1,0},{2,3},{3,2},{4,5},{5,4},{6,7},{7,6},{8,9},{9,8},{10,11... | collective-permute-start | bytes 786440 | tf_op jit(solution)/shard_map/ppermute | solution.py:413
  54.8 0.7 copy-start.5
  57.7 32.9 %all-to-all-start.2 = ((bf16[8,256,128]{2,1,0:T(8,128)(2,1)}), bf16[8,256,128]{2,1,0:T(8,128)(2,1)S(1)}, u32[]{:S(2)}, u32[]{:S(2)}) async-start(bf16[8,256,128]{2,1,0:T(8,128)(2,1)} %shard_map.164), calls=%async_computation.2 | async-start | bytes 1048576 | tf_op jit(solution)/shard_map/all_to_all | solution.py:416
  63.8 0.7 copy-start.9
  85.0 2.1 %collective-permute-start.5 = (bf16[1040,128]{1,0:T(8,128)(2,1)}, bf16[1040,128]{1,0:T(8,128)(2,1)S(1)}, u32[]{:S(2)}, u32[]{:S(2)}) collective-permute-start(bf16[1040,128]{1,0:T(8,128)(2,1)} %get-tuple-element.65), channel_id=1, source_target_pairs={{0,1},{1,0},{2,3},{3,2},{4,5},{5,4},{6,7},{7,6},{8,9},{9,8},{10,11... | collective-permute-start | bytes 798728 | tf_op jit(solution)/shard_map/ppermute | solution.py:413
  85.0 2.1 %collective-permute-start.4 = (bf16[1024,128]{1,0:T(8,128)(2,1)}, bf16[1024,128]{1,0:T(8,128)(2,1)S(1)}, u32[]{:S(2)}, u32[]{:S(2)}) collective-permute-start(bf16[1024,128]{1,0:T(8,128)(2,1)} %get-tuple-element.63), channel_id=1, source_target_pairs={{0,1},{1,0},{2,3},{3,2},{4,5},{5,4},{6,7},{7,6},{8,9},{9,8},{10,11... | collective-permute-start | bytes 786440 | tf_op jit(solution)/shard_map/ppermute | solution.py:413
  87.1 0.7 copy-start.6
  87.1 0.8 copy-start.4
  90.7 32.1 %copy-start.2 = (bf16[8,256,128]{2,1,0:T(8,128)(2,1)}, bf16[8,256,128]{2,1,0:T(8,128)(2,1)S(1)}, u32[]{:S(2)}) copy-start(bf16[8,256,128]{2,1,0:T(8,128)(2,1)S(1)} %all-to-all-done.2.got) | copy-start | bytes 1572868
  119.1 13.6 %all-to-all-start.4 = ((bf16[8,160,128]{2,1,0:T(8,128)(2,1)}), bf16[8,160,128]{2,1,0:T(8,128)(2,1)S(1)}, u32[]{:S(2)}, u32[]{:S(2)}) async-start(bf16[8,160,128]{2,1,0:T(8,128)(2,1)} %shard_map.169), calls=%async_computation.4 | async-start | bytes 655360 | tf_op jit(solution)/shard_map/all_to_all | solution.py:416
  132.7 0.7 copy-start.3

commit v6 on v5

--- a/solution.py
+++ b/solution.py
@@ -103,22 +103,7 @@
         out_cot[r, capacity : capacity + TAG_ROWS, :] = tag.astype(BF16)
 
 
-def place_rows(regions, capacity, got, marks, front, back):
-    for r in range(regions):
-        rows = got[r, 0:capacity, :].astype(F32)
-        front[pl.ds(marks[0, r], capacity), :] = rows
-        back[pl.ds(marks[1, r], capacity), :] = rows
-
-
-def bins_of(regions, capacity, core, marks, front, back):
-    row = iota((SLOTS, 1), 0)
-    first = jnp.where(row < marks[0, regions], front[0:SLOTS, :], 0.0)
-    second = jnp.where(row >= marks[1, regions], back[capacity : capacity + SLOTS, :], 0.0)
-    flag = core[0] > 0
-    return jnp.where(flag, second, first).astype(BF16), jnp.where(flag, first, second).astype(BF16)
-
-
-def group_kernel(regions, capacity, core, got, mine, theirs, keep, marks, front, back):
+def count_rows(regions, capacity, got, marks):
     start = jnp.int32(0)
     end = jnp.int32(SLOTS)
     for r in range(regions):
@@ -129,16 +114,24 @@
         end = end - jnp.max(block[1:2, :]).astype(I32)
     marks[0, regions] = start
     marks[1, regions] = end
-    place_rows(regions, capacity, got, marks, front, back)
-    mine[...], theirs[...] = bins_of(regions, capacity, core, marks, front, back)
-    lane = iota((8, SLOTS), 1)
-    filled = jnp.where(core[0] > 0, jnp.where(lane >= end, 1.0, 0.0), jnp.where(lane < start, 1.0, 0.0))
-    keep[...] = filled
-
-
-def regroup_kernel(regions, capacity, core, marks, got, mine, theirs, front, back):
-    place_rows(regions, capacity, got, marks, front, back)
-    mine[...], theirs[...] = bins_of(regions, capacity, core, marks, front, back)
+
+
+def is_filled(regions, core, marks, place):
+    first = jnp.where(place < marks[0, regions], 1.0, 0.0)
+    second = jnp.where(place >= marks[1, regions], 1.0, 0.0)
+    return jnp.where(core[0] > 0, second, first)
+
+
+def bin_rows(regions, capacity, core, marks, own, other, lift, lift_other):
+    flag = core[0] > 0
+    for r in range(regions):
+        place = pl.ds(marks[core[0], r], capacity)
+        lift[place, :] = own[r, 0:capacity, :].astype(F32)
+        lift_other[place, :] = other[r, 0:capacity, :].astype(F32)
+    place = pl.ds(pl.multiple_of(core[0] * capacity, capacity), SLOTS)
+    rows = jnp.concatenate(ordered(flag, lift[place, :], lift_other[place, :]), axis=1)
+    filled = is_filled(regions, core, marks, iota((SLOTS, 1), 0))
+    return jnp.where(filled > 0.5, rows, 0.0).astype(BF16)
 
 
 def arrival_rows(regions, capacity, core, marks, own, other, out, front, back):
@@ -160,10 +153,9 @@
     arrival_rows(regions, capacity, core, marks, own, other, out, front, back)
 
 
-def ungroup_grad_kernel(regions, capacity, core, marks, own, other, tagged, grad_own, grad_other, out, extra, front, back):
+def ungroup_grad_kernel(regions, capacity, core, marks, own, other, tagged, gain_part, out, extra, front, back):
     arrival_rows(regions, capacity, core, marks, own, other, out, front, back)
     total = jnp.zeros((KIND_ROWS, own.shape[1]), F32)
-    share = out.shape[1] - capacity
     for r in range(regions):
         block = tagged[r, capacity : capacity + TAG_ROWS, :].astype(F32)
         if capacity >= LANES:
@@ -172,40 +164,53 @@
             kind = block[0:1, 0:capacity]
         kinds_hot = hot(iota((KIND_ROWS, capacity), 0) == kind.astype(I32) - 1)
         total = total + mm(kinds_hot, out[r, 0:capacity, :])
+    place = iota((KIND_ROWS, 1), 0)
+    first = gain_part[0:1, :].astype(F32)
+    second = gain_part[1:2, :].astype(F32)
+    extra[...] = jnp.where(place == KINDS, first, jnp.where(place == KINDS + 1, second, total)).astype(BF16)
+
+
+def pair_kernel(regions, own, received, out, gain_part):
+    share = out.shape[1]
+    for r in range(regions):
         rows = slice(r * share, (r + 1) * share)
-        out[r, capacity:, :] = (grad_own[rows, :] + grad_other[rows, :].astype(F32)).astype(BF16)
-    extra[0:KIND_ROWS, :] = total.astype(BF16)
-    rows = slice(regions * share, regions * share + 16)
-    extra[KIND_ROWS:, :] = (grad_own[rows, :] + grad_other[rows, :].astype(F32)).astype(BF16)
-
-
-def share_kernel(regions, capacity, got, extra, out):
-    total = got[0, capacity:, :].astype(F32)
+        out[r] = (own[rows, :] + received[rows, :].astype(F32)).astype(BF16)
+    gain_part[...] = (own[regions * share :, :] + received[regions * share :, :].astype(F32)).astype(BF16)
+
+
+def share_kernel(regions, capacity, got, extra, packed, out, tail, sems):
+    total = got[0].astype(F32)
     for r in range(1, regions):
-        total = total + got[r, capacity:, :].astype(F32)
+        total = total + got[r].astype(F32)
     share = total.shape[0]
-    total = total.astype(BF16)
-    for r in range(regions):
-        out[r, 0:share, :] = total
-        out[r, share:, :] = extra[...]
-
-
-def spread_kernel(regions, factor, got, out_q, out_k, out_v, out_o, out_gain, out_embed, flat):
+    tail[0:share, :] = total.astype(BF16)
+    tail[share:, :] = extra[...]
+    copies = [
+        pltpu.make_async_copy(tail, out.at[r, pl.ds(capacity, share + KIND_ROWS), :], sems.at[r]) for r in range(regions)
+    ]
+    for copy in copies:
+        copy.start()
+    for copy in copies:
+        copy.wait()
+
+
+def last_kernel(regions, capacity, factor, target_ref, got, out, out_q, out_k, out_v, out_o, out_gain, out_embed, flat):
+    pick_kernel(target_ref, got, out)
     width, half = out_q.shape
     share = 4 * width // regions
-    extra = jnp.zeros((KIND_ROWS + 16, half), F32)
-    for r in range(regions):
-        chunk = got[r].astype(F32) * factor
-        flat[r * share : (r + 1) * share, :] = chunk[0:share]
-        extra = extra + chunk[share : share + KIND_ROWS + 16]
+    extra = jnp.zeros((KIND_ROWS, half), F32)
+    for r in range(regions):
+        flat[r * share : (r + 1) * share, :] = got[r, capacity : capacity + share, :].astype(F32) * factor
+        extra = extra + got[r, capacity + share : capacity + share + KIND_ROWS, :].astype(F32)
+    extra = extra * factor
     out_q[...] = flat[0:width]
     out_k[...] = flat[width : 2 * width]
     out_v[...] = flat[2 * width : 3 * width]
     out_o[:, 0:half] = flat[3 * width : 3 * width + half]
     out_o[:, half:] = flat[3 * width + half : 4 * width]
     out_embed[...] = extra[0:KINDS]
-    out_gain[:, 0:half] = extra[KIND_ROWS : KIND_ROWS + 1]
-    out_gain[:, half:] = extra[KIND_ROWS + 1 : KIND_ROWS + 2]
+    out_gain[:, 0:half] = extra[KINDS : KINDS + 1]
+    out_gain[:, half:] = extra[KINDS + 1 : KINDS + 2]
 
 
 def pick_kernel(target_ref, got, out):
@@ -252,8 +257,8 @@
 
 
 def forward_kernel(
-    heads, core, mine, other, w_own, w_other, gain, keep, queries_t, keys_out, values_t, exps_out, context_t, inv_t,
-    keep_out, send_out, keys_t, w_out
+    heads, regions, capacity, core, got, got_other, w_own, w_other, gain, slab_out, queries_t, keys_out, values_t, exps_out,
+    context_t, inv_t, keep_out, send_out, marks, keys_t, w_out, lift, lift_other
 ):
     step = pl.program_id(0)
     width = heads * HEAD_DIM
@@ -265,7 +270,9 @@
     def _():
         w_q, w_k, w_v, w_o = full_weights(core, w_own, w_other)
         w_out[...] = w_o
-        slab = jnp.concatenate(ordered(flag, mine[...], other[...]), axis=1)
+        count_rows(regions, capacity, got, marks)
+        slab = bin_rows(regions, capacity, core, marks, got, got_other, lift, lift_other)
+        slab_out[...] = slab
         _, _, normed = norm_rows(slab, gain[...], width)
         queries_t[...] = jnp.transpose(mm(normed, w_q)).astype(BF16)
         k = mm(normed, w_k)
@@ -273,14 +280,17 @@
         keys_t[...] = jnp.transpose(k).astype(BF16)
         values_t[...] = jnp.transpose(mm(normed, w_v)).astype(BF16)
 
-    bias = jnp.where(keep[0:1, :] > 0.5, 0.0, MASKED / scale)
+    bias = jnp.where(is_filled(regions, core, marks, iota((1, SLOTS), 1)) > 0.5, 0.0, MASKED / scale)
     for k in range(PER_STEP):
         h = step * PER_STEP + k
         head_rows = pl.ds(pl.multiple_of(h * HEAD_DIM, HEAD_DIM), HEAD_DIM)
-        left = jnp.transpose(stack_rows(queries_t[head_rows, :], (1.0,))).astype(BF16)
-        scores = mm(left, stack_rows(keys_t[head_rows, :], (bias,)).astype(BF16))
+        scaled = queries_t[head_rows, :].astype(F32) * (scale * LOG2E)
+        high = scaled.astype(BF16).astype(F32)
+        left = jnp.transpose(jnp.concatenate([high, stack_rows(scaled - high, (1.0,))], axis=0)).astype(BF16)
+        k_rows = keys_t[head_rows, :].astype(F32)
+        scores = mm(left, jnp.concatenate([k_rows, stack_rows(k_rows, (bias,))], axis=0).astype(BF16))
         top = jnp.max(scores, axis=1, keepdims=True)
-        exps = jnp.exp2((scores - top) * (scale * LOG2E)).astype(BF16)
+        exps = jnp.exp2(scores - top).astype(BF16)
         exps_out[k] = exps
         summed = mm_nt(stack_rows(values_t[head_rows, :], (1.0,)).astype(BF16), exps)
         inv = 1.0 / summed[HEAD_DIM : HEAD_DIM + 1]
@@ -295,8 +305,8 @@
 
 
 def backward_kernel(
-    heads, core, mine, other, g_mine, g_other, w_own, w_other, gain, queries_t, keys_in, values_t, exps_in, context_t,
-    inv_t, keep_out, send_out, grad_keep, grad_send, d_context_t, d_query, d_key_t, d_value_t
+    heads, regions, capacity, core, marks, slab_in, got, got_other, w_own, w_other, gain, queries_t, keys_in, values_t, exps_in,
+    context_t, inv_t, keep_out, send_out, grad_keep, grad_send, d_context_t, d_query, d_key_t, d_value_t, grad_slab, lift, lift_other
 ):
     step = pl.program_id(0)
     width = heads * HEAD_DIM
@@ -305,13 +315,11 @@
     lane = iota((1, width), 1)
     scale = HEAD_DIM**-0.5
 
-    def grad_rows():
-        return jnp.concatenate(ordered(flag, g_mine[...], g_other[...]), axis=1)
-
     @pl.when(step == 0)
     def _():
         w_o = full_weights(core, w_own, w_other)[3]
-        d_context_t[...] = mm_nt(w_o, grad_rows()).astype(BF16)
+        grad_slab[...] = bin_rows(regions, capacity, core, marks, got, got_other, lift, lift_other)
+        d_context_t[...] = mm_nt(w_o, grad_slab[...]).astype(BF16)
 
     for k in range(PER_STEP):
         h = step * PER_STEP + k
@@ -332,7 +340,7 @@
     @pl.when(step == heads // PER_STEP - 1)
     def _():
         w_q, w_k, w_v, _ = full_weights(core, w_own, w_other)
-        slab = jnp.concatenate(ordered(flag, mine[...], other[...]), axis=1)
+        slab = slab_in[...]
         wide, inverse, normed = norm_rows(slab, gain[...], width)
         dq = d_query[...].astype(BF16)
         dk = jnp.transpose(d_key_t[...]).astype(BF16)
@@ -350,7 +358,7 @@
             grad_keep[place : place + width, :] = jnp.where(flag, grad[:, half:], grad[:, :half])
             grad_send[place : place + width, :] = jnp.where(flag, grad[:, :half], grad[:, half:]).astype(BF16)
             place += width
-        grad = mm(context_t[...].astype(BF16), grad_rows())
+        grad = mm(context_t[...].astype(BF16), grad_slab[...])
         for part in range(2):
             block = grad[:, part * half : (part + 1) * half]
             grad_keep[place : place + half, :] = jnp.where(flag, block[half:], block[:half])
@@ -431,23 +439,16 @@
     )
     got_base, packed_cot = lax.optimization_barrier((got_base, packed_cot))
     got_cot = exchange(packed_cot)
+    got_base_other = other_core(got_base)
     rows_shape = shape((SLOTS, half), BF16)
     lift = pltpu.VMEM((SLOTS + capacity, half), F32)
-    mine, theirs, info, marks = simple_call(
-        functools.partial(group_kernel, regions, capacity),
-        (rows_shape, rows_shape, shape((8, SLOTS), F32), shape((2, regions + 1), I32)),
-        (core, got_base),
-        scratch=(lift, lift),
-        scalars=1,
-        scalar_outs=1,
-    )
-    other = other_core(theirs)
 
     turned_shape = shape((width, SLOTS), BF16)
     exps_shape = shape((heads, SLOTS, SLOTS), BF16)
     exps_spec = pl.BlockSpec((PER_STEP, SLOTS, SLOTS), lambda h: (h, 0, 0))
-    inputs = (core, mine, other, w_own, w_other, gain, info)
+    inputs = (core, got_base, got_base_other, w_own, w_other, gain)
     outs = (
+        shape((SLOTS, width), BF16),
         turned_shape,
         shape((SLOTS, width), BF16),
         turned_shape,
@@ -456,15 +457,16 @@
         shape((heads, SLOTS), F32),
         rows_shape,
         rows_shape,
+        shape((2, regions + 1), I32),
     )
     work = heads * SLOTS * SLOTS
-    queries_t, keys, values_t, exps, context_t, inv_t, attn_keep, attn_send = pl.pallas_call(
-        functools.partial(forward_kernel, heads),
+    slab, queries_t, keys, values_t, exps, context_t, inv_t, attn_keep, attn_send, marks = pl.pallas_call(
+        functools.partial(forward_kernel, heads, regions, capacity),
         grid=(heads // PER_STEP,),
         out_shape=outs,
         in_specs=[SMEM_SPEC] + [whole(x) for x in inputs[1:]],
-        out_specs=tuple(exps_spec if x is exps_shape else whole(x) for x in outs),
-        scratch_shapes=(pltpu.VMEM((width, SLOTS), BF16), pltpu.VMEM((width, width), BF16)),
+        out_specs=tuple(exps_spec if x is exps_shape else whole(x) for x in outs[:-1]) + (SMEM_SPEC,),
+        scratch_shapes=(pltpu.VMEM((width, SLOTS), BF16), pltpu.VMEM((width, width), BF16), lift, lift),
         cost_estimate=pl.CostEstimate(flops=4 * work * width, transcendentals=work, bytes_accessed=2 * work),
         name="forward",
     )(*inputs)
@@ -477,65 +479,73 @@
         scalars=2,
     )
 
-    g_mine, g_theirs = simple_call(
-        functools.partial(regroup_kernel, regions, capacity),
-        (rows_shape, rows_shape),
-        (core, marks, got_cot),
-        scratch=(lift, lift),
-        scalars=2,
-    )
-    g_other = other_core(g_theirs)
-
+    got_cot_other = other_core(got_cot)
     grad_rows = 4 * width + 16
-    inputs = (core, mine, other, g_mine, g_other, w_own, w_other, gain, queries_t, keys, values_t, exps, context_t, inv_t)
+    inputs = (core, marks, slab, got_cot, got_cot_other, w_own, w_other, gain, queries_t, keys, values_t, exps, context_t, inv_t)
     outs = (rows_shape, rows_shape, shape((grad_rows, half), F32), shape((grad_rows, half), BF16))
     d_keep, d_send, grad_keep, grad_send = pl.pallas_call(
-        functools.partial(backward_kernel, heads),
+        functools.partial(backward_kernel, heads, regions, capacity),
         grid=(heads // PER_STEP,),
         out_shape=outs,
-        in_specs=[SMEM_SPEC] + [exps_spec if x is exps else whole(x) for x in inputs[1:]],
+        in_specs=[SMEM_SPEC] * 2 + [exps_spec if x is exps else whole(x) for x in inputs[2:]],
         out_specs=tuple(whole(x) for x in outs),
         scratch_shapes=(
             pltpu.VMEM((width, SLOTS), BF16),
             pltpu.VMEM((SLOTS, width), F32),
             pltpu.VMEM((width, SLOTS), F32),
             pltpu.VMEM((width, SLOTS), F32),
+            pltpu.VMEM((SLOTS, width), BF16),
+            lift,
+            lift,
         ),
         cost_estimate=pl.CostEstimate(flops=8 * work * width, transcendentals=0, bytes_accessed=2 * work),
         name="backward",
     )(*inputs)
 
-    def pick(home):
-        (rows,) = simple_call(pick_kernel, (shape((count, half), BF16),), (target, home))
-        return rows
-
     share = 4 * width // regions
+    pairs, gain_part = simple_call(
+        functools.partial(pair_kernel, regions),
+        (shape((regions, share, half), BF16), shape((16, half), BF16)),
+        (grad_keep, other_core(grad_send)),
+    )
+    payload_shape = shape((regions, capacity + share + KIND_ROWS, half), BF16)
     packed_grad, extra = simple_call(
         functools.partial(ungroup_grad_kernel, regions, capacity),
-        (shape((regions, capacity + share, half), BF16), shape((KIND_ROWS + 16, half), BF16)),
-        (core, marks, d_keep, other_core(d_send), got_cot, grad_keep, other_core(grad_send)),
+        (payload_shape, shape((KIND_ROWS, half), BF16)),
+        (core, marks, d_keep, other_core(d_send), got_cot, gain_part),
         scratch=(lift, lift),
         scalars=2,
     )
     got_cot, packed_attn = lax.optimization_barrier((got_cot, packed_attn))
     home_attn = exchange(packed_attn)
-    home_attn, packed_grad = lax.optimization_barrier((home_attn, packed_grad))
-    home_grad = exchange(packed_grad)
-    (shares,) = simple_call(
+    home_attn, pairs = lax.optimization_barrier((home_attn, pairs))
+    shares = exchange(pairs)
+    payload = pl.pallas_call(
         functools.partial(share_kernel, regions, capacity),
-        (shape((regions, share + KIND_ROWS + 16, half), BF16),),
-        (home_grad, extra),
-    )
-    summed = exchange(shares)
+        out_shape=payload_shape,
+        in_specs=[whole(shares), whole(extra), pl.BlockSpec(memory_space=pl.ANY)],
+        out_specs=pl.BlockSpec(memory_space=pl.ANY),
+        scratch_shapes=(pltpu.VMEM((share + KIND_ROWS, half), BF16), pltpu.SemaphoreType.DMA((regions,))),
+        input_output_aliases={2: 0},
+        name="share",
+    )(shares, extra, packed_grad)
+    home_grad = exchange(payload)
+    (attended,) = simple_call(pick_kernel, (shape((count, half), BF16),), (target, home_attn))
     column_shape = shape((width, half), F32)
-    grad_q, grad_k, grad_v, grad_o, grad_gain, grad_embed = simple_call(
-        functools.partial(spread_kernel, regions, float(count * regions) ** (-0.5)),
-        (column_shape, column_shape, column_shape, shape((half, width), F32), shape((1, width), F32), shape((KINDS, half), F32)),
-        (summed,),
+    grad_feats, grad_q, grad_k, grad_v, grad_o, grad_gain, grad_embed = simple_call(
+        functools.partial(last_kernel, regions, capacity, float(count * regions) ** (-0.5)),
+        (
+            shape((count, half), BF16),
+            column_shape,
+            column_shape,
+            column_shape,
+            shape((half, width), F32),
+            shape((1, width), F32),
+            shape((KINDS, half), F32),
+        ),
+        (target, home_grad),
         scratch=(pltpu.VMEM((4 * width, half), F32),),
     )
-    attended = pick(home_attn)
-    grad_feats = pick(home_grad)
     return (attended, grad_feats, grad_q, grad_k, grad_v, grad_o, grad_gain.reshape(width), grad_embed)
 
 

time: 136 us -> 146 us (1.074)
  waiting for transfers between devices: 15.3 us -> 51.7 us
  blocking collectives: 26.5 us -> 0 us
  starting transfers between devices: 21.7 us -> 25.6 us
  Pallas kernels: 65.6 us -> 61.8 us
    all_to_all x4 -> x5, waiting for transfers between devices: 13.7 us -> 47.2 us  [exchange(): return lax.all_to_all(x, 'region', split_axis=0, concat_axis=0, tiled=True)]
    all_to_all x1 -> x0, blocking collectives: 26.5 us -> none  [exchange(): return lax.all_to_all(x, 'region', split_axis=0, concat_axis=0, tiled=True)]
    pallas_call x10 -> x7, Pallas kernels: 28.3 us -> 21.7 us  [simple_call(): pl.pallas_call(kernel, out_shape=outs, in_specs=specs, out_specs=tuple((w...]
    all_to_all x4 -> x5, starting transfers between devices: 20.6 us -> 24.2 us  [exchange(): return lax.all_to_all(x, 'region', split_axis=0, concat_axis=0, tiled=True)]
    ppermute x6, waiting for transfers between devices: 1.63 us -> 4.5 us  [other_core(): return lax.ppermute(x, 'head', swap)]
    pallas_call x2 -> x3, Pallas kernels: 37.3 us -> 40 us  [the longest x1 20.9 us: on_device(): pl.pallas_call(functools.partial(backward_kernel, heads, regions, capacit...]
    unnamed x20 -> x22, local copies, waits for them, and re-layouts: 5.39 us -> 5.49 us
  transfers between devices with their start and end apart: 10 -> 11, of which waited for: 3 -> 7; matrix products, arithmetic and copies ran while one was open for 0% -> 0% of each run, Pallas kernels for 43% -> 36%
where the time goes in v6:
time: 146 us; the launch traced here: 145 us
  Pallas kernels  61.8 us (42%)
  waiting for transfers between devices  51.7 us (35%)
  starting transfers between devices  25.6 us (18%)
  local copies, waits for them, and re-layouts  5.49 us (4%)
    all_to_all x5, waiting for transfers between devices, exchange(): return lax.all_to_all(x, 'region', split_axis=0, concat_axis=0, tiled=True)  47.2 us
    all_to_all x5, starting transfers between devices, exchange(): return lax.all_to_all(x, 'region', split_axis=0, concat_axis=0, tiled=True)  24.2 us
    pallas_call x7, Pallas kernels, simple_call(): pl.pallas_call(kernel, out_shape=outs, in_specs=specs, out_specs=tuple((w...  21.7 us
    pallas_call x1, Pallas kernels, on_device(): pl.pallas_call(functools.partial(backward_kernel, heads, regions, capacit...  20.9 us
    pallas_call x1, Pallas kernels, on_device(): pl.pallas_call(functools.partial(forward_kernel, heads, regions, capacity...  17.4 us
    unnamed x22, local copies, waits for them, and re-layouts  5.49 us
    ppermute x6, waiting for transfers between devices, other_core(): return lax.ppermute(x, 'head', swap)  4.5 us
  transfers between devices with their start and end apart: 11, of which 7 were waited for; matrix products, arithmetic and copies ran while one was open for 0% of the time, Pallas kernels for 36%

profile of v6, /device:TPU:0, one launch (start us, length us, event | category | flops | bytes accessed | tf_op | source)
XLA Modules:
  0.0 145.3 jit_solution(4887137071437123081)
XLA Ops:
  0.6 3.6 %shard_map.161 = (bf16[8,272,128]{2,1,0:T(8,128)(2,1)}, s32[1,1024]{1,0:T(1,128)}, bf16[4,256,128]{2,1,0:T(8,128)(2,1)}) custom-call(s32[1,1024]{1,0:T(1,128)} %bitcast.7, s32[1,1024]{1,0:T(1,128)} %bitcast.5, bf16[1024,128]{1,0:T(8,128)(2,1)} %feats.1, bf16[12,128]{1,0:T(8,128)(2,1)} %embed.1, bf16[256,128]{1,0:T(8,128)(2,1)} %w_q.1, bf16[256,128]{1,0:T(8,128)(2,1)} %w_k.1, ...), custom_call_target="tpu_custom_call" | custom-call | tf_op jit(solution)/shard_map/pallas_call | solution.py:388
  4.2 7.3 %all-to-all-start = ((bf16[8,272,128]{2,1,0:T(8,128)(2,1)}), bf16[8,272,128]{2,1,0:T(8,128)(2,1)S(1)}, u32[]{:S(2)}, u32[]{:S(2)}) async-start(bf16[8,272,128]{2,1,0:T(8,128)(2,1)} %get-tuple-element.42), calls=%async_computation | async-start | bytes 1114112 | tf_op jit(solution)/shard_map/all_to_all | solution.py:424
  11.5 4.1 %shard_map.162 = bf16[8,272,128]{2,1,0:T(8,128)(2,1)} custom-call(s32[1,1024]{1,0:T(1,128)} %get-tuple-element.41.target_ref, s32[1,1024]{1,0:T(1,128)} %bitcast.6, bf16[1024,128]{1,0:T(8,128)(2,1)} %cot.1), custom_call_target="tpu_custom_call" | custom-call | tf_op jit(solution)/shard_map/pallas_call | solution.py:388
  15.6 11.1 %all-to-all-done.got = bf16[8,272,128]{2,1,0:T(8,128)(2,1)S(1)} async-done(((bf16[8,272,128]{2,1,0:T(8,128)(2,1)}), bf16[8,272,128]{2,1,0:T(8,128)(2,1)S(1)}, u32[]{:S(2)}, u32[]{:S(2)}) %all-to-all-start) | async-done | bytes 557088 | tf_op jit(solution)/shard_map/all_to_all | solution.py:424
  26.7 3.6 %all-to-all-start.1 = ((bf16[8,272,128]{2,1,0:T(8,128)(2,1)}), bf16[8,272,128]{2,1,0:T(8,128)(2,1)S(1)}, u32[]{:S(2)}, u32[]{:S(2)}) async-start(bf16[8,272,128]{2,1,0:T(8,128)(2,1)} %shard_map.162), calls=%async_computation.1 | async-start | bytes 1114112 | tf_op jit(solution)/shard_map/all_to_all | solution.py:424
  30.9 14.8 %all-to-all-done.1.got.tagged = bf16[8,272,128]{2,1,0:T(8,128)(2,1)S(1)} async-done(((bf16[8,272,128]{2,1,0:T(8,128)(2,1)}), bf16[8,272,128]{2,1,0:T(8,128)(2,1)S(1)}, u32[]{:S(2)}, u32[]{:S(2)}) %all-to-all-start.1) | async-done | bytes 557088 | tf_op jit(solution)/shard_map/all_to_all | solution.py:424
  46.7 17.4 %forward.1 = (bf16[1024,256]{1,0:T(8,128)(2,1)}, bf16[256,1024]{1,0:T(8,128)(2,1)}, bf16[1024,256]{1,0:T(8,128)(2,1)}, bf16[256,1024]{1,0:T(8,128)(2,1)}, bf16[8...) custom-call(s32[1]{0:T(128)} %bitcast.2.core, ...), custom_call_target="tpu_custom_call" | custom-call | flops 8589934592 | bytes 16777216 | tf_op jit(solution)/shard_map/forward/pallas_call | solution.py:463
  64.6 1.4 collective-permute-done.2.other
  66.7 2.2 %shard_map.163 = bf16[8,256,128]{2,1,0:T(8,128)(2,1)} custom-call(s32[1]{0:T(128)} %bitcast.2.core, s32[2,9]{1,0:T(2,128)} %get-tuple-element.46.marks, bf16[1024,128]{1,0:T(8,128)(2,1)} %get-tuple-element.47.own, bf16[1024,128]{1,0:T(8,128)(2,1)} %copy-done.7), custom_call_target="tpu_custom_call" | custom-call | tf_op jit(solution)/shard_map/pallas_call | solution.py:388
  68.9 3.7 %all-to-all-start.2 = ((bf16[8,256,128]{2,1,0:T(8,128)(2,1)}), bf16[8,256,128]{2,1,0:T(8,128)(2,1)S(1)}, u32[]{:S(2)}, u32[]{:S(2)}) async-start(bf16[8,256,128]{2,1,0:T(8,128)(2,1)} %shard_map.163), calls=%async_computation.2 | async-start | bytes 1048576 | tf_op jit(solution)/shard_map/all_to_all | solution.py:424
  72.6 0.8 copy-done.8
  73.4 20.9 %backward.1 = (bf16[1024,128]{1,0:T(8,128)(2,1)}, bf16[1024,128]{1,0:T(8,128)(2,1)}, f32[1040,128]{1,0:T(8,128)}, bf16[1040,128]{1,0:T(8,128)(2,1)}) custom-call(s32[1]{0:T(128)} %bitcast.2.core, s32[2,9]{1,0:T(2,128)} %get-tuple-element.46.marks, bf16[1024,256]{1,0:T(8,128)(2,1)} %get-tuple-element.50.slab_in, bf16[8,272,128]{2,1,0:T(8,128)(2,1)} %copy-done.1, ...), custom_call_target="tpu_custom_call" | custom-call | flops 17179869184 | bytes 16777216 | tf_op jit(solution)/shard_map/backward/pallas_call | solution.py:486
  94.6 1.4 collective-permute-done.4.received
  96.7 1.9 %shard_map.164 = (bf16[8,128,128]{2,1,0:T(8,128)(2,1)}, bf16[16,128]{1,0:T(8,128)(2,1)}) custom-call(f32[1040,128]{1,0:T(8,128)} %get-tuple-element.57.own, bf16[1040,128]{1,0:T(8,128)(2,1)} %copy-done.5), custom_call_target="tpu_custom_call" | custom-call | tf_op jit(solution)/shard_map/pallas_call | solution.py:388
  98.6 6.0 %all-to-all-start.3 = ((bf16[8,128,128]{2,1,0:T(8,128)(2,1)}), bf16[8,128,128]{2,1,0:T(8,128)(2,1)S(1)}, u32[]{:S(2)}, u32[]{:S(2)}) async-start(bf16[8,128,128]{2,1,0:T(8,128)(2,1)} %get-tuple-element.61), calls=%async_computation.3 | async-start | bytes 524288 | tf_op jit(solution)/shard_map/all_to_all | solution.py:424
  104.6 1.7 %collective-permute-done.5.other = bf16[1024,128]{1,0:T(8,128)(2,1)S(1)} collective-permute-done((bf16[1024,128]{1,0:T(8,128)(2,1)}, bf16[1024,128]{1,0:T(8,128)(2,1)S(1)}, u32[]{:S(2)}, u32[]{:S(2)}) %collective-permute-start.5) | collective-permute-done | bytes 262176 | tf_op jit(solution)/shard_map/ppermute | solution.py:421
  107.0 2.5 %shard_map.166 = (bf16[8,400,128]{2,1,0:T(8,128)(2,1)}, bf16[16,128]{1,0:T(8,128)(2,1)}) custom-call(s32[1]{0:T(128)} %bitcast.2.core, s32[2,9]{1,0:T(2,128)} %get-tuple-element.46.marks, bf16[1024,128]{1,0:T(8,128)(2,1)} %get-tuple-element.62.own, bf16[1024,128]{1,0:T(8,128)(2,1)} %copy-done.6, bf16[8,272,128]{2,1,0:T(8,128)(2,1)} %copy-done.1, ...), custom_call_target="tpu_custom_call" | custom-call | tf_op jit(solution)/shard_map/pallas_call | solution.py:388
  109.6 4.3 %all-to-all-done.3.got = bf16[8,128,128]{2,1,0:T(8,128)(2,1)S(1)} async-done(((bf16[8,128,128]{2,1,0:T(8,128)(2,1)}), bf16[8,128,128]{2,1,0:T(8,128)(2,1)S(1)}, u32[]{:S(2)}, u32[]{:S(2)}) %all-to-all-start.3) | async-done | bytes 262176 | tf_op jit(solution)/shard_map/all_to_all | solution.py:424
  114.5 1.8 %share.1 = bf16[8,400,128]{2,1,0:T(8,128)(2,1)} custom-call(bf16[8,128,128]{2,1,0:T(8,128)(2,1)} %copy-done.3, bf16[16,128]{1,0:T(8,128)(2,1)} %get-tuple-element.65.extra, bf16[8,400,128]{2,1,0:T(8,128)(2,1)} %get-tuple-element.66.packed), custom_call_target="tpu_custom_call", output_to_operand_aliasing={{}: (2, {})} | custom-call | tf_op jit(solution)/shard_map/share/pallas_call | solution.py:523
  116.3 3.6 %all-to-all-start.4 = ((bf16[8,400,128]{2,1,0:T(8,128)(2,1)}), bf16[8,400,128]{2,1,0:T(8,128)(2,1)S(1)}, u32[]{:S(2)}, u32[]{:S(2)}) async-start(bf16[8,400,128]{2,1,0:T(8,128)(2,1)} %share.1), calls=%async_computation.4 | async-start | bytes 1638400 | tf_op jit(solution)/shard_map/all_to_all | solution.py:424
  119.9 3.6 %shard_map.165 = bf16[1024,128]{1,0:T(8,128)(2,1)} custom-call(s32[1,1024]{1,0:T(1,128)} %get-tuple-element.41.target_ref, bf16[8,256,128]{2,1,0:T(8,128)(2,1)} %copy-done.2), custom_call_target="tpu_custom_call" | custom-call | tf_op jit(solution)/shard_map/pallas_call | solution.py:388
  123.5 17.0 %all-to-all-done.4.got = bf16[8,400,128]{2,1,0:T(8,128)(2,1)S(1)} async-done(((bf16[8,400,128]{2,1,0:T(8,128)(2,1)}), bf16[8,400,128]{2,1,0:T(8,128)(2,1)S(1)}, u32[]{:S(2)}, u32[]{:S(2)}) %all-to-all-start.4) | async-done | bytes 819232 | tf_op jit(solution)/shard_map/all_to_all | solution.py:424
  140.5 0.9 copy-done
  141.5 3.9 %shard_map.167 = (bf16[1024,128]{1,0:T(8,128)(2,1)}, f32[256,128]{1,0:T(8,128)}, f32[256,128]{1,0:T(8,128)}, f32[256,128]{1,0:T(8,128)}, f32[128,256]{1,0:T(8,12...) custom-call(s32[1,1024]{1,0:T(1,128)} %get-tuple-element.41.target_ref, bf16[8,400,128]{2,1,0:T(8,128)(2,1)} %copy-done), custom_call_target="tpu_custom_call" | custom-call | tf_op jit(solution)/shard_map/pallas_call | solution.py:388
  (30 shorter events, 5.2 us)
Async XLA Ops:
  4.2 22.5 %all-to-all-start = ((bf16[8,272,128]{2,1,0:T(8,128)(2,1)}), bf16[8,272,128]{2,1,0:T(8,128)(2,1)S(1)}, u32[]{:S(2)}, u32[]{:S(2)}) async-start(bf16[8,272,128]{2,1,0:T(8,128)(2,1)} %get-tuple-element.42), calls=%async_computation | async-start | bytes 1114112 | tf_op jit(solution)/shard_map/all_to_all | solution.py:424
  26.7 19.1 %copy-start.4 = (bf16[8,272,128]{2,1,0:T(8,128)(2,1)}, bf16[8,272,128]{2,1,0:T(8,128)(2,1)S(1)}, u32[]{:S(2)}) copy-start(bf16[8,272,128]{2,1,0:T(8,128)(2,1)S(1)} %all-to-all-done.got) | copy-start | bytes 1671172
  26.7 19.0 %all-to-all-start.1 = ((bf16[8,272,128]{2,1,0:T(8,128)(2,1)}), bf16[8,272,128]{2,1,0:T(8,128)(2,1)S(1)}, u32[]{:S(2)}, u32[]{:S(2)}) async-start(bf16[8,272,128]{2,1,0:T(8,128)(2,1)} %shard_map.162), calls=%async_computation.1 | async-start | bytes 1114112 | tf_op jit(solution)/shard_map/all_to_all | solution.py:424
  30.4 15.4 %collective-permute-start = (bf16[8,272,128]{2,1,0:T(8,128)(2,1)S(1)}, bf16[8,272,128]{2,1,0:T(8,128)(2,1)S(1)}, u32[]{:S(2)}, u32[]{:S(2)}) collective-permute-start(bf16[8,272,128]{2,1,0:T(8,128)(2,1)S(1)} %all-to-all-done.got), channel_id=1, source_target_pairs={{0,1},{1,0},{2,3},{3,2},{4,5},{5,4},{6,7},{7,6},{8,9},{9,8},{10,11... | collective-permute-start | bytes 1671176 | tf_op jit(solution)/shard_map/ppermute | solution.py:421
  30.4 15.3 %collective-permute-start.1 = (bf16[4,256,128]{2,1,0:T(8,128)(2,1)}, bf16[4,256,128]{2,1,0:T(8,128)(2,1)S(1)}, u32[]{:S(2)}, u32[]{:S(2)}) collective-permute-start(bf16[4,256,128]{2,1,0:T(8,128)(2,1)} %get-tuple-element.45.w_own), channel_id=1, source_target_pairs={{0,1},{1,0},{2,3},{3,2},{4,5},{5,4},{6,7},{7,6},{8,9},{9,8},{10,11... | collective-permute-start | bytes 786440 | tf_op jit(solution)/shard_map/ppermute | solution.py:421
  45.7 23.1 %copy-start.1 = (bf16[8,272,128]{2,1,0:T(8,128)(2,1)}, bf16[8,272,128]{2,1,0:T(8,128)(2,1)S(1)}, u32[]{:S(2)}) copy-start(bf16[8,272,128]{2,1,0:T(8,128)(2,1)S(1)} %all-to-all-done.1.got.tagged) | copy-start | bytes 1671172
  45.7 26.8 %collective-permute-start.3 = (bf16[8,272,128]{2,1,0:T(8,128)(2,1)S(1)}, bf16[8,272,128]{2,1,0:T(8,128)(2,1)S(1)}, u32[]{:S(2)}, u32[]{:S(2)}) collective-permute-start(bf16[8,272,128]{2,1,0:T(8,128)(2,1)S(1)} %all-to-all-done.1.got.tagged), channel_id=1, source_target_pairs={{0,1},{1,0},{2,3},{3,2},{4,5},{5,4},{6,7},{7,6},{8,9},{9,8},{10,11... | collective-permute-start | bytes 1671176 | tf_op jit(solution)/shard_map/ppermute | solution.py:421
  45.7 0.7 copy-start.10
  45.8 0.9 copy-start.9
  64.1 1.9 %collective-permute-start.2 = (bf16[1024,128]{1,0:T(8,128)(2,1)}, bf16[1024,128]{1,0:T(8,128)(2,1)S(1)}, u32[]{:S(2)}, u32[]{:S(2)}) collective-permute-start(bf16[1024,128]{1,0:T(8,128)(2,1)} %get-tuple-element.48), channel_id=1, source_target_pairs={{0,1},{1,0},{2,3},{3,2},{4,5},{5,4},{6,7},{7,6},{8,9},{9,8},{10,11... | collective-permute-start | bytes 786440 | tf_op jit(solution)/shard_map/ppermute | solution.py:421
  66.0 0.7 copy-start.7
  68.9 29.7 %all-to-all-start.2 = ((bf16[8,256,128]{2,1,0:T(8,128)(2,1)}), bf16[8,256,128]{2,1,0:T(8,128)(2,1)S(1)}, u32[]{:S(2)}, u32[]{:S(2)}) async-start(bf16[8,256,128]{2,1,0:T(8,128)(2,1)} %shard_map.163), calls=%async_computation.2 | async-start | bytes 1048576 | tf_op jit(solution)/shard_map/all_to_all | solution.py:424
  72.6 0.8 copy-start.8
  94.3 1.8 %collective-permute-start.4 = (bf16[1040,128]{1,0:T(8,128)(2,1)}, bf16[1040,128]{1,0:T(8,128)(2,1)S(1)}, u32[]{:S(2)}, u32[]{:S(2)}) collective-permute-start(bf16[1040,128]{1,0:T(8,128)(2,1)} %get-tuple-element.58), channel_id=1, source_target_pairs={{0,1},{1,0},{2,3},{3,2},{4,5},{5,4},{6,7},{7,6},{8,9},{9,8},{10,11... | collective-permute-start | bytes 798728 | tf_op jit(solution)/shard_map/ppermute | solution.py:421
  96.0 0.7 copy-start.5
  98.6 21.3 %copy-start.2 = (bf16[8,256,128]{2,1,0:T(8,128)(2,1)}, bf16[8,256,128]{2,1,0:T(8,128)(2,1)S(1)}, u32[]{:S(2)}) copy-start(bf16[8,256,128]{2,1,0:T(8,128)(2,1)S(1)} %all-to-all-done.2.got) | copy-start | bytes 1572868
  98.6 15.2 %all-to-all-start.3 = ((bf16[8,128,128]{2,1,0:T(8,128)(2,1)}), bf16[8,128,128]{2,1,0:T(8,128)(2,1)S(1)}, u32[]{:S(2)}, u32[]{:S(2)}) async-start(bf16[8,128,128]{2,1,0:T(8,128)(2,1)} %get-tuple-element.61), calls=%async_computation.3 | async-start | bytes 524288 | tf_op jit(solution)/shard_map/all_to_all | solution.py:424
  104.6 1.7 %collective-permute-start.5 = (bf16[1024,128]{1,0:T(8,128)(2,1)}, bf16[1024,128]{1,0:T(8,128)(2,1)S(1)}, u32[]{:S(2)}, u32[]{:S(2)}) collective-permute-start(bf16[1024,128]{1,0:T(8,128)(2,1)} %get-tuple-element.63), channel_id=1, source_target_pairs={{0,1},{1,0},{2,3},{3,2},{4,5},{5,4},{6,7},{7,6},{8,9},{9,8},{10,11... | collective-permute-start | bytes 786440 | tf_op jit(solution)/shard_map/ppermute | solution.py:421
  106.3 0.7 copy-start.6
  113.8 0.7 copy-start.3
  116.3 24.2 %all-to-all-start.4 = ((bf16[8,400,128]{2,1,0:T(8,128)(2,1)}), bf16[8,400,128]{2,1,0:T(8,128)(2,1)S(1)}, u32[]{:S(2)}, u32[]{:S(2)}) async-start(bf16[8,400,128]{2,1,0:T(8,128)(2,1)} %share.1), calls=%async_computation.4 | async-start | bytes 1638400 | tf_op jit(solution)/shard_map/all_to_all | solution.py:424
  140.5 0.9 copy-start

commit v7 on v6

--- a/solution.py
+++ b/solution.py
@@ -52,34 +52,62 @@
     return n.bit_length() - 1
 
 
+def turned(row):
+    return jnp.transpose(jnp.broadcast_to(row.astype(F32), (LANES, row.shape[1])))
+
+
+def running(group_hot):
+    rows, count = group_hot.shape
+    blocks = count // LANES
+    stacked = jnp.concatenate([group_hot[:, k * LANES : (k + 1) * LANES] for k in range(blocks)], axis=0)
+    before = hot(iota((LANES, LANES), 0) < iota((LANES, LANES), 1))
+    inside = mm(stacked.astype(BF16), before)
+    sums = jnp.sum(stacked, axis=1, keepdims=True)
+    offset = jnp.zeros((rows, 1), F32)
+    pieces = []
+    for k in range(blocks):
+        part = slice(k * rows, (k + 1) * rows)
+        pieces.append(inside[part] + offset)
+        offset = offset + sums[part]
+    return jnp.concatenate(pieces, axis=1), offset
+
+
 def positions(regions, capacity, cell):
     count = cell.shape[1]
-    local_rows = BINS_DEV * SLOTS
-    owner = lax.shift_right_logical(cell, log2_of(local_rows))
+    owner = lax.shift_right_logical(cell, log2_of(BINS_DEV * SLOTS))
     group = lax.shift_right_logical(cell, log2_of(SLOTS))
     classes = max(BINS_DEV * regions, 16)
     group_hot = jnp.where(iota((classes, count), 0) == group, 1.0, 0.0)
-    before = hot(iota((count, count), 0) < iota((count, count), 1))
-    rank = jnp.sum(mm(group_hot.astype(BF16), before) * group_hot, axis=0, keepdims=True).astype(I32)
+    before, counts = running(group_hot)
+    rank = jnp.sum(before * group_hot, axis=0, keepdims=True).astype(I32)
     second = jnp.bitwise_and(group, 1) > 0
-    target = owner * capacity + jnp.where(second, capacity - 1 - rank, rank)
-    return target, jnp.sum(group_hot, axis=1, keepdims=True)
+    return owner, jnp.where(second, capacity - 1 - rank, rank), counts
+
+
+def to_chunks(capacity, place, owner_column, rows, first, many):
+    chosen = hot(iota((capacity, place.shape[1]), 0) == place)
+    wide = rows.astype(F32)
+    masked = [jnp.where(owner_column == float(first + k), wide, 0.0).astype(BF16) for k in range(many)]
+    return mm(chosen, jnp.concatenate(masked, axis=1)).astype(BF16)
 
 
 def pack_kernel(regions, capacity, cells, kinds, feats, embed, w_q, w_k, w_v, w_o, out_base, out_target, out_w):
     count, half = feats.shape
-    target, counts = positions(regions, capacity, cells[...])
-    out_target[...] = target
+    owner, place, counts = positions(regions, capacity, cells[...])
+    out_target[...] = owner * capacity + place
     kinds_hot = hot(iota((KINDS, count), 0) == kinds[...])
     base = (feats[...].astype(F32) + mm_tn(kinds_hot, embed[...])).astype(BF16)
-    place = iota((TAG_ROWS, half), 0)
-    for r in range(regions):
-        chosen = hot(iota((capacity, count), 0) + r * capacity == target)
-        out_base[r, 0:capacity, :] = mm(chosen, base).astype(BF16)
-        first = counts[2 * r : 2 * r + 1]
-        second = counts[2 * r + 1 : 2 * r + 2]
-        tags = jnp.where(place == 0, first, jnp.where(place == 1, second, 0.0))
-        out_base[r, capacity : capacity + TAG_ROWS, :] = tags.astype(BF16)
+    owner_column = turned(owner)
+    tag_place = iota((TAG_ROWS, half), 0)
+    for r in range(0, regions, 2):
+        moved = to_chunks(capacity, place, owner_column, base, r, 2)
+        for k in range(2):
+            out_base[r + k, 0:capacity, :] = moved[:, k * half : (k + 1) * half]
+            pair = 2 * (r + k)
+            first = counts[pair : pair + 1]
+            second = counts[pair + 1 : pair + 2]
+            tags = jnp.where(tag_place == 0, first, jnp.where(tag_place == 1, second, 0.0))
+            out_base[r + k, capacity : capacity + TAG_ROWS, :] = tags.astype(BF16)
     out_w[0] = w_q[...]
     out_w[1] = w_k[...]
     out_w[2] = w_v[...]
@@ -88,13 +116,18 @@
 
 
 def pack_cot_kernel(regions, capacity, target_ref, kinds, cot, out_cot):
-    count = cot.shape[0]
+    count, half = cot.shape
     target = target_ref[...]
-    rows = cot[...]
+    owner = lax.shift_right_logical(target, log2_of(capacity))
+    place = jnp.bitwise_and(target, capacity - 1)
+    owner_column = turned(owner)
     tags = jnp.where(iota((TAG_ROWS, count), 0) == 0, kinds[...] + 1, 0).astype(F32).astype(BF16)
+    for r in range(0, regions, 2):
+        moved = to_chunks(capacity, place, owner_column, cot[...], r, 2)
+        for k in range(2):
+            out_cot[r + k, 0:capacity, :] = moved[:, k * half : (k + 1) * half]
     for r in range(regions):
         chosen = hot(iota((capacity, count), 0) + r * capacity == target)
-        out_cot[r, 0:capacity, :] = mm(chosen, rows).astype(BF16)
         tag = mm_nt(tags, chosen)
         if capacity >= LANES:
             tag = jnp.concatenate([tag[0:8, 0:LANES], tag[0:8, LANES : 2 * LANES]], axis=0)
@@ -174,8 +207,8 @@
     share = out.shape[1]
     for r in range(regions):
         rows = slice(r * share, (r + 1) * share)
-        out[r] = (own[rows, :] + received[rows, :].astype(F32)).astype(BF16)
-    gain_part[...] = (own[regions * share :, :] + received[regions * share :, :].astype(F32)).astype(BF16)
+        out[r] = (own[rows, :].astype(F32) + received[rows, :].astype(F32)).astype(BF16)
+    gain_part[...] = (own[regions * share :, :].astype(F32) + received[regions * share :, :].astype(F32)).astype(BF16)
 
 
 def share_kernel(regions, capacity, got, extra, packed, out, tail, sems):
@@ -214,15 +247,26 @@
 
 
 def pick_kernel(target_ref, got, out):
-    capacity = BINS_DEV * SLOTS // got.shape[0]
-    total = got.shape[0] * capacity
-    count = out.shape[0]
-    column = jnp.transpose(jnp.broadcast_to(target_ref[...].astype(F32), (8, count)))[:, 0:1].astype(I32)
-    flat = got[:, 0:capacity, :].reshape(total, got.shape[2])
+    regions = got.shape[0]
+    capacity = BINS_DEV * SLOTS // regions
+    count, half = out.shape
+    target = target_ref[...]
+    owner_column = turned(lax.shift_right_logical(target, log2_of(capacity)))
+    place_column = turned(jnp.bitwise_and(target, capacity - 1))
+    width = min(capacity, LANES)
+    lane = iota((1, width), 1).astype(F32)
     step = 256
     for s in range(0, count, step):
-        chosen = hot(iota((step, total), 1) == column[s : s + step])
-        out[s : s + step, :] = mm(chosen, flat).astype(BF16)
+        owner = owner_column[s : s + step]
+        place = place_column[s : s + step, 0:width]
+        chosen = [hot(place - float(k) == lane) for k in range(0, capacity, width)]
+        chosen = jnp.concatenate(chosen, axis=1)
+        total = jnp.zeros((step, half), F32)
+        for r in range(0, regions, 2):
+            chunks = jnp.concatenate([got[r, 0:capacity, :], got[r + 1, 0:capacity, :]], axis=1)
+            rows = mm(chosen, chunks)
+            total = jnp.where(owner == float(r), rows[:, :half], jnp.where(owner == float(r + 1), rows[:, half:], total))
+        out[s : s + step, :] = total.astype(BF16)
 
 
 def ordered(flag, own, other):
@@ -355,19 +399,19 @@
         place = 0
         for d_rows in (dq, dk, dv):
             grad = mm(normed_t, d_rows)
-            grad_keep[place : place + width, :] = jnp.where(flag, grad[:, half:], grad[:, :half])
+            grad_keep[place : place + width, :] = jnp.where(flag, grad[:, half:], grad[:, :half]).astype(BF16)
             grad_send[place : place + width, :] = jnp.where(flag, grad[:, :half], grad[:, half:]).astype(BF16)
             place += width
         grad = mm(context_t[...].astype(BF16), grad_slab[...])
         for part in range(2):
             block = grad[:, part * half : (part + 1) * half]
-            grad_keep[place : place + half, :] = jnp.where(flag, block[half:], block[:half])
+            grad_keep[place : place + half, :] = jnp.where(flag, block[half:], block[:half]).astype(BF16)
             grad_send[place : place + half, :] = jnp.where(flag, block[:half], block[half:]).astype(BF16)
             place += half
         gain_grad = jnp.sum(d_normed * wide * inverse, axis=0, keepdims=True)
         pick = iota((16, half), 0)
         block = jnp.where(pick == 0, gain_grad[:, :half], jnp.where(pick == 1, gain_grad[:, half:], 0.0))
-        grad_keep[place : place + 16, :] = block
+        grad_keep[place : place + 16, :] = block.astype(BF16)
         grad_send[place : place + 16, :] = block.astype(BF16)
 
 
@@ -482,7 +526,7 @@
     got_cot_other = other_core(got_cot)
     grad_rows = 4 * width + 16
     inputs = (core, marks, slab, got_cot, got_cot_other, w_own, w_other, gain, queries_t, keys, values_t, exps, context_t, inv_t)
-    outs = (rows_shape, rows_shape, shape((grad_rows, half), F32), shape((grad_rows, half), BF16))
+    outs = (rows_shape, rows_shape, shape((grad_rows, half), BF16), shape((grad_rows, half), BF16))
     d_keep, d_send, grad_keep, grad_send = pl.pallas_call(
         functools.partial(backward_kernel, heads, regions, capacity),
         grid=(heads // PER_STEP,),

time: 146 us -> 144 us (0.986)
  Pallas kernels: 61.8 us -> 58.2 us
  waiting for transfers between devices: 51.7 us -> 53.3 us
    pallas_call x7, Pallas kernels: 21.7 us -> 18.3 us  [simple_call(): pl.pallas_call(kernel, out_shape=outs, in_specs=specs, out_specs=tuple((w...]
    all_to_all x5, waiting for transfers between devices: 47.2 us -> 48.8 us  [exchange(): return lax.all_to_all(x, 'region', split_axis=0, concat_axis=0, tiled=True)]
  transfers between devices with their start and end apart: 11 -> 11, of which waited for: 7 -> 7; matrix products, arithmetic and copies ran while one was open for 0% -> 0% of each run, Pallas kernels for 36% -> 35%
where the time goes in v7:
time: 144 us; the launch traced here: 143 us
  Pallas kernels  58.2 us (40%)
  waiting for transfers between devices  53.3 us (37%)
  starting transfers between devices  25.6 us (18%)
  local copies, waits for them, and re-layouts  5.46 us (4%)
    all_to_all x5, waiting for transfers between devices, exchange(): return lax.all_to_all(x, 'region', split_axis=0, concat_axis=0, tiled=True)  48.8 us
    all_to_all x5, starting transfers between devices, exchange(): return lax.all_to_all(x, 'region', split_axis=0, concat_axis=0, tiled=True)  24.2 us
    pallas_call x1, Pallas kernels, on_device(): pl.pallas_call(functools.partial(backward_kernel, heads, regions, capacit...  20.8 us
    pallas_call x7, Pallas kernels, simple_call(): pl.pallas_call(kernel, out_shape=outs, in_specs=specs, out_specs=tuple((w...  18.3 us
    pallas_call x1, Pallas kernels, on_device(): pl.pallas_call(functools.partial(forward_kernel, heads, regions, capacity...  17.4 us
    unnamed x22, local copies, waits for them, and re-layouts  5.46 us
    ppermute x6, waiting for transfers between devices, other_core(): return lax.ppermute(x, 'head', swap)  4.5 us
  transfers between devices with their start and end apart: 11, of which 7 were waited for; matrix products, arithmetic and copies ran while one was open for 0% of the time, Pallas kernels for 35%

profile of v7, /device:TPU:0, one launch (start us, length us, event | category | flops | bytes accessed | tf_op | source)
XLA Modules:
  0.0 143.3 jit_solution(12939711779623261276)
XLA Ops:
  0.6 2.9 %shard_map.161 = (bf16[8,272,128]{2,1,0:T(8,128)(2,1)}, s32[1,1024]{1,0:T(1,128)}, bf16[4,256,128]{2,1,0:T(8,128)(2,1)}) custom-call(s32[1,1024]{1,0:T(1,128)} %bitcast.7, s32[1,1024]{1,0:T(1,128)} %bitcast.5, bf16[1024,128]{1,0:T(8,128)(2,1)} %feats.1, bf16[12,128]{1,0:T(8,128)(2,1)} %embed.1, bf16[256,128]{1,0:T(8,128)(2,1)} %w_q.1, bf16[256,128]{1,0:T(8,128)(2,1)} %w_k.1, ...), custom_call_target="tpu_custom_call" | custom-call | tf_op jit(solution)/shard_map/pallas_call | solution.py:432
  3.5 7.3 %all-to-all-start = ((bf16[8,272,128]{2,1,0:T(8,128)(2,1)}), bf16[8,272,128]{2,1,0:T(8,128)(2,1)S(1)}, u32[]{:S(2)}, u32[]{:S(2)}) async-start(bf16[8,272,128]{2,1,0:T(8,128)(2,1)} %get-tuple-element.42), calls=%async_computation | async-start | bytes 1114112 | tf_op jit(solution)/shard_map/all_to_all | solution.py:468
  10.8 3.6 %shard_map.162 = bf16[8,272,128]{2,1,0:T(8,128)(2,1)} custom-call(s32[1,1024]{1,0:T(1,128)} %get-tuple-element.41.target_ref, s32[1,1024]{1,0:T(1,128)} %bitcast.6, bf16[1024,128]{1,0:T(8,128)(2,1)} %cot.1), custom_call_target="tpu_custom_call" | custom-call | tf_op jit(solution)/shard_map/pallas_call | solution.py:432
  14.4 11.6 %all-to-all-done.got = bf16[8,272,128]{2,1,0:T(8,128)(2,1)S(1)} async-done(((bf16[8,272,128]{2,1,0:T(8,128)(2,1)}), bf16[8,272,128]{2,1,0:T(8,128)(2,1)S(1)}, u32[]{:S(2)}, u32[]{:S(2)}) %all-to-all-start) | async-done | bytes 557088 | tf_op jit(solution)/shard_map/all_to_all | solution.py:468
  26.0 3.6 %all-to-all-start.1 = ((bf16[8,272,128]{2,1,0:T(8,128)(2,1)}), bf16[8,272,128]{2,1,0:T(8,128)(2,1)S(1)}, u32[]{:S(2)}, u32[]{:S(2)}) async-start(bf16[8,272,128]{2,1,0:T(8,128)(2,1)} %shard_map.162), calls=%async_computation.1 | async-start | bytes 1114112 | tf_op jit(solution)/shard_map/all_to_all | solution.py:468
  30.2 14.8 %all-to-all-done.1.got.tagged = bf16[8,272,128]{2,1,0:T(8,128)(2,1)S(1)} async-done(((bf16[8,272,128]{2,1,0:T(8,128)(2,1)}), bf16[8,272,128]{2,1,0:T(8,128)(2,1)S(1)}, u32[]{:S(2)}, u32[]{:S(2)}) %all-to-all-start.1) | async-done | bytes 557088 | tf_op jit(solution)/shard_map/all_to_all | solution.py:468
  46.0 17.4 %forward.1 = (bf16[1024,256]{1,0:T(8,128)(2,1)}, bf16[256,1024]{1,0:T(8,128)(2,1)}, bf16[1024,256]{1,0:T(8,128)(2,1)}, bf16[256,1024]{1,0:T(8,128)(2,1)}, bf16[8...) custom-call(s32[1]{0:T(128)} %bitcast.2.core, ...), custom_call_target="tpu_custom_call" | custom-call | flops 8589934592 | bytes 16777216 | tf_op jit(solution)/shard_map/forward/pallas_call | solution.py:507
  63.9 1.4 collective-permute-done.2.other
  65.9 2.2 %shard_map.163 = bf16[8,256,128]{2,1,0:T(8,128)(2,1)} custom-call(s32[1]{0:T(128)} %bitcast.2.core, s32[2,9]{1,0:T(2,128)} %get-tuple-element.46.marks, bf16[1024,128]{1,0:T(8,128)(2,1)} %get-tuple-element.47.own, bf16[1024,128]{1,0:T(8,128)(2,1)} %copy-done.7), custom_call_target="tpu_custom_call" | custom-call | tf_op jit(solution)/shard_map/pallas_call | solution.py:432
  68.2 3.7 %all-to-all-start.2 = ((bf16[8,256,128]{2,1,0:T(8,128)(2,1)}), bf16[8,256,128]{2,1,0:T(8,128)(2,1)S(1)}, u32[]{:S(2)}, u32[]{:S(2)}) async-start(bf16[8,256,128]{2,1,0:T(8,128)(2,1)} %shard_map.163), calls=%async_computation.2 | async-start | bytes 1048576 | tf_op jit(solution)/shard_map/all_to_all | solution.py:468
  71.9 0.8 copy-done.8
  72.7 20.8 %backward.1 = (bf16[1024,128]{1,0:T(8,128)(2,1)}, bf16[1024,128]{1,0:T(8,128)(2,1)}, bf16[1040,128]{1,0:T(8,128)(2,1)}, bf16[1040,128]{1,0:T(8,128)(2,1)}) custom-call(s32[1]{0:T(128)} %bitcast.2.core, s32[2,9]{1,0:T(2,128)} %get-tuple-element.46.marks, bf16[1024,256]{1,0:T(8,128)(2,1)} %get-tuple-element.50.slab_in, bf16[8,272,128]{2,1,0:T(8,128)(2,1)} %copy-done.1, ...), custom_call_target="tpu_custom_call" | custom-call | flops 17179869184 | bytes 16777216 | tf_op jit(solution)/shard_map/backward/pallas_call | solution.py:530
  93.8 1.4 collective-permute-done.4.received
  95.9 1.8 %shard_map.164 = (bf16[8,128,128]{2,1,0:T(8,128)(2,1)}, bf16[16,128]{1,0:T(8,128)(2,1)}) custom-call(bf16[1040,128]{1,0:T(8,128)(2,1)} %get-tuple-element.57.own, bf16[1040,128]{1,0:T(8,128)(2,1)} %copy-done.5), custom_call_target="tpu_custom_call" | custom-call | tf_op jit(solution)/shard_map/pallas_call | solution.py:432
  97.7 6.0 %all-to-all-start.3 = ((bf16[8,128,128]{2,1,0:T(8,128)(2,1)}), bf16[8,128,128]{2,1,0:T(8,128)(2,1)S(1)}, u32[]{:S(2)}, u32[]{:S(2)}) async-start(bf16[8,128,128]{2,1,0:T(8,128)(2,1)} %get-tuple-element.61), calls=%async_computation.3 | async-start | bytes 524288 | tf_op jit(solution)/shard_map/all_to_all | solution.py:468
  103.7 1.7 %collective-permute-done.5.other = bf16[1024,128]{1,0:T(8,128)(2,1)S(1)} collective-permute-done((bf16[1024,128]{1,0:T(8,128)(2,1)}, bf16[1024,128]{1,0:T(8,128)(2,1)S(1)}, u32[]{:S(2)}, u32[]{:S(2)}) %collective-permute-start.5) | collective-permute-done | bytes 262176 | tf_op jit(solution)/shard_map/ppermute | solution.py:465
  106.1 2.5 %shard_map.166 = (bf16[8,400,128]{2,1,0:T(8,128)(2,1)}, bf16[16,128]{1,0:T(8,128)(2,1)}) custom-call(s32[1]{0:T(128)} %bitcast.2.core, s32[2,9]{1,0:T(2,128)} %get-tuple-element.46.marks, bf16[1024,128]{1,0:T(8,128)(2,1)} %get-tuple-element.62.own, bf16[1024,128]{1,0:T(8,128)(2,1)} %copy-done.6, bf16[8,272,128]{2,1,0:T(8,128)(2,1)} %copy-done.1, ...), custom_call_target="tpu_custom_call" | custom-call | tf_op jit(solution)/shard_map/pallas_call | solution.py:432
  108.6 4.3 %all-to-all-done.3.got = bf16[8,128,128]{2,1,0:T(8,128)(2,1)S(1)} async-done(((bf16[8,128,128]{2,1,0:T(8,128)(2,1)}), bf16[8,128,128]{2,1,0:T(8,128)(2,1)S(1)}, u32[]{:S(2)}, u32[]{:S(2)}) %all-to-all-start.3) | async-done | bytes 262176 | tf_op jit(solution)/shard_map/all_to_all | solution.py:468
  113.6 1.8 %share.1 = bf16[8,400,128]{2,1,0:T(8,128)(2,1)} custom-call(bf16[8,128,128]{2,1,0:T(8,128)(2,1)} %copy-done.3, bf16[16,128]{1,0:T(8,128)(2,1)} %get-tuple-element.65.extra, bf16[8,400,128]{2,1,0:T(8,128)(2,1)} %get-tuple-element.66.packed), custom_call_target="tpu_custom_call", output_to_operand_aliasing={{}: (2, {})} | custom-call | tf_op jit(solution)/shard_map/share/pallas_call | solution.py:567
  115.4 3.6 %all-to-all-start.4 = ((bf16[8,400,128]{2,1,0:T(8,128)(2,1)}), bf16[8,400,128]{2,1,0:T(8,128)(2,1)S(1)}, u32[]{:S(2)}, u32[]{:S(2)}) async-start(bf16[8,400,128]{2,1,0:T(8,128)(2,1)} %share.1), calls=%async_computation.4 | async-start | bytes 1638400 | tf_op jit(solution)/shard_map/all_to_all | solution.py:468
  119.0 2.5 %shard_map.165 = bf16[1024,128]{1,0:T(8,128)(2,1)} custom-call(s32[1,1024]{1,0:T(1,128)} %get-tuple-element.41.target_ref, bf16[8,256,128]{2,1,0:T(8,128)(2,1)} %copy-done.2), custom_call_target="tpu_custom_call" | custom-call | tf_op jit(solution)/shard_map/pallas_call | solution.py:432
  121.5 18.1 %all-to-all-done.4.got = bf16[8,400,128]{2,1,0:T(8,128)(2,1)S(1)} async-done(((bf16[8,400,128]{2,1,0:T(8,128)(2,1)}), bf16[8,400,128]{2,1,0:T(8,128)(2,1)S(1)}, u32[]{:S(2)}, u32[]{:S(2)}) %all-to-all-start.4) | async-done | bytes 819232 | tf_op jit(solution)/shard_map/all_to_all | solution.py:468
  139.6 0.9 copy-done
  140.5 2.8 %shard_map.167 = (bf16[1024,128]{1,0:T(8,128)(2,1)}, f32[256,128]{1,0:T(8,128)}, f32[256,128]{1,0:T(8,128)}, f32[256,128]{1,0:T(8,128)}, f32[128,256]{1,0:T(8,12...) custom-call(s32[1,1024]{1,0:T(1,128)} %get-tuple-element.41.target_ref, bf16[8,400,128]{2,1,0:T(8,128)(2,1)} %copy-done), custom_call_target="tpu_custom_call" | custom-call | tf_op jit(solution)/shard_map/pallas_call | solution.py:432
  (30 shorter events, 5.2 us)
Async XLA Ops:
  3.5 22.5 %all-to-all-start = ((bf16[8,272,128]{2,1,0:T(8,128)(2,1)}), bf16[8,272,128]{2,1,0:T(8,128)(2,1)S(1)}, u32[]{:S(2)}, u32[]{:S(2)}) async-start(bf16[8,272,128]{2,1,0:T(8,128)(2,1)} %get-tuple-element.42), calls=%async_computation | async-start | bytes 1114112 | tf_op jit(solution)/shard_map/all_to_all | solution.py:468
  26.0 19.1 %copy-start.4 = (bf16[8,272,128]{2,1,0:T(8,128)(2,1)}, bf16[8,272,128]{2,1,0:T(8,128)(2,1)S(1)}, u32[]{:S(2)}) copy-start(bf16[8,272,128]{2,1,0:T(8,128)(2,1)S(1)} %all-to-all-done.got) | copy-start | bytes 1671172
  26.0 19.0 %all-to-all-start.1 = ((bf16[8,272,128]{2,1,0:T(8,128)(2,1)}), bf16[8,272,128]{2,1,0:T(8,128)(2,1)S(1)}, u32[]{:S(2)}, u32[]{:S(2)}) async-start(bf16[8,272,128]{2,1,0:T(8,128)(2,1)} %shard_map.162), calls=%async_computation.1 | async-start | bytes 1114112 | tf_op jit(solution)/shard_map/all_to_all | solution.py:468
  29.6 15.4 %collective-permute-start = (bf16[8,272,128]{2,1,0:T(8,128)(2,1)S(1)}, bf16[8,272,128]{2,1,0:T(8,128)(2,1)S(1)}, u32[]{:S(2)}, u32[]{:S(2)}) collective-permute-start(bf16[8,272,128]{2,1,0:T(8,128)(2,1)S(1)} %all-to-all-done.got), channel_id=1, source_target_pairs={{0,1},{1,0},{2,3},{3,2},{4,5},{5,4},{6,7},{7,6},{8,9},{9,8},{10,11... | collective-permute-start | bytes 1671176 | tf_op jit(solution)/shard_map/ppermute | solution.py:465
  29.7 15.3 %collective-permute-start.1 = (bf16[4,256,128]{2,1,0:T(8,128)(2,1)}, bf16[4,256,128]{2,1,0:T(8,128)(2,1)S(1)}, u32[]{:S(2)}, u32[]{:S(2)}) collective-permute-start(bf16[4,256,128]{2,1,0:T(8,128)(2,1)} %get-tuple-element.45.w_own), channel_id=1, source_target_pairs={{0,1},{1,0},{2,3},{3,2},{4,5},{5,4},{6,7},{7,6},{8,9},{9,8},{10,11... | collective-permute-start | bytes 786440 | tf_op jit(solution)/shard_map/ppermute | solution.py:465
  45.0 23.2 %copy-start.1 = (bf16[8,272,128]{2,1,0:T(8,128)(2,1)}, bf16[8,272,128]{2,1,0:T(8,128)(2,1)S(1)}, u32[]{:S(2)}) copy-start(bf16[8,272,128]{2,1,0:T(8,128)(2,1)S(1)} %all-to-all-done.1.got.tagged) | copy-start | bytes 1671172
  45.0 26.8 %collective-permute-start.3 = (bf16[8,272,128]{2,1,0:T(8,128)(2,1)S(1)}, bf16[8,272,128]{2,1,0:T(8,128)(2,1)S(1)}, u32[]{:S(2)}, u32[]{:S(2)}) collective-permute-start(bf16[8,272,128]{2,1,0:T(8,128)(2,1)S(1)} %all-to-all-done.1.got.tagged), channel_id=1, source_target_pairs={{0,1},{1,0},{2,3},{3,2},{4,5},{5,4},{6,7},{7,6},{8,9},{9,8},{10,11... | collective-permute-start | bytes 1671176 | tf_op jit(solution)/shard_map/ppermute | solution.py:465
  45.0 0.7 copy-start.10
  45.0 0.9 copy-start.9
  63.4 1.9 %collective-permute-start.2 = (bf16[1024,128]{1,0:T(8,128)(2,1)}, bf16[1024,128]{1,0:T(8,128)(2,1)S(1)}, u32[]{:S(2)}, u32[]{:S(2)}) collective-permute-start(bf16[1024,128]{1,0:T(8,128)(2,1)} %get-tuple-element.48), channel_id=1, source_target_pairs={{0,1},{1,0},{2,3},{3,2},{4,5},{5,4},{6,7},{7,6},{8,9},{9,8},{10,11... | collective-permute-start | bytes 786440 | tf_op jit(solution)/shard_map/ppermute | solution.py:465
  65.2 0.7 copy-start.7
  68.2 29.5 %all-to-all-start.2 = ((bf16[8,256,128]{2,1,0:T(8,128)(2,1)}), bf16[8,256,128]{2,1,0:T(8,128)(2,1)S(1)}, u32[]{:S(2)}, u32[]{:S(2)}) async-start(bf16[8,256,128]{2,1,0:T(8,128)(2,1)} %shard_map.163), calls=%async_computation.2 | async-start | bytes 1048576 | tf_op jit(solution)/shard_map/all_to_all | solution.py:468
  71.9 0.8 copy-start.8
  93.4 1.8 %collective-permute-start.4 = (bf16[1040,128]{1,0:T(8,128)(2,1)}, bf16[1040,128]{1,0:T(8,128)(2,1)S(1)}, u32[]{:S(2)}, u32[]{:S(2)}) collective-permute-start(bf16[1040,128]{1,0:T(8,128)(2,1)} %get-tuple-element.58), channel_id=1, source_target_pairs={{0,1},{1,0},{2,3},{3,2},{4,5},{5,4},{6,7},{7,6},{8,9},{9,8},{10,11... | collective-permute-start | bytes 798728 | tf_op jit(solution)/shard_map/ppermute | solution.py:465
  95.2 0.7 copy-start.5
  97.7 21.3 %copy-start.2 = (bf16[8,256,128]{2,1,0:T(8,128)(2,1)}, bf16[8,256,128]{2,1,0:T(8,128)(2,1)S(1)}, u32[]{:S(2)}) copy-start(bf16[8,256,128]{2,1,0:T(8,128)(2,1)S(1)} %all-to-all-done.2.got) | copy-start | bytes 1572868
  97.7 15.2 %all-to-all-start.3 = ((bf16[8,128,128]{2,1,0:T(8,128)(2,1)}), bf16[8,128,128]{2,1,0:T(8,128)(2,1)S(1)}, u32[]{:S(2)}, u32[]{:S(2)}) async-start(bf16[8,128,128]{2,1,0:T(8,128)(2,1)} %get-tuple-element.61), calls=%async_computation.3 | async-start | bytes 524288 | tf_op jit(solution)/shard_map/all_to_all | solution.py:468
  103.7 1.7 %collective-permute-start.5 = (bf16[1024,128]{1,0:T(8,128)(2,1)}, bf16[1024,128]{1,0:T(8,128)(2,1)S(1)}, u32[]{:S(2)}, u32[]{:S(2)}) collective-permute-start(bf16[1024,128]{1,0:T(8,128)(2,1)} %get-tuple-element.63), channel_id=1, source_target_pairs={{0,1},{1,0},{2,3},{3,2},{4,5},{5,4},{6,7},{7,6},{8,9},{9,8},{10,11... | collective-permute-start | bytes 786440 | tf_op jit(solution)/shard_map/ppermute | solution.py:465
  105.4 0.7 copy-start.6
  112.9 0.7 copy-start.3
  115.4 24.2 %all-to-all-start.4 = ((bf16[8,400,128]{2,1,0:T(8,128)(2,1)}), bf16[8,400,128]{2,1,0:T(8,128)(2,1)S(1)}, u32[]{:S(2)}, u32[]{:S(2)}) async-start(bf16[8,400,128]{2,1,0:T(8,128)(2,1)} %share.1), calls=%async_computation.4 | async-start | bytes 1638400 | tf_op jit(solution)/shard_map/all_to_all | solution.py:468
  139.6 0.9 copy-start

commit v8 on v7

--- a/solution.py
+++ b/solution.py
@@ -91,14 +91,18 @@
     return mm(chosen, jnp.concatenate(masked, axis=1)).astype(BF16)
 
 
-def pack_kernel(regions, capacity, cells, kinds, feats, embed, w_q, w_k, w_v, w_o, out_base, out_target, out_w):
+def pack_kernel(regions, capacity, cells, kinds, embed, feats_far, out_target, out_far, feats, out_base, sem, sems):
     count, half = feats.shape
+    arrive = pltpu.make_async_copy(feats_far, feats, sem)
+    arrive.start()
     owner, place, counts = positions(regions, capacity, cells[...])
     out_target[...] = owner * capacity + place
     kinds_hot = hot(iota((KINDS, count), 0) == kinds[...])
+    arrive.wait()
     base = (feats[...].astype(F32) + mm_tn(kinds_hot, embed[...])).astype(BF16)
     owner_column = turned(owner)
     tag_place = iota((TAG_ROWS, half), 0)
+    copies = []
     for r in range(0, regions, 2):
         moved = to_chunks(capacity, place, owner_column, base, r, 2)
         for k in range(2):
@@ -108,15 +112,19 @@
             second = counts[pair + 1 : pair + 2]
             tags = jnp.where(tag_place == 0, first, jnp.where(tag_place == 1, second, 0.0))
             out_base[r + k, capacity : capacity + TAG_ROWS, :] = tags.astype(BF16)
+        copies.append(pltpu.make_async_copy(out_base.at[pl.ds(r, 2)], out_far.at[pl.ds(r, 2)], sems.at[r // 2]))
+        copies[-1].start()
+    for copy in copies:
+        copy.wait()
+
+
+def pack_cot_kernel(regions, capacity, target_ref, kinds, cot, w_q, w_k, w_v, w_o, out_cot, out_w):
+    count, half = cot.shape
     out_w[0] = w_q[...]
     out_w[1] = w_k[...]
     out_w[2] = w_v[...]
     out_w[3, 0:half, :] = w_o[:, 0:half]
     out_w[3, half:, :] = w_o[:, half:]
-
-
-def pack_cot_kernel(regions, capacity, target_ref, kinds, cot, out_cot):
-    count, half = cot.shape
     target = target_ref[...]
     owner = lax.shift_right_logical(target, log2_of(capacity))
     place = jnp.bitwise_and(target, capacity - 1)
@@ -167,7 +175,7 @@
     return jnp.where(filled > 0.5, rows, 0.0).astype(BF16)
 
 
-def arrival_rows(regions, capacity, core, marks, own, other, out, front, back):
+def arrival_rows(regions, capacity, core, marks, own, other, out, far, sems, front, back):
     flag = core[0] > 0
     x = own[...].astype(F32)
     y = other[...].astype(F32)
@@ -179,15 +187,22 @@
     for r in range(regions):
         held = marks[0, r + 1] - marks[0, r]
         rows = jnp.where(row < held, front[pl.ds(marks[0, r], capacity), :], back[pl.ds(marks[1, r], capacity), :])
-        out[r, 0:capacity, :] = rows.astype(BF16)
-
-
-def ungroup_kernel(regions, capacity, core, marks, own, other, out, front, back):
-    arrival_rows(regions, capacity, core, marks, own, other, out, front, back)
-
-
-def ungroup_grad_kernel(regions, capacity, core, marks, own, other, tagged, gain_part, out, extra, front, back):
-    arrival_rows(regions, capacity, core, marks, own, other, out, front, back)
+        out[r] = rows.astype(BF16)
+        pltpu.make_async_copy(out.at[r], far.at[r, pl.ds(0, capacity), :], sems.at[r]).start()
+
+
+def finish_rows(regions, capacity, out, far, sems):
+    for r in range(regions):
+        pltpu.make_async_copy(out.at[r], far.at[r, pl.ds(0, capacity), :], sems.at[r]).wait()
+
+
+def ungroup_kernel(regions, capacity, core, marks, own, other, far, out, sems, front, back):
+    arrival_rows(regions, capacity, core, marks, own, other, out, far, sems, front, back)
+    finish_rows(regions, capacity, out, far, sems)
+
+
+def ungroup_grad_kernel(regions, capacity, core, marks, own, other, tagged, gain_part, extra, far, out, sems, front, back):
+    arrival_rows(regions, capacity, core, marks, own, other, out, far, sems, front, back)
     total = jnp.zeros((KIND_ROWS, own.shape[1]), F32)
     for r in range(regions):
         block = tagged[r, capacity : capacity + TAG_ROWS, :].astype(F32)
@@ -196,11 +211,12 @@
         else:
             kind = block[0:1, 0:capacity]
         kinds_hot = hot(iota((KIND_ROWS, capacity), 0) == kind.astype(I32) - 1)
-        total = total + mm(kinds_hot, out[r, 0:capacity, :])
+        total = total + mm(kinds_hot, out[r])
     place = iota((KIND_ROWS, 1), 0)
     first = gain_part[0:1, :].astype(F32)
     second = gain_part[1:2, :].astype(F32)
     extra[...] = jnp.where(place == KINDS, first, jnp.where(place == KINDS + 1, second, total)).astype(BF16)
+    finish_rows(regions, capacity, out, far, sems)
 
 
 def pair_kernel(regions, own, received, out, gain_part):
@@ -227,23 +243,38 @@
         copy.wait()
 
 
-def last_kernel(regions, capacity, factor, target_ref, got, out, out_q, out_k, out_v, out_o, out_gain, out_embed, flat):
-    pick_kernel(target_ref, got, out)
-    width, half = out_q.shape
+def last_kernel(
+    regions, capacity, factor, target_ref, far, out_gain, out_embed, out_q, out_k, out_v, out_o, out_feats,
+    got, sums, sums_o, feats, sems, out_sems
+):
+    _, half = feats.shape
+    width = 2 * half
+    for r in range(regions):
+        pltpu.make_async_copy(far.at[r], got.at[r], sems.at[r]).start()
     share = 4 * width // regions
     extra = jnp.zeros((KIND_ROWS, half), F32)
     for r in range(regions):
-        flat[r * share : (r + 1) * share, :] = got[r, capacity : capacity + share, :].astype(F32) * factor
+        pltpu.make_async_copy(far.at[r], got.at[r], sems.at[r]).wait()
+        sums[r * share : (r + 1) * share, :] = got[r, capacity : capacity + share, :].astype(F32) * factor
         extra = extra + got[r, capacity + share : capacity + share + KIND_ROWS, :].astype(F32)
+    sums_o[:, 0:half] = sums[3 * width : 3 * width + half]
+    sums_o[:, half:] = sums[3 * width + half : 4 * width]
+    copies = [
+        pltpu.make_async_copy(sums.at[pl.ds(k * width, width)], far_out, out_sems.at[k])
+        for k, far_out in enumerate((out_q, out_k, out_v))
+    ]
+    copies.append(pltpu.make_async_copy(sums_o, out_o, out_sems.at[3]))
+    for copy in copies:
+        copy.start()
     extra = extra * factor
-    out_q[...] = flat[0:width]
-    out_k[...] = flat[width : 2 * width]
-    out_v[...] = flat[2 * width : 3 * width]
-    out_o[:, 0:half] = flat[3 * width : 3 * width + half]
-    out_o[:, half:] = flat[3 * width + half : 4 * width]
     out_embed[...] = extra[0:KINDS]
     out_gain[:, 0:half] = extra[KINDS : KINDS + 1]
     out_gain[:, half:] = extra[KINDS + 1 : KINDS + 2]
+    pick_kernel(target_ref, got, feats)
+    copies.append(pltpu.make_async_copy(feats, out_feats, out_sems.at[4]))
+    copies[-1].start()
+    for copy in copies:
+        copy.wait()
 
 
 def pick_kernel(target_ref, got, out):
@@ -427,13 +458,16 @@
     return pl.BlockSpec(tuple(array.shape), lambda *_: zeros)
 
 
-def simple_call(kernel, outs, inputs, scratch=(), scalars=0, scalar_outs=0):
-    specs = [SMEM_SPEC] * scalars + [whole(x) for x in inputs[scalars:]]
+FAR_SPEC = pl.BlockSpec(memory_space=pl.ANY)
+
+
+def simple_call(kernel, outs, inputs, scratch=(), scalars=0, far=0, far_outs=0):
+    near = inputs[scalars : len(inputs) - far]
     return pl.pallas_call(
         kernel,
         out_shape=outs,
-        in_specs=specs,
-        out_specs=tuple(whole(x) for x in outs[: len(outs) - scalar_outs]) + (SMEM_SPEC,) * scalar_outs,
+        in_specs=[SMEM_SPEC] * scalars + [whole(x) for x in near] + [FAR_SPEC] * far,
+        out_specs=tuple(whole(x) for x in outs[: len(outs) - far_outs]) + (FAR_SPEC,) * far_outs,
         scratch_shapes=scratch,
     )(*inputs)
 
@@ -471,16 +505,26 @@
     kinds_row = element_kinds.reshape(1, count)
     packed_shape = shape((regions, capacity, half), BF16)
     tagged_shape = shape((regions, capacity + TAG_ROWS, half), BF16)
-    packed_base, target, w_own = simple_call(
+    target, packed_base = simple_call(
         functools.partial(pack_kernel, regions, capacity),
-        (tagged_shape, shape((1, count), I32), shape((4, width, half), BF16)),
-        (bin_cells.reshape(1, count), kinds_row, features, kind_embed, w_query, w_key, w_value, w_out),
+        (shape((1, count), I32), tagged_shape),
+        (bin_cells.reshape(1, count), kinds_row, kind_embed, features),
+        scratch=(
+            pltpu.VMEM((count, half), BF16),
+            pltpu.VMEM(tagged_shape.shape, BF16),
+            pltpu.SemaphoreType.DMA(()),
+            pltpu.SemaphoreType.DMA((regions // 2,)),
+        ),
+        far=1,
+        far_outs=1,
+    )
+    got_base = exchange(packed_base)
+    packed_cot, w_own = simple_call(
+        functools.partial(pack_cot_kernel, regions, capacity),
+        (tagged_shape, shape((4, width, half), BF16)),
+        (target, kinds_row, cotangent, w_query, w_key, w_value, w_out),
     )
     w_other = other_core(w_own)
-    got_base = exchange(packed_base)
-    (packed_cot,) = simple_call(
-        functools.partial(pack_cot_kernel, regions, capacity), (tagged_shape,), (target, kinds_row, cotangent)
-    )
     got_base, packed_cot = lax.optimization_barrier((got_base, packed_cot))
     got_cot = exchange(packed_cot)
     got_base_other = other_core(got_base)
@@ -519,8 +563,9 @@
         functools.partial(ungroup_kernel, regions, capacity),
         (packed_shape,),
         (core, marks, attn_keep, attn_other),
-        scratch=(lift, lift),
+        scratch=(pltpu.VMEM(packed_shape.shape, BF16), pltpu.SemaphoreType.DMA((regions,)), lift, lift),
         scalars=2,
+        far_outs=1,
     )
 
     got_cot_other = other_core(got_cot)
@@ -553,12 +598,13 @@
         (grad_keep, other_core(grad_send)),
     )
     payload_shape = shape((regions, capacity + share + KIND_ROWS, half), BF16)
-    packed_grad, extra = simple_call(
+    extra, packed_grad = simple_call(
         functools.partial(ungroup_grad_kernel, regions, capacity),
-        (payload_shape, shape((KIND_ROWS, half), BF16)),
+        (shape((KIND_ROWS, half), BF16), payload_shape),
         (core, marks, d_keep, other_core(d_send), got_cot, gain_part),
-        scratch=(lift, lift),
+        scratch=(pltpu.VMEM(packed_shape.shape, BF16), pltpu.SemaphoreType.DMA((regions,)), lift, lift),
         scalars=2,
+        far_outs=1,
     )
     got_cot, packed_attn = lax.optimization_barrier((got_cot, packed_attn))
     home_attn = exchange(packed_attn)
@@ -576,19 +622,28 @@
     home_grad = exchange(payload)
     (attended,) = simple_call(pick_kernel, (shape((count, half), BF16),), (target, home_attn))
     column_shape = shape((width, half), F32)
-    grad_feats, grad_q, grad_k, grad_v, grad_o, grad_gain, grad_embed = simple_call(
+    grad_gain, grad_embed, grad_q, grad_k, grad_v, grad_o, grad_feats = simple_call(
         functools.partial(last_kernel, regions, capacity, float(count * regions) ** (-0.5)),
         (
-            shape((count, half), BF16),
+            shape((1, width), F32),
+            shape((KINDS, half), F32),
             column_shape,
             column_shape,
             column_shape,
             shape((half, width), F32),
-            shape((1, width), F32),
-            shape((KINDS, half), F32),
+            shape((count, half), BF16),
         ),
         (target, home_grad),
-        scratch=(pltpu.VMEM((4 * width, half), F32),),
+        scratch=(
+            pltpu.VMEM(payload_shape.shape, BF16),
+            pltpu.VMEM((4 * width, half), F32),
+            pltpu.VMEM((half, width), F32),
+            pltpu.VMEM((count, half), BF16),
+            pltpu.SemaphoreType.DMA((regions,)),
+            pltpu.SemaphoreType.DMA((5,)),
+        ),
+        far=1,
+        far_outs=5,
     )
     return (attended, grad_feats, grad_q, grad_k, grad_v, grad_o, grad_gain.reshape(width), grad_embed)
 

time: 144 us -> 147 us (1.021)
  Pallas kernels: 58.2 us -> 61.1 us
    pallas_call x7, Pallas kernels: 18.3 us -> 21.2 us  [simple_call(): pl.pallas_call(kernel, out_shape=outs, in_specs=[SMEM_SPEC] * scalars + [...]
where the time goes in v8:
time: 147 us; the launch traced here: 146 us
  Pallas kernels  61.1 us (42%)
  waiting for transfers between devices  52.8 us (36%)
  starting transfers between devices  25.6 us (17%)
  local copies, waits for them, and re-layouts  5.5 us (4%)
    all_to_all x5, waiting for transfers between devices, exchange(): return lax.all_to_all(x, 'region', split_axis=0, concat_axis=0, tiled=True)  48.3 us
    all_to_all x5, starting transfers between devices, exchange(): return lax.all_to_all(x, 'region', split_axis=0, concat_axis=0, tiled=True)  24.2 us
    pallas_call x7, Pallas kernels, simple_call(): pl.pallas_call(kernel, out_shape=outs, in_specs=[SMEM_SPEC] * scalars + [...  21.2 us
    pallas_call x1, Pallas kernels, on_device(): pl.pallas_call(functools.partial(backward_kernel, heads, regions, capacit...  20.8 us
    pallas_call x1, Pallas kernels, on_device(): pl.pallas_call(functools.partial(forward_kernel, heads, regions, capacity...  17.4 us
    unnamed x22, local copies, waits for them, and re-layouts  5.5 us
    ppermute x6, waiting for transfers between devices, other_core(): return lax.ppermute(x, 'head', swap)  4.5 us
  transfers between devices with their start and end apart: 11, of which 7 were waited for; matrix products, arithmetic and copies ran while one was open for 0% of the time, Pallas kernels for 35%

profile of v8, /device:TPU:0, one launch (start us, length us, event | category | flops | bytes accessed | tf_op | source)
XLA Modules:
  0.0 145.9 jit_solution(9602947360318328603)
XLA Ops:
  0.6 3.9 %shard_map.161 = (s32[1,1024]{1,0:T(1,128)}, bf16[8,272,128]{2,1,0:T(8,128)(2,1)}) custom-call(s32[1,1024]{1,0:T(1,128)} %bitcast.7, s32[1,1024]{1,0:T(1,128)} %bitcast.5, bf16[12,128]{1,0:T(8,128)(2,1)} %embed.1, bf16[1024,128]{1,0:T(8,128)(2,1)} %feats_far.1), custom_call_target="tpu_custom_call" | custom-call | tf_op jit(solution)/shard_map/pallas_call | solution.py:466
  4.6 7.3 %all-to-all-start = ((bf16[8,272,128]{2,1,0:T(8,128)(2,1)}), bf16[8,272,128]{2,1,0:T(8,128)(2,1)S(1)}, u32[]{:S(2)}, u32[]{:S(2)}) async-start(bf16[8,272,128]{2,1,0:T(8,128)(2,1)} %get-tuple-element.43), calls=%async_computation | async-start | bytes 1114112 | tf_op jit(solution)/shard_map/all_to_all | solution.py:502
  11.9 3.7 %shard_map.162 = (bf16[8,272,128]{2,1,0:T(8,128)(2,1)}, bf16[4,256,128]{2,1,0:T(8,128)(2,1)}) custom-call(s32[1,1024]{1,0:T(1,128)} %get-tuple-element.42.target_ref, s32[1,1024]{1,0:T(1,128)} %bitcast.6, bf16[1024,128]{1,0:T(8,128)(2,1)} %cot.1, bf16[256,128]{1,0:T(8,128)(2,1)} %w_q.1, bf16[256,128]{1,0:T(8,128)(2,1)} %w_k.1, bf16[256,128]{1,0:T(8,128)(2,1)} %w_v.1, ...), custom_call_target="tpu_custom_call" | custom-call | tf_op jit(solution)/shard_map/pallas_call | solution.py:466
  15.6 11.5 %all-to-all-done.got = bf16[8,272,128]{2,1,0:T(8,128)(2,1)S(1)} async-done(((bf16[8,272,128]{2,1,0:T(8,128)(2,1)}), bf16[8,272,128]{2,1,0:T(8,128)(2,1)S(1)}, u32[]{:S(2)}, u32[]{:S(2)}) %all-to-all-start) | async-done | bytes 557088 | tf_op jit(solution)/shard_map/all_to_all | solution.py:502
  27.1 3.6 %all-to-all-start.1 = ((bf16[8,272,128]{2,1,0:T(8,128)(2,1)}), bf16[8,272,128]{2,1,0:T(8,128)(2,1)S(1)}, u32[]{:S(2)}, u32[]{:S(2)}) async-start(bf16[8,272,128]{2,1,0:T(8,128)(2,1)} %get-tuple-element.45), calls=%async_computation.1 | async-start | bytes 1114112 | tf_op jit(solution)/shard_map/all_to_all | solution.py:502
  31.3 14.8 %all-to-all-done.1.got.tagged = bf16[8,272,128]{2,1,0:T(8,128)(2,1)S(1)} async-done(((bf16[8,272,128]{2,1,0:T(8,128)(2,1)}), bf16[8,272,128]{2,1,0:T(8,128)(2,1)S(1)}, u32[]{:S(2)}, u32[]{:S(2)}) %all-to-all-start.1) | async-done | bytes 557088 | tf_op jit(solution)/shard_map/all_to_all | solution.py:502
  47.1 17.4 %forward.1 = (bf16[1024,256]{1,0:T(8,128)(2,1)}, bf16[256,1024]{1,0:T(8,128)(2,1)}, bf16[1024,256]{1,0:T(8,128)(2,1)}, bf16[256,1024]{1,0:T(8,128)(2,1)}, bf16[8...) custom-call(s32[1]{0:T(128)} %bitcast.2.core, ...), custom_call_target="tpu_custom_call" | custom-call | flops 8589934592 | bytes 16777216 | tf_op jit(solution)/shard_map/forward/pallas_call | solution.py:551
  65.0 1.4 collective-permute-done.2.other
  67.1 2.1 %shard_map.163 = bf16[8,256,128]{2,1,0:T(8,128)(2,1)} custom-call(s32[1]{0:T(128)} %bitcast.2.core, s32[2,9]{1,0:T(2,128)} %get-tuple-element.48.marks, bf16[1024,128]{1,0:T(8,128)(2,1)} %get-tuple-element.49.own, bf16[1024,128]{1,0:T(8,128)(2,1)} %copy-done.7), custom_call_target="tpu_custom_call" | custom-call | tf_op jit(solution)/shard_map/pallas_call | solution.py:466
  69.2 3.7 %all-to-all-start.2 = ((bf16[8,256,128]{2,1,0:T(8,128)(2,1)}), bf16[8,256,128]{2,1,0:T(8,128)(2,1)S(1)}, u32[]{:S(2)}, u32[]{:S(2)}) async-start(bf16[8,256,128]{2,1,0:T(8,128)(2,1)} %shard_map.163), calls=%async_computation.2 | async-start | bytes 1048576 | tf_op jit(solution)/shard_map/all_to_all | solution.py:502
  72.9 0.8 copy-done.8
  73.7 20.8 %backward.1 = (bf16[1024,128]{1,0:T(8,128)(2,1)}, bf16[1024,128]{1,0:T(8,128)(2,1)}, bf16[1040,128]{1,0:T(8,128)(2,1)}, bf16[1040,128]{1,0:T(8,128)(2,1)}) custom-call(s32[1]{0:T(128)} %bitcast.2.core, s32[2,9]{1,0:T(2,128)} %get-tuple-element.48.marks, bf16[1024,256]{1,0:T(8,128)(2,1)} %get-tuple-element.52.slab_in, bf16[8,272,128]{2,1,0:T(8,128)(2,1)} %copy-done.1, ...), custom_call_target="tpu_custom_call" | custom-call | flops 17179869184 | bytes 16777216 | tf_op jit(solution)/shard_map/backward/pallas_call | solution.py:575
  94.8 1.4 collective-permute-done.4.received
  96.9 1.8 %shard_map.164 = (bf16[8,128,128]{2,1,0:T(8,128)(2,1)}, bf16[16,128]{1,0:T(8,128)(2,1)}) custom-call(bf16[1040,128]{1,0:T(8,128)(2,1)} %get-tuple-element.59.own, bf16[1040,128]{1,0:T(8,128)(2,1)} %copy-done.5), custom_call_target="tpu_custom_call" | custom-call | tf_op jit(solution)/shard_map/pallas_call | solution.py:466
  98.7 6.0 %all-to-all-start.3 = ((bf16[8,128,128]{2,1,0:T(8,128)(2,1)}), bf16[8,128,128]{2,1,0:T(8,128)(2,1)S(1)}, u32[]{:S(2)}, u32[]{:S(2)}) async-start(bf16[8,128,128]{2,1,0:T(8,128)(2,1)} %get-tuple-element.63), calls=%async_computation.3 | async-start | bytes 524288 | tf_op jit(solution)/shard_map/all_to_all | solution.py:502
  104.7 1.7 %collective-permute-done.5.other = bf16[1024,128]{1,0:T(8,128)(2,1)S(1)} collective-permute-done((bf16[1024,128]{1,0:T(8,128)(2,1)}, bf16[1024,128]{1,0:T(8,128)(2,1)S(1)}, u32[]{:S(2)}, u32[]{:S(2)}) %collective-permute-start.5) | collective-permute-done | bytes 262176 | tf_op jit(solution)/shard_map/ppermute | solution.py:499
  107.2 2.9 %shard_map.166 = (bf16[16,128]{1,0:T(8,128)(2,1)}, bf16[8,400,128]{2,1,0:T(8,128)(2,1)}) custom-call(s32[1]{0:T(128)} %bitcast.2.core, s32[2,9]{1,0:T(2,128)} %get-tuple-element.48.marks, bf16[1024,128]{1,0:T(8,128)(2,1)} %get-tuple-element.64.own, bf16[1024,128]{1,0:T(8,128)(2,1)} %copy-done.6, bf16[8,272,128]{2,1,0:T(8,128)(2,1)} %copy-done.1, ...), custom_call_target="tpu_custom_call" | custom-call | tf_op jit(solution)/shard_map/pallas_call | solution.py:466
  110.1 3.8 %all-to-all-done.3.got = bf16[8,128,128]{2,1,0:T(8,128)(2,1)S(1)} async-done(((bf16[8,128,128]{2,1,0:T(8,128)(2,1)}), bf16[8,128,128]{2,1,0:T(8,128)(2,1)S(1)}, u32[]{:S(2)}, u32[]{:S(2)}) %all-to-all-start.3) | async-done | bytes 262176 | tf_op jit(solution)/shard_map/all_to_all | solution.py:502
  114.6 1.8 %share.1 = bf16[8,400,128]{2,1,0:T(8,128)(2,1)} custom-call(bf16[8,128,128]{2,1,0:T(8,128)(2,1)} %copy-done.3, bf16[16,128]{1,0:T(8,128)(2,1)} %get-tuple-element.67.extra, bf16[8,400,128]{2,1,0:T(8,128)(2,1)} %get-tuple-element.68.packed), custom_call_target="tpu_custom_call", output_to_operand_aliasing={{}: (2, {})} | custom-call | tf_op jit(solution)/shard_map/share/pallas_call | solution.py:613
  116.4 3.6 %all-to-all-start.4 = ((bf16[8,400,128]{2,1,0:T(8,128)(2,1)}), bf16[8,400,128]{2,1,0:T(8,128)(2,1)S(1)}, u32[]{:S(2)}, u32[]{:S(2)}) async-start(bf16[8,400,128]{2,1,0:T(8,128)(2,1)} %share.1), calls=%async_computation.4 | async-start | bytes 1638400 | tf_op jit(solution)/shard_map/all_to_all | solution.py:502
  120.0 2.5 %shard_map.165 = bf16[1024,128]{1,0:T(8,128)(2,1)} custom-call(s32[1,1024]{1,0:T(1,128)} %get-tuple-element.42.target_ref, bf16[8,256,128]{2,1,0:T(8,128)(2,1)} %copy-done.2), custom_call_target="tpu_custom_call" | custom-call | tf_op jit(solution)/shard_map/pallas_call | solution.py:466
  122.5 18.1 %all-to-all-done.4.far = bf16[8,400,128]{2,1,0:T(8,128)(2,1)S(1)} async-done(((bf16[8,400,128]{2,1,0:T(8,128)(2,1)}), bf16[8,400,128]{2,1,0:T(8,128)(2,1)S(1)}, u32[]{:S(2)}, u32[]{:S(2)}) %all-to-all-start.4) | async-done | bytes 819232 | tf_op jit(solution)/shard_map/all_to_all | solution.py:502
  140.7 0.9 copy-done
  141.6 4.2 %shard_map.167 = (f32[1,256]{1,0:T(1,128)}, f32[12,128]{1,0:T(8,128)}, f32[256,128]{1,0:T(8,128)}, f32[256,128]{1,0:T(8,128)}, f32[256,128]{1,0:T(8,128)}, /*ind...) custom-call(s32[1,1024]{1,0:T(1,128)} %get-tuple-element.42.target_ref, bf16[8,400,128]{2,1,0:T(8,128)(2,1)} %copy-done), custom_call_target="tpu_custom_call" | custom-call | tf_op jit(solution)/shard_map/pallas_call | solution.py:466
  (30 shorter events, 5.2 us)
Async XLA Ops:
  4.6 22.5 %all-to-all-start = ((bf16[8,272,128]{2,1,0:T(8,128)(2,1)}), bf16[8,272,128]{2,1,0:T(8,128)(2,1)S(1)}, u32[]{:S(2)}, u32[]{:S(2)}) async-start(bf16[8,272,128]{2,1,0:T(8,128)(2,1)} %get-tuple-element.43), calls=%async_computation | async-start | bytes 1114112 | tf_op jit(solution)/shard_map/all_to_all | solution.py:502
  27.1 19.1 %copy-start.4 = (bf16[8,272,128]{2,1,0:T(8,128)(2,1)}, bf16[8,272,128]{2,1,0:T(8,128)(2,1)S(1)}, u32[]{:S(2)}) copy-start(bf16[8,272,128]{2,1,0:T(8,128)(2,1)S(1)} %all-to-all-done.got) | copy-start | bytes 1671172
  27.1 19.0 %all-to-all-start.1 = ((bf16[8,272,128]{2,1,0:T(8,128)(2,1)}), bf16[8,272,128]{2,1,0:T(8,128)(2,1)S(1)}, u32[]{:S(2)}, u32[]{:S(2)}) async-start(bf16[8,272,128]{2,1,0:T(8,128)(2,1)} %get-tuple-element.45), calls=%async_computation.1 | async-start | bytes 1114112 | tf_op jit(solution)/shard_map/all_to_all | solution.py:502
  30.7 15.4 %collective-permute-start = (bf16[8,272,128]{2,1,0:T(8,128)(2,1)S(1)}, bf16[8,272,128]{2,1,0:T(8,128)(2,1)S(1)}, u32[]{:S(2)}, u32[]{:S(2)}) collective-permute-start(bf16[8,272,128]{2,1,0:T(8,128)(2,1)S(1)} %all-to-all-done.got), channel_id=1, source_target_pairs={{0,1},{1,0},{2,3},{3,2},{4,5},{5,4},{6,7},{7,6},{8,9},{9,8},{10,11... | collective-permute-start | bytes 1671176 | tf_op jit(solution)/shard_map/ppermute | solution.py:499
  30.8 15.3 %collective-permute-start.1 = (bf16[4,256,128]{2,1,0:T(8,128)(2,1)}, bf16[4,256,128]{2,1,0:T(8,128)(2,1)S(1)}, u32[]{:S(2)}, u32[]{:S(2)}) collective-permute-start(bf16[4,256,128]{2,1,0:T(8,128)(2,1)} %get-tuple-element.47.w_own), channel_id=1, source_target_pairs={{0,1},{1,0},{2,3},{3,2},{4,5},{5,4},{6,7},{7,6},{8,9},{9,8},{10,11... | collective-permute-start | bytes 786440 | tf_op jit(solution)/shard_map/ppermute | solution.py:499
  46.1 23.1 %copy-start.1 = (bf16[8,272,128]{2,1,0:T(8,128)(2,1)}, bf16[8,272,128]{2,1,0:T(8,128)(2,1)S(1)}, u32[]{:S(2)}) copy-start(bf16[8,272,128]{2,1,0:T(8,128)(2,1)S(1)} %all-to-all-done.1.got.tagged) | copy-start | bytes 1671172
  46.1 26.8 %collective-permute-start.3 = (bf16[8,272,128]{2,1,0:T(8,128)(2,1)S(1)}, bf16[8,272,128]{2,1,0:T(8,128)(2,1)S(1)}, u32[]{:S(2)}, u32[]{:S(2)}) collective-permute-start(bf16[8,272,128]{2,1,0:T(8,128)(2,1)S(1)} %all-to-all-done.1.got.tagged), channel_id=1, source_target_pairs={{0,1},{1,0},{2,3},{3,2},{4,5},{5,4},{6,7},{7,6},{8,9},{9,8},{10,11... | collective-permute-start | bytes 1671176 | tf_op jit(solution)/shard_map/ppermute | solution.py:499
  46.1 0.7 copy-start.10
  46.1 1.0 copy-start.9
  64.5 1.9 %collective-permute-start.2 = (bf16[1024,128]{1,0:T(8,128)(2,1)}, bf16[1024,128]{1,0:T(8,128)(2,1)S(1)}, u32[]{:S(2)}, u32[]{:S(2)}) collective-permute-start(bf16[1024,128]{1,0:T(8,128)(2,1)} %get-tuple-element.50), channel_id=1, source_target_pairs={{0,1},{1,0},{2,3},{3,2},{4,5},{5,4},{6,7},{7,6},{8,9},{9,8},{10,11... | collective-permute-start | bytes 786440 | tf_op jit(solution)/shard_map/ppermute | solution.py:499
  66.3 0.7 copy-start.7
  69.2 29.5 %all-to-all-start.2 = ((bf16[8,256,128]{2,1,0:T(8,128)(2,1)}), bf16[8,256,128]{2,1,0:T(8,128)(2,1)S(1)}, u32[]{:S(2)}, u32[]{:S(2)}) async-start(bf16[8,256,128]{2,1,0:T(8,128)(2,1)} %shard_map.163), calls=%async_computation.2 | async-start | bytes 1048576 | tf_op jit(solution)/shard_map/all_to_all | solution.py:502
  72.9 0.8 copy-start.8
  94.5 1.8 %collective-permute-start.4 = (bf16[1040,128]{1,0:T(8,128)(2,1)}, bf16[1040,128]{1,0:T(8,128)(2,1)S(1)}, u32[]{:S(2)}, u32[]{:S(2)}) collective-permute-start(bf16[1040,128]{1,0:T(8,128)(2,1)} %get-tuple-element.60), channel_id=1, source_target_pairs={{0,1},{1,0},{2,3},{3,2},{4,5},{5,4},{6,7},{7,6},{8,9},{9,8},{10,11... | collective-permute-start | bytes 798728 | tf_op jit(solution)/shard_map/ppermute | solution.py:499
  96.2 0.7 copy-start.5
  98.7 21.3 %copy-start.2 = (bf16[8,256,128]{2,1,0:T(8,128)(2,1)}, bf16[8,256,128]{2,1,0:T(8,128)(2,1)S(1)}, u32[]{:S(2)}) copy-start(bf16[8,256,128]{2,1,0:T(8,128)(2,1)S(1)} %all-to-all-done.2.got) | copy-start | bytes 1572868
  98.7 15.2 %all-to-all-start.3 = ((bf16[8,128,128]{2,1,0:T(8,128)(2,1)}), bf16[8,128,128]{2,1,0:T(8,128)(2,1)S(1)}, u32[]{:S(2)}, u32[]{:S(2)}) async-start(bf16[8,128,128]{2,1,0:T(8,128)(2,1)} %get-tuple-element.63), calls=%async_computation.3 | async-start | bytes 524288 | tf_op jit(solution)/shard_map/all_to_all | solution.py:502
  104.7 1.7 %collective-permute-start.5 = (bf16[1024,128]{1,0:T(8,128)(2,1)}, bf16[1024,128]{1,0:T(8,128)(2,1)S(1)}, u32[]{:S(2)}, u32[]{:S(2)}) collective-permute-start(bf16[1024,128]{1,0:T(8,128)(2,1)} %get-tuple-element.65), channel_id=1, source_target_pairs={{0,1},{1,0},{2,3},{3,2},{4,5},{5,4},{6,7},{7,6},{8,9},{9,8},{10,11... | collective-permute-start | bytes 786440 | tf_op jit(solution)/shard_map/ppermute | solution.py:499
  106.5 0.7 copy-start.6
  113.9 0.7 copy-start.3
  116.4 24.2 %all-to-all-start.4 = ((bf16[8,400,128]{2,1,0:T(8,128)(2,1)}), bf16[8,400,128]{2,1,0:T(8,128)(2,1)S(1)}, u32[]{:S(2)}, u32[]{:S(2)}) async-start(bf16[8,400,128]{2,1,0:T(8,128)(2,1)} %share.1), calls=%async_computation.4 | async-start | bytes 1638400 | tf_op jit(solution)/shard_map/all_to_all | solution.py:502
  140.7 0.9 copy-start

commit v9 on v7

--- a/solution.py
+++ b/solution.py
@@ -24,6 +24,9 @@
 KIND_ROWS = 16
 HEAD_PAD = 48
 PER_STEP = 2
+CHUNK = 256
+ATTENTION_BYTES = 40 << 20
+ROWS_BYTES = 16 << 20
 NT = (((1,), (1,)), ((), ()))
 TN = (((0,), (0,)), ((), ()))
 
@@ -91,7 +94,7 @@
     return mm(chosen, jnp.concatenate(masked, axis=1)).astype(BF16)
 
 
-def pack_kernel(regions, capacity, cells, kinds, feats, embed, w_q, w_k, w_v, w_o, out_base, out_target, out_w):
+def pack_kernel(regions, capacity, cells, kinds, feats, embed, out_base, out_target):
     count, half = feats.shape
     owner, place, counts = positions(regions, capacity, cells[...])
     out_target[...] = owner * capacity + place
@@ -108,15 +111,15 @@
             second = counts[pair + 1 : pair + 2]
             tags = jnp.where(tag_place == 0, first, jnp.where(tag_place == 1, second, 0.0))
             out_base[r + k, capacity : capacity + TAG_ROWS, :] = tags.astype(BF16)
+
+
+def pack_cot_kernel(regions, capacity, target_ref, kinds, cot, w_q, w_k, w_v, w_o, out_cot, out_w):
+    count, half = cot.shape
     out_w[0] = w_q[...]
     out_w[1] = w_k[...]
     out_w[2] = w_v[...]
     out_w[3, 0:half, :] = w_o[:, 0:half]
     out_w[3, half:, :] = w_o[:, half:]
-
-
-def pack_cot_kernel(regions, capacity, target_ref, kinds, cot, out_cot):
-    count, half = cot.shape
     target = target_ref[...]
     owner = lax.shift_right_logical(target, log2_of(capacity))
     place = jnp.bitwise_and(target, capacity - 1)
@@ -155,15 +158,17 @@
     return jnp.where(core[0] > 0, second, first)
 
 
-def bin_rows(regions, capacity, core, marks, own, other, lift, lift_other):
-    flag = core[0] > 0
+def lift_rows(regions, capacity, core, marks, own, other, lift, lift_other):
     for r in range(regions):
         place = pl.ds(marks[core[0], r], capacity)
         lift[place, :] = own[r, 0:capacity, :].astype(F32)
         lift_other[place, :] = other[r, 0:capacity, :].astype(F32)
-    place = pl.ds(pl.multiple_of(core[0] * capacity, capacity), SLOTS)
-    rows = jnp.concatenate(ordered(flag, lift[place, :], lift_other[place, :]), axis=1)
-    filled = is_filled(regions, core, marks, iota((SLOTS, 1), 0))
+
+
+def bin_rows(regions, capacity, core, marks, lift, lift_other, first, many):
+    place = pl.ds(pl.multiple_of(core[0] * capacity, capacity) + first, many)
+    rows = jnp.concatenate(ordered(core[0] > 0, lift[place, :], lift_other[place, :]), axis=1)
+    filled = is_filled(regions, core, marks, iota((many, 1), 0) + first)
     return jnp.where(filled > 0.5, rows, 0.0).astype(BF16)
 
 
@@ -201,14 +206,6 @@
     first = gain_part[0:1, :].astype(F32)
     second = gain_part[1:2, :].astype(F32)
     extra[...] = jnp.where(place == KINDS, first, jnp.where(place == KINDS + 1, second, total)).astype(BF16)
-
-
-def pair_kernel(regions, own, received, out, gain_part):
-    share = out.shape[1]
-    for r in range(regions):
-        rows = slice(r * share, (r + 1) * share)
-        out[r] = (own[rows, :].astype(F32) + received[rows, :].astype(F32)).astype(BF16)
-    gain_part[...] = (own[regions * share :, :].astype(F32) + received[regions * share :, :].astype(F32)).astype(BF16)
 
 
 def share_kernel(regions, capacity, got, extra, packed, out, tail, sems):
@@ -315,14 +312,17 @@
         w_q, w_k, w_v, w_o = full_weights(core, w_own, w_other)
         w_out[...] = w_o
         count_rows(regions, capacity, got, marks)
-        slab = bin_rows(regions, capacity, core, marks, got, got_other, lift, lift_other)
-        slab_out[...] = slab
-        _, _, normed = norm_rows(slab, gain[...], width)
-        queries_t[...] = jnp.transpose(mm(normed, w_q)).astype(BF16)
-        k = mm(normed, w_k)
-        keys_out[...] = k.astype(BF16)
-        keys_t[...] = jnp.transpose(k).astype(BF16)
-        values_t[...] = jnp.transpose(mm(normed, w_v)).astype(BF16)
+        lift_rows(regions, capacity, core, marks, got, got_other, lift, lift_other)
+        for first in range(0, SLOTS, CHUNK):
+            rows = slice(first, first + CHUNK)
+            slab = bin_rows(regions, capacity, core, marks, lift, lift_other, first, CHUNK)
+            slab_out[rows, :] = slab
+            _, _, normed = norm_rows(slab, gain[...], width)
+            queries_t[:, rows] = jnp.transpose(mm(normed, w_q)).astype(BF16)
+            k = mm(normed, w_k)
+            keys_out[rows, :] = k.astype(BF16)
+            keys_t[:, rows] = jnp.transpose(k).astype(BF16)
+            values_t[:, rows] = jnp.transpose(mm(normed, w_v)).astype(BF16)
 
     bias = jnp.where(is_filled(regions, core, marks, iota((1, SLOTS), 1)) > 0.5, 0.0, MASKED / scale)
     for k in range(PER_STEP):
@@ -350,7 +350,7 @@
 
 def backward_kernel(
     heads, regions, capacity, core, marks, slab_in, got, got_other, w_own, w_other, gain, queries_t, keys_in, values_t, exps_in,
-    context_t, inv_t, keep_out, send_out, grad_keep, grad_send, d_context_t, d_query, d_key_t, d_value_t, grad_slab, lift, lift_other
+    context_t, inv_t, keep_out, send_out, grad_keep, grad_send, d_context_t, d_query, d_key_t, d_value_t, grad_slab, lift, lift_other, normed_t, d_low
 ):
     step = pl.program_id(0)
     width = heads * HEAD_DIM
@@ -362,8 +362,12 @@
     @pl.when(step == 0)
     def _():
         w_o = full_weights(core, w_own, w_other)[3]
-        grad_slab[...] = bin_rows(regions, capacity, core, marks, got, got_other, lift, lift_other)
-        d_context_t[...] = mm_nt(w_o, grad_slab[...]).astype(BF16)
+        lift_rows(regions, capacity, core, marks, got, got_other, lift, lift_other)
+        for first in range(0, SLOTS, CHUNK):
+            rows = slice(first, first + CHUNK)
+            part = bin_rows(regions, capacity, core, marks, lift, lift_other, first, CHUNK)
+            grad_slab[rows, :] = part
+            d_context_t[:, rows] = mm_nt(w_o, part).astype(BF16)
 
     for k in range(PER_STEP):
         h = step * PER_STEP + k
@@ -384,21 +388,27 @@
     @pl.when(step == heads // PER_STEP - 1)
     def _():
         w_q, w_k, w_v, _ = full_weights(core, w_own, w_other)
-        slab = slab_in[...]
-        wide, inverse, normed = norm_rows(slab, gain[...], width)
-        dq = d_query[...].astype(BF16)
-        dk = jnp.transpose(d_key_t[...]).astype(BF16)
-        dv = jnp.transpose(d_value_t[...]).astype(BF16)
-        d_normed = mm_nt(dq, w_q) + mm_nt(dk, w_k) + mm_nt(dv, w_v)
-        scaled = gain[...] * d_normed
-        along = jnp.sum(scaled * wide, axis=1, keepdims=True)
-        d_slab = (inverse * scaled - wide * (inverse * inverse * inverse) * along / width).astype(BF16)
-        keep_out[...] = jnp.where(flag, d_slab[:, half:], d_slab[:, :half])
-        send_out[...] = jnp.where(flag, d_slab[:, :half], d_slab[:, half:])
-        normed_t = jnp.transpose(normed.astype(F32)).astype(BF16)
+        gain_grad = jnp.zeros((1, width), F32)
+        for first in range(0, SLOTS, CHUNK):
+            rows = slice(first, first + CHUNK)
+            wide, inverse, normed = norm_rows(slab_in[rows, :], gain[...], width)
+            dq = d_query[rows, :].astype(BF16)
+            dk = jnp.transpose(d_key_t[:, rows]).astype(BF16)
+            dv = jnp.transpose(d_value_t[:, rows]).astype(BF16)
+            d_normed = mm_nt(dq, w_q) + mm_nt(dk, w_k) + mm_nt(dv, w_v)
+            scaled = gain[...] * d_normed
+            along = jnp.sum(scaled * wide, axis=1, keepdims=True)
+            d_slab = (inverse * scaled - wide * (inverse * inverse * inverse) * along / width).astype(BF16)
+            keep_out[rows, :] = jnp.where(flag, d_slab[:, half:], d_slab[:, :half])
+            send_out[rows, :] = jnp.where(flag, d_slab[:, :half], d_slab[:, half:])
+            gain_grad = gain_grad + jnp.sum(d_normed * wide * inverse, axis=0, keepdims=True)
+            normed_t[:, rows] = jnp.transpose(normed.astype(F32)).astype(BF16)
+            d_low[0, rows, :] = dq
+            d_low[1, rows, :] = dk
+            d_low[2, rows, :] = dv
         place = 0
-        for d_rows in (dq, dk, dv):
-            grad = mm(normed_t, d_rows)
+        for k in range(3):
+            grad = mm(normed_t[...], d_low[k])
             grad_keep[place : place + width, :] = jnp.where(flag, grad[:, half:], grad[:, :half]).astype(BF16)
             grad_send[place : place + width, :] = jnp.where(flag, grad[:, :half], grad[:, half:]).astype(BF16)
             place += width
@@ -408,7 +418,6 @@
             grad_keep[place : place + half, :] = jnp.where(flag, block[half:], block[:half]).astype(BF16)
             grad_send[place : place + half, :] = jnp.where(flag, block[:half], block[half:]).astype(BF16)
             place += half
-        gain_grad = jnp.sum(d_normed * wide * inverse, axis=0, keepdims=True)
         pick = iota((16, half), 0)
         block = jnp.where(pick == 0, gain_grad[:, :half], jnp.where(pick == 1, gain_grad[:, half:], 0.0))
         grad_keep[place : place + 16, :] = block.astype(BF16)
@@ -435,6 +444,7 @@
         in_specs=specs,
         out_specs=tuple(whole(x) for x in outs[: len(outs) - scalar_outs]) + (SMEM_SPEC,) * scalar_outs,
         scratch_shapes=scratch,
+        compiler_params=pltpu.CompilerParams(vmem_limit_bytes=ROWS_BYTES),
     )(*inputs)
 
 
@@ -471,16 +481,18 @@
     kinds_row = element_kinds.reshape(1, count)
     packed_shape = shape((regions, capacity, half), BF16)
     tagged_shape = shape((regions, capacity + TAG_ROWS, half), BF16)
-    packed_base, target, w_own = simple_call(
+    packed_base, target = simple_call(
         functools.partial(pack_kernel, regions, capacity),
-        (tagged_shape, shape((1, count), I32), shape((4, width, half), BF16)),
-        (bin_cells.reshape(1, count), kinds_row, features, kind_embed, w_query, w_key, w_value, w_out),
+        (tagged_shape, shape((1, count), I32)),
+        (bin_cells.reshape(1, count), kinds_row, features, kind_embed),
+    )
+    got_base = exchange(packed_base)
+    packed_cot, w_own = simple_call(
+        functools.partial(pack_cot_kernel, regions, capacity),
+        (tagged_shape, shape((4, width, half), BF16)),
+        (target, kinds_row, cotangent, w_query, w_key, w_value, w_out),
     )
     w_other = other_core(w_own)
-    got_base = exchange(packed_base)
-    (packed_cot,) = simple_call(
-        functools.partial(pack_cot_kernel, regions, capacity), (tagged_shape,), (target, kinds_row, cotangent)
-    )
     got_base, packed_cot = lax.optimization_barrier((got_base, packed_cot))
     got_cot = exchange(packed_cot)
     got_base_other = other_core(got_base)
@@ -511,6 +523,7 @@
         in_specs=[SMEM_SPEC] + [whole(x) for x in inputs[1:]],
         out_specs=tuple(exps_spec if x is exps_shape else whole(x) for x in outs[:-1]) + (SMEM_SPEC,),
         scratch_shapes=(pltpu.VMEM((width, SLOTS), BF16), pltpu.VMEM((width, width), BF16), lift, lift),
+        compiler_params=pltpu.CompilerParams(vmem_limit_bytes=ATTENTION_BYTES),
         cost_estimate=pl.CostEstimate(flops=4 * work * width, transcendentals=work, bytes_accessed=2 * work),
         name="forward",
     )(*inputs)
@@ -541,17 +554,19 @@
             pltpu.VMEM((SLOTS, width), BF16),
             lift,
             lift,
+            pltpu.VMEM((width, SLOTS), BF16),
+            pltpu.VMEM((3, SLOTS, width), BF16),
         ),
+        compiler_params=pltpu.CompilerParams(vmem_limit_bytes=ATTENTION_BYTES),
         cost_estimate=pl.CostEstimate(flops=8 * work * width, transcendentals=0, bytes_accessed=2 * work),
         name="backward",
     )(*inputs)
 
     share = 4 * width // regions
-    pairs, gain_part = simple_call(
-        functools.partial(pair_kernel, regions),
-        (shape((regions, share, half), BF16), shape((16, half), BF16)),
-        (grad_keep, other_core(grad_send)),
-    )
+    grad_other = other_core(grad_send)
+    pairs = (grad_keep[: 4 * width].astype(F32) + grad_other[: 4 * width].astype(F32)).astype(BF16)
+    pairs = pairs.reshape(regions, share, half)
+    gain_part = (grad_keep[4 * width :].astype(F32) + grad_other[4 * width :].astype(F32)).astype(BF16)
     payload_shape = shape((regions, capacity + share + KIND_ROWS, half), BF16)
     packed_grad, extra = simple_call(
         functools.partial(ungroup_grad_kernel, regions, capacity),
@@ -571,6 +586,7 @@
         out_specs=pl.BlockSpec(memory_space=pl.ANY),
         scratch_shapes=(pltpu.VMEM((share + KIND_ROWS, half), BF16), pltpu.SemaphoreType.DMA((regions,))),
         input_output_aliases={2: 0},
+        compiler_params=pltpu.CompilerParams(vmem_limit_bytes=ROWS_BYTES),
         name="share",
     )(shares, extra, packed_grad)
     home_grad = exchange(payload)

time: 144 us -> 143 us (level)
  Pallas kernels: 58.2 us -> 45.3 us
  local copies, waits for them, and re-layouts: 5.46 us -> 18.3 us
  waiting for transfers between devices: 53.3 us -> 51.2 us
    unnamed x22 -> x44, local copies, waits for them, and re-layouts: 5.46 us -> 18.3 us
    pallas_call x7 -> x6, Pallas kernels: 18.3 us -> 11.1 us  [simple_call(): pl.pallas_call(kernel, out_shape=outs, in_specs=specs, out_specs=tuple((w...]
    pallas_call x1, Pallas kernels: 17.4 us -> 14.6 us  [on_device(): pl.pallas_call(functools.partial(forward_kernel, heads, regions, capacity...]
    pallas_call x1, Pallas kernels: 20.8 us -> 18.7 us  [on_device(): pl.pallas_call(functools.partial(backward_kernel, heads, regions, capacit...]
  transfers between devices with their start and end apart: 11 -> 11, of which waited for: 7 -> 7; matrix products, arithmetic and copies ran while one was open for 0% -> 1% of each run, Pallas kernels for 35% -> 29%
where the time goes in v9:
time: 143 us; the launch traced here: 142 us
  waiting for transfers between devices  51.2 us (36%)
  Pallas kernels  45.3 us (32%)
  starting transfers between devices  25.6 us (18%)
  local copies, waits for them, and re-layouts  18.3 us (13%)
    all_to_all x5, waiting for transfers between devices, exchange(): return lax.all_to_all(x, 'region', split_axis=0, concat_axis=0, tiled=True)  47.4 us
    all_to_all x5, starting transfers between devices, exchange(): return lax.all_to_all(x, 'region', split_axis=0, concat_axis=0, tiled=True)  24.2 us
    pallas_call x1, Pallas kernels, on_device(): pl.pallas_call(functools.partial(backward_kernel, heads, regions, capacit...  18.7 us
    unnamed x44, local copies, waits for them, and re-layouts  18.3 us
    pallas_call x1, Pallas kernels, on_device(): pl.pallas_call(functools.partial(forward_kernel, heads, regions, capacity...  14.6 us
    pallas_call x6, Pallas kernels, simple_call(): pl.pallas_call(kernel, out_shape=outs, in_specs=specs, out_specs=tuple((w...  11.1 us
    ppermute x6, waiting for transfers between devices, other_core(): return lax.ppermute(x, 'head', swap)  3.86 us
  transfers between devices with their start and end apart: 11, of which 7 were waited for; matrix products, arithmetic and copies ran while one was open for 1% of the time, Pallas kernels for 29%

profile of v9, /device:TPU:0, one launch (start us, length us, event | category | flops | bytes accessed | tf_op | source)
XLA Modules:
  0.0 141.9 jit_solution(9790342982347976886)
XLA Ops:
  3.6 1.8 %shard_map.161 = (bf16[8,272,128]{2,1,0:T(8,128)(2,1)}, s32[1,1024]{1,0:T(1,128)S(1)}) custom-call(s32[1,1024]{1,0:T(1,128)S(1)} %bitcast.8, s32[1,1024]{1,0:T(1,128)S(1)} %bitcast.6, bf16[1024,128]{1,0:T(8,128)(2,1)S(1)} %copy-done, bf16[12,128]{1,0:T(8,128)(2,1)S(1)} %copy-done.9), custom_call_target="tpu_custom_call" | custom-call | tf_op jit(solution)/shard_map/pallas_call | solution.py:441
  5.4 7.3 %all-to-all-start = ((bf16[8,272,128]{2,1,0:T(8,128)(2,1)}), bf16[8,272,128]{2,1,0:T(8,128)(2,1)S(1)}, u32[]{:S(2)}, u32[]{:S(2)}) async-start(bf16[8,272,128]{2,1,0:T(8,128)(2,1)} %get-tuple-element.41), calls=%async_computation | async-start | bytes 1114112 | tf_op jit(solution)/shard_map/all_to_all | solution.py:478
  17.7 2.7 %shard_map.162 = (bf16[8,272,128]{2,1,0:T(8,128)(2,1)}, bf16[4,256,128]{2,1,0:T(8,128)(2,1)S(1)}) custom-call(s32[1,1024]{1,0:T(1,128)S(1)} %get-tuple-element.40.target_ref, s32[1,1024]{1,0:T(1,128)S(1)} %bitcast.7, bf16[1024,128]{1,0:T(8,128)(2,1)S(1)} %copy-done.1, bf16[256,128]{1,0:T(8,128)(2,1)S(1)} %copy-done.2, bf16[256,128]{1,0:T(8,128)(2,1)S(1)} %copy-done.3, ...), custom_call_target="tpu_custom_call" | custom-call | tf_op jit(solution)/shard_map/pallas_call | solution.py:441
  20.4 7.5 %all-to-all-done.got = bf16[8,272,128]{2,1,0:T(8,128)(2,1)S(1)} async-done(((bf16[8,272,128]{2,1,0:T(8,128)(2,1)}), bf16[8,272,128]{2,1,0:T(8,128)(2,1)S(1)}, u32[]{:S(2)}, u32[]{:S(2)}) %all-to-all-start) | async-done | bytes 557088 | tf_op jit(solution)/shard_map/all_to_all | solution.py:478
  27.9 3.6 %all-to-all-start.1 = ((bf16[8,272,128]{2,1,0:T(8,128)(2,1)}), bf16[8,272,128]{2,1,0:T(8,128)(2,1)S(1)}, u32[]{:S(2)}, u32[]{:S(2)}) async-start(bf16[8,272,128]{2,1,0:T(8,128)(2,1)} %get-tuple-element.43), calls=%async_computation.1 | async-start | bytes 1114112 | tf_op jit(solution)/shard_map/all_to_all | solution.py:478
  32.1 14.8 %all-to-all-done.1.got.tagged = bf16[8,272,128]{2,1,0:T(8,128)(2,1)S(1)} async-done(((bf16[8,272,128]{2,1,0:T(8,128)(2,1)}), bf16[8,272,128]{2,1,0:T(8,128)(2,1)S(1)}, u32[]{:S(2)}, u32[]{:S(2)}) %all-to-all-start.1) | async-done | bytes 557088 | tf_op jit(solution)/shard_map/all_to_all | solution.py:478
  47.6 14.6 %forward.1 = (bf16[1024,256]{1,0:T(8,128)(2,1)S(1)}, bf16[256,1024]{1,0:T(8,128)(2,1)S(1)}, bf16[1024,256]{1,0:T(8,128)(2,1)S(1)}, bf16[256,1024]{1,0:T(8,128)(2...) custom-call(s32[1]{0:T(128)} %bitcast.2.core, ...), custom_call_target="tpu_custom_call" | custom-call | flops 8589934592 | bytes 16777216 | tf_op jit(solution)/shard_map/forward/pallas_call | solution.py:519
  66.9 1.2 collective-permute-done.2.other
  68.1 1.7 %shard_map.163 = bf16[8,256,128]{2,1,0:T(8,128)(2,1)} custom-call(s32[1]{0:T(128)} %bitcast.2.core, s32[2,9]{1,0:T(2,128)S(1)} %get-tuple-element.46.marks, bf16[1024,128]{1,0:T(8,128)(2,1)S(1)} %get-tuple-element.47.own, bf16[1024,128]{1,0:T(8,128)(2,1)S(1)} %collective-permute-done.2.other), custom_call_target="tpu_custom_call" | custom-call | tf_op jit(solution)/shard_map/pallas_call | solution.py:441
  69.8 3.7 %all-to-all-start.2 = ((bf16[8,256,128]{2,1,0:T(8,128)(2,1)}), bf16[8,256,128]{2,1,0:T(8,128)(2,1)S(1)}, u32[]{:S(2)}, u32[]{:S(2)}) async-start(bf16[8,256,128]{2,1,0:T(8,128)(2,1)} %shard_map.163), calls=%async_computation.2 | async-start | bytes 1048576 | tf_op jit(solution)/shard_map/all_to_all | solution.py:478
  73.5 1.2 copy-done.13
  74.7 1.0 copy-done.15
  75.8 1.0 copy-done.17
  76.8 1.0 copy-done.19
  78.9 18.7 %backward.1 = (bf16[1024,128]{1,0:T(8,128)(2,1)S(1)}, bf16[1024,128]{1,0:T(8,128)(2,1)S(1)}, bf16[1040,128]{1,0:T(8,128)(2,1)S(1)}, bf16[1040,128]{1,0:T(8,128)(2,1)S(1)}) custom-call(s32[1]{0:T(128)} %bitcast.2.core, s32[2,9]{1,0:T(2,128)S(1)} %get-tuple-element.46.marks, bf16[1024,256]{1,0:T(8,128)(2,1)S(1)} %copy-done.15, ...), custom_call_target="tpu_custom_call" | custom-call | flops 17179869184 | bytes 16777216 | tf_op jit(solution)/shard_map/backward/pallas_call | solution.py:543
  98.1 1.2 collective-permute-done.4
  100.0 6.0 %all-to-all-start.3 = ((bf16[8,128,128]{2,1,0:T(8,128)(2,1)}), bf16[8,128,128]{2,1,0:T(8,128)(2,1)S(1)}, u32[]{:S(2)}, u32[]{:S(2)}) async-start(bf16[8,128,128]{2,1,0:T(8,128)(2,1)} %bitcast.4), calls=%async_computation.3 | async-start | bytes 524288 | tf_op jit(solution)/shard_map/all_to_all | solution.py:478
  106.0 1.5 %collective-permute-done.5.other = bf16[1024,128]{1,0:T(8,128)(2,1)S(1)} collective-permute-done((bf16[1024,128]{1,0:T(8,128)(2,1)S(1)}, bf16[1024,128]{1,0:T(8,128)(2,1)S(1)}, u32[]{:S(2)}, u32[]{:S(2)}) %collective-permute-start.5) | collective-permute-done | bytes 262176 | tf_op jit(solution)/shard_map/ppermute | solution.py:475
  107.5 1.8 %shard_map.165 = (bf16[8,400,128]{2,1,0:T(8,128)(2,1)}, bf16[16,128]{1,0:T(8,128)(2,1)S(1)}) custom-call(s32[1]{0:T(128)} %bitcast.2.core, s32[2,9]{1,0:T(2,128)S(1)} %get-tuple-element.46.marks, bf16[1024,128]{1,0:T(8,128)(2,1)S(1)} %get-tuple-element.61.own, bf16[1024,128]{1,0:T(8,128)(2,1)S(1)} %collective-permute-done.5.other, ...), custom_call_target="tpu_custom_call" | custom-call | tf_op jit(solution)/shard_map/pallas_call | solution.py:441
  109.3 5.9 %all-to-all-done.3.got = bf16[8,128,128]{2,1,0:T(8,128)(2,1)S(1)} async-done(((bf16[8,128,128]{2,1,0:T(8,128)(2,1)}), bf16[8,128,128]{2,1,0:T(8,128)(2,1)S(1)}, u32[]{:S(2)}, u32[]{:S(2)}) %all-to-all-start.3) | async-done | bytes 262176 | tf_op jit(solution)/shard_map/all_to_all | solution.py:478
  116.1 3.6 %all-to-all-start.4 = ((bf16[8,400,128]{2,1,0:T(8,128)(2,1)}), bf16[8,400,128]{2,1,0:T(8,128)(2,1)S(1)}, u32[]{:S(2)}, u32[]{:S(2)}) async-start(bf16[8,400,128]{2,1,0:T(8,128)(2,1)} %share.1), calls=%async_computation.4 | async-start | bytes 1638400 | tf_op jit(solution)/shard_map/all_to_all | solution.py:478
  119.7 1.5 %shard_map.164 = bf16[1024,128]{1,0:T(8,128)(2,1)} custom-call(s32[1,1024]{1,0:T(1,128)S(1)} %get-tuple-element.40.target_ref, bf16[8,256,128]{2,1,0:T(8,128)(2,1)S(1)} %all-to-all-done.2.got), custom_call_target="tpu_custom_call" | custom-call | tf_op jit(solution)/shard_map/pallas_call | solution.py:441
  121.2 19.2 %all-to-all-done.4.got = bf16[8,400,128]{2,1,0:T(8,128)(2,1)S(1)} async-done(((bf16[8,400,128]{2,1,0:T(8,128)(2,1)}), bf16[8,400,128]{2,1,0:T(8,128)(2,1)S(1)}, u32[]{:S(2)}, u32[]{:S(2)}) %all-to-all-start.4) | async-done | bytes 819232 | tf_op jit(solution)/shard_map/all_to_all | solution.py:478
  140.3 1.6 %shard_map.166 = (bf16[1024,128]{1,0:T(8,128)(2,1)}, f32[256,128]{1,0:T(8,128)}, f32[256,128]{1,0:T(8,128)}, f32[256,128]{1,0:T(8,128)}, f32[128,256]{1,0:T(8,12...) custom-call(s32[1,1024]{1,0:T(1,128)S(1)} %get-tuple-element.40.target_ref, bf16[8,400,128]{2,1,0:T(8,128)(2,1)S(1)} %all-to-all-done.4.got), custom_call_target="tpu_custom_call" | custom-call | tf_op jit(solution)/shard_map/pallas_call | solution.py:441
  (53 shorter events, 17.0 us)
Async XLA Ops:
  0.6 1.0 copy-start
  5.4 22.5 %all-to-all-start = ((bf16[8,272,128]{2,1,0:T(8,128)(2,1)}), bf16[8,272,128]{2,1,0:T(8,128)(2,1)S(1)}, u32[]{:S(2)}, u32[]{:S(2)}) async-start(bf16[8,272,128]{2,1,0:T(8,128)(2,1)} %get-tuple-element.41), calls=%async_computation | async-start | bytes 1114112 | tf_op jit(solution)/shard_map/all_to_all | solution.py:478
  12.7 0.9 copy-start.1
  13.7 0.8 copy-start.2
  14.5 0.8 copy-start.3
  15.4 0.8 copy-start.4
  16.2 0.8 copy-start.5
  27.9 19.0 %all-to-all-start.1 = ((bf16[8,272,128]{2,1,0:T(8,128)(2,1)}), bf16[8,272,128]{2,1,0:T(8,128)(2,1)S(1)}, u32[]{:S(2)}, u32[]{:S(2)}) async-start(bf16[8,272,128]{2,1,0:T(8,128)(2,1)} %get-tuple-element.43), calls=%async_computation.1 | async-start | bytes 1114112 | tf_op jit(solution)/shard_map/all_to_all | solution.py:478
  31.6 15.4 %collective-permute-start = (bf16[8,272,128]{2,1,0:T(8,128)(2,1)S(1)}, bf16[8,272,128]{2,1,0:T(8,128)(2,1)S(1)}, u32[]{:S(2)}, u32[]{:S(2)}) collective-permute-start(bf16[8,272,128]{2,1,0:T(8,128)(2,1)S(1)} %all-to-all-done.got), channel_id=1, source_target_pairs={{0,1},{1,0},{2,3},{3,2},{4,5},{5,4},{6,7},{7,6},{8,9},{9,8},{10,11... | collective-permute-start | bytes 1671176 | tf_op jit(solution)/shard_map/ppermute | solution.py:475
  31.6 15.3 %collective-permute-start.1 = (bf16[4,256,128]{2,1,0:T(8,128)(2,1)S(1)}, bf16[4,256,128]{2,1,0:T(8,128)(2,1)S(1)}, u32[]{:S(2)}, u32[]{:S(2)}) collective-permute-start(bf16[4,256,128]{2,1,0:T(8,128)(2,1)S(1)} %get-tuple-element.45.w_own), channel_id=1, source_target_pairs={{0,1},{1,0},{2,3},{3,2},{4,5},{5,4},{6,7},{7,6},{8,9},{9,8},{10,11... | collective-permute-start | bytes 786440 | tf_op jit(solution)/shard_map/ppermute | solution.py:475
  46.9 26.6 %collective-permute-start.3 = (bf16[8,272,128]{2,1,0:T(8,128)(2,1)S(1)}, bf16[8,272,128]{2,1,0:T(8,128)(2,1)S(1)}, u32[]{:S(2)}, u32[]{:S(2)}) collective-permute-start(bf16[8,272,128]{2,1,0:T(8,128)(2,1)S(1)} %all-to-all-done.1.got.tagged), channel_id=1, source_target_pairs={{0,1},{1,0},{2,3},{3,2},{4,5},{5,4},{6,7},{7,6},{8,9},{9,8},{10,11... | collective-permute-start | bytes 1671176 | tf_op jit(solution)/shard_map/ppermute | solution.py:475
  47.6 25.9 %copy-start.11 = (f32[256]{0:T(256)S(1)}, f32[256]{0:T(256)}, u32[]{:S(2)}) copy-start(f32[256]{0:T(256)} %param.14) | copy-start | bytes 3076
  62.2 1.0 copy-start.12
  66.4 1.7 %collective-permute-start.2 = (bf16[1024,128]{1,0:T(8,128)(2,1)S(1)}, bf16[1024,128]{1,0:T(8,128)(2,1)S(1)}, u32[]{:S(2)}, u32[]{:S(2)}) collective-permute-start(bf16[1024,128]{1,0:T(8,128)(2,1)S(1)} %get-tuple-element.48), channel_id=1, source_target_pairs={{0,1},{1,0},{2,3},{3,2},{4,5},{5,4},{6,7},{7,6},{8,9},{9,8},{10,11... | collective-permute-start | bytes 786440 | tf_op jit(solution)/shard_map/ppermute | solution.py:475
  69.8 30.2 %all-to-all-start.2 = ((bf16[8,256,128]{2,1,0:T(8,128)(2,1)}), bf16[8,256,128]{2,1,0:T(8,128)(2,1)S(1)}, u32[]{:S(2)}, u32[]{:S(2)}) async-start(bf16[8,256,128]{2,1,0:T(8,128)(2,1)} %shard_map.163), calls=%async_computation.2 | async-start | bytes 1048576 | tf_op jit(solution)/shard_map/all_to_all | solution.py:478
  73.5 1.2 copy-start.13
  74.7 1.0 copy-start.15
  75.8 1.0 copy-start.17
  76.8 1.0 copy-start.19
  77.8 1.0 copy-start.21
  97.6 1.6 %collective-permute-start.4 = (bf16[1040,128]{1,0:T(8,128)(2,1)S(1)}, bf16[1040,128]{1,0:T(8,128)(2,1)S(1)}, u32[]{:S(2)}, u32[]{:S(2)}) collective-permute-start(bf16[1040,128]{1,0:T(8,128)(2,1)S(1)} %get-tuple-element.58), channel_id=1, source_target_pairs={{0,1},{1,0},{2,3},{3,2},{4,5},{5,4},{6,7},{7,6},{8,9},{9,8},{10,11... | collective-permute-start | bytes 798728 | tf_op jit(solution)/shard_map/ppermute | solution.py:475
  100.0 15.2 %all-to-all-start.3 = ((bf16[8,128,128]{2,1,0:T(8,128)(2,1)}), bf16[8,128,128]{2,1,0:T(8,128)(2,1)S(1)}, u32[]{:S(2)}, u32[]{:S(2)}) async-start(bf16[8,128,128]{2,1,0:T(8,128)(2,1)} %bitcast.4), calls=%async_computation.3 | async-start | bytes 524288 | tf_op jit(solution)/shard_map/all_to_all | solution.py:478
  106.0 1.5 %collective-permute-start.5 = (bf16[1024,128]{1,0:T(8,128)(2,1)S(1)}, bf16[1024,128]{1,0:T(8,128)(2,1)S(1)}, u32[]{:S(2)}, u32[]{:S(2)}) collective-permute-start(bf16[1024,128]{1,0:T(8,128)(2,1)S(1)} %get-tuple-element.62), channel_id=1, source_target_pairs={{0,1},{1,0},{2,3},{3,2},{4,5},{5,4},{6,7},{7,6},{8,9},{9,8},{10,11... | collective-permute-start | bytes 786440 | tf_op jit(solution)/shard_map/ppermute | solution.py:475
  116.1 24.2 %all-to-all-start.4 = ((bf16[8,400,128]{2,1,0:T(8,128)(2,1)}), bf16[8,400,128]{2,1,0:T(8,128)(2,1)S(1)}, u32[]{:S(2)}, u32[]{:S(2)}) async-start(bf16[8,400,128]{2,1,0:T(8,128)(2,1)} %share.1), calls=%async_computation.4 | async-start | bytes 1638400 | tf_op jit(solution)/shard_map/all_to_all | solution.py:478
  (9 other events, 6.6 us)

commit v10 on v9

--- a/solution.py
+++ b/solution.py
@@ -113,8 +113,9 @@
             out_base[r + k, capacity : capacity + TAG_ROWS, :] = tags.astype(BF16)
 
 
-def pack_cot_kernel(regions, capacity, target_ref, kinds, cot, w_q, w_k, w_v, w_o, out_cot, out_w):
+def pack_cot_kernel(regions, capacity, target_ref, kinds, cot, gain, w_q, w_k, w_v, w_o, out_cot, out_w, out_gain):
     count, half = cot.shape
+    out_gain[...] = gain[...]
     out_w[0] = w_q[...]
     out_w[1] = w_k[...]
     out_w[2] = w_v[...]
@@ -297,11 +298,33 @@
     return jnp.concatenate([rows.astype(F32), tail], axis=0)
 
 
+def held_places(heads, low, wide):
+    width = heads * HEAD_DIM
+    return (
+        low.at[pl.ds(2 * width, SLOTS), pl.ds(0, width)],
+        low.at[pl.ds(0, width), :],
+        low.at[pl.ds(2 * width, SLOTS), pl.ds(width, width)],
+        low.at[pl.ds(width, width), :],
+        wide.at[pl.ds(0, width), :],
+        wide.at[pl.ds(width, heads), :],
+    )
+
+
 def forward_kernel(
-    heads, regions, capacity, core, got, got_other, w_own, w_other, gain, slab_out, queries_t, keys_out, values_t, exps_out,
-    context_t, inv_t, keep_out, send_out, marks, keys_t, w_out, lift, lift_other
+    heads, regions, capacity, core, got, got_other, w_own, w_other, gain, low_far, exps_out, wide_far,
+    keep_out, send_out, marks, keys_t, w_out, lift, lift_other, slab_out, queries_t, keys_out, values_t,
+    context_t, inv_t, sems
 ):
     step = pl.program_id(0)
+    places = held_places(heads, low_far, wide_far)
+    early = [
+        pltpu.make_async_copy(near, far, sems.at[k])
+        for k, (near, far) in enumerate(zip((slab_out, queries_t, keys_out, values_t), places[:4]))
+    ]
+    late = [
+        pltpu.make_async_copy(near, far, sems.at[4 + k])
+        for k, (near, far) in enumerate(zip((context_t, inv_t), places[4:]))
+    ]
     width = heads * HEAD_DIM
     half = width // 2
     flag = core[0] > 0
@@ -323,6 +346,8 @@
             keys_out[rows, :] = k.astype(BF16)
             keys_t[:, rows] = jnp.transpose(k).astype(BF16)
             values_t[:, rows] = jnp.transpose(mm(normed, w_v)).astype(BF16)
+        for copy in early:
+            copy.start()
 
     bias = jnp.where(is_filled(regions, core, marks, iota((1, SLOTS), 1)) > 0.5, 0.0, MASKED / scale)
     for k in range(PER_STEP):
@@ -343,16 +368,26 @@
 
     @pl.when(step == heads // PER_STEP - 1)
     def _():
+        for copy in late:
+            copy.start()
         rows_out = mm(jnp.transpose(context_t[...]).astype(BF16), w_out[...]).astype(BF16)
         keep_out[...] = jnp.where(flag, rows_out[:, half:], rows_out[:, :half])
         send_out[...] = jnp.where(flag, rows_out[:, :half], rows_out[:, half:])
+        for copy in early + late:
+            copy.wait()
 
 
 def backward_kernel(
-    heads, regions, capacity, core, marks, slab_in, got, got_other, w_own, w_other, gain, queries_t, keys_in, values_t, exps_in,
-    context_t, inv_t, keep_out, send_out, grad_keep, grad_send, d_context_t, d_query, d_key_t, d_value_t, grad_slab, lift, lift_other, normed_t, d_low
+    heads, regions, capacity, core, marks, got, got_other, w_own, w_other, gain, low_far,
+    exps_in, wide_far, keep_out, send_out, grad_keep, grad_send, d_context_t, d_query, d_key_t, d_value_t, grad_slab, lift, lift_other, normed_t, d_low,
+    slab_in, queries_t, keys_in, values_t, context_t, inv_t, sems
 ):
     step = pl.program_id(0)
+    places = held_places(heads, low_far, wide_far)
+    early = [
+        pltpu.make_async_copy(far, near, sems.at[k])
+        for k, (far, near) in enumerate(zip(places, (slab_in, queries_t, keys_in, values_t, context_t, inv_t)))
+    ]
     width = heads * HEAD_DIM
     half = width // 2
     flag = core[0] > 0
@@ -361,6 +396,8 @@
 
     @pl.when(step == 0)
     def _():
+        for copy in early:
+            copy.start()
         w_o = full_weights(core, w_own, w_other)[3]
         lift_rows(regions, capacity, core, marks, got, got_other, lift, lift_other)
         for first in range(0, SLOTS, CHUNK):
@@ -368,6 +405,8 @@
             part = bin_rows(regions, capacity, core, marks, lift, lift_other, first, CHUNK)
             grad_slab[rows, :] = part
             d_context_t[:, rows] = mm_nt(w_o, part).astype(BF16)
+        for copy in early:
+            copy.wait()
 
     for k in range(PER_STEP):
         h = step * PER_STEP + k
@@ -429,6 +468,7 @@
 
 
 SMEM_SPEC = pl.BlockSpec(memory_space=pltpu.SMEM)
+FAR_SPEC = pl.BlockSpec(memory_space=pltpu.HBM)
 
 
 def whole(array):
@@ -436,7 +476,7 @@
     return pl.BlockSpec(tuple(array.shape), lambda *_: zeros)
 
 
-def simple_call(kernel, outs, inputs, scratch=(), scalars=0, scalar_outs=0):
+def simple_call(kernel, outs, inputs, scratch=(), scalars=0, scalar_outs=0, limit=ROWS_BYTES):
     specs = [SMEM_SPEC] * scalars + [whole(x) for x in inputs[scalars:]]
     return pl.pallas_call(
         kernel,
@@ -444,7 +484,7 @@
         in_specs=specs,
         out_specs=tuple(whole(x) for x in outs[: len(outs) - scalar_outs]) + (SMEM_SPEC,) * scalar_outs,
         scratch_shapes=scratch,
-        compiler_params=pltpu.CompilerParams(vmem_limit_bytes=ROWS_BYTES),
+        compiler_params=pltpu.CompilerParams(vmem_limit_bytes=limit),
     )(*inputs)
 
 
@@ -485,12 +525,13 @@
         functools.partial(pack_kernel, regions, capacity),
         (tagged_shape, shape((1, count), I32)),
         (bin_cells.reshape(1, count), kinds_row, features, kind_embed),
+        limit=None,
     )
     got_base = exchange(packed_base)
-    packed_cot, w_own = simple_call(
+    packed_cot, w_own, gain = simple_call(
         functools.partial(pack_cot_kernel, regions, capacity),
-        (tagged_shape, shape((4, width, half), BF16)),
-        (target, kinds_row, cotangent, w_query, w_key, w_value, w_out),
+        (tagged_shape, shape((4, width, half), BF16), shape((1, width), F32)),
+        (target, kinds_row, cotangent, gain, w_query, w_key, w_value, w_out),
     )
     w_other = other_core(w_own)
     got_base, packed_cot = lax.optimization_barrier((got_base, packed_cot))
@@ -499,30 +540,35 @@
     rows_shape = shape((SLOTS, half), BF16)
     lift = pltpu.VMEM((SLOTS + capacity, half), F32)
 
-    turned_shape = shape((width, SLOTS), BF16)
+    turned = (width, SLOTS)
     exps_shape = shape((heads, SLOTS, SLOTS), BF16)
     exps_spec = pl.BlockSpec((PER_STEP, SLOTS, SLOTS), lambda h: (h, 0, 0))
     inputs = (core, got_base, got_base_other, w_own, w_other, gain)
     outs = (
-        shape((SLOTS, width), BF16),
-        turned_shape,
-        shape((SLOTS, width), BF16),
-        turned_shape,
+        shape((heads * SLOTS, SLOTS), BF16),
         exps_shape,
-        shape((width, SLOTS), F32),
-        shape((heads, SLOTS), F32),
+        shape((heads * SLOTS // 2, SLOTS), F32),
         rows_shape,
         rows_shape,
         shape((2, regions + 1), I32),
     )
     work = heads * SLOTS * SLOTS
-    slab, queries_t, keys, values_t, exps, context_t, inv_t, attn_keep, attn_send, marks = pl.pallas_call(
+    held = (
+        pltpu.VMEM((SLOTS, width), BF16),
+        pltpu.VMEM(turned, BF16),
+        pltpu.VMEM((SLOTS, width), BF16),
+        pltpu.VMEM(turned, BF16),
+        pltpu.VMEM(turned, F32),
+        pltpu.VMEM((heads, SLOTS), F32),
+        pltpu.SemaphoreType.DMA((6,)),
+    )
+    low, exps, wide, attn_keep, attn_send, marks = pl.pallas_call(
         functools.partial(forward_kernel, heads, regions, capacity),
         grid=(heads // PER_STEP,),
         out_shape=outs,
         in_specs=[SMEM_SPEC] + [whole(x) for x in inputs[1:]],
-        out_specs=tuple(exps_spec if x is exps_shape else whole(x) for x in outs[:-1]) + (SMEM_SPEC,),
-        scratch_shapes=(pltpu.VMEM((width, SLOTS), BF16), pltpu.VMEM((width, width), BF16), lift, lift),
+        out_specs=(FAR_SPEC, exps_spec, FAR_SPEC) + tuple(whole(x) for x in outs[3:5]) + (SMEM_SPEC,),
+        scratch_shapes=(pltpu.VMEM((width, SLOTS), BF16), pltpu.VMEM((width, width), BF16), lift, lift) + held,
         compiler_params=pltpu.CompilerParams(vmem_limit_bytes=ATTENTION_BYTES),
         cost_estimate=pl.CostEstimate(flops=4 * work * width, transcendentals=work, bytes_accessed=2 * work),
         name="forward",
@@ -538,13 +584,13 @@
 
     got_cot_other = other_core(got_cot)
     grad_rows = 4 * width + 16
-    inputs = (core, marks, slab, got_cot, got_cot_other, w_own, w_other, gain, queries_t, keys, values_t, exps, context_t, inv_t)
+    inputs = (core, marks, got_cot, got_cot_other, w_own, w_other, gain, low, exps, wide)
     outs = (rows_shape, rows_shape, shape((grad_rows, half), BF16), shape((grad_rows, half), BF16))
     d_keep, d_send, grad_keep, grad_send = pl.pallas_call(
         functools.partial(backward_kernel, heads, regions, capacity),
         grid=(heads // PER_STEP,),
         out_shape=outs,
-        in_specs=[SMEM_SPEC] * 2 + [exps_spec if x is exps else whole(x) for x in inputs[2:]],
+        in_specs=[SMEM_SPEC] * 2 + [whole(x) for x in inputs[2:7]] + [FAR_SPEC, exps_spec, FAR_SPEC],
         out_specs=tuple(whole(x) for x in outs),
         scratch_shapes=(
             pltpu.VMEM((width, SLOTS), BF16),
@@ -556,7 +602,8 @@
             lift,
             pltpu.VMEM((width, SLOTS), BF16),
             pltpu.VMEM((3, SLOTS, width), BF16),
-        ),
+        )
+        + held,
         compiler_params=pltpu.CompilerParams(vmem_limit_bytes=ATTENTION_BYTES),
         cost_estimate=pl.CostEstimate(flops=8 * work * width, transcendentals=0, bytes_accessed=2 * work),
         name="backward",

time: 143 us -> 133 us (0.930)
  local copies, waits for them, and re-layouts: 18.3 us -> 6.36 us
  Pallas kernels: 45.3 us -> 48.9 us
    unnamed x44 -> x18, local copies, waits for them, and re-layouts: 18.3 us -> 6.36 us
    pallas_call x1, Pallas kernels: 18.7 us -> 20.6 us  [on_device(): pl.pallas_call(functools.partial(backward_kernel, heads, regions, capacit...]
  transfers between devices with their start and end apart: 11 -> 11, of which waited for: 7 -> 7; matrix products, arithmetic and copies ran while one was open for 1% -> 1% of each run, Pallas kernels for 29% -> 33%
where the time goes in v10:
time: 133 us; the launch traced here: 132 us
  waiting for transfers between devices  49.9 us (38%)
  Pallas kernels  48.9 us (37%)
  starting transfers between devices  25.7 us (19%)
  local copies, waits for them, and re-layouts  6.36 us (5%)
    all_to_all x5, waiting for transfers between devices, exchange(): return lax.all_to_all(x, 'region', split_axis=0, concat_axis=0, tiled=True)  46 us
    all_to_all x5, starting transfers between devices, exchange(): return lax.all_to_all(x, 'region', split_axis=0, concat_axis=0, tiled=True)  24.2 us
    pallas_call x1, Pallas kernels, on_device(): pl.pallas_call(functools.partial(backward_kernel, heads, regions, capacit...  20.6 us
    pallas_call x1, Pallas kernels, on_device(): pl.pallas_call(functools.partial(forward_kernel, heads, regions, capacity...  15.3 us
    pallas_call x6, Pallas kernels, simple_call(): pl.pallas_call(kernel, out_shape=outs, in_specs=specs, out_specs=tuple((w...  12.1 us
    unnamed x18, local copies, waits for them, and re-layouts  6.36 us
    ppermute x6, waiting for transfers between devices, other_core(): return lax.ppermute(x, 'head', swap)  3.85 us
  transfers between devices with their start and end apart: 11, of which 7 were waited for; matrix products, arithmetic and copies ran while one was open for 1% of the time, Pallas kernels for 33%

profile of v10, /device:TPU:0, one launch (start us, length us, event | category | flops | bytes accessed | tf_op | source)
XLA Modules:
  0.0 132.3 jit_solution(14438800374510507196)
XLA Ops:
  0.6 2.8 %shard_map.161 = (bf16[8,272,128]{2,1,0:T(8,128)(2,1)}, s32[1,1024]{1,0:T(1,128)}) custom-call(s32[1,1024]{1,0:T(1,128)} %bitcast.9, s32[1,1024]{1,0:T(1,128)} %bitcast.6, bf16[1024,128]{1,0:T(8,128)(2,1)} %feats.1, bf16[12,128]{1,0:T(8,128)(2,1)} %embed.1), custom_call_target="tpu_custom_call" | custom-call | tf_op jit(solution)/shard_map/pallas_call | solution.py:481
  3.4 7.3 %all-to-all-start = ((bf16[8,272,128]{2,1,0:T(8,128)(2,1)}), bf16[8,272,128]{2,1,0:T(8,128)(2,1)S(1)}, u32[]{:S(2)}, u32[]{:S(2)}) async-start(bf16[8,272,128]{2,1,0:T(8,128)(2,1)} %get-tuple-element.38), calls=%async_computation | async-start | bytes 1114112 | tf_op jit(solution)/shard_map/all_to_all | solution.py:518
  10.7 0.9 copy-done
  11.7 0.8 copy-done.1
  12.5 0.8 copy-done.2
  17.1 2.7 %shard_map.162 = (bf16[8,272,128]{2,1,0:T(8,128)(2,1)}, bf16[4,256,128]{2,1,0:T(8,128)(2,1)S(1)}, f32[1,256]{1,0:T(1,128)S(1)}) custom-call(s32[1,1024]{1,0:T(1,128)S(1)} %copy-done.5, s32[1,1024]{1,0:T(1,128)S(1)} %bitcast.7, bf16[1024,128]{1,0:T(8,128)(2,1)S(1)} %copy-done, f32[1,256]{1,0:T(1,128)S(1)} %bitcast.8, bf16[256,128]{1,0:T(8,128)(2,1)S(1)} %copy-done.1, ...), custom_call_target="tpu_custom_call" | custom-call | tf_op jit(solution)/shard_map/pallas_call | solution.py:481
  19.8 6.2 %all-to-all-done.got = bf16[8,272,128]{2,1,0:T(8,128)(2,1)S(1)} async-done(((bf16[8,272,128]{2,1,0:T(8,128)(2,1)}), bf16[8,272,128]{2,1,0:T(8,128)(2,1)S(1)}, u32[]{:S(2)}, u32[]{:S(2)}) %all-to-all-start) | async-done | bytes 557088 | tf_op jit(solution)/shard_map/all_to_all | solution.py:518
  25.9 3.6 %all-to-all-start.1 = ((bf16[8,272,128]{2,1,0:T(8,128)(2,1)}), bf16[8,272,128]{2,1,0:T(8,128)(2,1)S(1)}, u32[]{:S(2)}, u32[]{:S(2)}) async-start(bf16[8,272,128]{2,1,0:T(8,128)(2,1)} %get-tuple-element.40), calls=%async_computation.1 | async-start | bytes 1114112 | tf_op jit(solution)/shard_map/all_to_all | solution.py:518
  30.1 14.8 %all-to-all-done.1.got.tagged = bf16[8,272,128]{2,1,0:T(8,128)(2,1)S(1)} async-done(((bf16[8,272,128]{2,1,0:T(8,128)(2,1)}), bf16[8,272,128]{2,1,0:T(8,128)(2,1)S(1)}, u32[]{:S(2)}, u32[]{:S(2)}) %all-to-all-start.1) | async-done | bytes 557088 | tf_op jit(solution)/shard_map/all_to_all | solution.py:518
  44.9 15.3 %forward.1 = (bf16[8192,1024]{1,0:T(8,128)(2,1)}, bf16[8,1024,1024]{2,1,0:T(8,128)(2,1)}, f32[4096,1024]{1,0:T(8,128)}, bf16[1024,128]{1,0:T(8,128)(2,1)S(1)}, b...) custom-call(s32[1]{0:T(128)} %bitcast.3.core, bf16[8,272,128]{2,1,0:T(8,128)(2,1)S(1)} %all-to-all-done.got, ...), custom_call_target="tpu_custom_call" | custom-call | flops 8589934592 | bytes 16777216 | tf_op jit(solution)/shard_map/forward/pallas_call | solution.py:565
  60.8 1.2 collective-permute-done.2.other
  62.0 1.7 %shard_map.163 = bf16[8,256,128]{2,1,0:T(8,128)(2,1)} custom-call(s32[1]{0:T(128)} %bitcast.3.core, s32[2,9]{1,0:T(2,128)S(1)} %get-tuple-element.44.marks, bf16[1024,128]{1,0:T(8,128)(2,1)S(1)} %get-tuple-element.45.own, bf16[1024,128]{1,0:T(8,128)(2,1)S(1)} %collective-permute-done.2.other), custom_call_target="tpu_custom_call" | custom-call | tf_op jit(solution)/shard_map/pallas_call | solution.py:481
  63.7 3.7 %all-to-all-start.2 = ((bf16[8,256,128]{2,1,0:T(8,128)(2,1)}), bf16[8,256,128]{2,1,0:T(8,128)(2,1)S(1)}, u32[]{:S(2)}, u32[]{:S(2)}) async-start(bf16[8,256,128]{2,1,0:T(8,128)(2,1)} %shard_map.163), calls=%async_computation.2 | async-start | bytes 1048576 | tf_op jit(solution)/shard_map/all_to_all | solution.py:518
  67.4 20.6 %backward.1 = (bf16[1024,128]{1,0:T(8,128)(2,1)S(1)}, bf16[1024,128]{1,0:T(8,128)(2,1)S(1)}, bf16[1040,128]{1,0:T(8,128)(2,1)S(1)}, bf16[1040,128]{1,0:T(8,128)(2,1)S(1)}) custom-call(s32[1]{0:T(128)} %bitcast.3.core, s32[2,9]{1,0:T(2,128)S(1)} %get-tuple-element.44.marks, bf16[8,272,128]{2,1,0:T(8,128)(2,1)S(1)} %all-to-all-done.1.got.tagged, ...), custom_call_target="tpu_custom_call" | custom-call | flops 17179869184 | bytes 16777216 | tf_op jit(solution)/shard_map/backward/pallas_call | solution.py:589
  88.4 1.2 collective-permute-done.4
  90.4 5.9 %all-to-all-start.3 = ((bf16[8,128,128]{2,1,0:T(8,128)(2,1)}), bf16[8,128,128]{2,1,0:T(8,128)(2,1)S(1)}, u32[]{:S(2)}, u32[]{:S(2)}) async-start(bf16[8,128,128]{2,1,0:T(8,128)(2,1)} %bitcast.4), calls=%async_computation.3 | async-start | bytes 524288 | tf_op jit(solution)/shard_map/all_to_all | solution.py:518
  96.3 1.5 %collective-permute-done.5.other = bf16[1024,128]{1,0:T(8,128)(2,1)S(1)} collective-permute-done((bf16[1024,128]{1,0:T(8,128)(2,1)S(1)}, bf16[1024,128]{1,0:T(8,128)(2,1)S(1)}, u32[]{:S(2)}, u32[]{:S(2)}) %collective-permute-start.5) | collective-permute-done | bytes 262176 | tf_op jit(solution)/shard_map/ppermute | solution.py:515
  97.8 1.8 %shard_map.165 = (bf16[8,400,128]{2,1,0:T(8,128)(2,1)}, bf16[16,128]{1,0:T(8,128)(2,1)S(1)}) custom-call(s32[1]{0:T(128)} %bitcast.3.core, s32[2,9]{1,0:T(2,128)S(1)} %get-tuple-element.44.marks, bf16[1024,128]{1,0:T(8,128)(2,1)S(1)} %get-tuple-element.55.own, bf16[1024,128]{1,0:T(8,128)(2,1)S(1)} %collective-permute-done.5.other, ...), custom_call_target="tpu_custom_call" | custom-call | tf_op jit(solution)/shard_map/pallas_call | solution.py:481
  99.7 5.9 %all-to-all-done.3.got = bf16[8,128,128]{2,1,0:T(8,128)(2,1)S(1)} async-done(((bf16[8,128,128]{2,1,0:T(8,128)(2,1)}), bf16[8,128,128]{2,1,0:T(8,128)(2,1)S(1)}, u32[]{:S(2)}, u32[]{:S(2)}) %all-to-all-start.3) | async-done | bytes 262176 | tf_op jit(solution)/shard_map/all_to_all | solution.py:518
  105.5 0.9 share.1
  106.4 3.6 %all-to-all-start.4 = ((bf16[8,400,128]{2,1,0:T(8,128)(2,1)}), bf16[8,400,128]{2,1,0:T(8,128)(2,1)S(1)}, u32[]{:S(2)}, u32[]{:S(2)}) async-start(bf16[8,400,128]{2,1,0:T(8,128)(2,1)} %share.1), calls=%async_computation.4 | async-start | bytes 1638400 | tf_op jit(solution)/shard_map/all_to_all | solution.py:518
  110.0 1.5 %shard_map.164 = bf16[1024,128]{1,0:T(8,128)(2,1)} custom-call(s32[1,1024]{1,0:T(1,128)S(1)} %copy-done.6, bf16[8,256,128]{2,1,0:T(8,128)(2,1)S(1)} %all-to-all-done.2.got), custom_call_target="tpu_custom_call" | custom-call | tf_op jit(solution)/shard_map/pallas_call | solution.py:481
  111.5 19.1 %all-to-all-done.4.got = bf16[8,400,128]{2,1,0:T(8,128)(2,1)S(1)} async-done(((bf16[8,400,128]{2,1,0:T(8,128)(2,1)}), bf16[8,400,128]{2,1,0:T(8,128)(2,1)S(1)}, u32[]{:S(2)}, u32[]{:S(2)}) %all-to-all-start.4) | async-done | bytes 819232 | tf_op jit(solution)/shard_map/all_to_all | solution.py:518
  130.6 1.6 %shard_map.166 = (bf16[1024,128]{1,0:T(8,128)(2,1)}, f32[256,128]{1,0:T(8,128)}, f32[256,128]{1,0:T(8,128)}, f32[256,128]{1,0:T(8,128)}, f32[128,256]{1,0:T(8,12...) custom-call(s32[1,1024]{1,0:T(1,128)S(1)} %copy-done.6, bf16[8,400,128]{2,1,0:T(8,128)(2,1)S(1)} %all-to-all-done.4.got), custom_call_target="tpu_custom_call" | custom-call | tf_op jit(solution)/shard_map/pallas_call | solution.py:481
  (27 shorter events, 6.0 us)
Async XLA Ops:
  3.4 22.5 %all-to-all-start = ((bf16[8,272,128]{2,1,0:T(8,128)(2,1)}), bf16[8,272,128]{2,1,0:T(8,128)(2,1)S(1)}, u32[]{:S(2)}, u32[]{:S(2)}) async-start(bf16[8,272,128]{2,1,0:T(8,128)(2,1)} %get-tuple-element.38), calls=%async_computation | async-start | bytes 1114112 | tf_op jit(solution)/shard_map/all_to_all | solution.py:518
  10.7 0.9 copy-start
  11.7 0.8 copy-start.1
  12.5 0.8 copy-start.2
  13.4 0.8 copy-start.3
  14.2 0.8 copy-start.4
  15.0 0.7 copy-start.5
  15.7 0.7 copy-start.7
  16.4 0.7 copy-start.8
  25.9 19.0 %all-to-all-start.1 = ((bf16[8,272,128]{2,1,0:T(8,128)(2,1)}), bf16[8,272,128]{2,1,0:T(8,128)(2,1)S(1)}, u32[]{:S(2)}, u32[]{:S(2)}) async-start(bf16[8,272,128]{2,1,0:T(8,128)(2,1)} %get-tuple-element.40), calls=%async_computation.1 | async-start | bytes 1114112 | tf_op jit(solution)/shard_map/all_to_all | solution.py:518
  29.6 15.4 %collective-permute-start = (bf16[8,272,128]{2,1,0:T(8,128)(2,1)S(1)}, bf16[8,272,128]{2,1,0:T(8,128)(2,1)S(1)}, u32[]{:S(2)}, u32[]{:S(2)}) collective-permute-start(bf16[8,272,128]{2,1,0:T(8,128)(2,1)S(1)} %all-to-all-done.got), channel_id=1, source_target_pairs={{0,1},{1,0},{2,3},{3,2},{4,5},{5,4},{6,7},{7,6},{8,9},{9,8},{10,11... | collective-permute-start | bytes 1671176 | tf_op jit(solution)/shard_map/ppermute | solution.py:515
  29.6 15.3 %collective-permute-start.1 = (bf16[4,256,128]{2,1,0:T(8,128)(2,1)S(1)}, bf16[4,256,128]{2,1,0:T(8,128)(2,1)S(1)}, u32[]{:S(2)}, u32[]{:S(2)}) collective-permute-start(bf16[4,256,128]{2,1,0:T(8,128)(2,1)S(1)} %get-tuple-element.42.w_own), channel_id=1, source_target_pairs={{0,1},{1,0},{2,3},{3,2},{4,5},{5,4},{6,7},{7,6},{8,9},{9,8},{10,11... | collective-permute-start | bytes 786440 | tf_op jit(solution)/shard_map/ppermute | solution.py:515
  44.9 22.5 %collective-permute-start.3 = (bf16[8,272,128]{2,1,0:T(8,128)(2,1)S(1)}, bf16[8,272,128]{2,1,0:T(8,128)(2,1)S(1)}, u32[]{:S(2)}, u32[]{:S(2)}) collective-permute-start(bf16[8,272,128]{2,1,0:T(8,128)(2,1)S(1)} %all-to-all-done.1.got.tagged), channel_id=1, source_target_pairs={{0,1},{1,0},{2,3},{3,2},{4,5},{5,4},{6,7},{7,6},{8,9},{9,8},{10,11... | collective-permute-start | bytes 1671176 | tf_op jit(solution)/shard_map/ppermute | solution.py:515
  60.3 1.7 %collective-permute-start.2 = (bf16[1024,128]{1,0:T(8,128)(2,1)S(1)}, bf16[1024,128]{1,0:T(8,128)(2,1)S(1)}, u32[]{:S(2)}, u32[]{:S(2)}) collective-permute-start(bf16[1024,128]{1,0:T(8,128)(2,1)S(1)} %get-tuple-element.46), channel_id=1, source_target_pairs={{0,1},{1,0},{2,3},{3,2},{4,5},{5,4},{6,7},{7,6},{8,9},{9,8},{10,11... | collective-permute-start | bytes 786440 | tf_op jit(solution)/shard_map/ppermute | solution.py:515
  63.7 26.7 %all-to-all-start.2 = ((bf16[8,256,128]{2,1,0:T(8,128)(2,1)}), bf16[8,256,128]{2,1,0:T(8,128)(2,1)S(1)}, u32[]{:S(2)}, u32[]{:S(2)}) async-start(bf16[8,256,128]{2,1,0:T(8,128)(2,1)} %shard_map.163), calls=%async_computation.2 | async-start | bytes 1048576 | tf_op jit(solution)/shard_map/all_to_all | solution.py:518
  67.4 42.6 %copy-start.6 = (s32[1,1024]{1,0:T(1,128)S(1)}, s32[1,1024]{1,0:T(1,128)}, u32[]{:S(2)}) copy-start(s32[1,1024]{1,0:T(1,128)} %get-tuple-element.37.target_ref) | copy-start | bytes 12292
  88.0 1.6 %collective-permute-start.4 = (bf16[1040,128]{1,0:T(8,128)(2,1)S(1)}, bf16[1040,128]{1,0:T(8,128)(2,1)S(1)}, u32[]{:S(2)}, u32[]{:S(2)}) collective-permute-start(bf16[1040,128]{1,0:T(8,128)(2,1)S(1)} %get-tuple-element.52), channel_id=1, source_target_pairs={{0,1},{1,0},{2,3},{3,2},{4,5},{5,4},{6,7},{7,6},{8,9},{9,8},{10,11... | collective-permute-start | bytes 798728 | tf_op jit(solution)/shard_map/ppermute | solution.py:515
  90.4 15.2 %all-to-all-start.3 = ((bf16[8,128,128]{2,1,0:T(8,128)(2,1)}), bf16[8,128,128]{2,1,0:T(8,128)(2,1)S(1)}, u32[]{:S(2)}, u32[]{:S(2)}) async-start(bf16[8,128,128]{2,1,0:T(8,128)(2,1)} %bitcast.4), calls=%async_computation.3 | async-start | bytes 524288 | tf_op jit(solution)/shard_map/all_to_all | solution.py:518
  96.3 1.5 %collective-permute-start.5 = (bf16[1024,128]{1,0:T(8,128)(2,1)S(1)}, bf16[1024,128]{1,0:T(8,128)(2,1)S(1)}, u32[]{:S(2)}, u32[]{:S(2)}) collective-permute-start(bf16[1024,128]{1,0:T(8,128)(2,1)S(1)} %get-tuple-element.56), channel_id=1, source_target_pairs={{0,1},{1,0},{2,3},{3,2},{4,5},{5,4},{6,7},{7,6},{8,9},{9,8},{10,11... | collective-permute-start | bytes 786440 | tf_op jit(solution)/shard_map/ppermute | solution.py:515
  106.4 24.2 %all-to-all-start.4 = ((bf16[8,400,128]{2,1,0:T(8,128)(2,1)}), bf16[8,400,128]{2,1,0:T(8,128)(2,1)S(1)}, u32[]{:S(2)}, u32[]{:S(2)}) async-start(bf16[8,400,128]{2,1,0:T(8,128)(2,1)} %share.1), calls=%async_computation.4 | async-start | bytes 1638400 | tf_op jit(solution)/shard_map/all_to_all | solution.py:518

commit v11 on v10

--- a/solution.py
+++ b/solution.py
@@ -311,11 +311,18 @@
 
 
 def forward_kernel(
-    heads, regions, capacity, core, got, got_other, w_own, w_other, gain, low_far, exps_out, wide_far,
+    heads, regions, capacity, core, got, got_other, w_own, w_other, gain, low_far, exps_far, wide_far,
     keep_out, send_out, marks, keys_t, w_out, lift, lift_other, slab_out, queries_t, keys_out, values_t,
-    context_t, inv_t, sems
+    context_t, inv_t, sems, exps_near, exps_sems
 ):
     step = pl.program_id(0)
+    slot = jnp.bitwise_and(step, 1)
+    steps = heads // PER_STEP
+
+    def store(at, k):
+        where = jnp.bitwise_and(at, 1)
+        return pltpu.make_async_copy(exps_near.at[where, k], exps_far.at[at * PER_STEP + k], exps_sems.at[where, k])
+
     places = held_places(heads, low_far, wide_far)
     early = [
         pltpu.make_async_copy(near, far, sems.at[k])
@@ -350,6 +357,12 @@
             copy.start()
 
     bias = jnp.where(is_filled(regions, core, marks, iota((1, SLOTS), 1)) > 0.5, 0.0, MASKED / scale)
+
+    @pl.when(step >= 2)
+    def _():
+        for k in range(PER_STEP):
+            store(step - 2, k).wait()
+
     for k in range(PER_STEP):
         h = step * PER_STEP + k
         head_rows = pl.ds(pl.multiple_of(h * HEAD_DIM, HEAD_DIM), HEAD_DIM)
@@ -360,7 +373,8 @@
         scores = mm(left, jnp.concatenate([k_rows, stack_rows(k_rows, (bias,))], axis=0).astype(BF16))
         top = jnp.max(scores, axis=1, keepdims=True)
         exps = jnp.exp2(scores - top).astype(BF16)
-        exps_out[k] = exps
+        exps_near[slot, k] = exps
+        store(step, k).start()
         summed = mm_nt(stack_rows(values_t[head_rows, :], (1.0,)).astype(BF16), exps)
         inv = 1.0 / summed[HEAD_DIM : HEAD_DIM + 1]
         context_t[head_rows, :] = summed[0:HEAD_DIM] * inv
@@ -375,6 +389,9 @@
         send_out[...] = jnp.where(flag, rows_out[:, :half], rows_out[:, half:])
         for copy in early + late:
             copy.wait()
+        for at in range(steps - 2, steps):
+            for k in range(PER_STEP):
+                store(at, k).wait()
 
 
 def backward_kernel(
@@ -396,7 +413,7 @@
 
     @pl.when(step == 0)
     def _():
-        for copy in early:
+        for copy in early[1:] + early[:1]:
             copy.start()
         w_o = full_weights(core, w_own, w_other)[3]
         lift_rows(regions, capacity, core, marks, got, got_other, lift, lift_other)
@@ -405,7 +422,7 @@
             part = bin_rows(regions, capacity, core, marks, lift, lift_other, first, CHUNK)
             grad_slab[rows, :] = part
             d_context_t[:, rows] = mm_nt(w_o, part).astype(BF16)
-        for copy in early:
+        for copy in early[1:]:
             copy.wait()
 
     for k in range(PER_STEP):
@@ -427,6 +444,7 @@
     @pl.when(step == heads // PER_STEP - 1)
     def _():
         w_q, w_k, w_v, _ = full_weights(core, w_own, w_other)
+        early[0].wait()
         gain_grad = jnp.zeros((1, width), F32)
         for first in range(0, SLOTS, CHUNK):
             rows = slice(first, first + CHUNK)
@@ -562,13 +580,14 @@
         pltpu.VMEM((heads, SLOTS), F32),
         pltpu.SemaphoreType.DMA((6,)),
     )
+    staged = (pltpu.VMEM((2, PER_STEP, SLOTS, SLOTS), BF16), pltpu.SemaphoreType.DMA((2, PER_STEP)))
     low, exps, wide, attn_keep, attn_send, marks = pl.pallas_call(
         functools.partial(forward_kernel, heads, regions, capacity),
         grid=(heads // PER_STEP,),
         out_shape=outs,
         in_specs=[SMEM_SPEC] + [whole(x) for x in inputs[1:]],
-        out_specs=(FAR_SPEC, exps_spec, FAR_SPEC) + tuple(whole(x) for x in outs[3:5]) + (SMEM_SPEC,),
-        scratch_shapes=(pltpu.VMEM((width, SLOTS), BF16), pltpu.VMEM((width, width), BF16), lift, lift) + held,
+        out_specs=(FAR_SPEC,) * 3 + tuple(whole(x) for x in outs[3:5]) + (SMEM_SPEC,),
+        scratch_shapes=(pltpu.VMEM((width, SLOTS), BF16), pltpu.VMEM((width, width), BF16), lift, lift) + held + staged,
         compiler_params=pltpu.CompilerParams(vmem_limit_bytes=ATTENTION_BYTES),
         cost_estimate=pl.CostEstimate(flops=4 * work * width, transcendentals=work, bytes_accessed=2 * work),
         name="forward",

time: 133 us -> 132 us (level)
  transfers between devices with their start and end apart: 11 -> 11, of which waited for: 7 -> 7; matrix products, arithmetic and copies ran while one was open for 1% -> 1% of each run, Pallas kernels for 33% -> 32%
where the time goes in v11:
time: 132 us; the launch traced here: 131 us
  waiting for transfers between devices  49.9 us (38%)
  Pallas kernels  48 us (36%)
  starting transfers between devices  25.7 us (19%)
  local copies, waits for them, and re-layouts  6.36 us (5%)
    all_to_all x5, waiting for transfers between devices, exchange(): return lax.all_to_all(x, 'region', split_axis=0, concat_axis=0, tiled=True)  46 us
    all_to_all x5, starting transfers between devices, exchange(): return lax.all_to_all(x, 'region', split_axis=0, concat_axis=0, tiled=True)  24.2 us
    pallas_call x1, Pallas kernels, on_device(): pl.pallas_call(functools.partial(backward_kernel, heads, regions, capacit...  20.5 us
    pallas_call x1, Pallas kernels, on_device(): pl.pallas_call(functools.partial(forward_kernel, heads, regions, capacity...  14.5 us
    pallas_call x6, Pallas kernels, simple_call(): pl.pallas_call(kernel, out_shape=outs, in_specs=specs, out_specs=tuple((w...  12.1 us
    unnamed x18, local copies, waits for them, and re-layouts  6.36 us
    ppermute x6, waiting for transfers between devices, other_core(): return lax.ppermute(x, 'head', swap)  3.86 us
  transfers between devices with their start and end apart: 11, of which 7 were waited for; matrix products, arithmetic and copies ran while one was open for 1% of the time, Pallas kernels for 32%

profile of v11, /device:TPU:0, one launch (start us, length us, event | category | flops | bytes accessed | tf_op | source)
XLA Modules:
  0.0 131.4 jit_solution(6741821331492223329)
XLA Ops:
  0.6 2.8 %shard_map.161 = (bf16[8,272,128]{2,1,0:T(8,128)(2,1)}, s32[1,1024]{1,0:T(1,128)}) custom-call(s32[1,1024]{1,0:T(1,128)} %bitcast.9, s32[1,1024]{1,0:T(1,128)} %bitcast.6, bf16[1024,128]{1,0:T(8,128)(2,1)} %feats.1, bf16[12,128]{1,0:T(8,128)(2,1)} %embed.1), custom_call_target="tpu_custom_call" | custom-call | tf_op jit(solution)/shard_map/pallas_call | solution.py:499
  3.4 7.3 %all-to-all-start = ((bf16[8,272,128]{2,1,0:T(8,128)(2,1)}), bf16[8,272,128]{2,1,0:T(8,128)(2,1)S(1)}, u32[]{:S(2)}, u32[]{:S(2)}) async-start(bf16[8,272,128]{2,1,0:T(8,128)(2,1)} %get-tuple-element.38), calls=%async_computation | async-start | bytes 1114112 | tf_op jit(solution)/shard_map/all_to_all | solution.py:536
  10.7 0.9 copy-done
  11.7 0.8 copy-done.1
  12.5 0.8 copy-done.2
  17.1 2.7 %shard_map.162 = (bf16[8,272,128]{2,1,0:T(8,128)(2,1)}, bf16[4,256,128]{2,1,0:T(8,128)(2,1)S(1)}, f32[1,256]{1,0:T(1,128)S(1)}) custom-call(s32[1,1024]{1,0:T(1,128)S(1)} %copy-done.5, s32[1,1024]{1,0:T(1,128)S(1)} %bitcast.7, bf16[1024,128]{1,0:T(8,128)(2,1)S(1)} %copy-done, f32[1,256]{1,0:T(1,128)S(1)} %bitcast.8, bf16[256,128]{1,0:T(8,128)(2,1)S(1)} %copy-done.1, ...), custom_call_target="tpu_custom_call" | custom-call | tf_op jit(solution)/shard_map/pallas_call | solution.py:499
  19.8 6.2 %all-to-all-done.got = bf16[8,272,128]{2,1,0:T(8,128)(2,1)S(1)} async-done(((bf16[8,272,128]{2,1,0:T(8,128)(2,1)}), bf16[8,272,128]{2,1,0:T(8,128)(2,1)S(1)}, u32[]{:S(2)}, u32[]{:S(2)}) %all-to-all-start) | async-done | bytes 557088 | tf_op jit(solution)/shard_map/all_to_all | solution.py:536
  25.9 3.6 %all-to-all-start.1 = ((bf16[8,272,128]{2,1,0:T(8,128)(2,1)}), bf16[8,272,128]{2,1,0:T(8,128)(2,1)S(1)}, u32[]{:S(2)}, u32[]{:S(2)}) async-start(bf16[8,272,128]{2,1,0:T(8,128)(2,1)} %get-tuple-element.40), calls=%async_computation.1 | async-start | bytes 1114112 | tf_op jit(solution)/shard_map/all_to_all | solution.py:536
  30.1 14.8 %all-to-all-done.1.got.tagged = bf16[8,272,128]{2,1,0:T(8,128)(2,1)S(1)} async-done(((bf16[8,272,128]{2,1,0:T(8,128)(2,1)}), bf16[8,272,128]{2,1,0:T(8,128)(2,1)S(1)}, u32[]{:S(2)}, u32[]{:S(2)}) %all-to-all-start.1) | async-done | bytes 557088 | tf_op jit(solution)/shard_map/all_to_all | solution.py:536
  44.9 14.5 %forward.1 = (bf16[8192,1024]{1,0:T(8,128)(2,1)}, bf16[8,1024,1024]{2,1,0:T(8,128)(2,1)}, f32[4096,1024]{1,0:T(8,128)}, bf16[1024,128]{1,0:T(8,128)(2,1)S(1)}, b...) custom-call(s32[1]{0:T(128)} %bitcast.3.core, bf16[8,272,128]{2,1,0:T(8,128)(2,1)S(1)} %all-to-all-done.got, ...), custom_call_target="tpu_custom_call" | custom-call | flops 8589934592 | bytes 16777216 | tf_op jit(solution)/shard_map/forward/pallas_call | solution.py:584
  60.0 1.2 collective-permute-done.2.other
  61.2 1.7 %shard_map.163 = bf16[8,256,128]{2,1,0:T(8,128)(2,1)} custom-call(s32[1]{0:T(128)} %bitcast.3.core, s32[2,9]{1,0:T(2,128)S(1)} %get-tuple-element.44.marks, bf16[1024,128]{1,0:T(8,128)(2,1)S(1)} %get-tuple-element.45.own, bf16[1024,128]{1,0:T(8,128)(2,1)S(1)} %collective-permute-done.2.other), custom_call_target="tpu_custom_call" | custom-call | tf_op jit(solution)/shard_map/pallas_call | solution.py:499
  62.9 3.7 %all-to-all-start.2 = ((bf16[8,256,128]{2,1,0:T(8,128)(2,1)}), bf16[8,256,128]{2,1,0:T(8,128)(2,1)S(1)}, u32[]{:S(2)}, u32[]{:S(2)}) async-start(bf16[8,256,128]{2,1,0:T(8,128)(2,1)} %shard_map.163), calls=%async_computation.2 | async-start | bytes 1048576 | tf_op jit(solution)/shard_map/all_to_all | solution.py:536
  66.6 20.5 %backward.1 = (bf16[1024,128]{1,0:T(8,128)(2,1)S(1)}, bf16[1024,128]{1,0:T(8,128)(2,1)S(1)}, bf16[1040,128]{1,0:T(8,128)(2,1)S(1)}, bf16[1040,128]{1,0:T(8,128)(2,1)S(1)}) custom-call(s32[1]{0:T(128)} %bitcast.3.core, s32[2,9]{1,0:T(2,128)S(1)} %get-tuple-element.44.marks, bf16[8,272,128]{2,1,0:T(8,128)(2,1)S(1)} %all-to-all-done.1.got.tagged, ...), custom_call_target="tpu_custom_call" | custom-call | flops 17179869184 | bytes 16777216 | tf_op jit(solution)/shard_map/backward/pallas_call | solution.py:608
  87.5 1.2 collective-permute-done.4
  89.5 5.9 %all-to-all-start.3 = ((bf16[8,128,128]{2,1,0:T(8,128)(2,1)}), bf16[8,128,128]{2,1,0:T(8,128)(2,1)S(1)}, u32[]{:S(2)}, u32[]{:S(2)}) async-start(bf16[8,128,128]{2,1,0:T(8,128)(2,1)} %bitcast.4), calls=%async_computation.3 | async-start | bytes 524288 | tf_op jit(solution)/shard_map/all_to_all | solution.py:536
  95.4 1.5 %collective-permute-done.5.other = bf16[1024,128]{1,0:T(8,128)(2,1)S(1)} collective-permute-done((bf16[1024,128]{1,0:T(8,128)(2,1)S(1)}, bf16[1024,128]{1,0:T(8,128)(2,1)S(1)}, u32[]{:S(2)}, u32[]{:S(2)}) %collective-permute-start.5) | collective-permute-done | bytes 262176 | tf_op jit(solution)/shard_map/ppermute | solution.py:533
  96.9 1.8 %shard_map.165 = (bf16[8,400,128]{2,1,0:T(8,128)(2,1)}, bf16[16,128]{1,0:T(8,128)(2,1)S(1)}) custom-call(s32[1]{0:T(128)} %bitcast.3.core, s32[2,9]{1,0:T(2,128)S(1)} %get-tuple-element.44.marks, bf16[1024,128]{1,0:T(8,128)(2,1)S(1)} %get-tuple-element.55.own, bf16[1024,128]{1,0:T(8,128)(2,1)S(1)} %collective-permute-done.5.other, ...), custom_call_target="tpu_custom_call" | custom-call | tf_op jit(solution)/shard_map/pallas_call | solution.py:499
  98.8 5.9 %all-to-all-done.3.got = bf16[8,128,128]{2,1,0:T(8,128)(2,1)S(1)} async-done(((bf16[8,128,128]{2,1,0:T(8,128)(2,1)}), bf16[8,128,128]{2,1,0:T(8,128)(2,1)S(1)}, u32[]{:S(2)}, u32[]{:S(2)}) %all-to-all-start.3) | async-done | bytes 262176 | tf_op jit(solution)/shard_map/all_to_all | solution.py:536
  104.6 0.9 share.1
  105.5 3.6 %all-to-all-start.4 = ((bf16[8,400,128]{2,1,0:T(8,128)(2,1)}), bf16[8,400,128]{2,1,0:T(8,128)(2,1)S(1)}, u32[]{:S(2)}, u32[]{:S(2)}) async-start(bf16[8,400,128]{2,1,0:T(8,128)(2,1)} %share.1), calls=%async_computation.4 | async-start | bytes 1638400 | tf_op jit(solution)/shard_map/all_to_all | solution.py:536
  109.1 1.5 %shard_map.164 = bf16[1024,128]{1,0:T(8,128)(2,1)} custom-call(s32[1,1024]{1,0:T(1,128)S(1)} %copy-done.6, bf16[8,256,128]{2,1,0:T(8,128)(2,1)S(1)} %all-to-all-done.2.got), custom_call_target="tpu_custom_call" | custom-call | tf_op jit(solution)/shard_map/pallas_call | solution.py:499
  110.6 19.1 %all-to-all-done.4.got = bf16[8,400,128]{2,1,0:T(8,128)(2,1)S(1)} async-done(((bf16[8,400,128]{2,1,0:T(8,128)(2,1)}), bf16[8,400,128]{2,1,0:T(8,128)(2,1)S(1)}, u32[]{:S(2)}, u32[]{:S(2)}) %all-to-all-start.4) | async-done | bytes 819232 | tf_op jit(solution)/shard_map/all_to_all | solution.py:536
  129.7 1.6 %shard_map.166 = (bf16[1024,128]{1,0:T(8,128)(2,1)}, f32[256,128]{1,0:T(8,128)}, f32[256,128]{1,0:T(8,128)}, f32[256,128]{1,0:T(8,128)}, f32[128,256]{1,0:T(8,12...) custom-call(s32[1,1024]{1,0:T(1,128)S(1)} %copy-done.6, bf16[8,400,128]{2,1,0:T(8,128)(2,1)S(1)} %all-to-all-done.4.got), custom_call_target="tpu_custom_call" | custom-call | tf_op jit(solution)/shard_map/pallas_call | solution.py:499
  (27 shorter events, 6.0 us)
Async XLA Ops:
  3.4 22.5 %all-to-all-start = ((bf16[8,272,128]{2,1,0:T(8,128)(2,1)}), bf16[8,272,128]{2,1,0:T(8,128)(2,1)S(1)}, u32[]{:S(2)}, u32[]{:S(2)}) async-start(bf16[8,272,128]{2,1,0:T(8,128)(2,1)} %get-tuple-element.38), calls=%async_computation | async-start | bytes 1114112 | tf_op jit(solution)/shard_map/all_to_all | solution.py:536
  10.7 0.9 copy-start
  11.7 0.8 copy-start.1
  12.5 0.8 copy-start.2
  13.4 0.8 copy-start.3
  14.2 0.8 copy-start.4
  15.0 0.7 copy-start.5
  15.7 0.7 copy-start.7
  16.4 0.7 copy-start.8
  25.9 19.0 %all-to-all-start.1 = ((bf16[8,272,128]{2,1,0:T(8,128)(2,1)}), bf16[8,272,128]{2,1,0:T(8,128)(2,1)S(1)}, u32[]{:S(2)}, u32[]{:S(2)}) async-start(bf16[8,272,128]{2,1,0:T(8,128)(2,1)} %get-tuple-element.40), calls=%async_computation.1 | async-start | bytes 1114112 | tf_op jit(solution)/shard_map/all_to_all | solution.py:536
  29.6 15.4 %collective-permute-start = (bf16[8,272,128]{2,1,0:T(8,128)(2,1)S(1)}, bf16[8,272,128]{2,1,0:T(8,128)(2,1)S(1)}, u32[]{:S(2)}, u32[]{:S(2)}) collective-permute-start(bf16[8,272,128]{2,1,0:T(8,128)(2,1)S(1)} %all-to-all-done.got), channel_id=1, source_target_pairs={{0,1},{1,0},{2,3},{3,2},{4,5},{5,4},{6,7},{7,6},{8,9},{9,8},{10,11... | collective-permute-start | bytes 1671176 | tf_op jit(solution)/shard_map/ppermute | solution.py:533
  29.6 15.3 %collective-permute-start.1 = (bf16[4,256,128]{2,1,0:T(8,128)(2,1)S(1)}, bf16[4,256,128]{2,1,0:T(8,128)(2,1)S(1)}, u32[]{:S(2)}, u32[]{:S(2)}) collective-permute-start(bf16[4,256,128]{2,1,0:T(8,128)(2,1)S(1)} %get-tuple-element.42.w_own), channel_id=1, source_target_pairs={{0,1},{1,0},{2,3},{3,2},{4,5},{5,4},{6,7},{7,6},{8,9},{9,8},{10,11... | collective-permute-start | bytes 786440 | tf_op jit(solution)/shard_map/ppermute | solution.py:533
  44.9 21.6 %collective-permute-start.3 = (bf16[8,272,128]{2,1,0:T(8,128)(2,1)S(1)}, bf16[8,272,128]{2,1,0:T(8,128)(2,1)S(1)}, u32[]{:S(2)}, u32[]{:S(2)}) collective-permute-start(bf16[8,272,128]{2,1,0:T(8,128)(2,1)S(1)} %all-to-all-done.1.got.tagged), channel_id=1, source_target_pairs={{0,1},{1,0},{2,3},{3,2},{4,5},{5,4},{6,7},{7,6},{8,9},{9,8},{10,11... | collective-permute-start | bytes 1671176 | tf_op jit(solution)/shard_map/ppermute | solution.py:533
  59.5 1.7 %collective-permute-start.2 = (bf16[1024,128]{1,0:T(8,128)(2,1)S(1)}, bf16[1024,128]{1,0:T(8,128)(2,1)S(1)}, u32[]{:S(2)}, u32[]{:S(2)}) collective-permute-start(bf16[1024,128]{1,0:T(8,128)(2,1)S(1)} %get-tuple-element.46), channel_id=1, source_target_pairs={{0,1},{1,0},{2,3},{3,2},{4,5},{5,4},{6,7},{7,6},{8,9},{9,8},{10,11... | collective-permute-start | bytes 786440 | tf_op jit(solution)/shard_map/ppermute | solution.py:533
  62.9 26.6 %all-to-all-start.2 = ((bf16[8,256,128]{2,1,0:T(8,128)(2,1)}), bf16[8,256,128]{2,1,0:T(8,128)(2,1)S(1)}, u32[]{:S(2)}, u32[]{:S(2)}) async-start(bf16[8,256,128]{2,1,0:T(8,128)(2,1)} %shard_map.163), calls=%async_computation.2 | async-start | bytes 1048576 | tf_op jit(solution)/shard_map/all_to_all | solution.py:536
  66.6 42.5 %copy-start.6 = (s32[1,1024]{1,0:T(1,128)S(1)}, s32[1,1024]{1,0:T(1,128)}, u32[]{:S(2)}) copy-start(s32[1,1024]{1,0:T(1,128)} %get-tuple-element.37.target_ref) | copy-start | bytes 12292
  87.1 1.6 %collective-permute-start.4 = (bf16[1040,128]{1,0:T(8,128)(2,1)S(1)}, bf16[1040,128]{1,0:T(8,128)(2,1)S(1)}, u32[]{:S(2)}, u32[]{:S(2)}) collective-permute-start(bf16[1040,128]{1,0:T(8,128)(2,1)S(1)} %get-tuple-element.52), channel_id=1, source_target_pairs={{0,1},{1,0},{2,3},{3,2},{4,5},{5,4},{6,7},{7,6},{8,9},{9,8},{10,11... | collective-permute-start | bytes 798728 | tf_op jit(solution)/shard_map/ppermute | solution.py:533
  89.5 15.2 %all-to-all-start.3 = ((bf16[8,128,128]{2,1,0:T(8,128)(2,1)}), bf16[8,128,128]{2,1,0:T(8,128)(2,1)S(1)}, u32[]{:S(2)}, u32[]{:S(2)}) async-start(bf16[8,128,128]{2,1,0:T(8,128)(2,1)} %bitcast.4), calls=%async_computation.3 | async-start | bytes 524288 | tf_op jit(solution)/shard_map/all_to_all | solution.py:536
  95.4 1.5 %collective-permute-start.5 = (bf16[1024,128]{1,0:T(8,128)(2,1)S(1)}, bf16[1024,128]{1,0:T(8,128)(2,1)S(1)}, u32[]{:S(2)}, u32[]{:S(2)}) collective-permute-start(bf16[1024,128]{1,0:T(8,128)(2,1)S(1)} %get-tuple-element.56), channel_id=1, source_target_pairs={{0,1},{1,0},{2,3},{3,2},{4,5},{5,4},{6,7},{7,6},{8,9},{9,8},{10,11... | collective-permute-start | bytes 786440 | tf_op jit(solution)/shard_map/ppermute | solution.py:533
  105.5 24.2 %all-to-all-start.4 = ((bf16[8,400,128]{2,1,0:T(8,128)(2,1)}), bf16[8,400,128]{2,1,0:T(8,128)(2,1)S(1)}, u32[]{:S(2)}, u32[]{:S(2)}) async-start(bf16[8,400,128]{2,1,0:T(8,128)(2,1)} %share.1), calls=%async_computation.4 | async-start | bytes 1638400 | tf_op jit(solution)/shard_map/all_to_all | solution.py:536

commit v12 on v11

--- a/solution.py
+++ b/solution.py
@@ -21,6 +21,7 @@
 I32 = jnp.int32
 LANES = 128
 TAG_ROWS = 16
+COUNT_ROWS = 8
 KIND_ROWS = 16
 HEAD_PAD = 48
 PER_STEP = 2
@@ -101,7 +102,7 @@
     kinds_hot = hot(iota((KINDS, count), 0) == kinds[...])
     base = (feats[...].astype(F32) + mm_tn(kinds_hot, embed[...])).astype(BF16)
     owner_column = turned(owner)
-    tag_place = iota((TAG_ROWS, half), 0)
+    tag_place = iota((COUNT_ROWS, half), 0)
     for r in range(0, regions, 2):
         moved = to_chunks(capacity, place, owner_column, base, r, 2)
         for k in range(2):
@@ -110,7 +111,7 @@
             first = counts[pair : pair + 1]
             second = counts[pair + 1 : pair + 2]
             tags = jnp.where(tag_place == 0, first, jnp.where(tag_place == 1, second, 0.0))
-            out_base[r + k, capacity : capacity + TAG_ROWS, :] = tags.astype(BF16)
+            out_base[r + k, capacity : capacity + COUNT_ROWS, :] = tags.astype(BF16)
 
 
 def pack_cot_kernel(regions, capacity, target_ref, kinds, cot, gain, w_q, w_k, w_v, w_o, out_cot, out_w, out_gain):
@@ -144,7 +145,7 @@
     start = jnp.int32(0)
     end = jnp.int32(SLOTS)
     for r in range(regions):
-        block = got[r, capacity : capacity + TAG_ROWS, :].astype(F32)
+        block = got[r, capacity : capacity + COUNT_ROWS, :].astype(F32)
         marks[0, r] = start
         marks[1, r] = end
         start = start + jnp.max(block[0:1, :]).astype(I32)
@@ -541,7 +542,7 @@
     tagged_shape = shape((regions, capacity + TAG_ROWS, half), BF16)
     packed_base, target = simple_call(
         functools.partial(pack_kernel, regions, capacity),
-        (tagged_shape, shape((1, count), I32)),
+        (shape((regions, capacity + COUNT_ROWS, half), BF16), shape((1, count), I32)),
         (bin_cells.reshape(1, count), kinds_row, features, kind_embed),
         limit=None,
     )

time: 132 us -> 132 us (level)
  transfers between devices with their start and end apart: 11 -> 11, of which waited for: 7 -> 7; matrix products, arithmetic and copies ran while one was open for 1% -> 1% of each run, Pallas kernels for 32% -> 33%
where the time goes in v12:
time: 132 us; the launch traced here: 131 us
  waiting for transfers between devices  49.5 us (38%)
  Pallas kernels  47.9 us (36%)
  starting transfers between devices  25.7 us (19%)
  local copies, waits for them, and re-layouts  6.36 us (5%)
    all_to_all x5, waiting for transfers between devices, exchange(): return lax.all_to_all(x, 'region', split_axis=0, concat_axis=0, tiled=True)  45.7 us
    all_to_all x5, starting transfers between devices, exchange(): return lax.all_to_all(x, 'region', split_axis=0, concat_axis=0, tiled=True)  24.2 us
    pallas_call x1, Pallas kernels, on_device(): pl.pallas_call(functools.partial(backward_kernel, heads, regions, capacit...  20.5 us
    pallas_call x1, Pallas kernels, on_device(): pl.pallas_call(functools.partial(forward_kernel, heads, regions, capacity...  14.5 us
    pallas_call x6, Pallas kernels, simple_call(): pl.pallas_call(kernel, out_shape=outs, in_specs=specs, out_specs=tuple((w...  12.1 us
    unnamed x18, local copies, waits for them, and re-layouts  6.36 us
    ppermute x6, waiting for transfers between devices, other_core(): return lax.ppermute(x, 'head', swap)  3.86 us
  transfers between devices with their start and end apart: 11, of which 7 were waited for; matrix products, arithmetic and copies ran while one was open for 1% of the time, Pallas kernels for 33%

profile of v12, /device:TPU:0, one launch (start us, length us, event | category | flops | bytes accessed | tf_op | source)
XLA Modules:
  0.0 131.0 jit_solution(18292176535000474520)
XLA Ops:
  0.6 2.8 %shard_map.161 = (bf16[8,264,128]{2,1,0:T(8,128)(2,1)}, s32[1,1024]{1,0:T(1,128)}) custom-call(s32[1,1024]{1,0:T(1,128)} %bitcast.9, s32[1,1024]{1,0:T(1,128)} %bitcast.6, bf16[1024,128]{1,0:T(8,128)(2,1)} %feats.1, bf16[12,128]{1,0:T(8,128)(2,1)} %embed.1), custom_call_target="tpu_custom_call" | custom-call | tf_op jit(solution)/shard_map/pallas_call | solution.py:500
  3.4 7.3 %all-to-all-start = ((bf16[8,264,128]{2,1,0:T(8,128)(2,1)}), bf16[8,264,128]{2,1,0:T(8,128)(2,1)S(1)}, u32[]{:S(2)}, u32[]{:S(2)}) async-start(bf16[8,264,128]{2,1,0:T(8,128)(2,1)} %get-tuple-element.38), calls=%async_computation | async-start | bytes 1081344 | tf_op jit(solution)/shard_map/all_to_all | solution.py:537
  10.7 0.9 copy-done
  11.7 0.8 copy-done.1
  12.5 0.8 copy-done.2
  17.1 2.7 %shard_map.162 = (bf16[8,272,128]{2,1,0:T(8,128)(2,1)}, bf16[4,256,128]{2,1,0:T(8,128)(2,1)S(1)}, f32[1,256]{1,0:T(1,128)S(1)}) custom-call(s32[1,1024]{1,0:T(1,128)S(1)} %copy-done.5, s32[1,1024]{1,0:T(1,128)S(1)} %bitcast.7, bf16[1024,128]{1,0:T(8,128)(2,1)S(1)} %copy-done, f32[1,256]{1,0:T(1,128)S(1)} %bitcast.8, bf16[256,128]{1,0:T(8,128)(2,1)S(1)} %copy-done.1, ...), custom_call_target="tpu_custom_call" | custom-call | tf_op jit(solution)/shard_map/pallas_call | solution.py:500
  19.7 5.8 %all-to-all-done.got = bf16[8,264,128]{2,1,0:T(8,128)(2,1)S(1)} async-done(((bf16[8,264,128]{2,1,0:T(8,128)(2,1)}), bf16[8,264,128]{2,1,0:T(8,128)(2,1)S(1)}, u32[]{:S(2)}, u32[]{:S(2)}) %all-to-all-start) | async-done | bytes 540704 | tf_op jit(solution)/shard_map/all_to_all | solution.py:537
  25.5 3.6 %all-to-all-start.1 = ((bf16[8,272,128]{2,1,0:T(8,128)(2,1)}), bf16[8,272,128]{2,1,0:T(8,128)(2,1)S(1)}, u32[]{:S(2)}, u32[]{:S(2)}) async-start(bf16[8,272,128]{2,1,0:T(8,128)(2,1)} %get-tuple-element.40), calls=%async_computation.1 | async-start | bytes 1114112 | tf_op jit(solution)/shard_map/all_to_all | solution.py:537
  29.7 14.8 %all-to-all-done.1.got.tagged = bf16[8,272,128]{2,1,0:T(8,128)(2,1)S(1)} async-done(((bf16[8,272,128]{2,1,0:T(8,128)(2,1)}), bf16[8,272,128]{2,1,0:T(8,128)(2,1)S(1)}, u32[]{:S(2)}, u32[]{:S(2)}) %all-to-all-start.1) | async-done | bytes 557088 | tf_op jit(solution)/shard_map/all_to_all | solution.py:537
  44.6 14.5 %forward.1 = (bf16[8192,1024]{1,0:T(8,128)(2,1)}, bf16[8,1024,1024]{2,1,0:T(8,128)(2,1)}, f32[4096,1024]{1,0:T(8,128)}, bf16[1024,128]{1,0:T(8,128)(2,1)S(1)}, b...) custom-call(s32[1]{0:T(128)} %bitcast.3.core, bf16[8,264,128]{2,1,0:T(8,128)(2,1)S(1)} %all-to-all-done.got, ...), custom_call_target="tpu_custom_call" | custom-call | flops 8589934592 | bytes 16777216 | tf_op jit(solution)/shard_map/forward/pallas_call | solution.py:585
  59.6 1.2 collective-permute-done.2.other
  60.8 1.7 %shard_map.163 = bf16[8,256,128]{2,1,0:T(8,128)(2,1)} custom-call(s32[1]{0:T(128)} %bitcast.3.core, s32[2,9]{1,0:T(2,128)S(1)} %get-tuple-element.44.marks, bf16[1024,128]{1,0:T(8,128)(2,1)S(1)} %get-tuple-element.45.own, bf16[1024,128]{1,0:T(8,128)(2,1)S(1)} %collective-permute-done.2.other), custom_call_target="tpu_custom_call" | custom-call | tf_op jit(solution)/shard_map/pallas_call | solution.py:500
  62.5 3.7 %all-to-all-start.2 = ((bf16[8,256,128]{2,1,0:T(8,128)(2,1)}), bf16[8,256,128]{2,1,0:T(8,128)(2,1)S(1)}, u32[]{:S(2)}, u32[]{:S(2)}) async-start(bf16[8,256,128]{2,1,0:T(8,128)(2,1)} %shard_map.163), calls=%async_computation.2 | async-start | bytes 1048576 | tf_op jit(solution)/shard_map/all_to_all | solution.py:537
  66.2 20.5 %backward.1 = (bf16[1024,128]{1,0:T(8,128)(2,1)S(1)}, bf16[1024,128]{1,0:T(8,128)(2,1)S(1)}, bf16[1040,128]{1,0:T(8,128)(2,1)S(1)}, bf16[1040,128]{1,0:T(8,128)(2,1)S(1)}) custom-call(s32[1]{0:T(128)} %bitcast.3.core, s32[2,9]{1,0:T(2,128)S(1)} %get-tuple-element.44.marks, bf16[8,272,128]{2,1,0:T(8,128)(2,1)S(1)} %all-to-all-done.1.got.tagged, ...), custom_call_target="tpu_custom_call" | custom-call | flops 17179869184 | bytes 16777216 | tf_op jit(solution)/shard_map/backward/pallas_call | solution.py:609
  87.2 1.2 collective-permute-done.4
  89.1 5.9 %all-to-all-start.3 = ((bf16[8,128,128]{2,1,0:T(8,128)(2,1)}), bf16[8,128,128]{2,1,0:T(8,128)(2,1)S(1)}, u32[]{:S(2)}, u32[]{:S(2)}) async-start(bf16[8,128,128]{2,1,0:T(8,128)(2,1)} %bitcast.4), calls=%async_computation.3 | async-start | bytes 524288 | tf_op jit(solution)/shard_map/all_to_all | solution.py:537
  95.1 1.5 %collective-permute-done.5.other = bf16[1024,128]{1,0:T(8,128)(2,1)S(1)} collective-permute-done((bf16[1024,128]{1,0:T(8,128)(2,1)S(1)}, bf16[1024,128]{1,0:T(8,128)(2,1)S(1)}, u32[]{:S(2)}, u32[]{:S(2)}) %collective-permute-start.5) | collective-permute-done | bytes 262176 | tf_op jit(solution)/shard_map/ppermute | solution.py:534
  96.6 1.8 %shard_map.165 = (bf16[8,400,128]{2,1,0:T(8,128)(2,1)}, bf16[16,128]{1,0:T(8,128)(2,1)S(1)}) custom-call(s32[1]{0:T(128)} %bitcast.3.core, s32[2,9]{1,0:T(2,128)S(1)} %get-tuple-element.44.marks, bf16[1024,128]{1,0:T(8,128)(2,1)S(1)} %get-tuple-element.55.own, bf16[1024,128]{1,0:T(8,128)(2,1)S(1)} %collective-permute-done.5.other, ...), custom_call_target="tpu_custom_call" | custom-call | tf_op jit(solution)/shard_map/pallas_call | solution.py:500
  98.4 5.9 %all-to-all-done.3.got = bf16[8,128,128]{2,1,0:T(8,128)(2,1)S(1)} async-done(((bf16[8,128,128]{2,1,0:T(8,128)(2,1)}), bf16[8,128,128]{2,1,0:T(8,128)(2,1)S(1)}, u32[]{:S(2)}, u32[]{:S(2)}) %all-to-all-start.3) | async-done | bytes 262176 | tf_op jit(solution)/shard_map/all_to_all | solution.py:537
  104.3 0.9 share.1
  105.1 3.6 %all-to-all-start.4 = ((bf16[8,400,128]{2,1,0:T(8,128)(2,1)}), bf16[8,400,128]{2,1,0:T(8,128)(2,1)S(1)}, u32[]{:S(2)}, u32[]{:S(2)}) async-start(bf16[8,400,128]{2,1,0:T(8,128)(2,1)} %share.1), calls=%async_computation.4 | async-start | bytes 1638400 | tf_op jit(solution)/shard_map/all_to_all | solution.py:537
  108.7 1.5 %shard_map.164 = bf16[1024,128]{1,0:T(8,128)(2,1)} custom-call(s32[1,1024]{1,0:T(1,128)S(1)} %copy-done.6, bf16[8,256,128]{2,1,0:T(8,128)(2,1)S(1)} %all-to-all-done.2.got), custom_call_target="tpu_custom_call" | custom-call | tf_op jit(solution)/shard_map/pallas_call | solution.py:500
  110.2 19.1 %all-to-all-done.4.got = bf16[8,400,128]{2,1,0:T(8,128)(2,1)S(1)} async-done(((bf16[8,400,128]{2,1,0:T(8,128)(2,1)}), bf16[8,400,128]{2,1,0:T(8,128)(2,1)S(1)}, u32[]{:S(2)}, u32[]{:S(2)}) %all-to-all-start.4) | async-done | bytes 819232 | tf_op jit(solution)/shard_map/all_to_all | solution.py:537
  129.4 1.6 %shard_map.166 = (bf16[1024,128]{1,0:T(8,128)(2,1)}, f32[256,128]{1,0:T(8,128)}, f32[256,128]{1,0:T(8,128)}, f32[256,128]{1,0:T(8,128)}, f32[128,256]{1,0:T(8,12...) custom-call(s32[1,1024]{1,0:T(1,128)S(1)} %copy-done.6, bf16[8,400,128]{2,1,0:T(8,128)(2,1)S(1)} %all-to-all-done.4.got), custom_call_target="tpu_custom_call" | custom-call | tf_op jit(solution)/shard_map/pallas_call | solution.py:500
  (27 shorter events, 6.0 us)
Async XLA Ops:
  3.4 22.1 %all-to-all-start = ((bf16[8,264,128]{2,1,0:T(8,128)(2,1)}), bf16[8,264,128]{2,1,0:T(8,128)(2,1)S(1)}, u32[]{:S(2)}, u32[]{:S(2)}) async-start(bf16[8,264,128]{2,1,0:T(8,128)(2,1)} %get-tuple-element.38), calls=%async_computation | async-start | bytes 1081344 | tf_op jit(solution)/shard_map/all_to_all | solution.py:537
  10.7 0.9 copy-start
  11.7 0.8 copy-start.1
  12.5 0.8 copy-start.2
  13.3 0.8 copy-start.3
  14.2 0.8 copy-start.4
  15.0 0.7 copy-start.5
  15.7 0.7 copy-start.7
  16.4 0.7 copy-start.8
  25.5 19.0 %all-to-all-start.1 = ((bf16[8,272,128]{2,1,0:T(8,128)(2,1)}), bf16[8,272,128]{2,1,0:T(8,128)(2,1)S(1)}, u32[]{:S(2)}, u32[]{:S(2)}) async-start(bf16[8,272,128]{2,1,0:T(8,128)(2,1)} %get-tuple-element.40), calls=%async_computation.1 | async-start | bytes 1114112 | tf_op jit(solution)/shard_map/all_to_all | solution.py:537
  29.2 15.4 %collective-permute-start = (bf16[8,264,128]{2,1,0:T(8,128)(2,1)S(1)}, bf16[8,264,128]{2,1,0:T(8,128)(2,1)S(1)}, u32[]{:S(2)}, u32[]{:S(2)}) collective-permute-start(bf16[8,264,128]{2,1,0:T(8,128)(2,1)S(1)} %all-to-all-done.got), channel_id=1, source_target_pairs={{0,1},{1,0},{2,3},{3,2},{4,5},{5,4},{6,7},{7,6},{8,9},{9,8},{10,11... | collective-permute-start | bytes 1622024 | tf_op jit(solution)/shard_map/ppermute | solution.py:534
  29.2 15.3 %collective-permute-start.1 = (bf16[4,256,128]{2,1,0:T(8,128)(2,1)S(1)}, bf16[4,256,128]{2,1,0:T(8,128)(2,1)S(1)}, u32[]{:S(2)}, u32[]{:S(2)}) collective-permute-start(bf16[4,256,128]{2,1,0:T(8,128)(2,1)S(1)} %get-tuple-element.42.w_own), channel_id=1, source_target_pairs={{0,1},{1,0},{2,3},{3,2},{4,5},{5,4},{6,7},{7,6},{8,9},{9,8},{10,11... | collective-permute-start | bytes 786440 | tf_op jit(solution)/shard_map/ppermute | solution.py:534
  44.6 21.6 %collective-permute-start.3 = (bf16[8,272,128]{2,1,0:T(8,128)(2,1)S(1)}, bf16[8,272,128]{2,1,0:T(8,128)(2,1)S(1)}, u32[]{:S(2)}, u32[]{:S(2)}) collective-permute-start(bf16[8,272,128]{2,1,0:T(8,128)(2,1)S(1)} %all-to-all-done.1.got.tagged), channel_id=1, source_target_pairs={{0,1},{1,0},{2,3},{3,2},{4,5},{5,4},{6,7},{7,6},{8,9},{9,8},{10,11... | collective-permute-start | bytes 1671176 | tf_op jit(solution)/shard_map/ppermute | solution.py:534
  59.1 1.7 %collective-permute-start.2 = (bf16[1024,128]{1,0:T(8,128)(2,1)S(1)}, bf16[1024,128]{1,0:T(8,128)(2,1)S(1)}, u32[]{:S(2)}, u32[]{:S(2)}) collective-permute-start(bf16[1024,128]{1,0:T(8,128)(2,1)S(1)} %get-tuple-element.46), channel_id=1, source_target_pairs={{0,1},{1,0},{2,3},{3,2},{4,5},{5,4},{6,7},{7,6},{8,9},{9,8},{10,11... | collective-permute-start | bytes 786440 | tf_op jit(solution)/shard_map/ppermute | solution.py:534
  62.5 26.6 %all-to-all-start.2 = ((bf16[8,256,128]{2,1,0:T(8,128)(2,1)}), bf16[8,256,128]{2,1,0:T(8,128)(2,1)S(1)}, u32[]{:S(2)}, u32[]{:S(2)}) async-start(bf16[8,256,128]{2,1,0:T(8,128)(2,1)} %shard_map.163), calls=%async_computation.2 | async-start | bytes 1048576 | tf_op jit(solution)/shard_map/all_to_all | solution.py:537
  66.2 42.5 %copy-start.6 = (s32[1,1024]{1,0:T(1,128)S(1)}, s32[1,1024]{1,0:T(1,128)}, u32[]{:S(2)}) copy-start(s32[1,1024]{1,0:T(1,128)} %get-tuple-element.37.target_ref) | copy-start | bytes 12292
  86.7 1.6 %collective-permute-start.4 = (bf16[1040,128]{1,0:T(8,128)(2,1)S(1)}, bf16[1040,128]{1,0:T(8,128)(2,1)S(1)}, u32[]{:S(2)}, u32[]{:S(2)}) collective-permute-start(bf16[1040,128]{1,0:T(8,128)(2,1)S(1)} %get-tuple-element.52), channel_id=1, source_target_pairs={{0,1},{1,0},{2,3},{3,2},{4,5},{5,4},{6,7},{7,6},{8,9},{9,8},{10,11... | collective-permute-start | bytes 798728 | tf_op jit(solution)/shard_map/ppermute | solution.py:534
  89.1 15.2 %all-to-all-start.3 = ((bf16[8,128,128]{2,1,0:T(8,128)(2,1)}), bf16[8,128,128]{2,1,0:T(8,128)(2,1)S(1)}, u32[]{:S(2)}, u32[]{:S(2)}) async-start(bf16[8,128,128]{2,1,0:T(8,128)(2,1)} %bitcast.4), calls=%async_computation.3 | async-start | bytes 524288 | tf_op jit(solution)/shard_map/all_to_all | solution.py:537
  95.0 1.5 %collective-permute-start.5 = (bf16[1024,128]{1,0:T(8,128)(2,1)S(1)}, bf16[1024,128]{1,0:T(8,128)(2,1)S(1)}, u32[]{:S(2)}, u32[]{:S(2)}) collective-permute-start(bf16[1024,128]{1,0:T(8,128)(2,1)S(1)} %get-tuple-element.56), channel_id=1, source_target_pairs={{0,1},{1,0},{2,3},{3,2},{4,5},{5,4},{6,7},{7,6},{8,9},{9,8},{10,11... | collective-permute-start | bytes 786440 | tf_op jit(solution)/shard_map/ppermute | solution.py:534
  105.1 24.2 %all-to-all-start.4 = ((bf16[8,400,128]{2,1,0:T(8,128)(2,1)}), bf16[8,400,128]{2,1,0:T(8,128)(2,1)S(1)}, u32[]{:S(2)}, u32[]{:S(2)}) async-start(bf16[8,400,128]{2,1,0:T(8,128)(2,1)} %share.1), calls=%async_computation.4 | async-start | bytes 1638400 | tf_op jit(solution)/shard_map/all_to_all | solution.py:537
